TPU v7x, 32 devices: a whole 2x2x4 slice. The times are simulated.
32 devices in a mesh: section: 2 (over core), dom: 8 (over z, x), cls: 2 (over y).
Axes of the slice: x: 2, y: 2, z: 4, core: 2. Of those that a mesh axis runs over, the one named last changes fastest.
Arguments:
- images: bfloat16 [1536, 128, 128], P(('dom', 'cls'), 'section'), may hold values from -6 to 6
- defocus_bin: int32 [1536], P(('dom', 'cls')), may hold values from 0 to 15
- ctf_kernels: float32 [16, 128], replicated, may hold values from -0.25 to 0.25
- band_kernel: float32 [128], replicated, may hold values from -0.25 to 0.25
- references: bfloat16 [200, 3, 128, 128], P('cls'), may hold values from -6 to 6
- rot_index: int32 [200, 3], P('cls'), may hold values from 0 to 3
- class_mask: int32 [1536, 200], P('dom', 'cls'), may hold values from 0 to 1, as said below
- noise_var: float32 [1536], P('dom'), may hold values from 20 to 200
Outputs:
- class_sums: float32 [200, 128, 128], P('cls', ('section', 'dom'))
Inputs may be any that keep to these rules, and one draw needn't show every extreme that they name: `class_mask`: every particle may join at least one class.
All inputs are finite; a program needn't handle non-finite values.
Results may differ from a plain program's by a relative error of at most 0.012.
The roundings to bfloat16 on the way count: a program that leaves them out, or rounds other values in their place, can miss the bound.
Values may be sent and summed in bfloat16 or wider, within the bound.
No kernel may reach another device: no remote copies, remote signals or barrier semaphores. Data moves between devices by JAX's collectives and lax.ppermute only.
A program may use at most 128 MiB of HBM per device.

v0:
```python
import functools

import jax
import jax.numpy as jnp
from jax import lax
from jax.experimental import pallas as pl
from jax.experimental.pallas import tpu as pltpu
from jax.sharding import PartitionSpec as P

F32 = jnp.float32
BF16 = jnp.bfloat16
LOW = -1e30
GROUP = 16
MIB = 1 << 20


def nt(a, b, precision=None):
    return lax.dot_general(
        a, b, (((1,), (1,)), ((), ())), preferred_element_type=F32, precision=precision
    )


def nn(a, b):
    return lax.dot_general(a, b, (((1,), (0,)), ((), ())), preferred_element_type=F32)


def anti_identity(width):
    rows = lax.broadcasted_iota(jnp.int32, (width, width), 0)
    cols = lax.broadcasted_iota(jnp.int32, (width, width), 1)
    return jnp.where(rows + cols == width - 1, 1.0, 0.0).astype(BF16)


def filters_kernel(ctf, ctf_rev, band, band_rev, left, right):
    bins, width = ctf.shape
    delta = jnp.where(lax.broadcasted_iota(jnp.int32, (1, width), 1) == 0, 1.0, 0.0)

    def rolled(row):
        return pltpu.roll(jnp.broadcast_to(row, (width, width)), 0, 1, stride=1, stride_axis=0)

    highest = lax.Precision.HIGHEST
    forward = nt(ctf[...] + delta, rolled(band_rev[...] + delta), highest)
    backward = nt(ctf_rev[...] + delta, rolled(band[...] + delta), highest)
    flip = anti_identity(width)
    for b in range(bins):
        a = rolled(backward[b : b + 1]).astype(BF16)
        a_t = rolled(forward[b : b + 1]).astype(BF16)
        left[b, :width] = a
        left[b, width:] = nn(flip, a).astype(BF16)
        right[b, :, :width] = a_t
        right[b, :, width:] = nn(a_t, flip).astype(BF16)


def build_filters(ctf, band):
    bins, width = ctf.shape

    def negate(v):
        return jnp.concatenate([v[:, :1], jnp.flip(v[:, 1:], 1)], axis=1)

    band = band.reshape(1, width)
    return pl.pallas_call(
        filters_kernel,
        out_shape=(
            jax.ShapeDtypeStruct((bins, 2 * width, width), BF16),
            jax.ShapeDtypeStruct((bins, width, 2 * width), BF16),
        ),
        name="filters",
    )(ctf, negate(ctf), band, negate(band))


def refs_kernel(refs, out, norm, scratch, *, padded):
    classes, rots, rows, width = refs.shape

    def block(start, count, j):
        for k in range(GROUP):
            if k < count:
                scratch[pl.ds(k * rows, rows)] = refs[start + k, j].astype(F32)
            else:
                scratch[pl.ds(k * rows, rows)] = jnp.zeros((rows, width), F32)
        at = pl.multiple_of(j * padded + start, GROUP)

        def step(r, acc):
            v = scratch[pl.ds(r, GROUP, stride=rows)]
            out[r, pl.ds(at, GROUP)] = v.astype(BF16)
            return acc + v * v

        acc = lax.fori_loop(0, rows, step, jnp.zeros((GROUP, width), F32), unroll=8)
        total = 0.5 * jnp.sum(acc, axis=1, keepdims=True)
        norm[pl.ds(at, GROUP)] = jnp.broadcast_to(total, (GROUP, width))

    full = classes // GROUP

    @pl.loop(0, full * rots)
    def _(i):
        block((i // rots) * GROUP, GROUP, i % rots)

    if classes % GROUP:

        @pl.loop(0, rots)
        def _(j):
            block(full * GROUP, classes % GROUP, j)


def lay_refs(refs, padded):
    classes, rots, rows, width = refs.shape
    return pl.pallas_call(
        functools.partial(refs_kernel, padded=padded),
        out_shape=(
            jax.ShapeDtypeStruct((rows, rots * padded, width), BF16),
            jax.ShapeDtypeStruct((rots * padded, width), F32),
        ),
        scratch_shapes=[pltpu.VMEM((GROUP * rows, width), F32)],
        compiler_params=pltpu.CompilerParams(vmem_limit_bytes=28 * MIB),
        name="refs",
    )(refs)


def filter_kernel(where, bins, mine, sib, left, right, plain, turned, scr, scr1, scr2, scr3):
    count, half, width = mine.shape
    top = where[0] == 0
    rows = lax.broadcasted_iota(jnp.int32, (width, width), 0)
    cols = lax.broadcasted_iota(jnp.int32, (width, width), 1)
    shift = where[0] * half
    target = jnp.where(rows < half, rows + shift, width - 1 - (rows - half + shift))
    pick = jnp.where(cols == target, 1.0, 0.0).astype(BF16)

    @pl.loop(0, count // GROUP)
    def _(g):
        base = pl.multiple_of(g * GROUP, GROUP)
        for i in range(GROUP):
            p = base + i
            b = bins[p]
            a = mine[p]
            o = sib[p]
            x = jnp.concatenate([jnp.where(top, a, o), jnp.where(top, o, a)], axis=0)
            cols_out = nn(x, right[b]).astype(BF16)
            both = nn(left[b], cols_out)
            scr[pl.ds(i * width, width)] = both[:width, :width]
            scr2[pl.ds(i * half, half)] = jnp.where(
                top, both[width : width + half, width:], both[width + half :, width:]
            )
            t = nt(pick, both[:, :width].astype(BF16))
            scr1[pl.ds(i * half, half)] = t[:half, width:]
            scr3[pl.ds(i * half, half)] = t[half:, :width]

        @pl.loop(0, width, unroll=8)
        def _(r):
            plain[r, pl.ds(base, GROUP)] = scr[pl.ds(r, GROUP, stride=width)].astype(BF16)

        @pl.loop(0, half, unroll=8)
        def _(r):
            turned[r, pl.ds(base, GROUP)] = scr[pl.ds(r + shift, GROUP, stride=width)].astype(BF16)
            for q, s in ((1, scr1), (2, scr2), (3, scr3)):
                turned[r, pl.ds(q * count + base, GROUP)] = s[
                    pl.ds(r, GROUP, stride=half)
                ].astype(BF16)


def filter_chunk(where, bins, mine, sib, left, right):
    count, half, width = mine.shape
    smem = pl.BlockSpec(memory_space=pltpu.SMEM)
    vmem = pl.BlockSpec(memory_space=pltpu.VMEM)
    return pl.pallas_call(
        filter_kernel,
        in_specs=[smem, smem, vmem, vmem, vmem, vmem],
        out_shape=(
            jax.ShapeDtypeStruct((2 * half, count, width), BF16),
            jax.ShapeDtypeStruct((half, 4 * count, width), BF16),
        ),
        scratch_shapes=[pltpu.VMEM((GROUP * 2 * half, width), F32)]
        + [pltpu.VMEM((GROUP * half, width), F32)] * 3,
        compiler_params=pltpu.CompilerParams(vmem_limit_bytes=24 * MIB),
        name="filter",
    )(where, bins, mine, sib, left, right)


def score_kernel(*args, parts):
    plains = args[:parts]
    refs, norm, mask, noise, scaled, stats = args[parts:]
    rows, height, width = refs.shape
    count = mask.shape[1]

    def step(i, acc):
        r = 2 * i
        lhs = jnp.concatenate([refs[r], refs[r + 1]], axis=1)
        rhs = jnp.concatenate(
            [jnp.concatenate([p[r], p[r + 1]], axis=1) for p in plains], axis=0
        )
        return acc + nt(lhs, rhs)

    inner = lax.fori_loop(0, rows // 2, step, jnp.zeros((height, count), F32), unroll=2)
    rots = height // mask.shape[0]
    allowed = jnp.concatenate([mask[...]] * rots, axis=0) > 0
    s = jnp.where(allowed, (inner - norm[:, :1]) / noise[...], LOW)
    scaled[...] = s
    peak = jnp.max(s, axis=0, keepdims=True)
    total = jnp.sum(jnp.exp(s - peak), axis=0, keepdims=True)
    stats[0:1] = peak
    stats[1:2] = total
    stats[2:] = jnp.zeros((stats.shape[0] - 2, count), F32)


def score(plains, refs, norm, mask, noise):
    count = mask.shape[1]
    height = refs.shape[1]
    return pl.pallas_call(
        functools.partial(score_kernel, parts=len(plains)),
        out_shape=(
            jax.ShapeDtypeStruct((height, count), F32),
            jax.ShapeDtypeStruct((8, count), F32),
        ),
        compiler_params=pltpu.CompilerParams(vmem_limit_bytes=28 * MIB),
        name="score",
    )(*plains, refs, norm, mask, noise)


def weights_kernel(scaled, mine, other, rot, out, *, sizes):
    rots, padded, count = rot.shape
    theirs = jnp.concatenate([other[:, count // 2 :], other[:, : count // 2]], axis=1)
    peak = jnp.maximum(mine[0:1], theirs[0:1])
    total = mine[1:2] * jnp.exp(mine[0:1] - peak) + theirs[1:2] * jnp.exp(theirs[0:1] - peak)
    w = (jnp.exp(scaled[...] - peak) / total).astype(BF16).astype(F32)
    quarters = []
    for q in range(4):
        acc = jnp.zeros((padded, count), F32)
        for j in range(rots):
            acc = acc + jnp.where(rot[j] == q, w[j * padded : (j + 1) * padded], 0.0)
        quarters.append(acc)
    pieces = []
    start = 0
    for size in sizes:
        pieces += [acc[:, start : start + size] for acc in quarters]
        start += size
    out[...] = jnp.concatenate(pieces, axis=1).astype(BF16)


def make_weights(scaled, mine, other, rot, sizes):
    rots, padded, count = rot.shape
    return pl.pallas_call(
        functools.partial(weights_kernel, sizes=sizes),
        out_shape=jax.ShapeDtypeStruct((padded, 4 * count), BF16),
        name="weights",
    )(scaled, mine, other, rot)


def sums_kernel(where, weights, *args, classes):
    turned = args[:-2]
    send, keep = args[-2:]
    rows = send.shape[1]
    parity = where[1]
    w = weights[...]
    for r in range(rows):
        rhs = jnp.concatenate(
            [jnp.concatenate([t[1 - parity, r], t[parity, r]], axis=1) for t in turned], axis=0
        )
        out = nn(w, rhs)
        width = out.shape[1] // 2
        send[0, r] = out[:classes, :width].astype(BF16)
        keep[0, r] = out[:classes, width:]


def sums(where, weights, turned, chunk, rows, classes):
    dom = turned[0].shape[0]
    width = turned[0].shape[3]
    padded = weights.shape[0]
    return pl.pallas_call(
        functools.partial(sums_kernel, classes=classes),
        grid=(dom // 2,),
        in_specs=[
            pl.BlockSpec(memory_space=pltpu.SMEM),
            pl.BlockSpec(weights.shape, lambda g: (0, 0)),
        ]
        + [
            pl.BlockSpec((2, rows, t.shape[2], width), lambda g: (g, chunk, 0, 0)) for t in turned
        ],
        out_specs=(
            pl.BlockSpec((1, rows, classes, width), lambda g: (g, 0, 0, 0)),
            pl.BlockSpec((1, rows, classes, width), lambda g: (g, 0, 0, 0)),
        ),
        out_shape=(
            jax.ShapeDtypeStruct((dom // 2, rows, classes, width), BF16),
            jax.ShapeDtypeStruct((dom // 2, rows, classes, width), F32),
        ),
        compiler_params=pltpu.CompilerParams(vmem_limit_bytes=16 * MIB),
        name="sums",
    )(where, weights, *turned)


def local(
    images, defocus_bin, ctf_kernels, band_kernel, references, rot_index, class_mask, noise_var
):
    section_at = lax.axis_index("section")
    class_at = lax.axis_index("cls")
    dom_at = lax.axis_index("dom")
    dom = lax.axis_size("dom")
    particles, half, width = images.shape
    classes, rots = rot_index.shape
    padded = -(-classes // GROUP) * GROUP
    swap = [(0, 1), (1, 0)]
    over_cls = functools.partial(lax.ppermute, axis_name="cls", perm=swap)
    over_section = functools.partial(lax.ppermute, axis_name="section", perm=swap)

    cut = particles // 2
    sizes = (particles, cut, particles - cut)
    other_bins = over_cls(defocus_bin)
    remote = [over_cls(images[:cut]), over_cls(images[cut:])]
    own_sib = over_section(images)

    where = jnp.stack([section_at, dom_at % 2]).astype(jnp.int32)
    left, right = build_filters(ctf_kernels, band_kernel)
    refs, norm = lay_refs(references, padded)

    def arranged(a):
        parts = a.reshape((2, particles) + a.shape[1:])
        return jnp.concatenate(
            [
                lax.dynamic_index_in_dim(parts, class_at, 0, False),
                lax.dynamic_index_in_dim(parts, 1 - class_at, 0, False),
            ]
        )

    mask = jnp.pad(arranged(class_mask).T, ((0, padded - classes), (0, 0)))
    noise = arranged(noise_var).reshape(1, 2 * particles)
    rot = jnp.broadcast_to(
        jnp.pad(rot_index.T, ((0, 0), (0, padded - classes)))[:, :, None],
        (rots, padded, 2 * particles),
    )

    plains, turned = [], []
    plain, turn = filter_chunk(where, defocus_bin, images, own_sib, left, right)
    plains.append(plain)
    turned.append(turn)
    start = 0
    for piece in remote:
        n = piece.shape[0]
        plain, turn = filter_chunk(
            where, other_bins[start : start + n], piece, over_section(piece), left, right
        )
        start += n
        plains.append(plain)
        turned.append(turn)

    scaled, stats = score(plains, refs, norm, mask, noise)
    weights = make_weights(scaled, stats, over_cls(stats), rot, sizes)

    block_rows = half // dom
    turned = [t.reshape(dom, block_rows, t.shape[1], width) for t in turned]
    chunks = min(2, block_rows)
    rows = block_rows // chunks
    done = []
    for c in range(chunks):
        send, keep = sums(where, weights, turned, c, rows, classes)
        got = lax.ppermute(send, "dom", [(i, i ^ 1) for i in range(dom)])
        bit = 1
        while keep.shape[0] > 1:
            kept = keep.reshape((keep.shape[0] // 2, 2) + keep.shape[1:])
            came = got.reshape(kept.shape)
            mine = (dom_at >> bit) & 1

            def pick(index):
                return lax.dynamic_index_in_dim(
                    kept, index, 1, False
                ) + lax.dynamic_index_in_dim(came, index, 1, False).astype(F32)

            send = pick(1 - mine).astype(BF16)
            keep = pick(mine)
            got = lax.ppermute(send, "dom", [(i, i ^ (1 << bit)) for i in range(dom)])
            bit += 1
        done.append(keep[0] + got[0].astype(F32))
    return jnp.transpose(jnp.concatenate(done, axis=0), (1, 0, 2))


def solution(mesh):
    return jax.shard_map(
        local,
        mesh=mesh,
        in_specs=(
            P(("dom", "cls"), "section", None),
            P(("dom", "cls")),
            P(),
            P(),
            P("cls", None, None, None),
            P("cls", None),
            P("dom", "cls"),
            P("dom"),
        ),
        out_specs=P("cls", ("section", "dom"), None),
        check_vma=False,
    )
```

profile of v0, /device:TPU:0, one launch (start us, length us, event | category | flops | bytes accessed | tf_op | source)
XLA Modules:
  0.0 239.3 jit_solution(14868291753830770153)
XLA Ops:
  0.0 2.8 %fusion.12 = (bf16[48,64,128]{2,1,0:T(8,128)(2,1)}, bf16[48,64,128]{2,1,0:T(8,128)(2,1)}) fusion(bf16[96,64,128]{2,1,0:T(8,128)(2,1)} %mine.1), kind=kLoop, calls=%fused_computation.38 | loop fusion | bytes 3145728 | tf_op jit(solution)/shard_map/slice | solution.py:305
  2.8 3.0 %collective-permute-start.2 = (bf16[48,64,128]{2,1,0:T(8,128)(2,1)}, bf16[48,64,128]{2,1,0:T(8,128)(2,1)}, u32[]{:S(2)}, u32[]{:S(2)}) collective-permute-start(bf16[48,64,128]{2,1,0:T(8,128)(2,1)} %get-tuple-element.38), channel_id=1, source_target_pairs={{0,1},{1,0},{2,3},{3,2},{4,5},{5,4},{6,7},{7,6},{8,9},{9,8},{10,11... | collective-permute-start | bytes 2359304 | tf_op jit(solution)/shard_map/ppermute | solution.py:305
  5.8 0.0 collective-permute-start.4
  5.8 2.1 collective-permute-start.1
  7.9 0.1 slice.27
  8.0 0.1 rev.9
  8.1 0.1 slice.25
  8.1 0.1 rev.8
  8.2 0.1 copy.19
  8.3 0.1 copy.20
  8.4 0.1 reshape.100
  8.5 15.9 %collective-permute-done.2.mine = bf16[48,64,128]{2,1,0:T(8,128)(2,1)} collective-permute-done((bf16[48,64,128]{2,1,0:T(8,128)(2,1)}, bf16[48,64,128]{2,1,0:T(8,128)(2,1)}, u32[]{:S(2)}, u32[]{:S(2)}) %collective-permute-start.2) | collective-permute-done | bytes 786464 | tf_op jit(solution)/shard_map/ppermute | solution.py:305
  24.5 16.0 %collective-permute-done.4.mine = bf16[48,64,128]{2,1,0:T(8,128)(2,1)} collective-permute-done((bf16[48,64,128]{2,1,0:T(8,128)(2,1)}, bf16[48,64,128]{2,1,0:T(8,128)(2,1)}, u32[]{:S(2)}, u32[]{:S(2)}) %collective-permute-start.4) | collective-permute-done | bytes 786464 | tf_op jit(solution)/shard_map/ppermute | solution.py:305
  40.5 0.1 pad_add_fusion.where
  40.6 0.1 pad_maximum_fusion.1
  40.7 0.7 pad_maximum_fusion.ctf_rev
  41.3 0.1 add_bitcast_fusion
  41.4 0.6 pad_maximum_fusion.2.band_rev
  42.0 0.0 copy-start.8
  42.0 3.8 %copy-done.8 = bf16[100,3,128,128]{3,2,1,0:T(8,128)(2,1)S(1)} copy-done((bf16[100,3,128,128]{3,2,1,0:T(8,128)(2,1)S(1)}, bf16[100,3,128,128]{3,2,1,0:T(8,128)(2,1)}, u32[]{:S(2)}) %copy-start.8) | copy-done | bytes 9830424
  45.8 18.2 %refs.2 = (bf16[128,336,128]{2,1,0:T(8,128)(2,1)S(1)}, f32[336,128]{1,0:T(8,128)S(1)}) custom-call(bf16[100,3,128,128]{3,2,1,0:T(8,128)(2,1)S(1)} %copy-done.8), custom_call_target="tpu_custom_call" | custom-call | tf_op jit(solution)/shard_map/refs/pallas_call | solution.py:105
  64.0 4.2 %copy-done.6 = bf16[128,336,128]{2,1,0:T(8,128)(2,1)} copy-done((bf16[128,336,128]{2,1,0:T(8,128)(2,1)}, bf16[128,336,128]{2,1,0:T(8,128)(2,1)S(1)}, u32[]{:S(2)}) %copy-start.6) | copy-done | bytes 11010072
  68.2 3.1 %filters.1 = (bf16[16,256,128]{2,1,0:T(8,128)(2,1)}, bf16[16,128,256]{2,1,0:T(8,128)(2,1)}) custom-call(f32[16,128]{1,0:T(8,128)} %ctf.1, f32[16,128]{1,0:T(8,128)} %pad_maximum_fusion.ctf_rev, f32[1,128]{1,0:T(1,128)} %bitcast.69, f32[1,128]{1,0:T(1,128)} %pad_maximum_fusion.2.band_rev), custom_call_target="tpu_custom_call" | custom-call | tf_op jit(solution)/shard_map/filters/pallas_call | solution.py:60
  71.2 0.1 fusion.13
  71.3 1.2 copy-done.9
  72.5 1.2 copy-done.10
  73.7 49.5 %filter.3 = (bf16[128,96,128]{2,1,0:T(8,128)(2,1)S(1)}, bf16[64,384,128]{2,1,0:T(8,128)(2,1)S(1)}) custom-call(s32[2]{0:T(128)S(1)} %pad_add_fusion.where, s32[96]{0:T(128)S(1)} %copy-done.18, bf16[96,64,128]{2,1,0:T(8,128)(2,1)S(1)} %copy-done.11, bf16[96,64,128]{2,1,0:T(8,128)(2,1)S(1)} %collective-permute-done.sib, bf16[16,256,128]{2,1,0:T(8,128)(2,1)S(1)} %copy-done.9, ...), custom_call_target="tpu_custom_call" | custom-call | tf_op jit(solution)/shard_map/filter/pallas_call | solution.py:162
  123.2 27.0 %filter.4 = (bf16[128,48,128]{2,1,0:T(8,128)(2,1)S(1)}, bf16[64,192,128]{2,1,0:T(8,128)(2,1)S(1)}) custom-call(s32[2]{0:T(128)S(1)} %pad_add_fusion.where, s32[48]{0:T(128)S(1)} %get-tuple-element.52.bins, bf16[48,64,128]{2,1,0:T(8,128)(2,1)} %collective-permute-done.2.mine, bf16[48,64,128]{2,1,0:T(8,128)(2,1)} %collective-permute-done.3.sib, ...), custom_call_target="tpu_custom_call" | custom-call | tf_op jit(solution)/shard_map/filter/pallas_call | solution.py:162
  150.3 25.8 %filter.5 = (bf16[128,48,128]{2,1,0:T(8,128)(2,1)S(1)}, bf16[64,192,128]{2,1,0:T(8,128)(2,1)S(1)}) custom-call(s32[2]{0:T(128)S(1)} %pad_add_fusion.where, s32[48]{0:T(128)S(1)} %get-tuple-element.51.bins, bf16[48,64,128]{2,1,0:T(8,128)(2,1)} %collective-permute-done.4.mine, bf16[48,64,128]{2,1,0:T(8,128)(2,1)} %collective-permute-done.5.sib, ...), custom_call_target="tpu_custom_call" | custom-call | tf_op jit(solution)/shard_map/filter/pallas_call | solution.py:162
  176.2 1.6 copy-done.3
  177.8 9.1 %score.1 = (f32[336,192]{1,0:T(8,128)S(1)}, f32[8,192]{1,0:T(8,128)S(1)}) custom-call(bf16[128,96,128]{2,1,0:T(8,128)(2,1)S(1)} %get-tuple-element.23.args_0_, bf16[128,48,128]{2,1,0:T(8,128)(2,1)S(1)} %get-tuple-element.24.args_1_, bf16[128,48,128]{2,1,0:T(8,128)(2,1)S(1)} %get-tuple-element.25.args_2_, bf16[128,336,128]{2,1,0:T(8,128)(2,1)S(1)} %copy-done.7, ...), custom_call_target="tpu_custom_call" | custom-call | tf_op jit(solution)/shard_map/score/pallas_call | solution.py:205
  186.9 0.7 copy-done.16
  187.6 1.7 collective-permute-start.6
  189.4 1.9 collective-permute-done.6.other
  191.3 0.8 broadcast_in_dim.2.rot
  192.1 2.1 weights.1
  194.2 2.8 %copy-done.1 = bf16[64,384,128]{2,1,0:T(8,128)(2,1)S(1)} copy-done((bf16[64,384,128]{2,1,0:T(8,128)(2,1)S(1)}, bf16[64,384,128]{2,1,0:T(8,128)(2,1)}, u32[]{:S(2)}) %copy-start.1) | copy-done | bytes 6291480
  197.0 1.9 copy-done.4
  198.9 0.9 copy-done.12
  199.8 3.3 %sums.2 = (bf16[4,4,100,128]{3,2,1,0:T(8,128)(2,1)}, f32[4,4,100,128]{3,2,1,0:T(8,128)S(1)}) custom-call(s32[2]{0:T(128)S(1)} %pad_add_fusion.where, bf16[112,768]{1,0:T(8,128)(2,1)S(1)} %copy-done.12, bf16[8,8,384,128]{3,2,1,0:T(8,128)(2,1)S(1)} %bitcast.53, bf16[8,8,192,128]{3,2,1,0:T(8,128)(2,1)S(1)} %bitcast.55, bf16[8,8,192,128]{3,2,1,0:T(8,128)(2,1)S(1)} %bitcast.57), custom_call_target="tpu_custom_call" | custom-call | tf_op jit(solution)/shard_map/sums/pallas_call | solution.py:265
  203.1 0.9 copy-done.14
  204.1 1.7 collective-permute-start.7
  205.8 2.8 %copy-done.2 = bf16[64,384,128]{2,1,0:T(8,128)(2,1)S(1)} copy-done((bf16[64,384,128]{2,1,0:T(8,128)(2,1)S(1)}, bf16[64,384,128]{2,1,0:T(8,128)(2,1)}, u32[]{:S(2)}) %copy-start.2) | copy-done | bytes 6291480
  208.6 1.9 copy-done.5
  210.5 2.5 %sums.3 = (bf16[4,4,100,128]{3,2,1,0:T(8,128)(2,1)S(1)}, f32[4,4,100,128]{3,2,1,0:T(8,128)S(1)}) custom-call(s32[2]{0:T(128)S(1)} %pad_add_fusion.where, bf16[112,768]{1,0:T(8,128)(2,1)S(1)} %copy-done.13, bf16[8,8,384,128]{3,2,1,0:T(8,128)(2,1)S(1)} %bitcast.54, bf16[8,8,192,128]{3,2,1,0:T(8,128)(2,1)S(1)} %bitcast.56, bf16[8,8,192,128]{3,2,1,0:T(8,128)(2,1)S(1)} %bitcast.58), custom_call_target="tpu_custom_call" | custom-call | tf_op jit(solution)/shard_map/sums/pallas_call | solution.py:265
  212.9 0.4 collective-permute-start.10
  213.3 3.0 %collective-permute-done.7 = bf16[4,4,100,128]{3,2,1,0:T(8,128)(2,1)} collective-permute-done((bf16[4,4,100,128]{3,2,1,0:T(8,128)(2,1)}, bf16[4,4,100,128]{3,2,1,0:T(8,128)(2,1)}, u32[]{:S(2)}, u32[]{:S(2)}) %collective-permute-start.7) | collective-permute-done | bytes 409632 | tf_op jit(solution)/shard_map/ppermute | solution.py:352
  216.4 0.9 constant_dynamic-slice_fusion.5
  217.3 1.0 constant_dynamic-slice_fusion.6
  218.3 0.1 fusion.2
  218.5 1.8 collective-permute-start.8
  220.3 4.2 %collective-permute-done.10 = bf16[4,4,100,128]{3,2,1,0:T(8,128)(2,1)S(1)} collective-permute-done((bf16[4,4,100,128]{3,2,1,0:T(8,128)(2,1)S(1)}, bf16[4,4,100,128]{3,2,1,0:T(8,128)(2,1)S(1)}, u32[]{:S(2)}, u32[]{:S(2)}) %collective-permute-start.10) | collective-permute-done | bytes 409632 | tf_op jit(solution)/shard_map/ppermute | solution.py:352
  224.5 0.1 constant_dynamic-slice_fusion.2
  224.6 0.1 fusion.3
  224.7 1.9 collective-permute-start.11
  226.7 0.1 fusion.7
  226.8 2.7 %collective-permute-start.9 = (bf16[1,4,100,128]{3,1,2,0:T(4,128)(2,1)S(1)}, bf16[1,4,100,128]{3,1,2,0:T(4,128)(2,1)S(1)}, u32[]{:S(2)}, u32[]{:S(2)}) collective-permute-start(bf16[1,4,100,128]{3,1,2,0:T(4,128)(2,1)S(1)} %fusion.7), channel_id=1, source_target_pairs={{0,8},{2,10},{4,12},{6,14},{8,0},{10,2},{12,4},{14,6},{1,9},{3,11}... | collective-permute-start | bytes 307208 | tf_op jit(solution)/shard_map/ppermute | solution.py:366
  229.4 3.3 %collective-permute-done.11 = bf16[2,4,100,128]{3,1,2,0:T(4,128)(2,1)S(1)} collective-permute-done((bf16[2,4,100,128]{3,1,2,0:T(4,128)(2,1)S(1)}, bf16[2,4,100,128]{3,1,2,0:T(4,128)(2,1)S(1)}, u32[]{:S(2)}, u32[]{:S(2)}) %collective-permute-start.11) | collective-permute-done | bytes 204832 | tf_op jit(solution)/shard_map/ppermute | solution.py:366
  232.7 0.1 fusion.4
  232.7 2.3 collective-permute-start.12
  235.1 0.1 fusion.9
  235.2 3.2 %collective-permute-done.12 = bf16[1,4,100,128]{3,1,2,0:T(4,128)(2,1)S(1)} collective-permute-done((bf16[1,4,100,128]{3,1,2,0:T(4,128)(2,1)S(1)}, bf16[1,4,100,128]{3,1,2,0:T(4,128)(2,1)S(1)}, u32[]{:S(2)}, u32[]{:S(2)}) %collective-permute-start.12) | collective-permute-done | bytes 102432 | tf_op jit(solution)/shard_map/ppermute | solution.py:366
  238.4 0.1 fusion.6
  238.5 0.8 maximum_bitcast_fusion
  (53 shorter events, 0.2 us)
Async XLA Ops:
  0.0 5.8 %copy-start.11 = (bf16[96,64,128]{2,1,0:T(8,128)(2,1)S(1)}, bf16[96,64,128]{2,1,0:T(8,128)(2,1)}, u32[]{:S(2)}) copy-start(bf16[96,64,128]{2,1,0:T(8,128)(2,1)} %mine.1) | copy-start | bytes 4718596
  0.0 5.8 %copy-start.18 = (s32[96]{0:T(128)S(1)}, s32[96]{0:T(128)}, u32[]{:S(2)}) copy-start(s32[96]{0:T(128)} %bins.1) | copy-start | bytes 1156
  0.0 7.9 %copy-start.24 = (f32[128]{0:T(128)S(1)}, f32[128]{0:T(128)}, u32[]{:S(2)}) copy-start(f32[128]{0:T(128)} %param.11) | copy-start | bytes 1540
  0.0 8.1 %copy-start.20 = (f32[16,128]{1,0:T(8,128)S(1)}, f32[16,128]{1,0:T(8,128)}, u32[]{:S(2)}) copy-start(f32[16,128]{1,0:T(8,128)} %ctf.1) | copy-start | bytes 24580
  0.0 8.2 %copy-start.19 = (s32[192,100]{1,0:T(8,128)S(1)}, s32[192,100]{1,0:T(8,128)}, u32[]{:S(2)}) copy-start(s32[192,100]{1,0:T(8,128)} %param.14) | copy-start | bytes 230404
  0.0 8.4 %copy-start.23 = (f32[192]{0:T(256)S(1)}, f32[192]{0:T(256)}, u32[]{:S(2)}) copy-start(f32[192]{0:T(256)} %param.15) | copy-start | bytes 2308
  2.8 21.7 %collective-permute-start.2 = (bf16[48,64,128]{2,1,0:T(8,128)(2,1)}, bf16[48,64,128]{2,1,0:T(8,128)(2,1)}, u32[]{:S(2)}, u32[]{:S(2)}) collective-permute-start(bf16[48,64,128]{2,1,0:T(8,128)(2,1)} %get-tuple-element.38), channel_id=1, source_target_pairs={{0,1},{1,0},{2,3},{3,2},{4,5},{5,4},{6,7},{7,6},{8,9},{9,8},{10,11... | collective-permute-start | bytes 2359304 | tf_op jit(solution)/shard_map/ppermute | solution.py:305
  5.8 34.7 %collective-permute-start.4 = (bf16[48,64,128]{2,1,0:T(8,128)(2,1)}, bf16[48,64,128]{2,1,0:T(8,128)(2,1)}, u32[]{:S(2)}, u32[]{:S(2)}) collective-permute-start(bf16[48,64,128]{2,1,0:T(8,128)(2,1)} %get-tuple-element.37), channel_id=1, source_target_pairs={{0,1},{1,0},{2,3},{3,2},{4,5},{5,4},{6,7},{7,6},{8,9},{9,8},{10,11... | collective-permute-start | bytes 2359304 | tf_op jit(solution)/shard_map/ppermute | solution.py:305
  5.8 65.5 %collective-permute-start = (bf16[96,64,128]{2,1,0:T(8,128)(2,1)S(1)}, bf16[96,64,128]{2,1,0:T(8,128)(2,1)S(1)}, u32[]{:S(2)}, u32[]{:S(2)}) collective-permute-start(bf16[96,64,128]{2,1,0:T(8,128)(2,1)S(1)} %copy-done.11), channel_id=1, source_target_pairs={{0,16},{16,0},{1,17},{17,1},{2,18},{18,2},{3,19},{19,3},{4,20},{20... | collective-permute-start | bytes 4718600 | tf_op jit(solution)/shard_map/ppermute | solution.py:306
  5.8 65.4 %collective-permute-start.1 = (s32[96]{0:T(128)S(1)}, s32[96]{0:T(128)S(1)}, u32[]{:S(2)}, u32[]{:S(2)}) collective-permute-start(s32[96]{0:T(128)S(1)} %copy-done.18), channel_id=1, source_target_pairs={{0,1},{1,0},{2,3},{3,2},{4,5},{5,4},{6,7},{7,6},{8,9},{9,8},{10,11... | collective-permute-start | bytes 1160 | tf_op jit(solution)/shard_map/ppermute | solution.py:304
  24.5 98.8 %collective-permute-start.3 = (bf16[48,64,128]{2,1,0:T(8,128)(2,1)}, bf16[48,64,128]{2,1,0:T(8,128)(2,1)}, u32[]{:S(2)}, u32[]{:S(2)}) collective-permute-start(bf16[48,64,128]{2,1,0:T(8,128)(2,1)} %collective-permute-done.2.mine), channel_id=1, source_target_pairs={{0,16},{16,0},{1,17},{17,1},{2,18},{18,2},{3,19},{19,3},{4,20},{20... | collective-permute-start | bytes 2359304 | tf_op jit(solution)/shard_map/ppermute | solution.py:336
  40.5 109.8 %collective-permute-start.5 = (bf16[48,64,128]{2,1,0:T(8,128)(2,1)}, bf16[48,64,128]{2,1,0:T(8,128)(2,1)}, u32[]{:S(2)}, u32[]{:S(2)}) collective-permute-start(bf16[48,64,128]{2,1,0:T(8,128)(2,1)} %collective-permute-done.4.mine), channel_id=1, source_target_pairs={{0,16},{16,0},{1,17},{17,1},{2,18},{18,2},{3,19},{19,3},{4,20},{20... | collective-permute-start | bytes 2359304 | tf_op jit(solution)/shard_map/ppermute | solution.py:336
  42.0 3.8 %copy-start.8 = (bf16[100,3,128,128]{3,2,1,0:T(8,128)(2,1)S(1)}, bf16[100,3,128,128]{3,2,1,0:T(8,128)(2,1)}, u32[]{:S(2)}) copy-start(bf16[100,3,128,128]{3,2,1,0:T(8,128)(2,1)} %refs.3) | copy-start | bytes 29491204
  64.0 4.2 %copy-start.6 = (bf16[128,336,128]{2,1,0:T(8,128)(2,1)}, bf16[128,336,128]{2,1,0:T(8,128)(2,1)S(1)}, u32[]{:S(2)}) copy-start(bf16[128,336,128]{2,1,0:T(8,128)(2,1)S(1)} %get-tuple-element.26.args_3_) | copy-start | bytes 33030148
  71.3 1.2 copy-start.9
  72.5 1.2 copy-start.10
  73.7 104.0 %copy-start.7 = (bf16[128,336,128]{2,1,0:T(8,128)(2,1)S(1)}, bf16[128,336,128]{2,1,0:T(8,128)(2,1)}, u32[]{:S(2)}) copy-start(bf16[128,336,128]{2,1,0:T(8,128)(2,1)} %copy-done.6) | copy-start | bytes 33030148
  123.2 52.9 %copy-start = (bf16[64,384,128]{2,1,0:T(8,128)(2,1)}, bf16[64,384,128]{2,1,0:T(8,128)(2,1)S(1)}, u32[]{:S(2)}) copy-start(bf16[64,384,128]{2,1,0:T(8,128)(2,1)S(1)} %get-tuple-element.30) | copy-start | bytes 18874372
  176.1 1.6 copy-start.3
  177.8 11.6 %copy-start.22 = (s32[100,3]{0,1:T(4,128)S(1)}, s32[100,3]{0,1:T(4,128)}, u32[]{:S(2)}) copy-start(s32[100,3]{0,1:T(4,128)} %param.13) | copy-start | bytes 3604
  186.9 0.7 copy-start.16
  187.6 4.5 %copy-start.17 = (f32[8,192]{1,0:T(8,128)}, f32[8,192]{1,0:T(8,128)S(1)}, u32[]{:S(2)}) copy-start(f32[8,192]{1,0:T(8,128)S(1)} %get-tuple-element.29.mine) | copy-start | bytes 18436
  187.6 3.7 %collective-permute-start.6 = (f32[8,192]{1,0:T(8,128)S(1)}, f32[8,192]{1,0:T(8,128)S(1)}, u32[]{:S(2)}, u32[]{:S(2)}) collective-permute-start(f32[8,192]{1,0:T(8,128)S(1)} %get-tuple-element.29.mine), channel_id=1, source_target_pairs={{0,1},{1,0},{2,3},{3,2},{4,5},{5,4},{6,7},{7,6},{8,9},{9,8},{10,11... | collective-permute-start | bytes 18440 | tf_op jit(solution)/shard_map/ppermute | solution.py:343
  191.3 0.8 copy-start.21
  194.2 2.8 %copy-start.1 = (bf16[64,384,128]{2,1,0:T(8,128)(2,1)S(1)}, bf16[64,384,128]{2,1,0:T(8,128)(2,1)}, u32[]{:S(2)}) copy-start(bf16[64,384,128]{2,1,0:T(8,128)(2,1)} %copy-done) | copy-start | bytes 18874372
  197.0 1.9 copy-start.4
  198.9 0.9 copy-start.12
  199.8 5.9 %copy-start.13 = (bf16[112,768]{1,0:T(8,128)(2,1)S(1)}, bf16[112,768]{1,0:T(8,128)(2,1)}, u32[]{:S(2)}) copy-start(bf16[112,768]{1,0:T(8,128)(2,1)} %weights.1) | copy-start | bytes 516100
  203.1 0.9 copy-start.14
  204.1 12.3 %collective-permute-start.7 = (bf16[4,4,100,128]{3,2,1,0:T(8,128)(2,1)}, bf16[4,4,100,128]{3,2,1,0:T(8,128)(2,1)}, u32[]{:S(2)}, u32[]{:S(2)}) collective-permute-start(bf16[4,4,100,128]{3,2,1,0:T(8,128)(2,1)} %get-tuple-element.34), channel_id=1, source_target_pairs={{0,2},{2,0},{4,6},{6,4},{8,10},{10,8},{12,14},{14,12},{1,3},{3,1},... | collective-permute-start | bytes 1228808 | tf_op jit(solution)/shard_map/ppermute | solution.py:352
  205.8 2.8 %copy-start.2 = (bf16[64,384,128]{2,1,0:T(8,128)(2,1)S(1)}, bf16[64,384,128]{2,1,0:T(8,128)(2,1)}, u32[]{:S(2)}) copy-start(bf16[64,384,128]{2,1,0:T(8,128)(2,1)} %copy-done) | copy-start | bytes 18874372
  208.6 1.9 copy-start.5
  210.4 6.9 %copy-start.15 = (f32[4,4,100,128]{3,2,1,0:T(8,128)S(1)}, f32[4,4,100,128]{3,2,1,0:T(8,128)}, u32[]{:S(2)}) copy-start(f32[4,4,100,128]{3,2,1,0:T(8,128)} %copy-done.14) | copy-start | bytes 2457604
  212.9 11.5 %collective-permute-start.10 = (bf16[4,4,100,128]{3,2,1,0:T(8,128)(2,1)S(1)}, bf16[4,4,100,128]{3,2,1,0:T(8,128)(2,1)S(1)}, u32[]{:S(2)}, u32[]{:S(2)}) collective-permute-start(bf16[4,4,100,128]{3,2,1,0:T(8,128)(2,1)S(1)} %get-tuple-element.36), channel_id=1, source_target_pairs={{0,2},{2,0},{4,6},{6,4},{8,10},{10,8},{12,14},{14,12},{1,3},{3,1},... | collective-permute-start | bytes 1228808 | tf_op jit(solution)/shard_map/ppermute | solution.py:352
  218.5 8.2 %collective-permute-start.8 = (bf16[2,4,100,128]{3,1,2,0:T(4,128)(2,1)S(1)}, bf16[2,4,100,128]{3,1,2,0:T(4,128)(2,1)S(1)}, u32[]{:S(2)}, u32[]{:S(2)}) collective-permute-start(bf16[2,4,100,128]{3,1,2,0:T(4,128)(2,1)S(1)} %fusion.2), channel_id=1, source_target_pairs={{0,4},{2,6},{4,0},{6,2},{8,12},{10,14},{12,8},{14,10},{1,5},{3,7},... | collective-permute-start | bytes 614408 | tf_op jit(solution)/shard_map/ppermute | solution.py:366
  224.7 7.9 %collective-permute-start.11 = (bf16[2,4,100,128]{3,1,2,0:T(4,128)(2,1)S(1)}, bf16[2,4,100,128]{3,1,2,0:T(4,128)(2,1)S(1)}, u32[]{:S(2)}, u32[]{:S(2)}) collective-permute-start(bf16[2,4,100,128]{3,1,2,0:T(4,128)(2,1)S(1)} %fusion.3), channel_id=1, source_target_pairs={{0,4},{2,6},{4,0},{6,2},{8,12},{10,14},{12,8},{14,10},{1,5},{3,7},... | collective-permute-start | bytes 614408 | tf_op jit(solution)/shard_map/ppermute | solution.py:366
  226.8 8.3 %collective-permute-start.9 = (bf16[1,4,100,128]{3,1,2,0:T(4,128)(2,1)S(1)}, bf16[1,4,100,128]{3,1,2,0:T(4,128)(2,1)S(1)}, u32[]{:S(2)}, u32[]{:S(2)}) collective-permute-start(bf16[1,4,100,128]{3,1,2,0:T(4,128)(2,1)S(1)} %fusion.7), channel_id=1, source_target_pairs={{0,8},{2,10},{4,12},{6,14},{8,0},{10,2},{12,4},{14,6},{1,9},{3,11}... | collective-permute-start | bytes 307208 | tf_op jit(solution)/shard_map/ppermute | solution.py:366
  232.7 5.6 %collective-permute-start.12 = (bf16[1,4,100,128]{3,1,2,0:T(4,128)(2,1)S(1)}, bf16[1,4,100,128]{3,1,2,0:T(4,128)(2,1)S(1)}, u32[]{:S(2)}, u32[]{:S(2)}) collective-permute-start(bf16[1,4,100,128]{3,1,2,0:T(4,128)(2,1)S(1)} %fusion.4), channel_id=1, source_target_pairs={{0,8},{2,10},{4,12},{6,14},{8,0},{10,2},{12,4},{14,6},{1,9},{3,11}... | collective-permute-start | bytes 307208 | tf_op jit(solution)/shard_map/ppermute | solution.py:366
where the time goes:
time: 240 us; the launch traced here: 239 us
  Pallas kernels  141 us (59%)
  waiting for transfers between devices  47.6 us (20%)
  local copies, waits for them, and re-layouts  29.3 us (12%)
  starting transfers between devices  17.5 us (7%)
  other arithmetic  4.05 us (2%)
    pallas_call x3, Pallas kernels, filter_chunk(): pl.pallas_call(filter_kernel, in_specs=[smem, smem, vmem, vmem, vmem, vme...  102 us
    ppermute x2, waiting for transfers between devices, local(): remote = [over_cls(images[:cut]), over_cls(images[cut:])]  32 us
    unnamed x52, local copies, waits for them, and re-layouts  24.2 us
    pallas_call x1, Pallas kernels, lay_refs(): pl.pallas_call(functools.partial(refs_kernel, padded=padded), out_shape=(...  18.2 us
    pallas_call x1, Pallas kernels, score(): pl.pallas_call(functools.partial(score_kernel, parts=len(plains)), out_sh...  9.1 us
    ppermute x4, starting transfers between devices, local(): got = lax.ppermute(send, 'dom', [(i, i ^ 1 << bit) for i in range(dom)])  8.63 us
    ppermute x2, waiting for transfers between devices, local(): got = lax.ppermute(send, 'dom', [(i, i ^ 1) for i in range(dom)])  7.25 us
    ppermute x4, waiting for transfers between devices, local(): got = lax.ppermute(send, 'dom', [(i, i ^ 1 << bit) for i in range(dom)])  6.47 us
  transfers between devices with their start and end apart: 13, of which 7 were waited for; matrix products, arithmetic and copies ran while one was open for 2% of the time, Pallas kernels for 42%

commit v1 on v0

v1 whole, which is shorter than its diff:
```python
import functools

import jax
import jax.numpy as jnp
from jax import lax
from jax.experimental import pallas as pl
from jax.experimental.pallas import tpu as pltpu
from jax.sharding import PartitionSpec as P

F32 = jnp.float32
BF16 = jnp.bfloat16
LOW = -1e30
GROUP = 16
PAD = 8
DEEP = 16
MIB = 1 << 20


def nt(a, b, precision=None):
    return lax.dot_general(
        a, b, (((1,), (1,)), ((), ())), preferred_element_type=F32, precision=precision
    )


def nn(a, b):
    return lax.dot_general(a, b, (((1,), (0,)), ((), ())), preferred_element_type=F32)


def cost(microseconds):
    return pl.CostEstimate(
        flops=int(microseconds * 1e9), transcendentals=0, bytes_accessed=int(microseconds * 3e6)
    )


def filters_kernel(ctf, ctf_rev, band, band_rev, left, right):
    bins, width = ctf.shape
    delta = jnp.where(lax.broadcasted_iota(jnp.int32, (1, width), 1) == 0, 1.0, 0.0)

    def rolled(row):
        return pltpu.roll(jnp.broadcast_to(row, (width, width)), 0, 1, stride=1, stride_axis=0)

    highest = lax.Precision.HIGHEST
    forward = nt(ctf[...] + delta, rolled(band_rev[...] + delta), highest)
    backward = nt(ctf_rev[...] + delta, rolled(band[...] + delta), highest)
    for b in range(bins):
        left[b] = rolled(backward[b : b + 1]).astype(BF16)
        right[b] = rolled(forward[b : b + 1]).astype(BF16)


def build_filters(ctf, band):
    bins, width = ctf.shape

    def negate(v):
        return jnp.concatenate([v[:, :1], jnp.flip(v[:, 1:], 1)], axis=1)

    band = band.reshape(1, width)
    return pl.pallas_call(
        filters_kernel,
        out_shape=(
            jax.ShapeDtypeStruct((bins, width, width), BF16),
            jax.ShapeDtypeStruct((bins, width, width), BF16),
        ),
        cost_estimate=cost(3),
        name="filters",
    )(ctf, negate(ctf), band, negate(band))


def refs_kernel(refs, out, norm, scratch, *, padded):
    classes, rots, rows, width = refs.shape
    pitch = rows + PAD

    def block(start, count, j):
        for k in range(GROUP):
            if k < count:
                scratch[pl.ds(k * pitch, rows)] = refs[start + k, j].astype(F32)
            else:
                scratch[pl.ds(k * pitch, rows)] = jnp.zeros((rows, width), F32)
        at = pl.multiple_of(j * padded + start, GROUP)

        def step(r, acc):
            v = scratch[pl.ds(r, GROUP, stride=pitch)]
            out[r, pl.ds(at, GROUP)] = v.astype(BF16)
            return acc + v * v

        acc = lax.fori_loop(0, rows, step, jnp.zeros((GROUP, width), F32), unroll=32)
        total = 0.5 * jnp.sum(acc, axis=1, keepdims=True)
        norm[pl.ds(at, GROUP)] = jnp.broadcast_to(total, (GROUP, width))

    full = classes // GROUP

    @pl.loop(0, full * rots)
    def _(i):
        block((i // rots) * GROUP, GROUP, i % rots)

    if classes % GROUP:

        @pl.loop(0, rots)
        def _(j):
            block(full * GROUP, classes % GROUP, j)


def lay_refs(refs, padded):
    classes, rots, rows, width = refs.shape
    return pl.pallas_call(
        functools.partial(refs_kernel, padded=padded),
        out_shape=(
            jax.ShapeDtypeStruct((rows, rots * padded, width), BF16),
            jax.ShapeDtypeStruct((rots * padded, width), F32),
        ),
        scratch_shapes=[pltpu.VMEM((GROUP * (rows + PAD), width), F32)],
        compiler_params=pltpu.CompilerParams(vmem_limit_bytes=28 * MIB),
        cost_estimate=cost(11),
        name="refs",
    )(refs)


def filter_kernel(where, bins, mine, sib, left, right, plain, turned, scr, scr_t):
    count, half, width = mine.shape
    top = where[0] == 0
    pitch = width + PAD

    @pl.loop(0, count // GROUP)
    def _(g):
        base = pl.multiple_of(g * GROUP, GROUP)
        for i in range(GROUP):
            b = bins[base + i]
            a = mine[base + i]
            o = sib[base + i]
            x = jnp.concatenate([jnp.where(top, a, o), jnp.where(top, o, a)], axis=0)
            f = nn(left[b], nn(x, right[b]).astype(BF16))
            scr[pl.ds(i * pitch, width)] = f
            scr_t[pl.ds(i * pitch, width)] = f.T
        for r in range(width):
            plain[r, pl.ds(base, GROUP)] = scr[pl.ds(r, GROUP, stride=pitch)].astype(BF16)
            turned[r, pl.ds(base, GROUP)] = scr_t[pl.ds(r, GROUP, stride=pitch)].astype(BF16)


def filter_chunk(where, bins, mine, sib, left, right):
    count, half, width = mine.shape
    smem = pl.BlockSpec(memory_space=pltpu.SMEM)
    vmem = pl.BlockSpec(memory_space=pltpu.VMEM)
    return pl.pallas_call(
        filter_kernel,
        in_specs=[smem, smem, vmem, vmem, vmem, vmem],
        out_shape=(jax.ShapeDtypeStruct((2 * half, count, width), BF16),) * 2,
        scratch_shapes=[pltpu.VMEM((GROUP * (2 * half + PAD), width), F32)] * 2,
        compiler_params=pltpu.CompilerParams(vmem_limit_bytes=16 * MIB),
        cost_estimate=cost(count * 0.1),
        name="filter",
    )(where, bins, mine, sib, left, right)


def score_kernel(*args, parts):
    plains = args[:parts]
    refs, norm, mask, noise, scaled, stats = args[parts:]
    rows, height, width = refs.shape
    count = mask.shape[1]

    def step(i, acc):
        at = [DEEP * i + a for a in range(DEEP)]
        lhs = jnp.concatenate([refs[r] for r in at], axis=1)
        rhs = jnp.concatenate(
            [jnp.concatenate([p[r] for r in at], axis=1) for p in plains], axis=0
        )
        return acc + nt(lhs, rhs)

    inner = lax.fori_loop(0, rows // DEEP, step, jnp.zeros((height, count), F32))
    rots = height // mask.shape[0]
    allowed = jnp.concatenate([mask[...]] * rots, axis=0) > 0
    s = jnp.where(allowed, (inner - norm[:, :1]) / noise[...], LOW)
    scaled[...] = s
    peak = jnp.max(s, axis=0, keepdims=True)
    total = jnp.sum(jnp.exp(s - peak), axis=0, keepdims=True)
    stats[0:1] = peak
    stats[1:2] = total
    stats[2:] = jnp.zeros((stats.shape[0] - 2, count), F32)


def score(plains, refs, norm, mask, noise):
    count = mask.shape[1]
    height = refs.shape[1]
    return pl.pallas_call(
        functools.partial(score_kernel, parts=len(plains)),
        out_shape=(
            jax.ShapeDtypeStruct((height, count), F32),
            jax.ShapeDtypeStruct((8, count), F32),
        ),
        compiler_params=pltpu.CompilerParams(vmem_limit_bytes=28 * MIB),
        cost_estimate=cost(5),
        name="score",
    )(*plains, refs, norm, mask, noise)


def weights_kernel(scaled, mine, other, rot, out, *, sizes):
    rots, padded, count = rot.shape
    theirs = jnp.concatenate([other[:, count // 2 :], other[:, : count // 2]], axis=1)
    peak = jnp.maximum(mine[0:1], theirs[0:1])
    total = mine[1:2] * jnp.exp(mine[0:1] - peak) + theirs[1:2] * jnp.exp(theirs[0:1] - peak)
    w = (jnp.exp(scaled[...] - peak) / total).astype(BF16).astype(F32)
    quarters = []
    for q in range(4):
        acc = jnp.zeros((padded, count), F32)
        for j in range(rots):
            acc = acc + jnp.where(rot[j] == q, w[j * padded : (j + 1) * padded], 0.0)
        quarters.append(acc)
    for row, pair in enumerate(((0, 3), (2, 1))):
        pieces = []
        start = 0
        for size in sizes:
            pieces += [quarters[q][:, start : start + size] for q in pair]
            start += size
        out[row] = jnp.concatenate(pieces, axis=1).astype(BF16)


def make_weights(scaled, mine, other, rot, sizes):
    rots, padded, count = rot.shape
    return pl.pallas_call(
        functools.partial(weights_kernel, sizes=sizes),
        out_shape=jax.ShapeDtypeStruct((2, padded, 2 * count), BF16),
        cost_estimate=cost(2),
        name="weights",
    )(scaled, mine, other, rot)


def sums_kernel(where, weights, *args, parts, dom, chunk, classes):
    plains = args[:parts]
    turned = args[parts : 2 * parts]
    send, keep = args[2 * parts :]
    width = send.shape[3]
    rows = send.shape[1]
    height = plains[0].shape[0]
    block = height // 2 // dom
    first = where[0] * (height // 2) + chunk * rows
    parity = where[1]
    straight = weights[0]
    mirrored = weights[1]
    flip = width - 1 - lax.broadcasted_iota(jnp.int32, (straight.shape[0], width), 1)

    def stacked(up, down):
        return jnp.concatenate(
            [ref[at] for p, t in zip(plains, turned) for ref, at in ((p, up), (t, down))], axis=0
        )

    def one(g, r, rhs_at):
        return first + (2 * g + rhs_at) * block + r

    @pl.loop(0, dom // 2)
    def _(g):
        for r in range(rows):
            away = one(g, r, 1 - parity)
            here = one(g, r, parity)
            direct = nn(
                straight,
                jnp.concatenate(
                    [stacked(i, height - 1 - i) for i in (away, here)], axis=1
                ),
            )
            mirror = nn(
                mirrored,
                jnp.concatenate(
                    [stacked(height - 1 - i, i) for i in (away, here)], axis=1
                ),
            )
            out = [
                direct[:, at : at + width]
                + jnp.take_along_axis(mirror[:, at : at + width], flip, axis=1)
                for at in (0, width)
            ]
            send[g, r] = out[0][:classes].astype(BF16)
            keep[g, r] = out[1][:classes]


def sums(where, weights, plains, turned, dom, chunk, rows, classes):
    width = plains[0].shape[2]
    smem = pl.BlockSpec(memory_space=pltpu.SMEM)
    vmem = pl.BlockSpec(memory_space=pltpu.VMEM)
    return pl.pallas_call(
        functools.partial(
            sums_kernel, parts=len(plains), dom=dom, chunk=chunk, classes=classes
        ),
        in_specs=[smem] + [vmem] * (1 + 2 * len(plains)),
        out_shape=(
            jax.ShapeDtypeStruct((dom // 2, rows, classes, width), BF16),
            jax.ShapeDtypeStruct((dom // 2, rows, classes, width), F32),
        ),
        compiler_params=pltpu.CompilerParams(vmem_limit_bytes=24 * MIB),
        cost_estimate=cost(3),
        name="sums",
    )(where, weights, *plains, *turned)


def local(
    images, defocus_bin, ctf_kernels, band_kernel, references, rot_index, class_mask, noise_var
):
    section_at = lax.axis_index("section")
    class_at = lax.axis_index("cls")
    dom_at = lax.axis_index("dom")
    dom = lax.axis_size("dom")
    particles, half, width = images.shape
    classes, rots = rot_index.shape
    padded = -(-classes // GROUP) * GROUP
    swap = [(0, 1), (1, 0)]
    over_cls = functools.partial(lax.ppermute, axis_name="cls", perm=swap)
    over_section = functools.partial(lax.ppermute, axis_name="section", perm=swap)

    cut = (particles * 2 // 3) // GROUP * GROUP
    sizes = (particles, cut, particles - cut)
    other_bins = over_cls(defocus_bin)
    remote = [over_cls(images[:cut]), over_cls(images[cut:])]
    own_sib = over_section(images)

    where = jnp.stack([section_at, dom_at % 2]).astype(jnp.int32)
    left, right = build_filters(ctf_kernels, band_kernel)
    refs, norm = lay_refs(references, padded)

    def arranged(a):
        parts = a.reshape((2, particles) + a.shape[1:])
        return jnp.concatenate(
            [
                lax.dynamic_index_in_dim(parts, class_at, 0, False),
                lax.dynamic_index_in_dim(parts, 1 - class_at, 0, False),
            ]
        )

    mask = jnp.pad(arranged(class_mask).T, ((0, padded - classes), (0, 0)))
    noise = arranged(noise_var).reshape(1, 2 * particles)
    rot = jnp.broadcast_to(
        jnp.pad(rot_index.T, ((0, 0), (0, padded - classes)))[:, :, None],
        (rots, padded, 2 * particles),
    )

    plains, turned = [], []
    plain, turn = filter_chunk(where, defocus_bin, images, own_sib, left, right)
    plains.append(plain)
    turned.append(turn)
    start = 0
    for piece in remote:
        n = piece.shape[0]
        plain, turn = filter_chunk(
            where, other_bins[start : start + n], piece, over_section(piece), left, right
        )
        start += n
        plains.append(plain)
        turned.append(turn)

    scaled, stats = score(plains, refs, norm, mask, noise)
    weights = make_weights(scaled, stats, over_cls(stats), rot, sizes)

    block_rows = half // dom
    chunks = min(2, block_rows)
    rows = block_rows // chunks
    done = []
    for c in range(chunks):
        send, keep = sums(where, weights, plains, turned, dom, c, rows, classes)
        got = lax.ppermute(send, "dom", [(i, i ^ 1) for i in range(dom)])
        bit = 1
        while keep.shape[0] > 1:
            kept = keep.reshape((keep.shape[0] // 2, 2) + keep.shape[1:])
            came = got.reshape(kept.shape)
            mine = (dom_at >> bit) & 1

            def pick(index):
                return lax.dynamic_index_in_dim(
                    kept, index, 1, False
                ) + lax.dynamic_index_in_dim(came, index, 1, False).astype(F32)

            send = pick(1 - mine).astype(BF16)
            keep = pick(mine)
            got = lax.ppermute(send, "dom", [(i, i ^ (1 << bit)) for i in range(dom)])
            bit += 1
        done.append(keep[0] + got[0].astype(F32))
    return jnp.transpose(jnp.concatenate(done, axis=0), (1, 0, 2))


def solution(mesh):
    return jax.shard_map(
        local,
        mesh=mesh,
        in_specs=(
            P(("dom", "cls"), "section", None),
            P(("dom", "cls")),
            P(),
            P(),
            P("cls", None, None, None),
            P("cls", None),
            P("dom", "cls"),
            P("dom"),
        ),
        out_specs=P("cls", ("section", "dom"), None),
        check_vma=False,
    )
```

time: 240 us -> 128 us (0.53)
  Pallas kernels: 141 us -> 36.2 us
  waiting for transfers between devices: 47.6 us -> 28.4 us
  local copies, waits for them, and re-layouts: 29.3 us -> 40.3 us
    pallas_call x3, Pallas kernels: 102 us -> 14 us  [filter_chunk(): pl.pallas_call(filter_kernel, in_specs=[smem, smem, vmem, vmem, vmem, vme...]
    ppermute x2, waiting for transfers between devices: 32 us -> 15.9 us  [local(): remote = [over_cls(images[:cut]), over_cls(images[cut:])]]
    pallas_call x1, Pallas kernels: 18.2 us -> 7.1 us  [lay_refs(): pl.pallas_call(functools.partial(refs_kernel, padded=padded), out_shape=(...]
    unnamed x52 -> x78, local copies, waits for them, and re-layouts: 24.2 us -> 34.5 us
    pallas_call x1, Pallas kernels: 9.1 us -> 4.6 us  [score(): pl.pallas_call(functools.partial(score_kernel, parts=len(plains)), out_sh...]
  transfers between devices with their start and end apart: 13 -> 13, of which waited for: 7 -> 6; matrix products, arithmetic and copies ran while one was open for 2% -> 7% of each run, Pallas kernels for 42% -> 16%
where the time goes in v1:
time: 128 us; the launch traced here: 127 us
  local copies, waits for them, and re-layouts  40.3 us (31%)
  Pallas kernels  36.2 us (28%)
  waiting for transfers between devices  28.4 us (22%)
  starting transfers between devices  18.2 us (14%)
  other arithmetic  4.14 us (3%)
    unnamed x78, local copies, waits for them, and re-layouts  34.5 us
    ppermute x2, waiting for transfers between devices, local(): remote = [over_cls(images[:cut]), over_cls(images[cut:])]  15.9 us
    pallas_call x3, Pallas kernels, filter_chunk(): pl.pallas_call(filter_kernel, in_specs=[smem, smem, vmem, vmem, vmem, vme...  14 us
    ppermute x4, starting transfers between devices, local(): got = lax.ppermute(send, 'dom', [(i, i ^ 1 << bit) for i in range(dom)])  8.78 us
    pallas_call x1, Pallas kernels, lay_refs(): pl.pallas_call(functools.partial(refs_kernel, padded=padded), out_shape=(...  7.1 us
    ppermute x2, waiting for transfers between devices, local(): got = lax.ppermute(send, 'dom', [(i, i ^ 1) for i in range(dom)])  6.01 us
    pallas_call x2, Pallas kernels, sums(): pl.pallas_call(functools.partial(sums_kernel, parts=len(plains), dom=dom,...  5.84 us
    pallas_call x1, Pallas kernels, score(): pl.pallas_call(functools.partial(score_kernel, parts=len(plains)), out_sh...  4.6 us
  transfers between devices with their start and end apart: 13, of which 6 were waited for; matrix products, arithmetic and copies ran while one was open for 7% of the time, Pallas kernels for 16%

profile of v1, /device:TPU:0, one launch (start us, length us, event | category | flops | bytes accessed | tf_op | source)
XLA Modules:
  0.0 127.4 jit_solution(8026610370152165639)
XLA Ops:
  0.0 0.5 collective-permute-start
  0.5 2.3 %slice.29 = bf16[64,64,128]{2,1,0:T(8,128)(2,1)} slice(bf16[96,64,128]{2,1,0:T(8,128)(2,1)} %mine.1), slice={[0:64], [0:64], [0:128]} | slice | bytes 2097152 | tf_op jit(solution)/shard_map/slice | solution.py:309
  2.8 2.5 %collective-permute-start.2 = (bf16[64,64,128]{2,1,0:T(8,128)(2,1)}, bf16[64,64,128]{2,1,0:T(8,128)(2,1)}, u32[]{:S(2)}, u32[]{:S(2)}) collective-permute-start(bf16[64,64,128]{2,1,0:T(8,128)(2,1)} %slice.29), channel_id=1, source_target_pairs={{0,1},{1,0},{2,3},{3,2},{4,5},{5,4},{6,7},{7,6},{8,9},{9,8},{10,11... | collective-permute-start | bytes 3145736 | tf_op jit(solution)/shard_map/ppermute | solution.py:309
  5.3 1.1 slice.31
  6.4 2.1 %collective-permute-start.4 = (bf16[32,64,128]{2,1,0:T(8,128)(2,1)S(1)}, bf16[32,64,128]{2,1,0:T(8,128)(2,1)S(1)}, u32[]{:S(2)}, u32[]{:S(2)}) collective-permute-start(bf16[32,64,128]{2,1,0:T(8,128)(2,1)S(1)} %slice.31), channel_id=1, source_target_pairs={{0,1},{1,0},{2,3},{3,2},{4,5},{5,4},{6,7},{7,6},{8,9},{9,8},{10,11... | collective-permute-start | bytes 1572872 | tf_op jit(solution)/shard_map/ppermute | solution.py:309
  8.4 3.8 %copy-done.20 = bf16[100,3,128,128]{3,2,1,0:T(8,128)(2,1)S(1)} copy-done((bf16[100,3,128,128]{3,2,1,0:T(8,128)(2,1)S(1)}, bf16[100,3,128,128]{3,2,1,0:T(8,128)(2,1)}, u32[]{:S(2)}) %copy-start.20) | copy-done | bytes 9830424
  12.2 7.1 %refs.2 = (bf16[128,336,128]{2,1,0:T(8,128)(2,1)S(1)}, f32[336,128]{1,0:T(8,128)S(1)}) custom-call(bf16[100,3,128,128]{3,2,1,0:T(8,128)(2,1)S(1)} %copy-done.20), custom_call_target="tpu_custom_call" | custom-call | flops 11000000512 | bytes 33000000 | tf_op jit(solution)/shard_map/refs/pallas_call | solution.py:104
  19.3 4.1 %copy-done.25 = bf16[128,336,128]{2,1,0:T(8,128)(2,1)} copy-done((bf16[128,336,128]{2,1,0:T(8,128)(2,1)}, bf16[128,336,128]{2,1,0:T(8,128)(2,1)S(1)}, u32[]{:S(2)}) %copy-start.25) | copy-done | bytes 11010072
  23.6 0.1 rev.9
  24.0 0.7 pad_maximum_fusion.ctf_rev
  24.7 15.9 %collective-permute-done.4.mine = bf16[32,64,128]{2,1,0:T(8,128)(2,1)S(1)} collective-permute-done((bf16[32,64,128]{2,1,0:T(8,128)(2,1)S(1)}, bf16[32,64,128]{2,1,0:T(8,128)(2,1)S(1)}, u32[]{:S(2)}, u32[]{:S(2)}) %collective-permute-start.4) | collective-permute-done | bytes 524320 | tf_op jit(solution)/shard_map/ppermute | solution.py:309
  40.6 0.7 pad_maximum_fusion.2.band_rev
  41.2 0.1 copy.19
  41.3 0.1 copy.20
  41.4 0.1 add_bitcast_fusion
  41.5 2.5 %filters.1 = (bf16[16,128,128]{2,1,0:T(8,128)(2,1)}, bf16[16,128,128]{2,1,0:T(8,128)(2,1)}) custom-call(f32[16,128]{1,0:T(8,128)} %ctf.1, f32[16,128]{1,0:T(8,128)} %pad_maximum_fusion.ctf_rev, f32[1,128]{1,0:T(1,128)} %bitcast.64, f32[1,128]{1,0:T(1,128)} %pad_maximum_fusion.2.band_rev), custom_call_target="tpu_custom_call" | custom-call | flops 3000000000 | bytes 9000000 | tf_op jit(solution)/shard_map/filters/pallas_call | solution.py:57
  44.2 0.5 collective-permute-start.3
  44.7 1.0 copy-done.27
  45.8 1.0 copy-done.28
  46.8 2.5 %filter.5 = (bf16[128,32,128]{2,1,0:T(8,128)(2,1)S(1)}, bf16[128,32,128]{2,1,0:T(8,128)(2,1)S(1)}) custom-call(s32[2]{0:T(128)S(1)} %pad_add_fusion.where, s32[32]{0:T(128)S(1)} %slice.30.bins, bf16[32,64,128]{2,1,0:T(8,128)(2,1)S(1)} %collective-permute-done.4.mine, bf16[32,64,128]{2,1,0:T(8,128)(2,1)S(1)} %collective-permute-done.5.sib, ...), custom_call_target="tpu_custom_call" | custom-call | flops 3200000000 | bytes 9600000 | tf_op jit(solution)/shard_map/filter/pallas_call | solution.py:142
  49.3 1.0 copy-done.12
  50.3 1.2 copy-done.21
  51.5 1.4 %copy-done.22 = bf16[96,64,128]{2,1,0:T(8,128)(2,1)S(1)} copy-done((bf16[96,64,128]{2,1,0:T(8,128)(2,1)S(1)}, bf16[96,64,128]{2,1,0:T(8,128)(2,1)}, u32[]{:S(2)}) %copy-start.22) | copy-done | bytes 1572888
  52.9 6.3 %filter.3 = (bf16[128,96,128]{2,1,0:T(8,128)(2,1)S(1)}, bf16[128,96,128]{2,1,0:T(8,128)(2,1)S(1)}) custom-call(s32[2]{0:T(128)S(1)} %pad_add_fusion.where, s32[96]{0:T(128)S(1)} %copy-done.24, bf16[96,64,128]{2,1,0:T(8,128)(2,1)S(1)} %copy-done.15, bf16[96,64,128]{2,1,0:T(8,128)(2,1)S(1)} %copy-done.22, bf16[16,128,128]{2,1,0:T(8,128)(2,1)S(1)} %copy-done.27, ...), custom_call_target="tpu_custom_call" | custom-call | flops 9600000000 | bytes 28800000 | tf_op jit(solution)/shard_map/filter/pallas_call | solution.py:142
  59.3 1.7 %copy-done = bf16[128,96,128]{2,1,0:T(8,128)(2,1)} copy-done((bf16[128,96,128]{2,1,0:T(8,128)(2,1)}, bf16[128,96,128]{2,1,0:T(8,128)(2,1)S(1)}, u32[]{:S(2)}) %copy-start) | copy-done | bytes 3145752
  60.9 5.3 %filter.4 = (bf16[128,64,128]{2,1,0:T(8,128)(2,1)S(1)}, bf16[128,64,128]{2,1,0:T(8,128)(2,1)S(1)}) custom-call(s32[2]{0:T(128)S(1)} %pad_add_fusion.where, s32[64]{0:T(128)S(1)} %bitcast.54, bf16[64,64,128]{2,1,0:T(8,128)(2,1)} %collective-permute-done.2.mine, bf16[64,64,128]{2,1,0:T(8,128)(2,1)S(1)} %collective-permute-done.3.sib, ...), custom_call_target="tpu_custom_call" | custom-call | flops 6400000000 | bytes 19200000 | tf_op jit(solution)/shard_map/filter/pallas_call | solution.py:142
  66.2 1.3 %copy-done.6 = bf16[128,64,128]{2,1,0:T(8,128)(2,1)} copy-done((bf16[128,64,128]{2,1,0:T(8,128)(2,1)}, bf16[128,64,128]{2,1,0:T(8,128)(2,1)S(1)}, u32[]{:S(2)}) %copy-start.6) | copy-done | bytes 2097176
  67.6 4.6 %score.1 = (f32[336,192]{1,0:T(8,128)S(1)}, f32[8,192]{1,0:T(8,128)S(1)}) custom-call(bf16[128,96,128]{2,1,0:T(8,128)(2,1)S(1)} %get-tuple-element.23.args_0_, bf16[128,64,128]{2,1,0:T(8,128)(2,1)S(1)} %get-tuple-element.24.args_1_, bf16[128,32,128]{2,1,0:T(8,128)(2,1)S(1)} %get-tuple-element.25.args_2_, bf16[128,336,128]{2,1,0:T(8,128)(2,1)S(1)} %bitcast.56, ...), custom_call_target="tpu_custom_call" | custom-call | flops 5000000000 | bytes 15000000 | tf_op jit(solution)/shard_map/score/pallas_call | solution.py:182
  72.2 0.7 copy-done.26
  72.9 1.7 %collective-permute-start.6 = (f32[8,192]{1,0:T(8,128)S(1)}, f32[8,192]{1,0:T(8,128)S(1)}, u32[]{:S(2)}, u32[]{:S(2)}) collective-permute-start(f32[8,192]{1,0:T(8,128)S(1)} %get-tuple-element.29.mine), channel_id=1, source_target_pairs={{0,1},{1,0},{2,3},{3,2},{4,5},{5,4},{6,7},{7,6},{8,9},{9,8},{10,11... | collective-permute-start | bytes 18440 | tf_op jit(solution)/shard_map/ppermute | solution.py:347
  74.6 1.9 %collective-permute-done.6.other = f32[8,192]{1,0:T(8,128)S(1)} collective-permute-done((f32[8,192]{1,0:T(8,128)S(1)}, f32[8,192]{1,0:T(8,128)S(1)}, u32[]{:S(2)}, u32[]{:S(2)}) %collective-permute-start.6) | collective-permute-done | bytes 6176 | tf_op jit(solution)/shard_map/ppermute | solution.py:347
  76.5 0.8 broadcast_in_dim.2.rot
  77.4 2.2 %weights.1 = bf16[2,112,384]{2,1,0:T(8,128)(2,1)} custom-call(f32[336,192]{1,0:T(8,128)} %copy-done.26, f32[8,192]{1,0:T(8,128)} %copy-done.23, f32[8,192]{1,0:T(8,128)} %copy-done.33, s32[3,112,192]{2,1,0:T(8,128)} %broadcast_in_dim.2.rot), custom_call_target="tpu_custom_call" | custom-call | flops 2000000000 | bytes 6000000 | tf_op jit(solution)/shard_map/weights/pallas_call | solution.py:217
  79.6 1.9 %copy-done.1 = bf16[128,96,128]{2,1,0:T(8,128)(2,1)S(1)} copy-done((bf16[128,96,128]{2,1,0:T(8,128)(2,1)S(1)}, bf16[128,96,128]{2,1,0:T(8,128)(2,1)}, u32[]{:S(2)}) %copy-start.1) | copy-done | bytes 3145752
  81.5 1.6 %copy-done.4 = bf16[128,64,128]{2,1,0:T(8,128)(2,1)S(1)} copy-done((bf16[128,64,128]{2,1,0:T(8,128)(2,1)S(1)}, bf16[128,64,128]{2,1,0:T(8,128)(2,1)}, u32[]{:S(2)}) %copy-start.4) | copy-done | bytes 2097176
  83.0 1.6 %copy-done.7 = bf16[128,64,128]{2,1,0:T(8,128)(2,1)S(1)} copy-done((bf16[128,64,128]{2,1,0:T(8,128)(2,1)S(1)}, bf16[128,64,128]{2,1,0:T(8,128)(2,1)}, u32[]{:S(2)}) %copy-start.7) | copy-done | bytes 2097176
  84.6 1.2 copy-done.10
  85.9 1.2 copy-done.13
  87.1 0.9 copy-done.18
  88.0 3.3 %sums.2 = (bf16[4,4,100,128]{3,2,1,0:T(8,128)(2,1)}, f32[4,4,100,128]{3,2,1,0:T(8,128)S(1)}) custom-call(s32[2]{0:T(128)S(1)} %pad_add_fusion.where, bf16[2,112,384]{2,1,0:T(8,128)(2,1)S(1)} %copy-done.18, bf16[128,96,128]{2,1,0:T(8,128)(2,1)S(1)} %get-tuple-element.23.args_0_, bf16[128,64,128]{2,1,0:T(8,128)(2,1)S(1)} %copy-done.4, ...), custom_call_target="tpu_custom_call" | custom-call | flops 3000000000 | bytes 9000000 | tf_op jit(solution)/shard_map/sums/pallas_call | solution.py:277
  91.3 0.9 copy-done.16
  92.3 1.7 %collective-permute-start.7 = (bf16[4,4,100,128]{3,2,1,0:T(8,128)(2,1)}, bf16[4,4,100,128]{3,2,1,0:T(8,128)(2,1)}, u32[]{:S(2)}, u32[]{:S(2)}) collective-permute-start(bf16[4,4,100,128]{3,2,1,0:T(8,128)(2,1)} %get-tuple-element.34), channel_id=1, source_target_pairs={{0,2},{2,0},{4,6},{6,4},{8,10},{10,8},{12,14},{14,12},{1,3},{3,1},... | collective-permute-start | bytes 1228808 | tf_op jit(solution)/shard_map/ppermute | solution.py:355
  94.0 1.9 %copy-done.2 = bf16[128,96,128]{2,1,0:T(8,128)(2,1)S(1)} copy-done((bf16[128,96,128]{2,1,0:T(8,128)(2,1)S(1)}, bf16[128,96,128]{2,1,0:T(8,128)(2,1)}, u32[]{:S(2)}) %copy-start.2) | copy-done | bytes 3145752
  95.9 1.6 %copy-done.5 = bf16[128,64,128]{2,1,0:T(8,128)(2,1)S(1)} copy-done((bf16[128,64,128]{2,1,0:T(8,128)(2,1)S(1)}, bf16[128,64,128]{2,1,0:T(8,128)(2,1)}, u32[]{:S(2)}) %copy-start.5) | copy-done | bytes 2097176
  97.5 1.6 %copy-done.8 = bf16[128,64,128]{2,1,0:T(8,128)(2,1)S(1)} copy-done((bf16[128,64,128]{2,1,0:T(8,128)(2,1)S(1)}, bf16[128,64,128]{2,1,0:T(8,128)(2,1)}, u32[]{:S(2)}) %copy-start.8) | copy-done | bytes 2097176
  99.1 1.2 copy-done.11
  100.3 1.2 copy-done.14
  101.5 2.5 %sums.3 = (bf16[4,4,100,128]{3,2,1,0:T(8,128)(2,1)S(1)}, f32[4,4,100,128]{3,2,1,0:T(8,128)S(1)}) custom-call(s32[2]{0:T(128)S(1)} %pad_add_fusion.where, bf16[2,112,384]{2,1,0:T(8,128)(2,1)S(1)} %copy-done.19, bf16[128,96,128]{2,1,0:T(8,128)(2,1)S(1)} %get-tuple-element.23.args_0_, bf16[128,64,128]{2,1,0:T(8,128)(2,1)S(1)} %copy-done.5, ...), custom_call_target="tpu_custom_call" | custom-call | flops 3000000000 | bytes 9000000 | tf_op jit(solution)/shard_map/sums/pallas_call | solution.py:277
  104.0 0.4 collective-permute-start.10
  104.4 0.9 constant_dynamic-slice_fusion.5
  105.4 1.0 constant_dynamic-slice_fusion.6
  106.4 0.1 fusion.2
  106.5 1.9 %collective-permute-start.8 = (bf16[2,4,100,128]{3,1,2,0:T(4,128)(2,1)S(1)}, bf16[2,4,100,128]{3,1,2,0:T(4,128)(2,1)S(1)}, u32[]{:S(2)}, u32[]{:S(2)}) collective-permute-start(bf16[2,4,100,128]{3,1,2,0:T(4,128)(2,1)S(1)} %fusion.2), channel_id=1, source_target_pairs={{0,4},{2,6},{4,0},{6,2},{8,12},{10,14},{12,8},{14,10},{1,5},{3,7},... | collective-permute-start | bytes 614408 | tf_op jit(solution)/shard_map/ppermute | solution.py:369
  108.4 6.0 %collective-permute-done.10 = bf16[4,4,100,128]{3,2,1,0:T(8,128)(2,1)S(1)} collective-permute-done((bf16[4,4,100,128]{3,2,1,0:T(8,128)(2,1)S(1)}, bf16[4,4,100,128]{3,2,1,0:T(8,128)(2,1)S(1)}, u32[]{:S(2)}, u32[]{:S(2)}) %collective-permute-start.10) | collective-permute-done | bytes 409632 | tf_op jit(solution)/shard_map/ppermute | solution.py:355
  114.5 0.1 fusion.3
  114.7 1.6 %collective-permute-start.11 = (bf16[2,4,100,128]{3,1,2,0:T(4,128)(2,1)S(1)}, bf16[2,4,100,128]{3,1,2,0:T(4,128)(2,1)S(1)}, u32[]{:S(2)}, u32[]{:S(2)}) collective-permute-start(bf16[2,4,100,128]{3,1,2,0:T(4,128)(2,1)S(1)} %fusion.3), channel_id=1, source_target_pairs={{0,4},{2,6},{4,0},{6,2},{8,12},{10,14},{12,8},{14,10},{1,5},{3,7},... | collective-permute-start | bytes 614408 | tf_op jit(solution)/shard_map/ppermute | solution.py:369
  116.5 2.7 %collective-permute-start.9 = (bf16[1,4,100,128]{3,1,2,0:T(4,128)(2,1)S(1)}, bf16[1,4,100,128]{3,1,2,0:T(4,128)(2,1)S(1)}, u32[]{:S(2)}, u32[]{:S(2)}) collective-permute-start(bf16[1,4,100,128]{3,1,2,0:T(4,128)(2,1)S(1)} %fusion.7), channel_id=1, source_target_pairs={{0,8},{2,10},{4,12},{6,14},{8,0},{10,2},{12,4},{14,6},{1,9},{3,11}... | collective-permute-start | bytes 307208 | tf_op jit(solution)/shard_map/ppermute | solution.py:369
  119.1 1.6 %collective-permute-done.11 = bf16[2,4,100,128]{3,1,2,0:T(4,128)(2,1)S(1)} collective-permute-done((bf16[2,4,100,128]{3,1,2,0:T(4,128)(2,1)S(1)}, bf16[2,4,100,128]{3,1,2,0:T(4,128)(2,1)S(1)}, u32[]{:S(2)}, u32[]{:S(2)}) %collective-permute-start.11) | collective-permute-done | bytes 204832 | tf_op jit(solution)/shard_map/ppermute | solution.py:369
  120.8 2.6 %collective-permute-start.12 = (bf16[1,4,100,128]{3,1,2,0:T(4,128)(2,1)S(1)}, bf16[1,4,100,128]{3,1,2,0:T(4,128)(2,1)S(1)}, u32[]{:S(2)}, u32[]{:S(2)}) collective-permute-start(bf16[1,4,100,128]{3,1,2,0:T(4,128)(2,1)S(1)} %fusion.4), channel_id=1, source_target_pairs={{0,8},{2,10},{4,12},{6,14},{8,0},{10,2},{12,4},{14,6},{1,9},{3,11}... | collective-permute-start | bytes 307208 | tf_op jit(solution)/shard_map/ppermute | solution.py:369
  123.4 1.9 %collective-permute-done.9 = bf16[1,4,100,128]{3,1,2,0:T(4,128)(2,1)S(1)} collective-permute-done((bf16[1,4,100,128]{3,1,2,0:T(4,128)(2,1)S(1)}, bf16[1,4,100,128]{3,1,2,0:T(4,128)(2,1)S(1)}, u32[]{:S(2)}, u32[]{:S(2)}) %collective-permute-start.9) | collective-permute-done | bytes 102432 | tf_op jit(solution)/shard_map/ppermute | solution.py:369
  125.3 0.1 fusion.9
  125.4 1.1 collective-permute-done.12
  126.5 0.1 fusion.6
  126.6 0.8 maximum_bitcast_fusion
  (81 shorter events, 1.0 us)
Async XLA Ops:
  0.0 50.3 %collective-permute-start = (bf16[96,64,128]{2,1,0:T(8,128)(2,1)}, bf16[96,64,128]{2,1,0:T(8,128)(2,1)S(1)}, u32[]{:S(2)}, u32[]{:S(2)}) collective-permute-start(bf16[96,64,128]{2,1,0:T(8,128)(2,1)} %mine.1), channel_id=1, source_target_pairs={{0,16},{16,0},{1,17},{17,1},{2,18},{18,2},{3,19},{19,3},{4,20},{20... | collective-permute-start | bytes 4718600 | tf_op jit(solution)/shard_map/ppermute | solution.py:310
  2.8 41.4 %collective-permute-start.2 = (bf16[64,64,128]{2,1,0:T(8,128)(2,1)}, bf16[64,64,128]{2,1,0:T(8,128)(2,1)}, u32[]{:S(2)}, u32[]{:S(2)}) collective-permute-start(bf16[64,64,128]{2,1,0:T(8,128)(2,1)} %slice.29), channel_id=1, source_target_pairs={{0,1},{1,0},{2,3},{3,2},{4,5},{5,4},{6,7},{7,6},{8,9},{9,8},{10,11... | collective-permute-start | bytes 3145736 | tf_op jit(solution)/shard_map/ppermute | solution.py:309
  5.3 38.8 %collective-permute-start.1 = (s32[96]{0:T(128)}, s32[96]{0:T(128)S(1)}, u32[]{:S(2)}, u32[]{:S(2)}) collective-permute-start(s32[96]{0:T(128)} %bins.1), channel_id=1, source_target_pairs={{0,1},{1,0},{2,3},{3,2},{4,5},{5,4},{6,7},{7,6},{8,9},{9,8},{10,11... | collective-permute-start | bytes 1160 | tf_op jit(solution)/shard_map/ppermute | solution.py:308
  6.4 34.2 %collective-permute-start.4 = (bf16[32,64,128]{2,1,0:T(8,128)(2,1)S(1)}, bf16[32,64,128]{2,1,0:T(8,128)(2,1)S(1)}, u32[]{:S(2)}, u32[]{:S(2)}) collective-permute-start(bf16[32,64,128]{2,1,0:T(8,128)(2,1)S(1)} %slice.31), channel_id=1, source_target_pairs={{0,1},{1,0},{2,3},{3,2},{4,5},{5,4},{6,7},{7,6},{8,9},{9,8},{10,11... | collective-permute-start | bytes 1572872 | tf_op jit(solution)/shard_map/ppermute | solution.py:309
  8.4 3.8 %copy-start.20 = (bf16[100,3,128,128]{3,2,1,0:T(8,128)(2,1)S(1)}, bf16[100,3,128,128]{3,2,1,0:T(8,128)(2,1)}, u32[]{:S(2)}) copy-start(bf16[100,3,128,128]{3,2,1,0:T(8,128)(2,1)} %refs.3) | copy-start | bytes 29491204
  12.2 11.2 %copy-start.34 = (f32[128]{0:T(128)S(1)}, f32[128]{0:T(128)}, u32[]{:S(2)}) copy-start(f32[128]{0:T(128)} %param.11) | copy-start | bytes 1540
  12.2 11.4 %copy-start.30 = (f32[16,128]{1,0:T(8,128)S(1)}, f32[16,128]{1,0:T(8,128)}, u32[]{:S(2)}) copy-start(f32[16,128]{1,0:T(8,128)} %ctf.1) | copy-start | bytes 24580
  12.2 11.6 %copy-start.32 = (f32[192]{0:T(256)S(1)}, f32[192]{0:T(256)}, u32[]{:S(2)}) copy-start(f32[192]{0:T(256)} %param.15) | copy-start | bytes 2308
  12.2 12.4 %copy-start.29 = (s32[192,100]{1,0:T(8,128)S(1)}, s32[192,100]{1,0:T(8,128)}, u32[]{:S(2)}) copy-start(s32[192,100]{1,0:T(8,128)} %param.14) | copy-start | bytes 230404
  19.3 4.1 %copy-start.25 = (bf16[128,336,128]{2,1,0:T(8,128)(2,1)}, bf16[128,336,128]{2,1,0:T(8,128)(2,1)S(1)}, u32[]{:S(2)}) copy-start(bf16[128,336,128]{2,1,0:T(8,128)(2,1)S(1)} %get-tuple-element.26.args_3_) | copy-start | bytes 33030148
  40.6 4.1 %collective-permute-start.5 = (bf16[32,64,128]{2,1,0:T(8,128)(2,1)S(1)}, bf16[32,64,128]{2,1,0:T(8,128)(2,1)S(1)}, u32[]{:S(2)}, u32[]{:S(2)}) collective-permute-start(bf16[32,64,128]{2,1,0:T(8,128)(2,1)S(1)} %collective-permute-done.4.mine), channel_id=1, source_target_pairs={{0,16},{16,0},{1,17},{17,1},{2,18},{18,2},{3,19},{19,3},{4,20},{20... | collective-permute-start | bytes 1572872 | tf_op jit(solution)/shard_map/ppermute | solution.py:340
  44.2 16.7 %collective-permute-start.3 = (bf16[64,64,128]{2,1,0:T(8,128)(2,1)}, bf16[64,64,128]{2,1,0:T(8,128)(2,1)S(1)}, u32[]{:S(2)}, u32[]{:S(2)}) collective-permute-start(bf16[64,64,128]{2,1,0:T(8,128)(2,1)} %collective-permute-done.2.mine), channel_id=1, source_target_pairs={{0,16},{16,0},{1,17},{17,1},{2,18},{18,2},{3,19},{19,3},{4,20},{20... | collective-permute-start | bytes 3145736 | tf_op jit(solution)/shard_map/ppermute | solution.py:340
  44.7 1.0 copy-start.27
  45.7 1.0 copy-start.28
  46.8 4.7 %copy-start.15 = (bf16[96,64,128]{2,1,0:T(8,128)(2,1)S(1)}, bf16[96,64,128]{2,1,0:T(8,128)(2,1)}, u32[]{:S(2)}) copy-start(bf16[96,64,128]{2,1,0:T(8,128)(2,1)} %mine.1) | copy-start | bytes 4718596
  46.8 4.7 %copy-start.24 = (s32[96]{0:T(128)S(1)}, s32[96]{0:T(128)}, u32[]{:S(2)}) copy-start(s32[96]{0:T(128)} %bins.1) | copy-start | bytes 1156
  49.3 1.0 copy-start.12
  50.3 17.2 %copy-start.9 = (bf16[128,32,128]{2,1,0:T(8,128)(2,1)}, bf16[128,32,128]{2,1,0:T(8,128)(2,1)S(1)}, u32[]{:S(2)}) copy-start(bf16[128,32,128]{2,1,0:T(8,128)(2,1)S(1)} %get-tuple-element.25.args_2_) | copy-start | bytes 3145732
  50.3 1.2 copy-start.21
  51.5 1.4 %copy-start.22 = (bf16[96,64,128]{2,1,0:T(8,128)(2,1)S(1)}, bf16[96,64,128]{2,1,0:T(8,128)(2,1)}, u32[]{:S(2)}) copy-start(bf16[96,64,128]{2,1,0:T(8,128)(2,1)} %copy-done.21) | copy-start | bytes 4718596
  52.9 14.6 %slice-start = ((s8[11010048]{0:T(1024)(128)(4,1)}), s8[4194304]{0:T(1024)(128)(4,1)S(1)}, s32[]{:S(2)}) async-start(s8[11010048]{0:T(1024)(128)(4,1)} %bitcast.55), calls=%async_computation | async-start | bytes 8388608
  52.9 14.6 %slice-start.1 = ((s8[11010048]{0:T(1024)(128)(4,1)}), s8[4194304]{0:T(1024)(128)(4,1)S(1)}, s32[]{:S(2)}) async-start(s8[11010048]{0:T(1024)(128)(4,1)} %bitcast.55), calls=%async_computation.1 | async-start | bytes 8388608
  59.2 1.7 %copy-start = (bf16[128,96,128]{2,1,0:T(8,128)(2,1)}, bf16[128,96,128]{2,1,0:T(8,128)(2,1)S(1)}, u32[]{:S(2)}) copy-start(bf16[128,96,128]{2,1,0:T(8,128)(2,1)S(1)} %get-tuple-element.30.args_3_) | copy-start | bytes 9437188
  60.9 6.6 %slice-start.2 = ((s8[11010048]{0:T(1024)(128)(4,1)}), s8[2621440]{0:T(1024)(128)(4,1)S(1)}, s32[]{:S(2)}) async-start(s8[11010048]{0:T(1024)(128)(4,1)} %bitcast.55), calls=%async_computation.2 | async-start | bytes 5242880
  66.2 1.3 %copy-start.6 = (bf16[128,64,128]{2,1,0:T(8,128)(2,1)}, bf16[128,64,128]{2,1,0:T(8,128)(2,1)S(1)}, u32[]{:S(2)}) copy-start(bf16[128,64,128]{2,1,0:T(8,128)(2,1)S(1)} %get-tuple-element.31.args_4_) | copy-start | bytes 6291460
  67.5 4.6 %copy-start.3 = (bf16[128,64,128]{2,1,0:T(8,128)(2,1)}, bf16[128,64,128]{2,1,0:T(8,128)(2,1)S(1)}, u32[]{:S(2)}) copy-start(bf16[128,64,128]{2,1,0:T(8,128)(2,1)S(1)} %get-tuple-element.24.args_1_) | copy-start | bytes 6291460
  67.5 7.1 %copy-start.31 = (s32[100,3]{0,1:T(4,128)S(1)}, s32[100,3]{0,1:T(4,128)}, u32[]{:S(2)}) copy-start(s32[100,3]{0,1:T(4,128)} %param.13) | copy-start | bytes 3604
  72.2 0.7 copy-start.26
  72.9 4.5 %copy-start.23 = (f32[8,192]{1,0:T(8,128)}, f32[8,192]{1,0:T(8,128)S(1)}, u32[]{:S(2)}) copy-start(f32[8,192]{1,0:T(8,128)S(1)} %get-tuple-element.29.mine) | copy-start | bytes 18436
  72.9 3.7 %collective-permute-start.6 = (f32[8,192]{1,0:T(8,128)S(1)}, f32[8,192]{1,0:T(8,128)S(1)}, u32[]{:S(2)}, u32[]{:S(2)}) collective-permute-start(f32[8,192]{1,0:T(8,128)S(1)} %get-tuple-element.29.mine), channel_id=1, source_target_pairs={{0,1},{1,0},{2,3},{3,2},{4,5},{5,4},{6,7},{7,6},{8,9},{9,8},{10,11... | collective-permute-start | bytes 18440 | tf_op jit(solution)/shard_map/ppermute | solution.py:347
  76.5 0.9 copy-start.33
  79.6 1.9 %copy-start.1 = (bf16[128,96,128]{2,1,0:T(8,128)(2,1)S(1)}, bf16[128,96,128]{2,1,0:T(8,128)(2,1)}, u32[]{:S(2)}) copy-start(bf16[128,96,128]{2,1,0:T(8,128)(2,1)} %copy-done) | copy-start | bytes 9437188
  81.5 1.6 %copy-start.4 = (bf16[128,64,128]{2,1,0:T(8,128)(2,1)S(1)}, bf16[128,64,128]{2,1,0:T(8,128)(2,1)}, u32[]{:S(2)}) copy-start(bf16[128,64,128]{2,1,0:T(8,128)(2,1)} %copy-done.3) | copy-start | bytes 6291460
  83.0 1.6 %copy-start.7 = (bf16[128,64,128]{2,1,0:T(8,128)(2,1)S(1)}, bf16[128,64,128]{2,1,0:T(8,128)(2,1)}, u32[]{:S(2)}) copy-start(bf16[128,64,128]{2,1,0:T(8,128)(2,1)} %copy-done.6) | copy-start | bytes 6291460
  84.6 1.2 copy-start.10
  85.9 1.2 copy-start.13
  87.1 0.9 copy-start.18
  88.0 6.0 %copy-start.19 = (bf16[2,112,384]{2,1,0:T(8,128)(2,1)S(1)}, bf16[2,112,384]{2,1,0:T(8,128)(2,1)}, u32[]{:S(2)}) copy-start(bf16[2,112,384]{2,1,0:T(8,128)(2,1)} %weights.1) | copy-start | bytes 516100
  91.3 0.9 copy-start.16
  92.3 12.2 %collective-permute-start.7 = (bf16[4,4,100,128]{3,2,1,0:T(8,128)(2,1)}, bf16[4,4,100,128]{3,2,1,0:T(8,128)(2,1)}, u32[]{:S(2)}, u32[]{:S(2)}) collective-permute-start(bf16[4,4,100,128]{3,2,1,0:T(8,128)(2,1)} %get-tuple-element.34), channel_id=1, source_target_pairs={{0,2},{2,0},{4,6},{6,4},{8,10},{10,8},{12,14},{14,12},{1,3},{3,1},... | collective-permute-start | bytes 1228808 | tf_op jit(solution)/shard_map/ppermute | solution.py:355
  94.0 1.9 %copy-start.2 = (bf16[128,96,128]{2,1,0:T(8,128)(2,1)S(1)}, bf16[128,96,128]{2,1,0:T(8,128)(2,1)}, u32[]{:S(2)}) copy-start(bf16[128,96,128]{2,1,0:T(8,128)(2,1)} %copy-done) | copy-start | bytes 9437188
  95.9 1.6 %copy-start.5 = (bf16[128,64,128]{2,1,0:T(8,128)(2,1)S(1)}, bf16[128,64,128]{2,1,0:T(8,128)(2,1)}, u32[]{:S(2)}) copy-start(bf16[128,64,128]{2,1,0:T(8,128)(2,1)} %copy-done.3) | copy-start | bytes 6291460
  97.5 1.6 %copy-start.8 = (bf16[128,64,128]{2,1,0:T(8,128)(2,1)S(1)}, bf16[128,64,128]{2,1,0:T(8,128)(2,1)}, u32[]{:S(2)}) copy-start(bf16[128,64,128]{2,1,0:T(8,128)(2,1)} %copy-done.6) | copy-start | bytes 6291460
  99.0 1.2 copy-start.11
  100.3 1.2 copy-start.14
  101.5 3.9 %copy-start.17 = (f32[4,4,100,128]{3,2,1,0:T(8,128)S(1)}, f32[4,4,100,128]{3,2,1,0:T(8,128)}, u32[]{:S(2)}) copy-start(f32[4,4,100,128]{3,2,1,0:T(8,128)} %copy-done.16) | copy-start | bytes 2457604
  104.0 10.4 %collective-permute-start.10 = (bf16[4,4,100,128]{3,2,1,0:T(8,128)(2,1)S(1)}, bf16[4,4,100,128]{3,2,1,0:T(8,128)(2,1)S(1)}, u32[]{:S(2)}, u32[]{:S(2)}) collective-permute-start(bf16[4,4,100,128]{3,2,1,0:T(8,128)(2,1)S(1)} %get-tuple-element.36), channel_id=1, source_target_pairs={{0,2},{2,0},{4,6},{6,4},{8,10},{10,8},{12,14},{14,12},{1,3},{3,1},... | collective-permute-start | bytes 1228808 | tf_op jit(solution)/shard_map/ppermute | solution.py:355
  106.5 9.8 %collective-permute-start.8 = (bf16[2,4,100,128]{3,1,2,0:T(4,128)(2,1)S(1)}, bf16[2,4,100,128]{3,1,2,0:T(4,128)(2,1)S(1)}, u32[]{:S(2)}, u32[]{:S(2)}) collective-permute-start(bf16[2,4,100,128]{3,1,2,0:T(4,128)(2,1)S(1)} %fusion.2), channel_id=1, source_target_pairs={{0,4},{2,6},{4,0},{6,2},{8,12},{10,14},{12,8},{14,10},{1,5},{3,7},... | collective-permute-start | bytes 614408 | tf_op jit(solution)/shard_map/ppermute | solution.py:369
  114.7 6.1 %collective-permute-start.11 = (bf16[2,4,100,128]{3,1,2,0:T(4,128)(2,1)S(1)}, bf16[2,4,100,128]{3,1,2,0:T(4,128)(2,1)S(1)}, u32[]{:S(2)}, u32[]{:S(2)}) collective-permute-start(bf16[2,4,100,128]{3,1,2,0:T(4,128)(2,1)S(1)} %fusion.3), channel_id=1, source_target_pairs={{0,4},{2,6},{4,0},{6,2},{8,12},{10,14},{12,8},{14,10},{1,5},{3,7},... | collective-permute-start | bytes 614408 | tf_op jit(solution)/shard_map/ppermute | solution.py:369
  116.5 8.9 %collective-permute-start.9 = (bf16[1,4,100,128]{3,1,2,0:T(4,128)(2,1)S(1)}, bf16[1,4,100,128]{3,1,2,0:T(4,128)(2,1)S(1)}, u32[]{:S(2)}, u32[]{:S(2)}) collective-permute-start(bf16[1,4,100,128]{3,1,2,0:T(4,128)(2,1)S(1)} %fusion.7), channel_id=1, source_target_pairs={{0,8},{2,10},{4,12},{6,14},{8,0},{10,2},{12,4},{14,6},{1,9},{3,11}... | collective-permute-start | bytes 307208 | tf_op jit(solution)/shard_map/ppermute | solution.py:369
  120.8 5.7 %collective-permute-start.12 = (bf16[1,4,100,128]{3,1,2,0:T(4,128)(2,1)S(1)}, bf16[1,4,100,128]{3,1,2,0:T(4,128)(2,1)S(1)}, u32[]{:S(2)}, u32[]{:S(2)}) collective-permute-start(bf16[1,4,100,128]{3,1,2,0:T(4,128)(2,1)S(1)} %fusion.4), channel_id=1, source_target_pairs={{0,8},{2,10},{4,12},{6,14},{8,0},{10,2},{12,4},{14,6},{1,9},{3,11}... | collective-permute-start | bytes 307208 | tf_op jit(solution)/shard_map/ppermute | solution.py:369

commit v2 on v1

v2 whole, which is shorter than its diff:
```python
import functools

import jax
import jax.numpy as jnp
from jax import lax
from jax.experimental import pallas as pl
from jax.experimental.pallas import tpu as pltpu
from jax.sharding import PartitionSpec as P

F32 = jnp.float32
BF16 = jnp.bfloat16
LOW = -1e30
GROUP = 16
PAD = 8
DEEP = 16
MIB = 1 << 20


def nt(a, b, precision=None):
    return lax.dot_general(
        a, b, (((1,), (1,)), ((), ())), preferred_element_type=F32, precision=precision
    )


def nn(a, b):
    return lax.dot_general(a, b, (((1,), (0,)), ((), ())), preferred_element_type=F32)


def cost(microseconds):
    return pl.CostEstimate(
        flops=int(microseconds * 1e9), transcendentals=0, bytes_accessed=int(microseconds * 3e6)
    )


def pinned(shape, dtype):
    return pltpu.VMEM(shape, dtype)


def held(x):
    return pltpu.with_memory_space_constraint(x, pltpu.VMEM)


def filters_kernel(ctf, band, left, right):
    bins, width = ctf.shape

    def negated(v):
        at = (width - lax.broadcasted_iota(jnp.int32, v.shape, 1)) % width
        return jnp.take_along_axis(v, at, axis=1)

    def rolled(row):
        return pltpu.roll(jnp.broadcast_to(row, (width, width)), 0, 1, stride=1, stride_axis=0)

    def with_delta(v):
        return v + jnp.where(lax.broadcasted_iota(jnp.int32, v.shape, 1) == 0, 1.0, 0.0)

    highest = lax.Precision.HIGHEST
    kernels = with_delta(ctf[...])
    bands = with_delta(jnp.broadcast_to(band[...], (8, width)))
    forward = nt(kernels, rolled(negated(bands)[:1]), highest)
    backward = nt(negated(kernels), rolled(bands[:1]), highest)
    for b in range(bins):
        left[b] = rolled(backward[b : b + 1]).astype(BF16)
        right[b] = rolled(forward[b : b + 1]).astype(BF16)


def build_filters(ctf, band):
    bins, width = ctf.shape
    return pl.pallas_call(
        filters_kernel,
        out_shape=(pinned((bins, width, width), BF16),) * 2,
        cost_estimate=cost(3),
        name="filters",
    )(ctf, band.reshape(1, width))


def refs_kernel(refs, out, norm, scratch, *, padded):
    classes, _, rows, width = refs.shape
    pitch = rows + PAD
    j = pl.program_id(0)

    def block(start, count):
        for k in range(GROUP):
            if k < count:
                scratch[pl.ds(k * pitch, rows)] = refs[start + k, 0].astype(F32)
            else:
                scratch[pl.ds(k * pitch, rows)] = jnp.zeros((rows, width), F32)
        at = pl.multiple_of(j * padded + start, GROUP)

        def step(r, acc):
            v = scratch[pl.ds(r, GROUP, stride=pitch)]
            out[r, pl.ds(at, GROUP)] = v.astype(BF16)
            return acc + v * v

        acc = lax.fori_loop(0, rows, step, jnp.zeros((GROUP, width), F32), unroll=32)
        total = 0.5 * jnp.sum(acc, axis=1, keepdims=True)
        norm[pl.ds(at, GROUP)] = jnp.broadcast_to(total, (GROUP, width))

    full = classes // GROUP

    @pl.loop(0, full)
    def _(i):
        block(i * GROUP, GROUP)

    if classes % GROUP:
        block(full * GROUP, classes % GROUP)


def lay_refs(refs, padded):
    classes, rots, rows, width = refs.shape
    vmem = pl.BlockSpec(memory_space=pltpu.VMEM)
    return pl.pallas_call(
        functools.partial(refs_kernel, padded=padded),
        grid=(rots,),
        in_specs=[pl.BlockSpec((classes, 1, rows, width), lambda j: (0, j, 0, 0))],
        out_specs=(vmem, vmem),
        out_shape=(
            pinned((rows, rots * padded, width), BF16),
            pinned((rots * padded, width), F32),
        ),
        scratch_shapes=[pltpu.VMEM((GROUP * (rows + PAD), width), F32)],
        compiler_params=pltpu.CompilerParams(vmem_limit_bytes=28 * MIB),
        cost_estimate=cost(9),
        name="refs",
    )(pltpu.with_memory_space_constraint(refs, pltpu.HBM))


def filter_kernel(where, bins, mine, sib, left, right, *rest, skip, at):
    plain, turned, scr, scr_t = rest[-4:]
    count, half, width = mine.shape
    top = where[0] == 0
    pitch = width + PAD

    @pl.loop(0, count // GROUP)
    def _(g):
        base = pl.multiple_of(g * GROUP, GROUP)
        for i in range(GROUP):
            b = bins[skip + base + i]
            a = mine[base + i]
            o = sib[base + i]
            x = jnp.concatenate([jnp.where(top, a, o), jnp.where(top, o, a)], axis=0)
            f = nn(left[b], nn(x, right[b]).astype(BF16))
            scr[pl.ds(i * pitch, width)] = f
            scr_t[pl.ds(i * pitch, width)] = f.T
        to = pl.multiple_of(at + base, GROUP)
        for r in range(width):
            plain[r, pl.ds(to, GROUP)] = scr[pl.ds(r, GROUP, stride=pitch)].astype(BF16)
            turned[r, pl.ds(to, GROUP)] = scr_t[pl.ds(r, GROUP, stride=pitch)].astype(BF16)


def filter_chunk(where, bins, mine, sib, left, right, buffers, total, skip, at):
    count, half, width = mine.shape
    smem = pl.BlockSpec(memory_space=pltpu.SMEM)
    vmem = pl.BlockSpec(memory_space=pltpu.VMEM)
    buffers = [held(b) for b in buffers]
    return pl.pallas_call(
        functools.partial(filter_kernel, skip=skip, at=at),
        in_specs=[smem, smem] + [vmem] * (4 + len(buffers)),
        out_specs=(vmem, vmem),
        out_shape=(pinned((2 * half, total, width), BF16),) * 2,
        scratch_shapes=[pltpu.VMEM((GROUP * (2 * half + PAD), width), F32)] * 2,
        input_output_aliases={6 + i: i for i in range(len(buffers))},
        compiler_params=pltpu.CompilerParams(vmem_limit_bytes=24 * MIB),
        cost_estimate=cost(count * 0.1),
        name="filter",
    )(where, bins, mine, sib, held(left), held(right), *buffers)


def score_kernel(plain, refs, norm, mask, noise, scaled, stats):
    rows, height, width = refs.shape
    count = mask.shape[1]

    def step(i, acc):
        at = [DEEP * i + a for a in range(DEEP)]
        lhs = jnp.concatenate([refs[r] for r in at], axis=1)
        rhs = jnp.concatenate([plain[r] for r in at], axis=1)
        return acc + nt(lhs, rhs)

    inner = lax.fori_loop(0, rows // DEEP, step, jnp.zeros((height, count), F32))
    rots = height // mask.shape[0]
    allowed = jnp.concatenate([mask[...]] * rots, axis=0) > 0
    s = jnp.where(allowed, (inner - norm[:, :1]) / noise[...], LOW)
    scaled[...] = s
    peak = jnp.max(s, axis=0, keepdims=True)
    total = jnp.sum(jnp.exp(s - peak), axis=0, keepdims=True)
    stats[0:1] = peak
    stats[1:2] = total
    stats[2:] = jnp.zeros((stats.shape[0] - 2, count), F32)


def score(plain, refs, norm, mask, noise):
    count = mask.shape[1]
    height = refs.shape[1]
    return pl.pallas_call(
        score_kernel,
        out_shape=(
            pinned((height, count), F32),
            pinned((8, count), F32),
        ),
        compiler_params=pltpu.CompilerParams(vmem_limit_bytes=24 * MIB),
        cost_estimate=cost(5),
        name="score",
    )(held(plain), held(refs), held(norm), mask, noise)


def weights_kernel(scaled, mine, other, rot, out):
    rots, padded, _ = rot.shape
    count = scaled.shape[1]
    theirs = jnp.concatenate([other[:, count // 2 :], other[:, : count // 2]], axis=1)
    peak = jnp.maximum(mine[0:1], theirs[0:1])
    total = mine[1:2] * jnp.exp(mine[0:1] - peak) + theirs[1:2] * jnp.exp(theirs[0:1] - peak)
    w = (jnp.exp(scaled[...] - peak) / total).astype(BF16).astype(F32)
    quarters = []
    for q in range(4):
        acc = jnp.zeros((padded, count), F32)
        for j in range(rots):
            acc = acc + jnp.where(rot[j] == q, w[j * padded : (j + 1) * padded], 0.0)
        quarters.append(acc)
    for row, pair in enumerate(((0, 3), (2, 1))):
        out[row] = jnp.concatenate([quarters[q] for q in pair], axis=1).astype(BF16)


def make_weights(scaled, mine, other, rot):
    _, padded, _ = rot.shape
    count = scaled.shape[1]
    return pl.pallas_call(
        weights_kernel,
        out_shape=pinned((2, padded, 2 * count), BF16),
        cost_estimate=cost(2),
        name="weights",
    )(held(scaled), held(mine), other, rot)


def sums_kernel(where, weights, plain, turned, send, keep, *, dom, start, classes):
    _, rows, _, width = send.shape
    height = plain.shape[0]
    block = height // 2 // dom
    first = where[0] * (height // 2) + start
    parity = where[1]
    straight = weights[0]
    mirrored = weights[1]
    flip = width - 1 - lax.broadcasted_iota(jnp.int32, (straight.shape[0], width), 1)

    @pl.loop(0, dom // 2)
    def _(g):
        for r in range(rows):
            both = [first + (2 * g + side) * block + r for side in (1 - parity, parity)]
            direct = jnp.concatenate(
                [jnp.concatenate([plain[i], turned[height - 1 - i]], axis=0) for i in both], axis=1
            )
            mirror = jnp.concatenate(
                [jnp.concatenate([plain[height - 1 - i], turned[i]], axis=0) for i in both], axis=1
            )
            direct = nn(straight, direct)
            mirror = nn(mirrored, mirror)
            away, here = [
                direct[:, at : at + width]
                + jnp.take_along_axis(mirror[:, at : at + width], flip, axis=1)
                for at in (0, width)
            ]
            send[g, r] = away[:classes].astype(BF16)
            keep[g, r] = here[:classes]


def sums(where, weights, plain, turned, dom, start, rows, classes):
    width = plain.shape[2]
    smem = pl.BlockSpec(memory_space=pltpu.SMEM)
    vmem = pl.BlockSpec(memory_space=pltpu.VMEM)
    return pl.pallas_call(
        functools.partial(sums_kernel, dom=dom, start=start, classes=classes),
        in_specs=[smem] + [vmem] * 3,
        out_shape=(
            jax.ShapeDtypeStruct((dom // 2, rows, classes, width), BF16),
            pinned((dom // 2, rows, classes, width), F32),
        ),
        compiler_params=pltpu.CompilerParams(vmem_limit_bytes=24 * MIB),
        cost_estimate=cost(rows * 0.8),
        name="sums",
    )(where, held(weights), held(plain), held(turned))


def fold_kernel(at, keep, got, *outs, fan):
    rest = keep.shape[0] // fan
    for m, out in enumerate(outs):
        for i in range(rest):
            b = i * fan + (at[0] ^ m)
            value = keep[b] + got[b].astype(F32)
            out[i] = value.astype(out.dtype)


def fold(at, keep, got, fan):
    rest = (keep.shape[0] // fan,) + keep.shape[1:]
    return pl.pallas_call(
        functools.partial(fold_kernel, fan=fan),
        in_specs=[pl.BlockSpec(memory_space=pltpu.SMEM)]
        + [pl.BlockSpec(memory_space=pltpu.VMEM)] * 2,
        out_shape=(pinned(rest, F32),) + (jax.ShapeDtypeStruct(rest, BF16),) * (fan - 1),
        compiler_params=pltpu.CompilerParams(vmem_limit_bytes=24 * MIB),
        cost_estimate=cost(1),
        name="fold",
    )(at.reshape(1), held(keep), got)


def finish_kernel(*args, counts):
    out = args[-1]
    block_rows = sum(rows for rows, _ in counts)
    classes = args[0].shape[2]
    at = 0
    row = 0
    for rows, pieces in counts:
        for r in range(rows):
            value = args[at][0, r]
            for other in args[at + 1 : at + pieces]:
                value = value + other[0, r].astype(F32)
            out[pl.ds(row, classes, stride=block_rows)] = value
            row += 1
        at += pieces


def finish(done):
    counts = tuple((pieces[0].shape[1], len(pieces)) for pieces in done)
    _, _, classes, width = done[0][0].shape
    block_rows = sum(rows for rows, _ in counts)
    flat = [held(p) if i == 0 else p for pieces in done for i, p in enumerate(pieces)]
    out = pl.pallas_call(
        functools.partial(finish_kernel, counts=counts),
        out_shape=jax.ShapeDtypeStruct((classes * block_rows, width), F32),
        compiler_params=pltpu.CompilerParams(vmem_limit_bytes=24 * MIB),
        cost_estimate=cost(1),
        name="finish",
    )(*flat)
    return out.reshape(classes, block_rows, width)


def y_pieces(particles):
    last = GROUP
    first = particles // 3 // GROUP * GROUP
    return (first, particles - first - last, last)


def row_pieces(rows):
    if rows < 4:
        return (rows,)
    part = -(-rows // 3)
    return (part, part, rows - 2 * part)


def local(
    images, defocus_bin, ctf_kernels, band_kernel, references, rot_index, class_mask, noise_var
):
    section_at = lax.axis_index("section")
    class_at = lax.axis_index("cls")
    dom_at = lax.axis_index("dom")
    dom = lax.axis_size("dom")
    particles, half, width = images.shape
    classes, rots = rot_index.shape
    padded = -(-classes // GROUP) * GROUP
    swap = [(0, 1), (1, 0)]
    over_cls = functools.partial(lax.ppermute, axis_name="cls", perm=swap)
    over_section = functools.partial(lax.ppermute, axis_name="section", perm=swap)

    sizes = y_pieces(particles)
    starts = [sum(sizes[:i]) for i in range(len(sizes))]
    remote = [over_cls(images[a : a + n]) for a, n in zip(starts, sizes)]
    other_bins = over_cls(defocus_bin)
    own_sib = over_section(images)

    where = jnp.stack([section_at, dom_at % 2]).astype(jnp.int32)
    left, right = build_filters(ctf_kernels, band_kernel)
    refs, norm = lay_refs(references, padded)

    def arranged(a):
        parts = a.reshape((2, particles) + a.shape[1:])
        return jnp.concatenate(
            [
                lax.dynamic_index_in_dim(parts, class_at, 0, False),
                lax.dynamic_index_in_dim(parts, 1 - class_at, 0, False),
            ]
        )

    mask = jnp.pad(arranged(class_mask).T, ((0, padded - classes), (0, 0)))
    noise = arranged(noise_var).reshape(1, 2 * particles)
    rot = jnp.pad(rot_index.T, ((0, 0), (0, padded - classes)))[:, :, None]

    total = 2 * particles
    buffers = filter_chunk(
        where, defocus_bin, images, own_sib, left, right, (), total, 0, 0
    )
    for a, piece in zip(starts, remote):
        buffers = filter_chunk(
            where, other_bins, piece, over_section(piece), left, right, buffers, total, a,
            particles + a,
        )
    plain, turned = buffers

    scaled, stats = score(plain, refs, norm, mask, noise)
    weights = make_weights(scaled, stats, over_cls(stats), rot)

    start = 0
    done = []
    for rows in row_pieces(half // dom):
        send, keep = sums(where, weights, plain, turned, dom, start, rows, classes)
        start += rows
        got = lax.ppermute(send, "dom", [(i, i ^ 1) for i in range(dom)])
        bit = 1
        while keep.shape[0] > 4:
            at = ((dom_at >> bit) & 1).astype(jnp.int32)
            keep, send = fold(at, keep, got, 2)
            got = lax.ppermute(send, "dom", [(i, i ^ (1 << bit)) for i in range(dom)])
            bit += 1
        fan = keep.shape[0]
        at = ((dom_at >> bit) & (fan - 1)).astype(jnp.int32)
        keep, *sends = fold(at, keep, got, fan)
        done.append(
            [keep]
            + [
                lax.ppermute(s, "dom", [(i, i ^ ((m + 1) << bit)) for i in range(dom)])
                for m, s in enumerate(sends)
            ]
        )
    return finish(done)


def solution(mesh):
    return jax.shard_map(
        local,
        mesh=mesh,
        in_specs=(
            P(("dom", "cls"), "section", None),
            P(("dom", "cls")),
            P(),
            P(),
            P("cls", None, None, None),
            P("cls", None),
            P("dom", "cls"),
            P("dom"),
        ),
        out_specs=P("cls", ("section", "dom"), None),
        check_vma=False,
    )
```

time: 128 us -> 116 us (0.906)
  local copies, waits for them, and re-layouts: 40.3 us -> 18.4 us
  starting transfers between devices: 18.2 us -> 24.1 us
  waiting for transfers between devices: 28.4 us -> 33.1 us
  other arithmetic: 4.14 us -> 0.25 us
  Pallas kernels: 36.2 us -> 39.9 us
    unnamed x78 -> x34, local copies, waits for them, and re-layouts: 34.5 us -> 11.8 us
    pallas_call x9 -> x15, Pallas kernels: 36.2 us -> 39.9 us  [the longest x4 15.4 us: filter_chunk(): pl.pallas_call(functools.partial(filter_kernel, skip=skip, at=at), in_spe...]
    ppermute x1, starting transfers between devices: 0.03 us -> 2.52 us  [local(): other_bins = over_cls(defocus_bin)]
    ppermute x7 -> x13, waiting for transfers between devices: 22.4 us -> 24.8 us  [the longest x3 15.2 us: local(): remote = [over_cls(images[a:a + n]) for a, n in zip(starts, sizes)]]
    ppermute x2 -> x3, waiting for transfers between devices: 6.01 us -> 8.3 us  [local(): got = lax.ppermute(send, 'dom', [(i, i ^ 1) for i in range(dom)])]
    slice x5 -> x3, local copies, waits for them, and re-layouts: 3.59 us -> 5.63 us  [local(): remote = [over_cls(images[a:a + n]) for a, n in zip(starts, sizes)]]
    ppermute x7 -> x13, starting transfers between devices: 15.1 us -> 16.9 us  [the longest x9 14.5 us: local(): lax.ppermute(s, 'dom', [(i, i ^ m + 1 << bit) for i in range(dom)])]
    ppermute x2 -> x3, starting transfers between devices: 2.09 us -> 3.65 us  [local(): got = lax.ppermute(send, 'dom', [(i, i ^ 1) for i in range(dom)])]
  transfers between devices with their start and end apart: 13 -> 21, of which waited for: 6 -> 7; matrix products, arithmetic and copies ran while one was open for 7% -> 6% of each run, Pallas kernels for 16% -> 23%
where the time goes in v2:
time: 116 us
  Pallas kernels  39.9 us (34%)
  waiting for transfers between devices  33.1 us (29%)
  starting transfers between devices  24.1 us (21%)
  local copies, waits for them, and re-layouts  18.4 us (16%)
    pallas_call x4, Pallas kernels, filter_chunk(): pl.pallas_call(functools.partial(filter_kernel, skip=skip, at=at), in_spe...  15.4 us
    ppermute x3, waiting for transfers between devices, local(): remote = [over_cls(images[a:a + n]) for a, n in zip(starts, sizes)]  15.2 us
    ppermute x9, starting transfers between devices, local(): lax.ppermute(s, 'dom', [(i, i ^ m + 1 << bit) for i in range(dom)])  14.5 us
    unnamed x34, local copies, waits for them, and re-layouts  11.8 us
    pallas_call x1, Pallas kernels, lay_refs(): pl.pallas_call(functools.partial(refs_kernel, padded=padded), grid=(rots,...  8.85 us
    ppermute x3, waiting for transfers between devices, local(): got = lax.ppermute(send, 'dom', [(i, i ^ 1) for i in range(dom)])  8.3 us
    pallas_call x3, Pallas kernels, sums(): pl.pallas_call(functools.partial(sums_kernel, dom=dom, start=start, class...  7.16 us
    ppermute x9, waiting for transfers between devices, local(): lax.ppermute(s, 'dom', [(i, i ^ m + 1 << bit) for i in range(dom)])  7.06 us
  transfers between devices with their start and end apart: 21, of which 7 were waited for; matrix products, arithmetic and copies ran while one was open for 6% of the time, Pallas kernels for 23%

profile of v2, /device:TPU:0, one launch (start us, length us, event | category | flops | bytes accessed | tf_op | source)
XLA Modules:
  0.0 115.9 jit_solution(1136200410461926511)
XLA Ops:
  0.0 0.5 collective-permute-start.7
  0.5 2.5 %collective-permute-start = (s32[96]{0:T(128)}, s32[96]{0:T(128)S(1)}, u32[]{:S(2)}, u32[]{:S(2)}) collective-permute-start(s32[96]{0:T(128)} %bins.1), channel_id=1, source_target_pairs={{0,1},{1,0},{2,3},{3,2},{4,5},{5,4},{6,7},{7,6},{8,9},{9,8},{10,11... | collective-permute-start | bytes 1160 | tf_op jit(solution)/shard_map/ppermute | solution.py:364
  3.0 1.9 %slice.11 = bf16[32,64,128]{2,1,0:T(8,128)(2,1)} slice(bf16[96,64,128]{2,1,0:T(8,128)(2,1)} %mine.1), slice={[0:32], [0:64], [0:128]} | slice | bytes 1048576 | tf_op jit(solution)/shard_map/slice | solution.py:363
  4.8 0.0 collective-permute-start.5
  4.9 2.1 %slice.10 = bf16[48,64,128]{2,1,0:T(8,128)(2,1)} slice(bf16[96,64,128]{2,1,0:T(8,128)(2,1)} %mine.1), slice={[32:80], [0:64], [0:128]} | slice | bytes 1572864 | tf_op jit(solution)/shard_map/slice | solution.py:363
  6.9 2.0 %collective-permute-start.3 = (bf16[48,64,128]{2,1,0:T(8,128)(2,1)}, bf16[48,64,128]{2,1,0:T(8,128)(2,1)}, u32[]{:S(2)}, u32[]{:S(2)}) collective-permute-start(bf16[48,64,128]{2,1,0:T(8,128)(2,1)} %slice.10), channel_id=1, source_target_pairs={{0,1},{1,0},{2,3},{3,2},{4,5},{5,4},{6,7},{7,6},{8,9},{9,8},{10,11... | collective-permute-start | bytes 2359304 | tf_op jit(solution)/shard_map/ppermute | solution.py:363
  9.0 1.7 %slice.9 = bf16[16,64,128]{2,1,0:T(8,128)(2,1)} slice(bf16[96,64,128]{2,1,0:T(8,128)(2,1)} %mine.1), slice={[80:96], [0:64], [0:128]} | slice | bytes 524288 | tf_op jit(solution)/shard_map/slice | solution.py:363
  10.6 0.0 collective-permute-start.1
  10.6 8.9 %refs.2 = (bf16[128,336,128]{2,1,0:T(8,128)(2,1)S(1)}, f32[336,128]{1,0:T(8,128)S(1)}) custom-call(bf16[100,3,128,128]{3,2,1,0:T(8,128)(2,1)} %refs.3), custom_call_target="tpu_custom_call" | custom-call | flops 8999999488 | bytes 27000000 | tf_op jit(solution)/shard_map/refs/pallas_call | solution.py:111
  19.5 4.2 %copy-done.6 = bf16[128,336,128]{2,1,0:T(8,128)(2,1)} copy-done((bf16[128,336,128]{2,1,0:T(8,128)(2,1)}, bf16[128,336,128]{2,1,0:T(8,128)(2,1)S(1)}, u32[]{:S(2)}) %copy-start.6) | copy-done | bytes 11010072
  23.6 0.7 copy-done.7
  24.3 0.1 copy.20
  24.4 0.1 copy.21
  24.5 0.1 add_bitcast_fusion
  24.6 0.1 pad_add_fusion.where
  24.7 0.1 reshape.23
  24.8 0.1 pad_maximum_fusion
  24.9 1.5 %filters.1 = (bf16[16,128,128]{2,1,0:T(8,128)(2,1)S(1)}, bf16[16,128,128]{2,1,0:T(8,128)(2,1)S(1)}) custom-call(f32[16,128]{1,0:T(8,128)} %ctf.1, f32[1,128]{1,0:T(1,128)} %bitcast.25), custom_call_target="tpu_custom_call" | custom-call | flops 3000000000 | bytes 9000000 | tf_op jit(solution)/shard_map/filters/pallas_call | solution.py:68
  26.4 15.2 %collective-permute-done.1.mine = bf16[16,64,128]{2,1,0:T(8,128)(2,1)S(1)} collective-permute-done((bf16[16,64,128]{2,1,0:T(8,128)(2,1)}, bf16[16,64,128]{2,1,0:T(8,128)(2,1)S(1)}, u32[]{:S(2)}, u32[]{:S(2)}) %collective-permute-start.1) | collective-permute-done | bytes 262176 | tf_op jit(solution)/shard_map/ppermute | solution.py:363
  41.6 0.0 collective-permute-done.5.mine
  41.6 0.5 collective-permute-start.6
  42.1 0.0 collective-permute-done.3.mine
  42.1 0.1 collective-permute-start.4
  42.2 7.2 %filter.4 = (bf16[128,192,128]{2,1,0:T(8,128)(2,1)S(1)}, bf16[128,192,128]{2,1,0:T(8,128)(2,1)S(1)}) custom-call(s32[2]{0:T(128)S(1)} %pad_add_fusion.where, s32[96]{0:T(128)S(1)} %copy-done.5, bf16[96,64,128]{2,1,0:T(8,128)(2,1)S(1)} %copy-done.4, bf16[96,64,128]{2,1,0:T(8,128)(2,1)} %collective-permute-done.7.sib, ...), custom_call_target="tpu_custom_call" | custom-call | flops 9600000000 | bytes 28800000 | tf_op jit(solution)/shard_map/filter/pallas_call | solution.py:155
  49.4 0.0 collective-permute-done.bins
  49.4 0.0 collective-permute-done.6.sib
  49.4 2.5 %filter.5 = (bf16[128,192,128]{2,1,0:T(8,128)(2,1)S(1)}, bf16[128,192,128]{2,1,0:T(8,128)(2,1)S(1)}) custom-call(s32[2]{0:T(128)S(1)} %pad_add_fusion.where, s32[96]{0:T(128)S(1)} %collective-permute-done.bins, bf16[32,64,128]{2,1,0:T(8,128)(2,1)S(1)} %collective-permute-done.5.mine, ...), custom_call_target="tpu_custom_call", output_to_operand_aliasing={{0}: (6, {}), {1}: (7, {})} | custom-call | flops 3200000000 | bytes 9600000 | tf_op jit(solution)/shard_map/filter/pallas_call | solution.py:155
  51.9 0.0 slice-start
  51.9 0.0 slice-start.1
  51.9 4.2 %filter.6 = (bf16[128,192,128]{2,1,0:T(8,128)(2,1)S(1)}, bf16[128,192,128]{2,1,0:T(8,128)(2,1)S(1)}) custom-call(s32[2]{0:T(128)S(1)} %pad_add_fusion.where, s32[96]{0:T(128)S(1)} %collective-permute-done.bins, bf16[48,64,128]{2,1,0:T(8,128)(2,1)} %collective-permute-done.3.mine, ...), custom_call_target="tpu_custom_call", output_to_operand_aliasing={{0}: (6, {}), {1}: (7, {})} | custom-call | flops 4800000000 | bytes 14400000 | tf_op jit(solution)/shard_map/filter/pallas_call | solution.py:155
  56.2 0.0 slice-start.2
  56.2 1.5 %filter.7 = (bf16[128,192,128]{2,1,0:T(8,128)(2,1)S(1)}, bf16[128,192,128]{2,1,0:T(8,128)(2,1)S(1)}) custom-call(s32[2]{0:T(128)S(1)} %pad_add_fusion.where, s32[96]{0:T(128)S(1)} %collective-permute-done.bins, bf16[16,64,128]{2,1,0:T(8,128)(2,1)S(1)} %collective-permute-done.1.mine, ...), custom_call_target="tpu_custom_call", output_to_operand_aliasing={{0}: (6, {}), {1}: (7, {})} | custom-call | flops 1600000000 | bytes 4800000 | tf_op jit(solution)/shard_map/filter/pallas_call | solution.py:155
  57.7 0.6 slice-done.2
  58.4 4.6 %score.1 = (f32[336,192]{1,0:T(8,128)S(1)}, f32[8,192]{1,0:T(8,128)S(1)}) custom-call(bf16[128,192,128]{2,1,0:T(8,128)(2,1)S(1)} %get-tuple-element.45.plain, bf16[128,336,128]{2,1,0:T(8,128)(2,1)S(1)} %bitcast.20, f32[336,128]{1,0:T(8,128)S(1)} %copy-done.8, s32[112,192]{1,0:T(8,128)S(1)} %pad.8.mask, f32[1,192]{1,0:T(1,128)S(1)} %bitcast.18), custom_call_target="tpu_custom_call" | custom-call | flops 5000000000 | bytes 15000000 | tf_op jit(solution)/shard_map/score/pallas_call | solution.py:193
  63.0 0.3 collective-permute-start.8
  63.3 0.8 copy.19.rot
  64.1 2.5 %collective-permute-done.8.other = f32[8,192]{1,0:T(8,128)S(1)} collective-permute-done((f32[8,192]{1,0:T(8,128)S(1)}, f32[8,192]{1,0:T(8,128)S(1)}, u32[]{:S(2)}, u32[]{:S(2)}) %collective-permute-start.8) | collective-permute-done | bytes 6176 | tf_op jit(solution)/shard_map/ppermute | solution.py:396
  66.7 0.6 copy-done.12
  67.3 1.3 %weights.1 = bf16[2,112,384]{2,1,0:T(8,128)(2,1)S(1)} custom-call(f32[336,192]{1,0:T(8,128)S(1)} %get-tuple-element.48.scaled, f32[8,192]{1,0:T(8,128)S(1)} %get-tuple-element.49.mine, f32[8,192]{1,0:T(8,128)} %copy-done.12, s32[3,112,1]{2,1,0:T(8,128)} %copy.19.rot), custom_call_target="tpu_custom_call" | custom-call | flops 2000000000 | bytes 6000000 | tf_op jit(solution)/shard_map/weights/pallas_call | solution.py:225
  68.6 2.8 %copy-done.1 = bf16[128,192,128]{2,1,0:T(8,128)(2,1)S(1)} copy-done((bf16[128,192,128]{2,1,0:T(8,128)(2,1)S(1)}, bf16[128,192,128]{2,1,0:T(8,128)(2,1)}, u32[]{:S(2)}) %copy-start.1) | copy-done | bytes 6291480
  71.4 2.8 %copy-done.3 = bf16[128,192,128]{2,1,0:T(8,128)(2,1)S(1)} copy-done((bf16[128,192,128]{2,1,0:T(8,128)(2,1)S(1)}, bf16[128,192,128]{2,1,0:T(8,128)(2,1)}, u32[]{:S(2)}) %copy-start.3) | copy-done | bytes 6291480
  74.1 2.7 %sums.5 = (bf16[4,2,100,128]{3,2,1,0:T(8,128)(2,1)}, f32[4,2,100,128]{3,2,1,0:T(8,128)S(1)}) custom-call(s32[2]{0:T(128)S(1)} %pad_add_fusion.where, bf16[2,112,384]{2,1,0:T(8,128)(2,1)S(1)} %weights.1, bf16[128,192,128]{2,1,0:T(8,128)(2,1)S(1)} %copy-done.1, bf16[128,192,128]{2,1,0:T(8,128)(2,1)S(1)} %copy-done.3), custom_call_target="tpu_custom_call" | custom-call | flops 1600000000 | bytes 4800000 | tf_op jit(solution)/shard_map/sums/pallas_call | solution.py:268
  76.8 2.2 %sums.4 = (bf16[4,3,100,128]{3,2,1,0:T(8,128)(2,1)S(1)}, f32[4,3,100,128]{3,2,1,0:T(8,128)S(1)}) custom-call(s32[2]{0:T(128)S(1)} %pad_add_fusion.where, bf16[2,112,384]{2,1,0:T(8,128)(2,1)S(1)} %weights.1, bf16[128,192,128]{2,1,0:T(8,128)(2,1)S(1)} %copy-done.1, bf16[128,192,128]{2,1,0:T(8,128)(2,1)S(1)} %copy-done.3), custom_call_target="tpu_custom_call" | custom-call | flops 2400000000 | bytes 7200000 | tf_op jit(solution)/shard_map/sums/pallas_call | solution.py:268
  79.1 1.6 %collective-permute-start.17 = (bf16[4,2,100,128]{3,2,1,0:T(8,128)(2,1)}, bf16[4,2,100,128]{3,2,1,0:T(8,128)(2,1)S(1)}, u32[]{:S(2)}, u32[]{:S(2)}) collective-permute-start(bf16[4,2,100,128]{3,2,1,0:T(8,128)(2,1)} %get-tuple-element.64), channel_id=1, source_target_pairs={{0,2},{2,0},{4,6},{6,4},{8,10},{10,8},{12,14},{14,12},{1,3},{3,1},... | collective-permute-start | bytes 614408 | tf_op jit(solution)/shard_map/ppermute | solution.py:403
  80.6 0.5 collective-permute-start.13
  81.2 2.2 %sums.3 = (bf16[4,3,100,128]{3,2,1,0:T(8,128)(2,1)S(1)}, f32[4,3,100,128]{3,2,1,0:T(8,128)S(1)}) custom-call(s32[2]{0:T(128)S(1)} %pad_add_fusion.where, bf16[2,112,384]{2,1,0:T(8,128)(2,1)S(1)} %weights.1, bf16[128,192,128]{2,1,0:T(8,128)(2,1)S(1)} %copy-done.1, bf16[128,192,128]{2,1,0:T(8,128)(2,1)S(1)} %copy-done.3), custom_call_target="tpu_custom_call" | custom-call | flops 2400000000 | bytes 7200000 | tf_op jit(solution)/shard_map/sums/pallas_call | solution.py:268
  83.4 1.6 %collective-permute-start.9 = (bf16[4,3,100,128]{3,2,1,0:T(8,128)(2,1)S(1)}, bf16[4,3,100,128]{3,2,1,0:T(8,128)(2,1)S(1)}, u32[]{:S(2)}, u32[]{:S(2)}) collective-permute-start(bf16[4,3,100,128]{3,2,1,0:T(8,128)(2,1)S(1)} %get-tuple-element.52), channel_id=1, source_target_pairs={{0,2},{2,0},{4,6},{6,4},{8,10},{10,8},{12,14},{14,12},{1,3},{3,1},... | collective-permute-start | bytes 921608 | tf_op jit(solution)/shard_map/ppermute | solution.py:403
  85.0 2.6 %collective-permute-done.17.got = bf16[4,2,100,128]{3,2,1,0:T(8,128)(2,1)S(1)} collective-permute-done((bf16[4,2,100,128]{3,2,1,0:T(8,128)(2,1)}, bf16[4,2,100,128]{3,2,1,0:T(8,128)(2,1)S(1)}, u32[]{:S(2)}, u32[]{:S(2)}) %collective-permute-start.17) | collective-permute-done | bytes 204832 | tf_op jit(solution)/shard_map/ppermute | solution.py:403
  87.6 1.6 %collective-permute-start.18 = (bf16[1,2,100,128]{3,2,1,0:T(8,128)(2,1)S(1)}, bf16[1,2,100,128]{3,2,1,0:T(8,128)(2,1)S(1)}, u32[]{:S(2)}, u32[]{:S(2)}) collective-permute-start(bf16[1,2,100,128]{3,2,1,0:T(8,128)(2,1)S(1)} %get-tuple-element.66), channel_id=1, source_target_pairs={{0,4},{2,6},{4,0},{6,2},{8,12},{10,14},{12,8},{14,10},{1,5},{3,7},... | collective-permute-start | bytes 153608 | tf_op jit(solution)/shard_map/ppermute | solution.py:416
  89.2 2.6 %collective-permute-start.19 = (bf16[1,2,100,128]{3,2,1,0:T(8,128)(2,1)S(1)}, bf16[1,2,100,128]{3,2,1,0:T(8,128)(2,1)S(1)}, u32[]{:S(2)}, u32[]{:S(2)}) collective-permute-start(bf16[1,2,100,128]{3,2,1,0:T(8,128)(2,1)S(1)} %get-tuple-element.67), channel_id=1, source_target_pairs={{0,8},{2,10},{4,12},{6,14},{8,0},{10,2},{12,4},{14,6},{1,9},{3,11}... | collective-permute-start | bytes 153608 | tf_op jit(solution)/shard_map/ppermute | solution.py:416
  91.8 0.2 collective-permute-start.20
  92.0 2.3 %collective-permute-done.13.got = bf16[4,3,100,128]{3,2,1,0:T(8,128)(2,1)S(1)} collective-permute-done((bf16[4,3,100,128]{3,2,1,0:T(8,128)(2,1)S(1)}, bf16[4,3,100,128]{3,2,1,0:T(8,128)(2,1)S(1)}, u32[]{:S(2)}, u32[]{:S(2)}) %collective-permute-start.13) | collective-permute-done | bytes 307232 | tf_op jit(solution)/shard_map/ppermute | solution.py:403
  94.4 0.1 fold.4
  94.5 1.6 %collective-permute-start.14 = (bf16[1,3,100,128]{3,2,1,0:T(8,128)(2,1)S(1)}, bf16[1,3,100,128]{3,2,1,0:T(8,128)(2,1)S(1)}, u32[]{:S(2)}, u32[]{:S(2)}) collective-permute-start(bf16[1,3,100,128]{3,2,1,0:T(8,128)(2,1)S(1)} %get-tuple-element.60), channel_id=1, source_target_pairs={{0,4},{2,6},{4,0},{6,2},{8,12},{10,14},{12,8},{14,10},{1,5},{3,7},... | collective-permute-start | bytes 230408 | tf_op jit(solution)/shard_map/ppermute | solution.py:416
  96.1 3.4 %collective-permute-done.9.got = bf16[4,3,100,128]{3,2,1,0:T(8,128)(2,1)S(1)} collective-permute-done((bf16[4,3,100,128]{3,2,1,0:T(8,128)(2,1)S(1)}, bf16[4,3,100,128]{3,2,1,0:T(8,128)(2,1)S(1)}, u32[]{:S(2)}, u32[]{:S(2)}) %collective-permute-start.9) | collective-permute-done | bytes 307232 | tf_op jit(solution)/shard_map/ppermute | solution.py:403
  99.5 2.6 %collective-permute-start.15 = (bf16[1,3,100,128]{3,2,1,0:T(8,128)(2,1)S(1)}, bf16[1,3,100,128]{3,2,1,0:T(8,128)(2,1)S(1)}, u32[]{:S(2)}, u32[]{:S(2)}) collective-permute-start(bf16[1,3,100,128]{3,2,1,0:T(8,128)(2,1)S(1)} %get-tuple-element.61), channel_id=1, source_target_pairs={{0,8},{2,10},{4,12},{6,14},{8,0},{10,2},{12,4},{14,6},{1,9},{3,11}... | collective-permute-start | bytes 230408 | tf_op jit(solution)/shard_map/ppermute | solution.py:416
  102.1 0.1 fold.3
  102.2 1.4 %collective-permute-start.16 = (bf16[1,3,100,128]{3,2,1,0:T(8,128)(2,1)S(1)}, bf16[1,3,100,128]{3,2,1,0:T(8,128)(2,1)S(1)}, u32[]{:S(2)}, u32[]{:S(2)}) collective-permute-start(bf16[1,3,100,128]{3,2,1,0:T(8,128)(2,1)S(1)} %get-tuple-element.62), channel_id=1, source_target_pairs={{0,12},{2,14},{4,8},{6,10},{8,4},{10,6},{12,0},{14,2},{1,13},{3,15... | collective-permute-start | bytes 230408 | tf_op jit(solution)/shard_map/ppermute | solution.py:416
  103.6 0.3 collective-permute-start.10
  103.9 2.7 %collective-permute-start.11 = (bf16[1,3,100,128]{3,2,1,0:T(8,128)(2,1)S(1)}, bf16[1,3,100,128]{3,2,1,0:T(8,128)(2,1)S(1)}, u32[]{:S(2)}, u32[]{:S(2)}) collective-permute-start(bf16[1,3,100,128]{3,2,1,0:T(8,128)(2,1)S(1)} %get-tuple-element.55), channel_id=1, source_target_pairs={{0,8},{2,10},{4,12},{6,14},{8,0},{10,2},{12,4},{14,6},{1,9},{3,11}... | collective-permute-start | bytes 230408 | tf_op jit(solution)/shard_map/ppermute | solution.py:416
  106.6 1.4 %collective-permute-start.12 = (bf16[1,3,100,128]{3,2,1,0:T(8,128)(2,1)S(1)}, bf16[1,3,100,128]{3,2,1,0:T(8,128)(2,1)S(1)}, u32[]{:S(2)}, u32[]{:S(2)}) collective-permute-start(bf16[1,3,100,128]{3,2,1,0:T(8,128)(2,1)S(1)} %get-tuple-element.56), channel_id=1, source_target_pairs={{0,12},{2,14},{4,8},{6,10},{8,4},{10,6},{12,0},{14,2},{1,13},{3,15... | collective-permute-start | bytes 230408 | tf_op jit(solution)/shard_map/ppermute | solution.py:416
  108.0 1.5 %collective-permute-done.16.args_7_ = bf16[1,3,100,128]{3,2,1,0:T(8,128)(2,1)S(1)} collective-permute-done((bf16[1,3,100,128]{3,2,1,0:T(8,128)(2,1)S(1)}, bf16[1,3,100,128]{3,2,1,0:T(8,128)(2,1)S(1)}, u32[]{:S(2)}, u32[]{:S(2)}) %collective-permute-start.16) | collective-permute-done | bytes 76832 | tf_op jit(solution)/shard_map/ppermute | solution.py:416
  109.5 5.6 %collective-permute-done.11.args_2_ = bf16[1,3,100,128]{3,2,1,0:T(8,128)(2,1)S(1)} collective-permute-done((bf16[1,3,100,128]{3,2,1,0:T(8,128)(2,1)S(1)}, bf16[1,3,100,128]{3,2,1,0:T(8,128)(2,1)S(1)}, u32[]{:S(2)}, u32[]{:S(2)}) %collective-permute-start.11) | collective-permute-done | bytes 76832 | tf_op jit(solution)/shard_map/ppermute | solution.py:416
  115.0 0.9 finish.1
  (40 shorter events, 0.2 us)
Async XLA Ops:
  0.0 42.2 %collective-permute-start.7 = (bf16[96,64,128]{2,1,0:T(8,128)(2,1)}, bf16[96,64,128]{2,1,0:T(8,128)(2,1)}, u32[]{:S(2)}, u32[]{:S(2)}) collective-permute-start(bf16[96,64,128]{2,1,0:T(8,128)(2,1)} %mine.1), channel_id=1, source_target_pairs={{0,16},{16,0},{1,17},{17,1},{2,18},{18,2},{3,19},{19,3},{4,20},{20... | collective-permute-start | bytes 4718600 | tf_op jit(solution)/shard_map/ppermute | solution.py:365
  0.5 49.0 %collective-permute-start = (s32[96]{0:T(128)}, s32[96]{0:T(128)S(1)}, u32[]{:S(2)}, u32[]{:S(2)}) collective-permute-start(s32[96]{0:T(128)} %bins.1), channel_id=1, source_target_pairs={{0,1},{1,0},{2,3},{3,2},{4,5},{5,4},{6,7},{7,6},{8,9},{9,8},{10,11... | collective-permute-start | bytes 1160 | tf_op jit(solution)/shard_map/ppermute | solution.py:364
  4.8 36.7 %collective-permute-start.5 = (bf16[32,64,128]{2,1,0:T(8,128)(2,1)}, bf16[32,64,128]{2,1,0:T(8,128)(2,1)S(1)}, u32[]{:S(2)}, u32[]{:S(2)}) collective-permute-start(bf16[32,64,128]{2,1,0:T(8,128)(2,1)} %slice.11), channel_id=1, source_target_pairs={{0,1},{1,0},{2,3},{3,2},{4,5},{5,4},{6,7},{7,6},{8,9},{9,8},{10,11... | collective-permute-start | bytes 1572872 | tf_op jit(solution)/shard_map/ppermute | solution.py:363
  6.9 35.2 %collective-permute-start.3 = (bf16[48,64,128]{2,1,0:T(8,128)(2,1)}, bf16[48,64,128]{2,1,0:T(8,128)(2,1)}, u32[]{:S(2)}, u32[]{:S(2)}) collective-permute-start(bf16[48,64,128]{2,1,0:T(8,128)(2,1)} %slice.10), channel_id=1, source_target_pairs={{0,1},{1,0},{2,3},{3,2},{4,5},{5,4},{6,7},{7,6},{8,9},{9,8},{10,11... | collective-permute-start | bytes 2359304 | tf_op jit(solution)/shard_map/ppermute | solution.py:363
  10.6 31.0 %collective-permute-start.1 = (bf16[16,64,128]{2,1,0:T(8,128)(2,1)}, bf16[16,64,128]{2,1,0:T(8,128)(2,1)S(1)}, u32[]{:S(2)}, u32[]{:S(2)}) collective-permute-start(bf16[16,64,128]{2,1,0:T(8,128)(2,1)} %slice.9), channel_id=1, source_target_pairs={{0,1},{1,0},{2,3},{3,2},{4,5},{5,4},{6,7},{7,6},{8,9},{9,8},{10,11... | collective-permute-start | bytes 786440 | tf_op jit(solution)/shard_map/ppermute | solution.py:363
  10.6 13.7 %copy-start.9 = (s32[192,100]{1,0:T(8,128)S(1)}, s32[192,100]{1,0:T(8,128)}, u32[]{:S(2)}) copy-start(s32[192,100]{1,0:T(8,128)} %param.14) | copy-start | bytes 230404
  10.6 14.1 %copy-start.11 = (f32[192]{0:T(256)S(1)}, f32[192]{0:T(256)}, u32[]{:S(2)}) copy-start(f32[192]{0:T(256)} %param.15) | copy-start | bytes 2308
  19.5 4.2 %copy-start.6 = (bf16[128,336,128]{2,1,0:T(8,128)(2,1)}, bf16[128,336,128]{2,1,0:T(8,128)(2,1)S(1)}, u32[]{:S(2)}) copy-start(bf16[128,336,128]{2,1,0:T(8,128)(2,1)S(1)} %get-tuple-element.46.refs) | copy-start | bytes 33030148
  23.6 0.7 copy-start.7
  24.3 17.9 %copy-start.4 = (bf16[96,64,128]{2,1,0:T(8,128)(2,1)S(1)}, bf16[96,64,128]{2,1,0:T(8,128)(2,1)}, u32[]{:S(2)}) copy-start(bf16[96,64,128]{2,1,0:T(8,128)(2,1)} %mine.1) | copy-start | bytes 4718596
  24.3 17.9 %copy-start.5 = (s32[96]{0:T(128)S(1)}, s32[96]{0:T(128)}, u32[]{:S(2)}) copy-start(s32[96]{0:T(128)} %bins.1) | copy-start | bytes 1156
  41.6 14.6 %collective-permute-start.2 = (bf16[16,64,128]{2,1,0:T(8,128)(2,1)S(1)}, bf16[16,64,128]{2,1,0:T(8,128)(2,1)S(1)}, u32[]{:S(2)}, u32[]{:S(2)}) collective-permute-start(bf16[16,64,128]{2,1,0:T(8,128)(2,1)S(1)} %collective-permute-done.1.mine), channel_id=1, source_target_pairs={{0,16},{16,0},{1,17},{17,1},{2,18},{18,2},{3,19},{19,3},{4,20},{20... | collective-permute-start | bytes 786440 | tf_op jit(solution)/shard_map/ppermute | solution.py:390
  41.6 7.8 %collective-permute-start.6 = (bf16[32,64,128]{2,1,0:T(8,128)(2,1)S(1)}, bf16[32,64,128]{2,1,0:T(8,128)(2,1)S(1)}, u32[]{:S(2)}, u32[]{:S(2)}) collective-permute-start(bf16[32,64,128]{2,1,0:T(8,128)(2,1)S(1)} %collective-permute-done.5.mine), channel_id=1, source_target_pairs={{0,16},{16,0},{1,17},{17,1},{2,18},{18,2},{3,19},{19,3},{4,20},{20... | collective-permute-start | bytes 1572872 | tf_op jit(solution)/shard_map/ppermute | solution.py:390
  42.1 9.8 %collective-permute-start.4 = (bf16[48,64,128]{2,1,0:T(8,128)(2,1)}, bf16[48,64,128]{2,1,0:T(8,128)(2,1)S(1)}, u32[]{:S(2)}, u32[]{:S(2)}) collective-permute-start(bf16[48,64,128]{2,1,0:T(8,128)(2,1)} %collective-permute-done.3.mine), channel_id=1, source_target_pairs={{0,16},{16,0},{1,17},{17,1},{2,18},{18,2},{3,19},{19,3},{4,20},{20... | collective-permute-start | bytes 2359304 | tf_op jit(solution)/shard_map/ppermute | solution.py:390
  51.9 5.8 %slice-start = ((s8[11010048]{0:T(1024)(128)(4,1)}), s8[2621440]{0:T(1024)(128)(4,1)S(1)}, s32[]{:S(2)}) async-start(s8[11010048]{0:T(1024)(128)(4,1)} %bitcast.19), calls=%async_computation | async-start | bytes 5242880
  51.9 5.8 %slice-start.1 = ((s8[11010048]{0:T(1024)(128)(4,1)}), s8[4194304]{0:T(1024)(128)(4,1)S(1)}, s32[]{:S(2)}) async-start(s8[11010048]{0:T(1024)(128)(4,1)} %bitcast.19), calls=%async_computation.1 | async-start | bytes 8388608
  56.2 2.2 %slice-start.2 = ((s8[11010048]{0:T(1024)(128)(4,1)}), s8[4194304]{0:T(1024)(128)(4,1)S(1)}, s32[]{:S(2)}) async-start(s8[11010048]{0:T(1024)(128)(4,1)} %bitcast.19), calls=%async_computation.2 | async-start | bytes 8388608
  56.2 2.2 %copy-start.8 = (f32[336,128]{1,0:T(8,128)S(1)}, f32[336,128]{1,0:T(8,128)}, u32[]{:S(2)}) copy-start(f32[336,128]{1,0:T(8,128)} %copy-done.7) | copy-start | bytes 516100
  57.7 5.3 %copy-start = (bf16[128,192,128]{2,1,0:T(8,128)(2,1)}, bf16[128,192,128]{2,1,0:T(8,128)(2,1)S(1)}, u32[]{:S(2)}) copy-start(bf16[128,192,128]{2,1,0:T(8,128)(2,1)S(1)} %get-tuple-element.45.plain) | copy-start | bytes 18874372
  57.7 5.3 %copy-start.2 = (bf16[128,192,128]{2,1,0:T(8,128)(2,1)}, bf16[128,192,128]{2,1,0:T(8,128)(2,1)S(1)}, u32[]{:S(2)}) copy-start(bf16[128,192,128]{2,1,0:T(8,128)(2,1)S(1)} %get-tuple-element.50.turned) | copy-start | bytes 18874372
  58.3 5.0 %copy-start.10 = (s32[100,3]{0,1:T(4,128)S(1)}, s32[100,3]{0,1:T(4,128)}, u32[]{:S(2)}) copy-start(s32[100,3]{0,1:T(4,128)} %param.13) | copy-start | bytes 3604
  63.0 3.7 %collective-permute-start.8 = (f32[8,192]{1,0:T(8,128)S(1)}, f32[8,192]{1,0:T(8,128)S(1)}, u32[]{:S(2)}, u32[]{:S(2)}) collective-permute-start(f32[8,192]{1,0:T(8,128)S(1)} %get-tuple-element.49.mine), channel_id=1, source_target_pairs={{0,1},{1,0},{2,3},{3,2},{4,5},{5,4},{6,7},{7,6},{8,9},{9,8},{10,11... | collective-permute-start | bytes 18440 | tf_op jit(solution)/shard_map/ppermute | solution.py:396
  66.7 0.6 copy-start.12
  68.6 2.8 %copy-start.1 = (bf16[128,192,128]{2,1,0:T(8,128)(2,1)S(1)}, bf16[128,192,128]{2,1,0:T(8,128)(2,1)}, u32[]{:S(2)}) copy-start(bf16[128,192,128]{2,1,0:T(8,128)(2,1)} %copy-done) | copy-start | bytes 18874372
  71.4 2.8 %copy-start.3 = (bf16[128,192,128]{2,1,0:T(8,128)(2,1)S(1)}, bf16[128,192,128]{2,1,0:T(8,128)(2,1)}, u32[]{:S(2)}) copy-start(bf16[128,192,128]{2,1,0:T(8,128)(2,1)} %copy-done.2) | copy-start | bytes 18874372
  79.1 8.5 %collective-permute-start.17 = (bf16[4,2,100,128]{3,2,1,0:T(8,128)(2,1)}, bf16[4,2,100,128]{3,2,1,0:T(8,128)(2,1)S(1)}, u32[]{:S(2)}, u32[]{:S(2)}) collective-permute-start(bf16[4,2,100,128]{3,2,1,0:T(8,128)(2,1)} %get-tuple-element.64), channel_id=1, source_target_pairs={{0,2},{2,0},{4,6},{6,4},{8,10},{10,8},{12,14},{14,12},{1,3},{3,1},... | collective-permute-start | bytes 614408 | tf_op jit(solution)/shard_map/ppermute | solution.py:403
  80.6 13.8 %collective-permute-start.13 = (bf16[4,3,100,128]{3,2,1,0:T(8,128)(2,1)S(1)}, bf16[4,3,100,128]{3,2,1,0:T(8,128)(2,1)S(1)}, u32[]{:S(2)}, u32[]{:S(2)}) collective-permute-start(bf16[4,3,100,128]{3,2,1,0:T(8,128)(2,1)S(1)} %get-tuple-element.58), channel_id=1, source_target_pairs={{0,2},{2,0},{4,6},{6,4},{8,10},{10,8},{12,14},{14,12},{1,3},{3,1},... | collective-permute-start | bytes 921608 | tf_op jit(solution)/shard_map/ppermute | solution.py:403
  83.4 16.1 %collective-permute-start.9 = (bf16[4,3,100,128]{3,2,1,0:T(8,128)(2,1)S(1)}, bf16[4,3,100,128]{3,2,1,0:T(8,128)(2,1)S(1)}, u32[]{:S(2)}, u32[]{:S(2)}) collective-permute-start(bf16[4,3,100,128]{3,2,1,0:T(8,128)(2,1)S(1)} %get-tuple-element.52), channel_id=1, source_target_pairs={{0,2},{2,0},{4,6},{6,4},{8,10},{10,8},{12,14},{14,12},{1,3},{3,1},... | collective-permute-start | bytes 921608 | tf_op jit(solution)/shard_map/ppermute | solution.py:403
  87.6 14.6 %collective-permute-start.18 = (bf16[1,2,100,128]{3,2,1,0:T(8,128)(2,1)S(1)}, bf16[1,2,100,128]{3,2,1,0:T(8,128)(2,1)S(1)}, u32[]{:S(2)}, u32[]{:S(2)}) collective-permute-start(bf16[1,2,100,128]{3,2,1,0:T(8,128)(2,1)S(1)} %get-tuple-element.66), channel_id=1, source_target_pairs={{0,4},{2,6},{4,0},{6,2},{8,12},{10,14},{12,8},{14,10},{1,5},{3,7},... | collective-permute-start | bytes 153608 | tf_op jit(solution)/shard_map/ppermute | solution.py:416
  89.2 14.4 %collective-permute-start.19 = (bf16[1,2,100,128]{3,2,1,0:T(8,128)(2,1)S(1)}, bf16[1,2,100,128]{3,2,1,0:T(8,128)(2,1)S(1)}, u32[]{:S(2)}, u32[]{:S(2)}) collective-permute-start(bf16[1,2,100,128]{3,2,1,0:T(8,128)(2,1)S(1)} %get-tuple-element.67), channel_id=1, source_target_pairs={{0,8},{2,10},{4,12},{6,14},{8,0},{10,2},{12,4},{14,6},{1,9},{3,11}... | collective-permute-start | bytes 153608 | tf_op jit(solution)/shard_map/ppermute | solution.py:416
  91.8 12.1 %collective-permute-start.20 = (bf16[1,2,100,128]{3,2,1,0:T(8,128)(2,1)S(1)}, bf16[1,2,100,128]{3,2,1,0:T(8,128)(2,1)S(1)}, u32[]{:S(2)}, u32[]{:S(2)}) collective-permute-start(bf16[1,2,100,128]{3,2,1,0:T(8,128)(2,1)S(1)} %get-tuple-element.68), channel_id=1, source_target_pairs={{0,12},{2,14},{4,8},{6,10},{8,4},{10,6},{12,0},{14,2},{1,13},{3,15... | collective-permute-start | bytes 153608 | tf_op jit(solution)/shard_map/ppermute | solution.py:416
  94.5 12.2 %collective-permute-start.14 = (bf16[1,3,100,128]{3,2,1,0:T(8,128)(2,1)S(1)}, bf16[1,3,100,128]{3,2,1,0:T(8,128)(2,1)S(1)}, u32[]{:S(2)}, u32[]{:S(2)}) collective-permute-start(bf16[1,3,100,128]{3,2,1,0:T(8,128)(2,1)S(1)} %get-tuple-element.60), channel_id=1, source_target_pairs={{0,4},{2,6},{4,0},{6,2},{8,12},{10,14},{12,8},{14,10},{1,5},{3,7},... | collective-permute-start | bytes 230408 | tf_op jit(solution)/shard_map/ppermute | solution.py:416
  99.5 8.5 %collective-permute-start.15 = (bf16[1,3,100,128]{3,2,1,0:T(8,128)(2,1)S(1)}, bf16[1,3,100,128]{3,2,1,0:T(8,128)(2,1)S(1)}, u32[]{:S(2)}, u32[]{:S(2)}) collective-permute-start(bf16[1,3,100,128]{3,2,1,0:T(8,128)(2,1)S(1)} %get-tuple-element.61), channel_id=1, source_target_pairs={{0,8},{2,10},{4,12},{6,14},{8,0},{10,2},{12,4},{14,6},{1,9},{3,11}... | collective-permute-start | bytes 230408 | tf_op jit(solution)/shard_map/ppermute | solution.py:416
  102.2 7.3 %collective-permute-start.16 = (bf16[1,3,100,128]{3,2,1,0:T(8,128)(2,1)S(1)}, bf16[1,3,100,128]{3,2,1,0:T(8,128)(2,1)S(1)}, u32[]{:S(2)}, u32[]{:S(2)}) collective-permute-start(bf16[1,3,100,128]{3,2,1,0:T(8,128)(2,1)S(1)} %get-tuple-element.62), channel_id=1, source_target_pairs={{0,12},{2,14},{4,8},{6,10},{8,4},{10,6},{12,0},{14,2},{1,13},{3,15... | collective-permute-start | bytes 230408 | tf_op jit(solution)/shard_map/ppermute | solution.py:416
  103.6 5.9 %collective-permute-start.10 = (bf16[1,3,100,128]{3,2,1,0:T(8,128)(2,1)S(1)}, bf16[1,3,100,128]{3,2,1,0:T(8,128)(2,1)S(1)}, u32[]{:S(2)}, u32[]{:S(2)}) collective-permute-start(bf16[1,3,100,128]{3,2,1,0:T(8,128)(2,1)S(1)} %get-tuple-element.54), channel_id=1, source_target_pairs={{0,4},{2,6},{4,0},{6,2},{8,12},{10,14},{12,8},{14,10},{1,5},{3,7},... | collective-permute-start | bytes 230408 | tf_op jit(solution)/shard_map/ppermute | solution.py:416
  103.9 11.1 %collective-permute-start.11 = (bf16[1,3,100,128]{3,2,1,0:T(8,128)(2,1)S(1)}, bf16[1,3,100,128]{3,2,1,0:T(8,128)(2,1)S(1)}, u32[]{:S(2)}, u32[]{:S(2)}) collective-permute-start(bf16[1,3,100,128]{3,2,1,0:T(8,128)(2,1)S(1)} %get-tuple-element.55), channel_id=1, source_target_pairs={{0,8},{2,10},{4,12},{6,14},{8,0},{10,2},{12,4},{14,6},{1,9},{3,11}... | collective-permute-start | bytes 230408 | tf_op jit(solution)/shard_map/ppermute | solution.py:416
  106.6 8.4 %collective-permute-start.12 = (bf16[1,3,100,128]{3,2,1,0:T(8,128)(2,1)S(1)}, bf16[1,3,100,128]{3,2,1,0:T(8,128)(2,1)S(1)}, u32[]{:S(2)}, u32[]{:S(2)}) collective-permute-start(bf16[1,3,100,128]{3,2,1,0:T(8,128)(2,1)S(1)} %get-tuple-element.56), channel_id=1, source_target_pairs={{0,12},{2,14},{4,8},{6,10},{8,4},{10,6},{12,0},{14,2},{1,13},{3,15... | collective-permute-start | bytes 230408 | tf_op jit(solution)/shard_map/ppermute | solution.py:416

commit v3 on v2

--- a/solution.py
+++ b/solution.py
@@ -13,6 +13,9 @@
 GROUP = 16
 PAD = 8
 DEEP = 16
+SUMS = 0.8
+SCALE = 0.1
+FOLD = 1
 MIB = 1 << 20
 
 
@@ -28,7 +31,7 @@
 
 def cost(microseconds):
     return pl.CostEstimate(
-        flops=int(microseconds * 1e9), transcendentals=0, bytes_accessed=int(microseconds * 3e6)
+        flops=int(microseconds * SCALE * 1e9), transcendentals=0, bytes_accessed=int(microseconds * SCALE * 3e6)
     )
 
 
@@ -40,8 +43,12 @@
     return pltpu.with_memory_space_constraint(x, pltpu.VMEM)
 
 
-def filters_kernel(ctf, band, left, right):
+def prepare_kernel(ctf, band, mask, noise, rot, left, right, mask_out, noise_out, rot_out, scr):
     bins, width = ctf.shape
+    rots, classes = rot.shape
+    padded = rot_out.shape[1]
+    total = mask.shape[0]
+    count = total // 2
 
     def negated(v):
         at = (width - lax.broadcasted_iota(jnp.int32, v.shape, 1)) % width
@@ -62,15 +69,61 @@
         left[b] = rolled(backward[b : b + 1]).astype(BF16)
         right[b] = rolled(forward[b : b + 1]).astype(BF16)
 
-
-def build_filters(ctf, band):
+    scr[...] = jnp.zeros_like(scr)
+    group = lax.axis_index("cls")
+    for half in range(2):
+        come = group if half == 0 else 1 - group
+        start = pl.multiple_of(come * count, 8)
+        scr[half * count : (half + 1) * count, :classes] = mask[pl.ds(start, count)].astype(F32)
+    mask_out[...] = scr[...].T[:padded, :total]
+    n = noise[...]
+    other = jnp.concatenate([n[:, count:], n[:, :count]], axis=1)
+    noise_out[...] = jnp.where(group == 0, n, other)
+    square = scr.shape[1]
+    scr[:square] = jnp.zeros((square, square), F32)
+    scr[:rots, :classes] = rot[...].astype(F32)
+    turned = scr[:square].T
+    for j in range(rots):
+        rot_out[j] = jnp.broadcast_to(turned[:padded, j : j + 1], (padded, square))
+
+
+def prepare(ctf, band, mask, noise, rot, padded):
     bins, width = ctf.shape
-    return pl.pallas_call(
-        filters_kernel,
-        out_shape=(pinned((bins, width, width), BF16),) * 2,
+    total = noise.shape[0]
+    lanes = max(128, -(-padded // 128) * 128)
+    tall = -(-max(total, lanes) // 128) * 128
+    return pl.pallas_call(
+        prepare_kernel,
+        out_shape=(
+            pinned((bins, width, width), BF16),
+            pinned((bins, width, width), BF16),
+            pinned((padded, total), F32),
+            pinned((1, total), F32),
+            pinned((rot.shape[0], padded, lanes), F32),
+        ),
+        scratch_shapes=[pltpu.VMEM((tall, lanes), F32)],
+        compiler_params=pltpu.CompilerParams(vmem_limit_bytes=4 * MIB),
         cost_estimate=cost(3),
-        name="filters",
-    )(ctf, band.reshape(1, width))
+        name="prepare",
+    )(ctf, band.reshape(1, width), mask, noise.reshape(1, total), rot)
+
+
+def gate_kernel(piece, token, out):
+    del piece, token, out
+
+
+def gate(piece, token):
+    anywhere = pl.BlockSpec(memory_space=pl.ANY)
+    return pl.pallas_call(
+        gate_kernel,
+        in_specs=[anywhere, anywhere],
+        out_specs=anywhere,
+        out_shape=jax.ShapeDtypeStruct(piece.shape, piece.dtype),
+        input_output_aliases={0: 0},
+        compiler_params=pltpu.CompilerParams(vmem_limit_bytes=MIB),
+        cost_estimate=cost(0.1),
+        name="gate",
+    )(piece, token)
 
 
 def refs_kernel(refs, out, norm, scratch, *, padded):
@@ -118,16 +171,17 @@
             pinned((rots * padded, width), F32),
         ),
         scratch_shapes=[pltpu.VMEM((GROUP * (rows + PAD), width), F32)],
-        compiler_params=pltpu.CompilerParams(vmem_limit_bytes=28 * MIB),
+        compiler_params=pltpu.CompilerParams(vmem_limit_bytes=12 * MIB),
         cost_estimate=cost(9),
         name="refs",
     )(pltpu.with_memory_space_constraint(refs, pltpu.HBM))
 
 
-def filter_kernel(where, bins, mine, sib, left, right, *rest, skip, at):
-    plain, turned, scr, scr_t = rest[-4:]
+def filter_kernel(bins, mine, sib, left, right, *rest, skip, at):
+    plain, turned, token, scr, scr_t = rest[-5:]
+    token[...] = jnp.zeros_like(token)
     count, half, width = mine.shape
-    top = where[0] == 0
+    top = lax.axis_index("section") == 0
     pitch = width + PAD
 
     @pl.loop(0, count // GROUP)
@@ -147,22 +201,23 @@
             turned[r, pl.ds(to, GROUP)] = scr_t[pl.ds(r, GROUP, stride=pitch)].astype(BF16)
 
 
-def filter_chunk(where, bins, mine, sib, left, right, buffers, total, skip, at):
+def filter_chunk(bins, mine, sib, left, right, buffers, total, skip, at):
     count, half, width = mine.shape
     smem = pl.BlockSpec(memory_space=pltpu.SMEM)
     vmem = pl.BlockSpec(memory_space=pltpu.VMEM)
     buffers = [held(b) for b in buffers]
     return pl.pallas_call(
         functools.partial(filter_kernel, skip=skip, at=at),
-        in_specs=[smem, smem] + [vmem] * (4 + len(buffers)),
-        out_specs=(vmem, vmem),
-        out_shape=(pinned((2 * half, total, width), BF16),) * 2,
+        in_specs=[smem] + [vmem] * (4 + len(buffers)),
+        out_specs=(vmem, vmem, vmem),
+        out_shape=(pinned((2 * half, total, width), BF16),) * 2
+        + (jax.ShapeDtypeStruct((8, width), F32),),
         scratch_shapes=[pltpu.VMEM((GROUP * (2 * half + PAD), width), F32)] * 2,
-        input_output_aliases={6 + i: i for i in range(len(buffers))},
-        compiler_params=pltpu.CompilerParams(vmem_limit_bytes=24 * MIB),
+        input_output_aliases={5 + i: i for i in range(len(buffers))},
+        compiler_params=pltpu.CompilerParams(vmem_limit_bytes=8 * MIB),
         cost_estimate=cost(count * 0.1),
         name="filter",
-    )(where, bins, mine, sib, held(left), held(right), *buffers)
+    )(bins, mine, sib, held(left), held(right), *buffers)
 
 
 def score_kernel(plain, refs, norm, mask, noise, scaled, stats):
@@ -196,10 +251,10 @@
             pinned((height, count), F32),
             pinned((8, count), F32),
         ),
-        compiler_params=pltpu.CompilerParams(vmem_limit_bytes=24 * MIB),
+        compiler_params=pltpu.CompilerParams(vmem_limit_bytes=8 * MIB),
         cost_estimate=cost(5),
         name="score",
-    )(held(plain), held(refs), held(norm), mask, noise)
+    )(held(plain), held(refs), held(norm), held(mask), held(noise))
 
 
 def weights_kernel(scaled, mine, other, rot, out):
@@ -213,7 +268,7 @@
     for q in range(4):
         acc = jnp.zeros((padded, count), F32)
         for j in range(rots):
-            acc = acc + jnp.where(rot[j] == q, w[j * padded : (j + 1) * padded], 0.0)
+            acc = acc + jnp.where(rot[j][:, :1] == q, w[j * padded : (j + 1) * padded], 0.0)
         quarters.append(acc)
     for row, pair in enumerate(((0, 3), (2, 1))):
         out[row] = jnp.concatenate([quarters[q] for q in pair], axis=1).astype(BF16)
@@ -225,17 +280,18 @@
     return pl.pallas_call(
         weights_kernel,
         out_shape=pinned((2, padded, 2 * count), BF16),
+        compiler_params=pltpu.CompilerParams(vmem_limit_bytes=8 * MIB),
         cost_estimate=cost(2),
         name="weights",
-    )(held(scaled), held(mine), other, rot)
-
-
-def sums_kernel(where, weights, plain, turned, send, keep, *, dom, start, classes):
+    )(held(scaled), held(mine), other, held(rot))
+
+
+def sums_kernel(weights, plain, turned, send, keep, *, dom, start, classes):
     _, rows, _, width = send.shape
     height = plain.shape[0]
     block = height // 2 // dom
-    first = where[0] * (height // 2) + start
-    parity = where[1]
+    first = lax.axis_index("section") * (height // 2) + start
+    parity = lax.axis_index("dom") % 2
     straight = weights[0]
     mirrored = weights[1]
     flip = width - 1 - lax.broadcasted_iota(jnp.int32, (straight.shape[0], width), 1)
@@ -261,43 +317,42 @@
             keep[g, r] = here[:classes]
 
 
-def sums(where, weights, plain, turned, dom, start, rows, classes):
+def sums(weights, plain, turned, dom, start, rows, classes):
     width = plain.shape[2]
-    smem = pl.BlockSpec(memory_space=pltpu.SMEM)
     vmem = pl.BlockSpec(memory_space=pltpu.VMEM)
     return pl.pallas_call(
         functools.partial(sums_kernel, dom=dom, start=start, classes=classes),
-        in_specs=[smem] + [vmem] * 3,
+        in_specs=[vmem] * 3,
         out_shape=(
             jax.ShapeDtypeStruct((dom // 2, rows, classes, width), BF16),
             pinned((dom // 2, rows, classes, width), F32),
         ),
-        compiler_params=pltpu.CompilerParams(vmem_limit_bytes=24 * MIB),
-        cost_estimate=cost(rows * 0.8),
+        compiler_params=pltpu.CompilerParams(vmem_limit_bytes=8 * MIB),
+        cost_estimate=cost(SUMS * rows),
         name="sums",
-    )(where, held(weights), held(plain), held(turned))
-
-
-def fold_kernel(at, keep, got, *outs, fan):
+    )(held(weights), held(plain), held(turned))
+
+
+def fold_kernel(keep, got, *outs, fan, bit):
     rest = keep.shape[0] // fan
+    at = (lax.axis_index("dom") // (1 << bit)) % fan
     for m, out in enumerate(outs):
         for i in range(rest):
-            b = i * fan + (at[0] ^ m)
+            b = i * fan + jnp.bitwise_xor(at, m)
             value = keep[b] + got[b].astype(F32)
             out[i] = value.astype(out.dtype)
 
 
-def fold(at, keep, got, fan):
+def fold(keep, got, fan, bit):
     rest = (keep.shape[0] // fan,) + keep.shape[1:]
     return pl.pallas_call(
-        functools.partial(fold_kernel, fan=fan),
-        in_specs=[pl.BlockSpec(memory_space=pltpu.SMEM)]
-        + [pl.BlockSpec(memory_space=pltpu.VMEM)] * 2,
+        functools.partial(fold_kernel, fan=fan, bit=bit),
+        in_specs=[pl.BlockSpec(memory_space=pltpu.VMEM)] * 2,
         out_shape=(pinned(rest, F32),) + (jax.ShapeDtypeStruct(rest, BF16),) * (fan - 1),
-        compiler_params=pltpu.CompilerParams(vmem_limit_bytes=24 * MIB),
-        cost_estimate=cost(1),
+        compiler_params=pltpu.CompilerParams(vmem_limit_bytes=8 * MIB),
+        cost_estimate=cost(FOLD),
         name="fold",
-    )(at.reshape(1), held(keep), got)
+    )(held(keep), got)
 
 
 def finish_kernel(*args, counts):
@@ -324,7 +379,7 @@
     out = pl.pallas_call(
         functools.partial(finish_kernel, counts=counts),
         out_shape=jax.ShapeDtypeStruct((classes * block_rows, width), F32),
-        compiler_params=pltpu.CompilerParams(vmem_limit_bytes=24 * MIB),
+        compiler_params=pltpu.CompilerParams(vmem_limit_bytes=8 * MIB),
         cost_estimate=cost(1),
         name="finish",
     )(*flat)
@@ -332,9 +387,8 @@
 
 
 def y_pieces(particles):
-    last = GROUP
-    first = particles // 3 // GROUP * GROUP
-    return (first, particles - first - last, last)
+    last = particles // 3 // GROUP * GROUP
+    return (particles - last, last)
 
 
 def row_pieces(rows):
@@ -347,12 +401,9 @@
 def local(
     images, defocus_bin, ctf_kernels, band_kernel, references, rot_index, class_mask, noise_var
 ):
-    section_at = lax.axis_index("section")
-    class_at = lax.axis_index("cls")
-    dom_at = lax.axis_index("dom")
     dom = lax.axis_size("dom")
     particles, half, width = images.shape
-    classes, rots = rot_index.shape
+    classes = rot_index.shape[0]
     padded = -(-classes // GROUP) * GROUP
     swap = [(0, 1), (1, 0)]
     over_cls = functools.partial(lax.ppermute, axis_name="cls", perm=swap)
@@ -364,32 +415,23 @@
     other_bins = over_cls(defocus_bin)
     own_sib = over_section(images)
 
-    where = jnp.stack([section_at, dom_at % 2]).astype(jnp.int32)
-    left, right = build_filters(ctf_kernels, band_kernel)
     refs, norm = lay_refs(references, padded)
-
-    def arranged(a):
-        parts = a.reshape((2, particles) + a.shape[1:])
-        return jnp.concatenate(
-            [
-                lax.dynamic_index_in_dim(parts, class_at, 0, False),
-                lax.dynamic_index_in_dim(parts, 1 - class_at, 0, False),
-            ]
+    left, right, mask, noise, rot = prepare(
+        ctf_kernels, band_kernel, class_mask, noise_var, rot_index.T, padded
+    )
+    total = 2 * particles
+    remote[0] = gate(remote[0], norm)
+    sib = over_section(remote[0])
+    *buffers, token = filter_chunk(
+        defocus_bin, images, own_sib, left, right, (), total, 0, 0
+    )
+    for i, a in enumerate(starts):
+        *buffers, token = filter_chunk(
+            other_bins, remote[i], sib, left, right, buffers, total, a, particles + a
         )
-
-    mask = jnp.pad(arranged(class_mask).T, ((0, padded - classes), (0, 0)))
-    noise = arranged(noise_var).reshape(1, 2 * particles)
-    rot = jnp.pad(rot_index.T, ((0, 0), (0, padded - classes)))[:, :, None]
-
-    total = 2 * particles
-    buffers = filter_chunk(
-        where, defocus_bin, images, own_sib, left, right, (), total, 0, 0
-    )
-    for a, piece in zip(starts, remote):
-        buffers = filter_chunk(
-            where, other_bins, piece, over_section(piece), left, right, buffers, total, a,
-            particles + a,
-        )
+        if i + 1 < len(starts):
+            remote[i + 1] = gate(remote[i + 1], token)
+            sib = over_section(remote[i + 1])
     plain, turned = buffers
 
     scaled, stats = score(plain, refs, norm, mask, noise)
@@ -398,18 +440,15 @@
     start = 0
     done = []
     for rows in row_pieces(half // dom):
-        send, keep = sums(where, weights, plain, turned, dom, start, rows, classes)
+        send, keep = sums(weights, plain, turned, dom, start, rows, classes)
         start += rows
         got = lax.ppermute(send, "dom", [(i, i ^ 1) for i in range(dom)])
         bit = 1
         while keep.shape[0] > 4:
-            at = ((dom_at >> bit) & 1).astype(jnp.int32)
-            keep, send = fold(at, keep, got, 2)
+            keep, send = fold(keep, got, 2, bit)
             got = lax.ppermute(send, "dom", [(i, i ^ (1 << bit)) for i in range(dom)])
             bit += 1
-        fan = keep.shape[0]
-        at = ((dom_at >> bit) & (fan - 1)).astype(jnp.int32)
-        keep, *sends = fold(at, keep, got, fan)
+        keep, *sends = fold(keep, got, keep.shape[0], bit)
         done.append(
             [keep]
             + [

time: 116 us -> 104 us (0.90)
  local copies, waits for them, and re-layouts: 18.4 us -> 1.37 us
  waiting for transfers between devices: 33.1 us -> 43.3 us
  Pallas kernels: 39.9 us -> 33.8 us
  starting transfers between devices: 24.1 us -> 25.6 us
    unnamed x34 -> x14, local copies, waits for them, and re-layouts: 11.8 us -> 0.04 us
    ppermute x1, waiting for transfers between devices: 0.01 us -> 5.12 us  [local(): other_bins = over_cls(defocus_bin)]
    slice x3 -> x2, local copies, waits for them, and re-layouts: 5.63 us -> 1.33 us  [local(): remote = [over_cls(images[a:a + n]) for a, n in zip(starts, sizes)]]
    ppermute x3 -> x2, starting transfers between devices: 2.03 us -> 4.84 us  [local(): remote = [over_cls(images[a:a + n]) for a, n in zip(starts, sizes)]]
    ppermute x3, waiting for transfers between devices: 8.3 us -> 10.9 us  [local(): got = lax.ppermute(send, 'dom', [(i, i ^ 1) for i in range(dom)])]
    pallas_call x3, Pallas kernels: 7.16 us -> 4.85 us  [sums(): pl.pallas_call(functools.partial(sums_kernel, dom=dom, start=start, class...]
    ppermute x1, starting transfers between devices: 2.52 us -> 0.29 us  [local(): other_bins = over_cls(defocus_bin)]
    ppermute x9, waiting for transfers between devices: 7.06 us -> 9.19 us  [local(): lax.ppermute(s, 'dom', [(i, i ^ m + 1 << bit) for i in range(dom)])]
  transfers between devices with their start and end apart: 21 -> 19, of which waited for: 7 -> 11; matrix products, arithmetic and copies ran while one was open for 6% -> 0% of each run, Pallas kernels for 23% -> 23%
where the time goes in v3:
time: 104 us
  waiting for transfers between devices  43.3 us (42%)
  Pallas kernels  33.8 us (32%)
  starting transfers between devices  25.6 us (25%)
  local copies, waits for them, and re-layouts  1.37 us (1%)
    ppermute x9, starting transfers between devices, local(): lax.ppermute(s, 'dom', [(i, i ^ m + 1 << bit) for i in range(dom)])  14.6 us
    ppermute x2, waiting for transfers between devices, local(): remote = [over_cls(images[a:a + n]) for a, n in zip(starts, sizes)]  14.3 us
    pallas_call x3, Pallas kernels, filter_chunk(): pl.pallas_call(functools.partial(filter_kernel, skip=skip, at=at), in_spe...  13.3 us
    ppermute x3, waiting for transfers between devices, local(): got = lax.ppermute(send, 'dom', [(i, i ^ 1) for i in range(dom)])  10.9 us
    ppermute x9, waiting for transfers between devices, local(): lax.ppermute(s, 'dom', [(i, i ^ m + 1 << bit) for i in range(dom)])  9.19 us
    pallas_call x1, Pallas kernels, lay_refs(): pl.pallas_call(functools.partial(refs_kernel, padded=padded), grid=(rots,...  8.81 us
    ppermute x1, waiting for transfers between devices, local(): other_bins = over_cls(defocus_bin)  5.12 us
    pallas_call x3, Pallas kernels, sums(): pl.pallas_call(functools.partial(sums_kernel, dom=dom, start=start, class...  4.85 us
  transfers between devices with their start and end apart: 19, of which 11 were waited for; matrix products, arithmetic and copies ran while one was open for 0% of the time, Pallas kernels for 23%

profile of v3, /device:TPU:0, one launch (start us, length us, event | category | flops | bytes accessed | tf_op | source)
XLA Modules:
  0.0 104.3 jit_solution(3687264053501736139)
XLA Ops:
  0.0 1.3 %slice.7 = bf16[64,64,128]{2,1,0:T(8,128)(2,1)S(1)} slice(bf16[96,64,128]{2,1,0:T(8,128)(2,1)} %mine.1), slice={[0:64], [0:64], [0:128]} | slice | bytes 2097152 | tf_op jit(solution)/shard_map/slice | solution.py:414
  1.3 0.0 copy-start
  1.3 0.0 copy-start.1
  1.3 0.0 copy-start.2
  1.3 0.0 copy-start.3
  1.3 0.0 copy-start.4
  1.4 0.0 copy-start.5
  1.4 0.0 copy-start.6
  1.4 3.0 %collective-permute-start.2 = (bf16[64,64,128]{2,1,0:T(8,128)(2,1)S(1)}, bf16[64,64,128]{2,1,0:T(8,128)(2,1)S(1)}, u32[]{:S(2)}, u32[]{:S(2)}) collective-permute-start(bf16[64,64,128]{2,1,0:T(8,128)(2,1)S(1)} %slice.7), channel_id=1, source_target_pairs={{0,1},{1,0},{2,3},{3,2},{4,5},{5,4},{6,7},{7,6},{8,9},{9,8},{10,11... | collective-permute-start | bytes 3145736 | tf_op jit(solution)/shard_map/ppermute | solution.py:414
  4.4 0.0 collective-permute-start.4
  4.4 8.8 %refs.2 = (bf16[128,336,128]{2,1,0:T(8,128)(2,1)S(1)}, f32[336,128]{1,0:T(8,128)S(1)}) custom-call(bf16[100,3,128,128]{3,2,1,0:T(8,128)(2,1)} %refs.3), custom_call_target="tpu_custom_call" | custom-call | flops 900000000 | bytes 2700000 | tf_op jit(solution)/shard_map/refs/pallas_call | solution.py:164
  13.2 14.3 %collective-permute-done.2.piece = bf16[64,64,128]{2,1,0:T(8,128)(2,1)S(1)} collective-permute-done((bf16[64,64,128]{2,1,0:T(8,128)(2,1)S(1)}, bf16[64,64,128]{2,1,0:T(8,128)(2,1)S(1)}, u32[]{:S(2)}, u32[]{:S(2)}) %collective-permute-start.2) | collective-permute-done | bytes 1048608 | tf_op jit(solution)/shard_map/ppermute | solution.py:414
  27.6 0.0 collective-permute-start.3
  27.6 0.0 copy-done
  27.6 1.8 %collective-permute-start.1 = (bf16[32,64,128]{2,1,0:T(8,128)(2,1)S(1)}, bf16[32,64,128]{2,1,0:T(8,128)(2,1)S(1)}, u32[]{:S(2)}, u32[]{:S(2)}) collective-permute-start(bf16[32,64,128]{2,1,0:T(8,128)(2,1)S(1)} %slice.6), channel_id=1, source_target_pairs={{0,1},{1,0},{2,3},{3,2},{4,5},{5,4},{6,7},{7,6},{8,9},{9,8},{10,11... | collective-permute-start | bytes 1572872 | tf_op jit(solution)/shard_map/ppermute | solution.py:414
  29.4 0.0 copy-done.1
  29.4 0.3 collective-permute-start
  29.7 0.0 copy-done.5
  29.7 0.0 copy-done.6
  29.7 0.8 prepare.1
  30.6 0.0 collective-permute-done.4.sib
  30.6 6.4 %filter.3 = (bf16[128,192,128]{2,1,0:T(8,128)(2,1)S(1)}, bf16[128,192,128]{2,1,0:T(8,128)(2,1)S(1)}, f32[8,128]{1,0:T(8,128)}) custom-call(s32[96]{0:T(128)S(1)} %copy-done.1, bf16[96,64,128]{2,1,0:T(8,128)(2,1)S(1)} %copy-done, bf16[96,64,128]{2,1,0:T(8,128)(2,1)S(1)} %collective-permute-done.4.sib, bf16[16,128,128]{2,1,0:T(8,128)(2,1)S(1)} %get-tuple-element.40.left, ...), custom_call_target="tpu_custom_call" | custom-call | flops 960000000 | bytes 2880000 | tf_op jit(solution)/shard_map/filter/pallas_call | solution.py:209
  37.0 5.1 %collective-permute-done.bins = s32[96]{0:T(128)S(1)} collective-permute-done((s32[96]{0:T(128)S(1)}, s32[96]{0:T(128)S(1)}, u32[]{:S(2)}, u32[]{:S(2)}) %collective-permute-start) | collective-permute-done | bytes 416 | tf_op jit(solution)/shard_map/ppermute | solution.py:415
  42.1 0.0 collective-permute-done.3.sib
  42.1 4.4 %filter.4 = (bf16[128,192,128]{2,1,0:T(8,128)(2,1)S(1)}, bf16[128,192,128]{2,1,0:T(8,128)(2,1)S(1)}, f32[8,128]{1,0:T(8,128)S(1)}) custom-call(s32[96]{0:T(128)S(1)} %collective-permute-done.bins, bf16[64,64,128]{2,1,0:T(8,128)(2,1)S(1)} %gate.2.mine, ...), custom_call_target="tpu_custom_call", output_to_operand_aliasing={{0}: (5, {}), {1}: (6, {})} | custom-call | flops 640000000 | bytes 1920000 | tf_op jit(solution)/shard_map/filter/pallas_call | solution.py:209
  46.5 0.0 collective-permute-done.1.piece
  46.5 0.1 collective-permute-start.5
  46.6 1.9 %collective-permute-done.5.sib = bf16[32,64,128]{2,1,0:T(8,128)(2,1)S(1)} collective-permute-done((bf16[32,64,128]{2,1,0:T(8,128)(2,1)S(1)}, bf16[32,64,128]{2,1,0:T(8,128)(2,1)S(1)}, u32[]{:S(2)}, u32[]{:S(2)}) %collective-permute-start.5) | collective-permute-done | bytes 524320 | tf_op jit(solution)/shard_map/ppermute | solution.py:434
  48.5 2.5 %filter.5 = (bf16[128,192,128]{2,1,0:T(8,128)(2,1)S(1)}, bf16[128,192,128]{2,1,0:T(8,128)(2,1)S(1)}, f32[8,128]{1,0:T(8,128)}) custom-call(s32[96]{0:T(128)S(1)} %collective-permute-done.bins, bf16[32,64,128]{2,1,0:T(8,128)(2,1)S(1)} %gate.3.mine, bf16[32,64,128]{2,1,0:T(8,128)(2,1)S(1)} %collective-permute-done.5.sib, ...), custom_call_target="tpu_custom_call", output_to_operand_aliasing={{0}: (5, {}), {1}: (6, {})} | custom-call | flops 320000000 | bytes 960000 | tf_op jit(solution)/shard_map/filter/pallas_call | solution.py:209
  51.0 4.6 %score.1 = (f32[336,192]{1,0:T(8,128)S(1)}, f32[8,192]{1,0:T(8,128)S(1)}) custom-call(bf16[128,192,128]{2,1,0:T(8,128)(2,1)S(1)} %get-tuple-element.47.plain, bf16[128,336,128]{2,1,0:T(8,128)(2,1)S(1)} %get-tuple-element.48.refs, f32[336,128]{1,0:T(8,128)S(1)} %get-tuple-element.39.token.norm, f32[112,192]{1,0:T(8,128)S(1)} %get-tuple-element.49.mask, ...), custom_call_target="tpu_custom_call" | custom-call | flops 500000000 | bytes 1500000 | tf_op jit(solution)/shard_map/score/pallas_call | solution.py:248
  55.6 1.8 %collective-permute-start.6 = (f32[8,192]{1,0:T(8,128)S(1)}, f32[8,192]{1,0:T(8,128)S(1)}, u32[]{:S(2)}, u32[]{:S(2)}) collective-permute-start(f32[8,192]{1,0:T(8,128)S(1)} %get-tuple-element.52.mine), channel_id=1, source_target_pairs={{0,1},{1,0},{2,3},{3,2},{4,5},{5,4},{6,7},{7,6},{8,9},{9,8},{10,11... | collective-permute-start | bytes 18440 | tf_op jit(solution)/shard_map/ppermute | solution.py:438
  57.4 1.9 %collective-permute-done.6.other = f32[8,192]{1,0:T(8,128)S(1)} collective-permute-done((f32[8,192]{1,0:T(8,128)S(1)}, f32[8,192]{1,0:T(8,128)S(1)}, u32[]{:S(2)}, u32[]{:S(2)}) %collective-permute-start.6) | collective-permute-done | bytes 6176 | tf_op jit(solution)/shard_map/ppermute | solution.py:438
  59.3 0.4 weights.1
  59.7 1.7 %sums.4 = (bf16[4,3,100,128]{3,2,1,0:T(8,128)(2,1)S(1)}, f32[4,3,100,128]{3,2,1,0:T(8,128)S(1)}) custom-call(bf16[2,112,384]{2,1,0:T(8,128)(2,1)S(1)} %weights.1, bf16[128,192,128]{2,1,0:T(8,128)(2,1)S(1)} %get-tuple-element.47.plain, bf16[128,192,128]{2,1,0:T(8,128)(2,1)S(1)} %get-tuple-element.54.turned), custom_call_target="tpu_custom_call" | custom-call | flops 240000000 | bytes 720000 | tf_op jit(solution)/shard_map/sums/pallas_call | solution.py:323
  61.4 1.8 %collective-permute-start.11 = (bf16[4,3,100,128]{3,2,1,0:T(8,128)(2,1)S(1)}, bf16[4,3,100,128]{3,2,1,0:T(8,128)(2,1)S(1)}, u32[]{:S(2)}, u32[]{:S(2)}) collective-permute-start(bf16[4,3,100,128]{3,2,1,0:T(8,128)(2,1)S(1)} %get-tuple-element.62), channel_id=1, source_target_pairs={{0,2},{2,0},{4,6},{6,4},{8,10},{10,8},{12,14},{14,12},{1,3},{3,1},... | collective-permute-start | bytes 921608 | tf_op jit(solution)/shard_map/ppermute | solution.py:445
  63.2 1.7 %sums.3 = (bf16[4,3,100,128]{3,2,1,0:T(8,128)(2,1)S(1)}, f32[4,3,100,128]{3,2,1,0:T(8,128)S(1)}) custom-call(bf16[2,112,384]{2,1,0:T(8,128)(2,1)S(1)} %weights.1, bf16[128,192,128]{2,1,0:T(8,128)(2,1)S(1)} %get-tuple-element.47.plain, bf16[128,192,128]{2,1,0:T(8,128)(2,1)S(1)} %get-tuple-element.54.turned), custom_call_target="tpu_custom_call" | custom-call | flops 240000000 | bytes 720000 | tf_op jit(solution)/shard_map/sums/pallas_call | solution.py:323
  64.9 0.4 collective-permute-start.7
  65.3 1.5 %sums.5 = (bf16[4,2,100,128]{3,2,1,0:T(8,128)(2,1)S(1)}, f32[4,2,100,128]{3,2,1,0:T(8,128)S(1)}) custom-call(bf16[2,112,384]{2,1,0:T(8,128)(2,1)S(1)} %weights.1, bf16[128,192,128]{2,1,0:T(8,128)(2,1)S(1)} %get-tuple-element.47.plain, bf16[128,192,128]{2,1,0:T(8,128)(2,1)S(1)} %get-tuple-element.54.turned), custom_call_target="tpu_custom_call" | custom-call | flops 160000000 | bytes 480000 | tf_op jit(solution)/shard_map/sums/pallas_call | solution.py:323
  66.7 1.8 %collective-permute-start.15 = (bf16[4,2,100,128]{3,2,1,0:T(8,128)(2,1)S(1)}, bf16[4,2,100,128]{3,2,1,0:T(8,128)(2,1)S(1)}, u32[]{:S(2)}, u32[]{:S(2)}) collective-permute-start(bf16[4,2,100,128]{3,2,1,0:T(8,128)(2,1)S(1)} %get-tuple-element.68), channel_id=1, source_target_pairs={{0,2},{2,0},{4,6},{6,4},{8,10},{10,8},{12,14},{14,12},{1,3},{3,1},... | collective-permute-start | bytes 614408 | tf_op jit(solution)/shard_map/ppermute | solution.py:445
  68.5 3.4 %collective-permute-done.11.got = bf16[4,3,100,128]{3,2,1,0:T(8,128)(2,1)S(1)} collective-permute-done((bf16[4,3,100,128]{3,2,1,0:T(8,128)(2,1)S(1)}, bf16[4,3,100,128]{3,2,1,0:T(8,128)(2,1)S(1)}, u32[]{:S(2)}, u32[]{:S(2)}) %collective-permute-start.11) | collective-permute-done | bytes 307232 | tf_op jit(solution)/shard_map/ppermute | solution.py:445
  71.9 0.1 fold.4
  72.0 1.9 %collective-permute-start.12 = (bf16[1,3,100,128]{3,2,1,0:T(8,128)(2,1)S(1)}, bf16[1,3,100,128]{3,2,1,0:T(8,128)(2,1)S(1)}, u32[]{:S(2)}, u32[]{:S(2)}) collective-permute-start(bf16[1,3,100,128]{3,2,1,0:T(8,128)(2,1)S(1)} %get-tuple-element.64), channel_id=1, source_target_pairs={{0,4},{2,6},{4,0},{6,2},{8,12},{10,14},{12,8},{14,10},{1,5},{3,7},... | collective-permute-start | bytes 230408 | tf_op jit(solution)/shard_map/ppermute | solution.py:455
  73.9 7.4 %collective-permute-done.15.got = bf16[4,2,100,128]{3,2,1,0:T(8,128)(2,1)S(1)} collective-permute-done((bf16[4,2,100,128]{3,2,1,0:T(8,128)(2,1)S(1)}, bf16[4,2,100,128]{3,2,1,0:T(8,128)(2,1)S(1)}, u32[]{:S(2)}, u32[]{:S(2)}) %collective-permute-start.15) | collective-permute-done | bytes 204832 | tf_op jit(solution)/shard_map/ppermute | solution.py:445
  81.3 0.1 fold.5
  81.4 1.9 %collective-permute-start.16 = (bf16[1,2,100,128]{3,2,1,0:T(8,128)(2,1)S(1)}, bf16[1,2,100,128]{3,2,1,0:T(8,128)(2,1)S(1)}, u32[]{:S(2)}, u32[]{:S(2)}) collective-permute-start(bf16[1,2,100,128]{3,2,1,0:T(8,128)(2,1)S(1)} %get-tuple-element.70), channel_id=1, source_target_pairs={{0,4},{2,6},{4,0},{6,2},{8,12},{10,14},{12,8},{14,10},{1,5},{3,7},... | collective-permute-start | bytes 153608 | tf_op jit(solution)/shard_map/ppermute | solution.py:455
  83.2 2.6 %collective-permute-start.17 = (bf16[1,2,100,128]{3,2,1,0:T(8,128)(2,1)S(1)}, bf16[1,2,100,128]{3,2,1,0:T(8,128)(2,1)S(1)}, u32[]{:S(2)}, u32[]{:S(2)}) collective-permute-start(bf16[1,2,100,128]{3,2,1,0:T(8,128)(2,1)S(1)} %get-tuple-element.71), channel_id=1, source_target_pairs={{0,8},{2,10},{4,12},{6,14},{8,0},{10,2},{12,4},{14,6},{1,9},{3,11}... | collective-permute-start | bytes 153608 | tf_op jit(solution)/shard_map/ppermute | solution.py:455
  85.8 0.0 collective-permute-start.18
  85.8 0.0 collective-permute-done.7.got
  85.8 1.9 %collective-permute-start.13 = (bf16[1,3,100,128]{3,2,1,0:T(8,128)(2,1)S(1)}, bf16[1,3,100,128]{3,2,1,0:T(8,128)(2,1)S(1)}, u32[]{:S(2)}, u32[]{:S(2)}) collective-permute-start(bf16[1,3,100,128]{3,2,1,0:T(8,128)(2,1)S(1)} %get-tuple-element.65), channel_id=1, source_target_pairs={{0,8},{2,10},{4,12},{6,14},{8,0},{10,2},{12,4},{14,6},{1,9},{3,11}... | collective-permute-start | bytes 230408 | tf_op jit(solution)/shard_map/ppermute | solution.py:455
  87.7 0.1 fold.3
  87.8 0.0 collective-permute-done.16.args_9_
  87.8 2.0 %collective-permute-start.14 = (bf16[1,3,100,128]{3,2,1,0:T(8,128)(2,1)S(1)}, bf16[1,3,100,128]{3,2,1,0:T(8,128)(2,1)S(1)}, u32[]{:S(2)}, u32[]{:S(2)}) collective-permute-start(bf16[1,3,100,128]{3,2,1,0:T(8,128)(2,1)S(1)} %get-tuple-element.66), channel_id=1, source_target_pairs={{0,12},{2,14},{4,8},{6,10},{8,4},{10,6},{12,0},{14,2},{1,13},{3,15... | collective-permute-start | bytes 230408 | tf_op jit(solution)/shard_map/ppermute | solution.py:455
  89.8 3.9 %collective-permute-done.17.args_10_ = bf16[1,2,100,128]{3,2,1,0:T(8,128)(2,1)S(1)} collective-permute-done((bf16[1,2,100,128]{3,2,1,0:T(8,128)(2,1)S(1)}, bf16[1,2,100,128]{3,2,1,0:T(8,128)(2,1)S(1)}, u32[]{:S(2)}, u32[]{:S(2)}) %collective-permute-start.17) | collective-permute-done | bytes 51232 | tf_op jit(solution)/shard_map/ppermute | solution.py:455
  93.7 1.8 %collective-permute-start.10 = (bf16[1,3,100,128]{3,2,1,0:T(8,128)(2,1)S(1)}, bf16[1,3,100,128]{3,2,1,0:T(8,128)(2,1)S(1)}, u32[]{:S(2)}, u32[]{:S(2)}) collective-permute-start(bf16[1,3,100,128]{3,2,1,0:T(8,128)(2,1)S(1)} %get-tuple-element.60), channel_id=1, source_target_pairs={{0,12},{2,14},{4,8},{6,10},{8,4},{10,6},{12,0},{14,2},{1,13},{3,15... | collective-permute-start | bytes 230408 | tf_op jit(solution)/shard_map/ppermute | solution.py:455
  95.5 0.0 collective-permute-done.18.args_11_
  95.5 1.8 %collective-permute-start.8 = (bf16[1,3,100,128]{3,2,1,0:T(8,128)(2,1)S(1)}, bf16[1,3,100,128]{3,2,1,0:T(8,128)(2,1)S(1)}, u32[]{:S(2)}, u32[]{:S(2)}) collective-permute-start(bf16[1,3,100,128]{3,2,1,0:T(8,128)(2,1)S(1)} %get-tuple-element.58), channel_id=1, source_target_pairs={{0,4},{2,6},{4,0},{6,2},{8,12},{10,14},{12,8},{14,10},{1,5},{3,7},... | collective-permute-start | bytes 230408 | tf_op jit(solution)/shard_map/ppermute | solution.py:455
  97.3 0.0 collective-permute-done.12.args_5_
  97.3 0.8 collective-permute-start.9
  98.1 0.4 collective-permute-done.13.args_6_
  98.4 0.0 collective-permute-done.14.args_7_
  98.4 1.7 %collective-permute-done.10.args_3_ = bf16[1,3,100,128]{3,2,1,0:T(8,128)(2,1)S(1)} collective-permute-done((bf16[1,3,100,128]{3,2,1,0:T(8,128)(2,1)S(1)}, bf16[1,3,100,128]{3,2,1,0:T(8,128)(2,1)S(1)}, u32[]{:S(2)}, u32[]{:S(2)}) %collective-permute-start.10) | collective-permute-done | bytes 76832 | tf_op jit(solution)/shard_map/ppermute | solution.py:455
  100.1 1.1 %collective-permute-done.8.args_1_ = bf16[1,3,100,128]{3,2,1,0:T(8,128)(2,1)S(1)} collective-permute-done((bf16[1,3,100,128]{3,2,1,0:T(8,128)(2,1)S(1)}, bf16[1,3,100,128]{3,2,1,0:T(8,128)(2,1)S(1)}, u32[]{:S(2)}, u32[]{:S(2)}) %collective-permute-start.8) | collective-permute-done | bytes 76832 | tf_op jit(solution)/shard_map/ppermute | solution.py:455
  101.2 2.3 %collective-permute-done.9.args_2_ = bf16[1,3,100,128]{3,2,1,0:T(8,128)(2,1)S(1)} collective-permute-done((bf16[1,3,100,128]{3,2,1,0:T(8,128)(2,1)S(1)}, bf16[1,3,100,128]{3,2,1,0:T(8,128)(2,1)S(1)}, u32[]{:S(2)}, u32[]{:S(2)}) %collective-permute-start.9) | collective-permute-done | bytes 76832 | tf_op jit(solution)/shard_map/ppermute | solution.py:455
  103.4 0.9 finish.1
  (6 shorter events, 0.0 us)
Async XLA Ops:
  1.3 26.3 %copy-start = (bf16[96,64,128]{2,1,0:T(8,128)(2,1)S(1)}, bf16[96,64,128]{2,1,0:T(8,128)(2,1)}, u32[]{:S(2)}) copy-start(bf16[96,64,128]{2,1,0:T(8,128)(2,1)} %mine.1) | copy-start | bytes 4718596
  1.3 28.1 %copy-start.1 = (s32[96]{0:T(128)S(1)}, s32[96]{0:T(128)}, u32[]{:S(2)}) copy-start(s32[96]{0:T(128)} %bins.1) | copy-start | bytes 1156
  1.3 28.4 %copy-start.2 = (s32[192,100]{1,0:T(8,128)S(1)}, s32[192,100]{1,0:T(8,128)}, u32[]{:S(2)}) copy-start(s32[192,100]{1,0:T(8,128)} %mask.1) | copy-start | bytes 230404
  1.3 28.4 %copy-start.3 = (f32[16,128]{1,0:T(8,128)S(1)}, f32[16,128]{1,0:T(8,128)}, u32[]{:S(2)}) copy-start(f32[16,128]{1,0:T(8,128)} %ctf.1) | copy-start | bytes 24580
  1.3 28.4 %copy-start.4 = (s32[100,3]{0,1:T(4,128)S(1)}, s32[100,3]{0,1:T(4,128)}, u32[]{:S(2)}) copy-start(s32[100,3]{0,1:T(4,128)} %param.13) | copy-start | bytes 3604
  1.4 28.4 %copy-start.5 = (f32[192]{0:T(256)S(1)}, f32[192]{0:T(256)}, u32[]{:S(2)}) copy-start(f32[192]{0:T(256)} %param.15) | copy-start | bytes 2308
  1.4 28.4 %copy-start.6 = (f32[128]{0:T(128)S(1)}, f32[128]{0:T(128)}, u32[]{:S(2)}) copy-start(f32[128]{0:T(128)} %param.11) | copy-start | bytes 1540
  1.4 26.2 %collective-permute-start.2 = (bf16[64,64,128]{2,1,0:T(8,128)(2,1)S(1)}, bf16[64,64,128]{2,1,0:T(8,128)(2,1)S(1)}, u32[]{:S(2)}, u32[]{:S(2)}) collective-permute-start(bf16[64,64,128]{2,1,0:T(8,128)(2,1)S(1)} %slice.7), channel_id=1, source_target_pairs={{0,1},{1,0},{2,3},{3,2},{4,5},{5,4},{6,7},{7,6},{8,9},{9,8},{10,11... | collective-permute-start | bytes 3145736 | tf_op jit(solution)/shard_map/ppermute | solution.py:414
  4.4 26.1 %collective-permute-start.4 = (bf16[96,64,128]{2,1,0:T(8,128)(2,1)}, bf16[96,64,128]{2,1,0:T(8,128)(2,1)S(1)}, u32[]{:S(2)}, u32[]{:S(2)}) collective-permute-start(bf16[96,64,128]{2,1,0:T(8,128)(2,1)} %mine.1), channel_id=1, source_target_pairs={{0,16},{16,0},{1,17},{17,1},{2,18},{18,2},{3,19},{19,3},{4,20},{20... | collective-permute-start | bytes 4718600 | tf_op jit(solution)/shard_map/ppermute | solution.py:416
  27.6 14.5 %collective-permute-start.3 = (bf16[64,64,128]{2,1,0:T(8,128)(2,1)S(1)}, bf16[64,64,128]{2,1,0:T(8,128)(2,1)S(1)}, u32[]{:S(2)}, u32[]{:S(2)}) collective-permute-start(bf16[64,64,128]{2,1,0:T(8,128)(2,1)S(1)} %gate.2.mine), channel_id=1, source_target_pairs={{0,16},{16,0},{1,17},{17,1},{2,18},{18,2},{3,19},{19,3},{4,20},{20... | collective-permute-start | bytes 3145736 | tf_op jit(solution)/shard_map/ppermute | solution.py:424
  27.6 18.9 %collective-permute-start.1 = (bf16[32,64,128]{2,1,0:T(8,128)(2,1)S(1)}, bf16[32,64,128]{2,1,0:T(8,128)(2,1)S(1)}, u32[]{:S(2)}, u32[]{:S(2)}) collective-permute-start(bf16[32,64,128]{2,1,0:T(8,128)(2,1)S(1)} %slice.6), channel_id=1, source_target_pairs={{0,1},{1,0},{2,3},{3,2},{4,5},{5,4},{6,7},{7,6},{8,9},{9,8},{10,11... | collective-permute-start | bytes 1572872 | tf_op jit(solution)/shard_map/ppermute | solution.py:414
  29.4 12.7 %collective-permute-start = (s32[96]{0:T(128)S(1)}, s32[96]{0:T(128)S(1)}, u32[]{:S(2)}, u32[]{:S(2)}) collective-permute-start(s32[96]{0:T(128)S(1)} %copy-done.1), channel_id=1, source_target_pairs={{0,1},{1,0},{2,3},{3,2},{4,5},{5,4},{6,7},{7,6},{8,9},{9,8},{10,11... | collective-permute-start | bytes 1160 | tf_op jit(solution)/shard_map/ppermute | solution.py:415
  46.5 2.0 %collective-permute-start.5 = (bf16[32,64,128]{2,1,0:T(8,128)(2,1)S(1)}, bf16[32,64,128]{2,1,0:T(8,128)(2,1)S(1)}, u32[]{:S(2)}, u32[]{:S(2)}) collective-permute-start(bf16[32,64,128]{2,1,0:T(8,128)(2,1)S(1)} %gate.3.mine), channel_id=1, source_target_pairs={{0,16},{16,0},{1,17},{17,1},{2,18},{18,2},{3,19},{19,3},{4,20},{20... | collective-permute-start | bytes 1572872 | tf_op jit(solution)/shard_map/ppermute | solution.py:434
  55.6 3.7 %collective-permute-start.6 = (f32[8,192]{1,0:T(8,128)S(1)}, f32[8,192]{1,0:T(8,128)S(1)}, u32[]{:S(2)}, u32[]{:S(2)}) collective-permute-start(f32[8,192]{1,0:T(8,128)S(1)} %get-tuple-element.52.mine), channel_id=1, source_target_pairs={{0,1},{1,0},{2,3},{3,2},{4,5},{5,4},{6,7},{7,6},{8,9},{9,8},{10,11... | collective-permute-start | bytes 18440 | tf_op jit(solution)/shard_map/ppermute | solution.py:438
  61.4 10.5 %collective-permute-start.11 = (bf16[4,3,100,128]{3,2,1,0:T(8,128)(2,1)S(1)}, bf16[4,3,100,128]{3,2,1,0:T(8,128)(2,1)S(1)}, u32[]{:S(2)}, u32[]{:S(2)}) collective-permute-start(bf16[4,3,100,128]{3,2,1,0:T(8,128)(2,1)S(1)} %get-tuple-element.62), channel_id=1, source_target_pairs={{0,2},{2,0},{4,6},{6,4},{8,10},{10,8},{12,14},{14,12},{1,3},{3,1},... | collective-permute-start | bytes 921608 | tf_op jit(solution)/shard_map/ppermute | solution.py:445
  64.9 20.9 %collective-permute-start.7 = (bf16[4,3,100,128]{3,2,1,0:T(8,128)(2,1)S(1)}, bf16[4,3,100,128]{3,2,1,0:T(8,128)(2,1)S(1)}, u32[]{:S(2)}, u32[]{:S(2)}) collective-permute-start(bf16[4,3,100,128]{3,2,1,0:T(8,128)(2,1)S(1)} %get-tuple-element.56), channel_id=1, source_target_pairs={{0,2},{2,0},{4,6},{6,4},{8,10},{10,8},{12,14},{14,12},{1,3},{3,1},... | collective-permute-start | bytes 921608 | tf_op jit(solution)/shard_map/ppermute | solution.py:445
  66.7 14.6 %collective-permute-start.15 = (bf16[4,2,100,128]{3,2,1,0:T(8,128)(2,1)S(1)}, bf16[4,2,100,128]{3,2,1,0:T(8,128)(2,1)S(1)}, u32[]{:S(2)}, u32[]{:S(2)}) collective-permute-start(bf16[4,2,100,128]{3,2,1,0:T(8,128)(2,1)S(1)} %get-tuple-element.68), channel_id=1, source_target_pairs={{0,2},{2,0},{4,6},{6,4},{8,10},{10,8},{12,14},{14,12},{1,3},{3,1},... | collective-permute-start | bytes 614408 | tf_op jit(solution)/shard_map/ppermute | solution.py:445
  72.0 25.3 %collective-permute-start.12 = (bf16[1,3,100,128]{3,2,1,0:T(8,128)(2,1)S(1)}, bf16[1,3,100,128]{3,2,1,0:T(8,128)(2,1)S(1)}, u32[]{:S(2)}, u32[]{:S(2)}) collective-permute-start(bf16[1,3,100,128]{3,2,1,0:T(8,128)(2,1)S(1)} %get-tuple-element.64), channel_id=1, source_target_pairs={{0,4},{2,6},{4,0},{6,2},{8,12},{10,14},{12,8},{14,10},{1,5},{3,7},... | collective-permute-start | bytes 230408 | tf_op jit(solution)/shard_map/ppermute | solution.py:455
  81.4 6.4 %collective-permute-start.16 = (bf16[1,2,100,128]{3,2,1,0:T(8,128)(2,1)S(1)}, bf16[1,2,100,128]{3,2,1,0:T(8,128)(2,1)S(1)}, u32[]{:S(2)}, u32[]{:S(2)}) collective-permute-start(bf16[1,2,100,128]{3,2,1,0:T(8,128)(2,1)S(1)} %get-tuple-element.70), channel_id=1, source_target_pairs={{0,4},{2,6},{4,0},{6,2},{8,12},{10,14},{12,8},{14,10},{1,5},{3,7},... | collective-permute-start | bytes 153608 | tf_op jit(solution)/shard_map/ppermute | solution.py:455
  83.2 10.5 %collective-permute-start.17 = (bf16[1,2,100,128]{3,2,1,0:T(8,128)(2,1)S(1)}, bf16[1,2,100,128]{3,2,1,0:T(8,128)(2,1)S(1)}, u32[]{:S(2)}, u32[]{:S(2)}) collective-permute-start(bf16[1,2,100,128]{3,2,1,0:T(8,128)(2,1)S(1)} %get-tuple-element.71), channel_id=1, source_target_pairs={{0,8},{2,10},{4,12},{6,14},{8,0},{10,2},{12,4},{14,6},{1,9},{3,11}... | collective-permute-start | bytes 153608 | tf_op jit(solution)/shard_map/ppermute | solution.py:455
  85.8 9.7 %collective-permute-start.18 = (bf16[1,2,100,128]{3,2,1,0:T(8,128)(2,1)S(1)}, bf16[1,2,100,128]{3,2,1,0:T(8,128)(2,1)S(1)}, u32[]{:S(2)}, u32[]{:S(2)}) collective-permute-start(bf16[1,2,100,128]{3,2,1,0:T(8,128)(2,1)S(1)} %get-tuple-element.72), channel_id=1, source_target_pairs={{0,12},{2,14},{4,8},{6,10},{8,4},{10,6},{12,0},{14,2},{1,13},{3,15... | collective-permute-start | bytes 153608 | tf_op jit(solution)/shard_map/ppermute | solution.py:455
  85.8 12.6 %collective-permute-start.13 = (bf16[1,3,100,128]{3,2,1,0:T(8,128)(2,1)S(1)}, bf16[1,3,100,128]{3,2,1,0:T(8,128)(2,1)S(1)}, u32[]{:S(2)}, u32[]{:S(2)}) collective-permute-start(bf16[1,3,100,128]{3,2,1,0:T(8,128)(2,1)S(1)} %get-tuple-element.65), channel_id=1, source_target_pairs={{0,8},{2,10},{4,12},{6,14},{8,0},{10,2},{12,4},{14,6},{1,9},{3,11}... | collective-permute-start | bytes 230408 | tf_op jit(solution)/shard_map/ppermute | solution.py:455
  87.8 10.6 %collective-permute-start.14 = (bf16[1,3,100,128]{3,2,1,0:T(8,128)(2,1)S(1)}, bf16[1,3,100,128]{3,2,1,0:T(8,128)(2,1)S(1)}, u32[]{:S(2)}, u32[]{:S(2)}) collective-permute-start(bf16[1,3,100,128]{3,2,1,0:T(8,128)(2,1)S(1)} %get-tuple-element.66), channel_id=1, source_target_pairs={{0,12},{2,14},{4,8},{6,10},{8,4},{10,6},{12,0},{14,2},{1,13},{3,15... | collective-permute-start | bytes 230408 | tf_op jit(solution)/shard_map/ppermute | solution.py:455
  93.7 6.4 %collective-permute-start.10 = (bf16[1,3,100,128]{3,2,1,0:T(8,128)(2,1)S(1)}, bf16[1,3,100,128]{3,2,1,0:T(8,128)(2,1)S(1)}, u32[]{:S(2)}, u32[]{:S(2)}) collective-permute-start(bf16[1,3,100,128]{3,2,1,0:T(8,128)(2,1)S(1)} %get-tuple-element.60), channel_id=1, source_target_pairs={{0,12},{2,14},{4,8},{6,10},{8,4},{10,6},{12,0},{14,2},{1,13},{3,15... | collective-permute-start | bytes 230408 | tf_op jit(solution)/shard_map/ppermute | solution.py:455
  95.5 5.6 %collective-permute-start.8 = (bf16[1,3,100,128]{3,2,1,0:T(8,128)(2,1)S(1)}, bf16[1,3,100,128]{3,2,1,0:T(8,128)(2,1)S(1)}, u32[]{:S(2)}, u32[]{:S(2)}) collective-permute-start(bf16[1,3,100,128]{3,2,1,0:T(8,128)(2,1)S(1)} %get-tuple-element.58), channel_id=1, source_target_pairs={{0,4},{2,6},{4,0},{6,2},{8,12},{10,14},{12,8},{14,10},{1,5},{3,7},... | collective-permute-start | bytes 230408 | tf_op jit(solution)/shard_map/ppermute | solution.py:455
  97.3 6.1 %collective-permute-start.9 = (bf16[1,3,100,128]{3,2,1,0:T(8,128)(2,1)S(1)}, bf16[1,3,100,128]{3,2,1,0:T(8,128)(2,1)S(1)}, u32[]{:S(2)}, u32[]{:S(2)}) collective-permute-start(bf16[1,3,100,128]{3,2,1,0:T(8,128)(2,1)S(1)} %get-tuple-element.59), channel_id=1, source_target_pairs={{0,8},{2,10},{4,12},{6,14},{8,0},{10,2},{12,4},{14,6},{1,9},{3,11}... | collective-permute-start | bytes 230408 | tf_op jit(solution)/shard_map/ppermute | solution.py:455

commit v4 on v3

--- a/solution.py
+++ b/solution.py
@@ -43,7 +43,8 @@
     return pltpu.with_memory_space_constraint(x, pltpu.VMEM)
 
 
-def prepare_kernel(ctf, band, mask, noise, rot, left, right, mask_out, noise_out, rot_out, scr):
+def prepare_kernel(ctf, band, mask, noise, rot, after, left, right, mask_out, noise_out, rot_out, scr):
+    del after
     bins, width = ctf.shape
     rots, classes = rot.shape
     padded = rot_out.shape[1]
@@ -87,7 +88,7 @@
         rot_out[j] = jnp.broadcast_to(turned[:padded, j : j + 1], (padded, square))
 
 
-def prepare(ctf, band, mask, noise, rot, padded):
+def prepare(ctf, band, mask, noise, rot, after, padded):
     bins, width = ctf.shape
     total = noise.shape[0]
     lanes = max(128, -(-padded // 128) * 128)
@@ -105,25 +106,25 @@
         compiler_params=pltpu.CompilerParams(vmem_limit_bytes=4 * MIB),
         cost_estimate=cost(3),
         name="prepare",
-    )(ctf, band.reshape(1, width), mask, noise.reshape(1, total), rot)
-
-
-def gate_kernel(piece, token, out):
-    del piece, token, out
-
-
-def gate(piece, token):
+    )(ctf, band.reshape(1, width), mask, noise.reshape(1, total), rot, held(after))
+
+
+def gate_kernel(*refs):
+    del refs
+
+
+def gate(piece, *tokens):
     anywhere = pl.BlockSpec(memory_space=pl.ANY)
     return pl.pallas_call(
         gate_kernel,
-        in_specs=[anywhere, anywhere],
+        in_specs=[anywhere] * (1 + len(tokens)),
         out_specs=anywhere,
         out_shape=jax.ShapeDtypeStruct(piece.shape, piece.dtype),
         input_output_aliases={0: 0},
         compiler_params=pltpu.CompilerParams(vmem_limit_bytes=MIB),
         cost_estimate=cost(0.1),
         name="gate",
-    )(piece, token)
+    )(piece, *tokens)
 
 
 def refs_kernel(refs, out, norm, scratch, *, padded):
@@ -177,47 +178,54 @@
     )(pltpu.with_memory_space_constraint(refs, pltpu.HBM))
 
 
-def filter_kernel(bins, mine, sib, left, right, *rest, skip, at):
+def filter_kernel(bins, mine, left, right, *rest, parts, skip, at):
+    sibs = rest[:parts]
     plain, turned, token, scr, scr_t = rest[-5:]
     token[...] = jnp.zeros_like(token)
-    count, half, width = mine.shape
+    width = mine.shape[2]
     top = lax.axis_index("section") == 0
     pitch = width + PAD
 
-    @pl.loop(0, count // GROUP)
-    def _(g):
-        base = pl.multiple_of(g * GROUP, GROUP)
-        for i in range(GROUP):
-            b = bins[skip + base + i]
-            a = mine[base + i]
-            o = sib[base + i]
-            x = jnp.concatenate([jnp.where(top, a, o), jnp.where(top, o, a)], axis=0)
-            f = nn(left[b], nn(x, right[b]).astype(BF16))
-            scr[pl.ds(i * pitch, width)] = f
-            scr_t[pl.ds(i * pitch, width)] = f.T
-        to = pl.multiple_of(at + base, GROUP)
-        for r in range(width):
-            plain[r, pl.ds(to, GROUP)] = scr[pl.ds(r, GROUP, stride=pitch)].astype(BF16)
-            turned[r, pl.ds(to, GROUP)] = scr_t[pl.ds(r, GROUP, stride=pitch)].astype(BF16)
-
-
-def filter_chunk(bins, mine, sib, left, right, buffers, total, skip, at):
+    def part(sib, first):
+        @pl.loop(0, sib.shape[0] // GROUP)
+        def _(g):
+            base = pl.multiple_of(g * GROUP, GROUP)
+            for i in range(GROUP):
+                b = bins[skip + first + base + i]
+                a = mine[first + base + i]
+                o = sib[base + i]
+                x = jnp.concatenate([jnp.where(top, a, o), jnp.where(top, o, a)], axis=0)
+                f = nn(left[b], nn(x, right[b]).astype(BF16))
+                scr[pl.ds(i * pitch, width)] = f
+                scr_t[pl.ds(i * pitch, width)] = f.T
+            to = pl.multiple_of(at + first + base, GROUP)
+            for r in range(width):
+                plain[r, pl.ds(to, GROUP)] = scr[pl.ds(r, GROUP, stride=pitch)].astype(BF16)
+                turned[r, pl.ds(to, GROUP)] = scr_t[pl.ds(r, GROUP, stride=pitch)].astype(BF16)
+
+    first = 0
+    for sib in sibs:
+        part(sib, first)
+        first += sib.shape[0]
+
+
+def filter_chunk(bins, mine, sibs, left, right, buffers, total, skip, at):
     count, half, width = mine.shape
     smem = pl.BlockSpec(memory_space=pltpu.SMEM)
     vmem = pl.BlockSpec(memory_space=pltpu.VMEM)
-    buffers = [held(b) for b in buffers]
-    return pl.pallas_call(
-        functools.partial(filter_kernel, skip=skip, at=at),
-        in_specs=[smem] + [vmem] * (4 + len(buffers)),
+    parts = len(sibs)
+    return pl.pallas_call(
+        functools.partial(filter_kernel, parts=parts, skip=skip, at=at),
+        in_specs=[smem] + [vmem] * (3 + parts + len(buffers)),
         out_specs=(vmem, vmem, vmem),
         out_shape=(pinned((2 * half, total, width), BF16),) * 2
         + (jax.ShapeDtypeStruct((8, width), F32),),
         scratch_shapes=[pltpu.VMEM((GROUP * (2 * half + PAD), width), F32)] * 2,
-        input_output_aliases={5 + i: i for i in range(len(buffers))},
+        input_output_aliases={4 + parts + i: i for i in range(len(buffers))},
         compiler_params=pltpu.CompilerParams(vmem_limit_bytes=8 * MIB),
         cost_estimate=cost(count * 0.1),
         name="filter",
-    )(bins, mine, sib, held(left), held(right), *buffers)
+    )(bins, mine, held(left), held(right), *sibs, *[held(b) for b in buffers])
 
 
 def score_kernel(plain, refs, norm, mask, noise, scaled, stats):
@@ -286,7 +294,8 @@
     )(held(scaled), held(mine), other, held(rot))
 
 
-def sums_kernel(weights, plain, turned, send, keep, *, dom, start, classes):
+def sums_kernel(weights, plain, turned, *rest, dom, start, classes):
+    send, keep = rest[-2:]
     _, rows, _, width = send.shape
     height = plain.shape[0]
     block = height // 2 // dom
@@ -317,12 +326,12 @@
             keep[g, r] = here[:classes]
 
 
-def sums(weights, plain, turned, dom, start, rows, classes):
+def sums(weights, plain, turned, after, dom, start, rows, classes):
     width = plain.shape[2]
     vmem = pl.BlockSpec(memory_space=pltpu.VMEM)
     return pl.pallas_call(
         functools.partial(sums_kernel, dom=dom, start=start, classes=classes),
-        in_specs=[vmem] * 3,
+        in_specs=[vmem] * 3 + [pl.BlockSpec(memory_space=pl.ANY)] * len(after),
         out_shape=(
             jax.ShapeDtypeStruct((dom // 2, rows, classes, width), BF16),
             pinned((dom // 2, rows, classes, width), F32),
@@ -330,10 +339,11 @@
         compiler_params=pltpu.CompilerParams(vmem_limit_bytes=8 * MIB),
         cost_estimate=cost(SUMS * rows),
         name="sums",
-    )(held(weights), held(plain), held(turned))
+    )(held(weights), held(plain), held(turned), *after)
 
 
 def fold_kernel(keep, got, *outs, fan, bit):
+    outs = outs[-fan:]
     rest = keep.shape[0] // fan
     at = (lax.axis_index("dom") // (1 << bit)) % fan
     for m, out in enumerate(outs):
@@ -343,16 +353,17 @@
             out[i] = value.astype(out.dtype)
 
 
-def fold(keep, got, fan, bit):
+def fold(keep, got, after, fan, bit):
     rest = (keep.shape[0] // fan,) + keep.shape[1:]
     return pl.pallas_call(
         functools.partial(fold_kernel, fan=fan, bit=bit),
-        in_specs=[pl.BlockSpec(memory_space=pltpu.VMEM)] * 2,
+        in_specs=[pl.BlockSpec(memory_space=pltpu.VMEM)] * 2
+        + [pl.BlockSpec(memory_space=pl.ANY)] * len(after),
         out_shape=(pinned(rest, F32),) + (jax.ShapeDtypeStruct(rest, BF16),) * (fan - 1),
         compiler_params=pltpu.CompilerParams(vmem_limit_bytes=8 * MIB),
         cost_estimate=cost(FOLD),
         name="fold",
-    )(held(keep), got)
+    )(held(keep), got, *after)
 
 
 def finish_kernel(*args, counts):
@@ -417,21 +428,21 @@
 
     refs, norm = lay_refs(references, padded)
     left, right, mask, noise, rot = prepare(
-        ctf_kernels, band_kernel, class_mask, noise_var, rot_index.T, padded
+        ctf_kernels, band_kernel, class_mask, noise_var, rot_index.T, norm, padded
     )
     total = 2 * particles
-    remote[0] = gate(remote[0], norm)
-    sib = over_section(remote[0])
     *buffers, token = filter_chunk(
-        defocus_bin, images, own_sib, left, right, (), total, 0, 0
+        defocus_bin, images, [own_sib], left, right, (), total, 0, 0
     )
+    tokens = (token, other_bins)
     for i, a in enumerate(starts):
+        piece = gate(remote[i], *tokens)
+        step = GROUP if i + 1 < len(starts) else sizes[i]
+        sibs = [over_section(piece[b : b + step]) for b in range(0, sizes[i], step)]
         *buffers, token = filter_chunk(
-            other_bins, remote[i], sib, left, right, buffers, total, a, particles + a
+            other_bins, piece, sibs, left, right, buffers, total, a, particles + a
         )
-        if i + 1 < len(starts):
-            remote[i + 1] = gate(remote[i + 1], token)
-            sib = over_section(remote[i + 1])
+        tokens = (token,)
     plain, turned = buffers
 
     scaled, stats = score(plain, refs, norm, mask, noise)
@@ -439,23 +450,23 @@
 
     start = 0
     done = []
+    summed, folded = (), ()
     for rows in row_pieces(half // dom):
-        send, keep = sums(weights, plain, turned, dom, start, rows, classes)
+        send, keep = sums(weights, plain, turned, summed, dom, start, rows, classes)
+        summed = (send,)
         start += rows
         got = lax.ppermute(send, "dom", [(i, i ^ 1) for i in range(dom)])
         bit = 1
         while keep.shape[0] > 4:
-            keep, send = fold(keep, got, 2, bit)
+            keep, send = fold(keep, got, folded, 2, bit)
             got = lax.ppermute(send, "dom", [(i, i ^ (1 << bit)) for i in range(dom)])
             bit += 1
-        keep, *sends = fold(keep, got, keep.shape[0], bit)
-        done.append(
-            [keep]
-            + [
-                lax.ppermute(s, "dom", [(i, i ^ ((m + 1) << bit)) for i in range(dom)])
-                for m, s in enumerate(sends)
-            ]
+        keep, *sends = fold(keep, got, folded, keep.shape[0], bit)
+        folded = tuple(
+            lax.ppermute(s, "dom", [(i, i ^ ((m + 1) << bit)) for i in range(dom)])
+            for m, s in enumerate(sends)
         )
+        done.append((keep,) + folded)
     return finish(done)
 
 

time: 104 us -> 95 us (0.913)
  waiting for transfers between devices: 43.3 us -> 33.7 us
  local copies, waits for them, and re-layouts: 1.37 us -> 2.47 us
    ppermute x2, waiting for transfers between devices: 14.3 us -> 4.56 us  [local(): remote = [over_cls(images[a:a + n]) for a, n in zip(starts, sizes)]]
    ppermute x3, waiting for transfers between devices: 10.9 us -> 5.76 us  [local(): got = lax.ppermute(send, 'dom', [(i, i ^ 1) for i in range(dom)])]
    ppermute x9, waiting for transfers between devices: 9.19 us -> 13.1 us  [local(): lax.ppermute(s, 'dom', [(i, i ^ m + 1 << bit) for i in range(dom)])]
    ppermute x2 -> x5, waiting for transfers between devices: 1.9 us -> 3.54 us  [local(): sibs = [over_section(piece[b:b + step]) for b in range(0, sizes[i], step)]]
    ppermute x9, starting transfers between devices: 14.6 us -> 13.4 us  [local(): lax.ppermute(s, 'dom', [(i, i ^ m + 1 << bit) for i in range(dom)])]
    slice x2, local copies, waits for them, and re-layouts: 1.33 us -> 2.37 us  [local(): remote = [over_cls(images[a:a + n]) for a, n in zip(starts, sizes)]]
  transfers between devices with their start and end apart: 19 -> 22, of which waited for: 11 -> 16; matrix products, arithmetic and copies ran while one was open for 0% -> 3% of each run, Pallas kernels for 23% -> 24%
where the time goes in v4:
time: 95 us; the launch traced here: 94.8 us
  waiting for transfers between devices  33.7 us (35%)
  Pallas kernels  33 us (35%)
  starting transfers between devices  25.4 us (27%)
  local copies, waits for them, and re-layouts  2.47 us (3%)
    ppermute x9, starting transfers between devices, local(): lax.ppermute(s, 'dom', [(i, i ^ m + 1 << bit) for i in range(dom)])  13.4 us
    ppermute x9, waiting for transfers between devices, local(): lax.ppermute(s, 'dom', [(i, i ^ m + 1 << bit) for i in range(dom)])  13.1 us
    pallas_call x3, Pallas kernels, filter_chunk(): pl.pallas_call(functools.partial(filter_kernel, parts=parts, skip=skip, a...  12.5 us
    pallas_call x1, Pallas kernels, lay_refs(): pl.pallas_call(functools.partial(refs_kernel, padded=padded), grid=(rots,...  8.81 us
    ppermute x3, waiting for transfers between devices, local(): got = lax.ppermute(send, 'dom', [(i, i ^ 1) for i in range(dom)])  5.76 us
    pallas_call x3, Pallas kernels, sums(): pl.pallas_call(functools.partial(sums_kernel, dom=dom, start=start, class...  4.84 us
    ppermute x1, waiting for transfers between devices, local(): other_bins = over_cls(defocus_bin)  4.8 us
    ppermute x2, starting transfers between devices, local(): remote = [over_cls(images[a:a + n]) for a, n in zip(starts, sizes)]  4.61 us
  transfers between devices with their start and end apart: 22, of which 16 were waited for; matrix products, arithmetic and copies ran while one was open for 3% of the time, Pallas kernels for 24%

profile of v4, /device:TPU:0, one launch (start us, length us, event | category | flops | bytes accessed | tf_op | source)
XLA Modules:
  0.0 94.8 jit_solution(6663548050652739314)
XLA Ops:
  0.0 0.5 collective-permute-start.3
  0.5 1.3 %slice.19 = bf16[64,64,128]{2,1,0:T(8,128)(2,1)S(1)} slice(bf16[96,64,128]{2,1,0:T(8,128)(2,1)} %mine.1), slice={[0:64], [0:64], [0:128]} | slice | bytes 2097152 | tf_op jit(solution)/shard_map/slice | solution.py:425
  1.8 0.0 copy-start
  1.9 0.0 copy-start.1
  1.9 2.6 %collective-permute-start.2 = (bf16[64,64,128]{2,1,0:T(8,128)(2,1)S(1)}, bf16[64,64,128]{2,1,0:T(8,128)(2,1)S(1)}, u32[]{:S(2)}, u32[]{:S(2)}) collective-permute-start(bf16[64,64,128]{2,1,0:T(8,128)(2,1)S(1)} %slice.19), channel_id=1, source_target_pairs={{0,1},{1,0},{2,3},{3,2},{4,5},{5,4},{6,7},{7,6},{8,9},{9,8},{10,11... | collective-permute-start | bytes 3145736 | tf_op jit(solution)/shard_map/ppermute | solution.py:425
  4.5 0.1 collective-permute-start
  4.5 1.1 %slice.18 = bf16[32,64,128]{2,1,0:T(8,128)(2,1)S(1)} slice(bf16[96,64,128]{2,1,0:T(8,128)(2,1)} %mine.1), slice={[64:96], [0:64], [0:128]} | slice | bytes 1048576 | tf_op jit(solution)/shard_map/slice | solution.py:425
  5.6 2.0 %collective-permute-start.1 = (bf16[32,64,128]{2,1,0:T(8,128)(2,1)S(1)}, bf16[32,64,128]{2,1,0:T(8,128)(2,1)S(1)}, u32[]{:S(2)}, u32[]{:S(2)}) collective-permute-start(bf16[32,64,128]{2,1,0:T(8,128)(2,1)S(1)} %slice.18), channel_id=1, source_target_pairs={{0,1},{1,0},{2,3},{3,2},{4,5},{5,4},{6,7},{7,6},{8,9},{9,8},{10,11... | collective-permute-start | bytes 1572872 | tf_op jit(solution)/shard_map/ppermute | solution.py:425
  7.6 8.8 %refs.2 = (bf16[128,336,128]{2,1,0:T(8,128)(2,1)S(1)}, f32[336,128]{1,0:T(8,128)S(1)}) custom-call(bf16[100,3,128,128]{3,2,1,0:T(8,128)(2,1)} %refs.3), custom_call_target="tpu_custom_call" | custom-call | flops 900000000 | bytes 2700000 | tf_op jit(solution)/shard_map/refs/pallas_call | solution.py:165
  16.5 0.0 copy-done.3
  16.5 0.0 copy-done.2
  16.5 0.8 prepare.1
  17.3 0.0 collective-permute-done.3.rest_0_
  17.3 6.4 %filter.3 = (bf16[128,192,128]{2,1,0:T(8,128)(2,1)S(1)}, bf16[128,192,128]{2,1,0:T(8,128)(2,1)S(1)}, f32[8,128]{1,0:T(8,128)S(1)}) custom-call(s32[96]{0:T(128)S(1)} %copy-done.1, bf16[96,64,128]{2,1,0:T(8,128)(2,1)S(1)} %copy-done, bf16[16,128,128]{2,1,0:T(8,128)(2,1)S(1)} %get-tuple-element.41.left, bf16[16,128,128]{2,1,0:T(8,128)(2,1)S(1)} %get-tuple-element.42.right, ...), custom_call_target="tpu_custom_call" | custom-call | flops 960000000 | bytes 2880000 | tf_op jit(solution)/shard_map/filter/pallas_call | solution.py:217
  23.7 4.8 %collective-permute-done.refs_2_.bins = s32[96]{0:T(128)S(1)} collective-permute-done((s32[96]{0:T(128)}, s32[96]{0:T(128)S(1)}, u32[]{:S(2)}, u32[]{:S(2)}) %collective-permute-start) | collective-permute-done | bytes 416 | tf_op jit(solution)/shard_map/ppermute | solution.py:426
  28.5 0.0 collective-permute-done.2.refs_0_
  28.5 0.1 fusion
  28.6 0.1 collective-permute-start.4
  28.7 0.5 collective-permute-start.5
  29.2 0.1 collective-permute-start.6
  29.3 0.4 collective-permute-start.7
  29.7 0.5 collective-permute-done.4.rest_0_
  30.2 0.4 collective-permute-done.5.rest_1_
  30.6 0.4 collective-permute-done.6.rest_2_
  31.0 0.4 collective-permute-done.7.rest_3_
  31.3 3.6 %filter.4 = (bf16[128,192,128]{2,1,0:T(8,128)(2,1)S(1)}, bf16[128,192,128]{2,1,0:T(8,128)(2,1)S(1)}, f32[8,128]{1,0:T(8,128)S(1)}) custom-call(s32[96]{0:T(128)S(1)} %collective-permute-done.refs_2_.bins, bf16[64,64,128]{2,1,0:T(8,128)(2,1)S(1)} %gate.2.mine, ...), custom_call_target="tpu_custom_call", output_to_operand_aliasing={{0}: (8, {}), {1}: (9, {})} | custom-call | flops 640000000 | bytes 1920000 | tf_op jit(solution)/shard_map/filter/pallas_call | solution.py:217
  35.0 4.6 %collective-permute-done.1.refs_0_ = bf16[32,64,128]{2,1,0:T(8,128)(2,1)S(1)} collective-permute-done((bf16[32,64,128]{2,1,0:T(8,128)(2,1)S(1)}, bf16[32,64,128]{2,1,0:T(8,128)(2,1)S(1)}, u32[]{:S(2)}, u32[]{:S(2)}) %collective-permute-start.1) | collective-permute-done | bytes 524320 | tf_op jit(solution)/shard_map/ppermute | solution.py:425
  39.5 0.0 collective-permute-start.8
  39.5 1.9 %collective-permute-done.8.rest_0_ = bf16[32,64,128]{2,1,0:T(8,128)(2,1)S(1)} collective-permute-done((bf16[32,64,128]{2,1,0:T(8,128)(2,1)S(1)}, bf16[32,64,128]{2,1,0:T(8,128)(2,1)S(1)}, u32[]{:S(2)}, u32[]{:S(2)}) %collective-permute-start.8) | collective-permute-done | bytes 524320 | tf_op jit(solution)/shard_map/ppermute | solution.py:441
  41.4 2.5 %filter.5 = (bf16[128,192,128]{2,1,0:T(8,128)(2,1)S(1)}, bf16[128,192,128]{2,1,0:T(8,128)(2,1)S(1)}, f32[8,128]{1,0:T(8,128)}) custom-call(s32[96]{0:T(128)S(1)} %collective-permute-done.refs_2_.bins, bf16[32,64,128]{2,1,0:T(8,128)(2,1)S(1)} %gate.3.mine, ...), custom_call_target="tpu_custom_call", output_to_operand_aliasing={{0}: (5, {}), {1}: (6, {})} | custom-call | flops 320000000 | bytes 960000 | tf_op jit(solution)/shard_map/filter/pallas_call | solution.py:217
  44.0 4.6 %score.1 = (f32[336,192]{1,0:T(8,128)S(1)}, f32[8,192]{1,0:T(8,128)S(1)}) custom-call(bf16[128,192,128]{2,1,0:T(8,128)(2,1)S(1)} %get-tuple-element.49.plain, bf16[128,336,128]{2,1,0:T(8,128)(2,1)S(1)} %get-tuple-element.50.refs, f32[336,128]{1,0:T(8,128)S(1)} %get-tuple-element.40.after.norm, f32[112,192]{1,0:T(8,128)S(1)} %get-tuple-element.51.mask, ...), custom_call_target="tpu_custom_call" | custom-call | flops 500000000 | bytes 1500000 | tf_op jit(solution)/shard_map/score/pallas_call | solution.py:256
  48.5 1.8 %collective-permute-start.9 = (f32[8,192]{1,0:T(8,128)S(1)}, f32[8,192]{1,0:T(8,128)S(1)}, u32[]{:S(2)}, u32[]{:S(2)}) collective-permute-start(f32[8,192]{1,0:T(8,128)S(1)} %get-tuple-element.54.mine), channel_id=1, source_target_pairs={{0,1},{1,0},{2,3},{3,2},{4,5},{5,4},{6,7},{7,6},{8,9},{9,8},{10,11... | collective-permute-start | bytes 18440 | tf_op jit(solution)/shard_map/ppermute | solution.py:449
  50.4 1.9 %collective-permute-done.9.other = f32[8,192]{1,0:T(8,128)S(1)} collective-permute-done((f32[8,192]{1,0:T(8,128)S(1)}, f32[8,192]{1,0:T(8,128)S(1)}, u32[]{:S(2)}, u32[]{:S(2)}) %collective-permute-start.9) | collective-permute-done | bytes 6176 | tf_op jit(solution)/shard_map/ppermute | solution.py:449
  52.3 0.4 weights.1
  52.6 1.7 %sums.3 = (bf16[4,3,100,128]{3,2,1,0:T(8,128)(2,1)S(1)}, f32[4,3,100,128]{3,2,1,0:T(8,128)S(1)}) custom-call(bf16[2,112,384]{2,1,0:T(8,128)(2,1)S(1)} %weights.1, bf16[128,192,128]{2,1,0:T(8,128)(2,1)S(1)} %get-tuple-element.49.plain, bf16[128,192,128]{2,1,0:T(8,128)(2,1)S(1)} %get-tuple-element.56.turned), custom_call_target="tpu_custom_call" | custom-call | flops 240000000 | bytes 720000 | tf_op jit(solution)/shard_map/sums/pallas_call | solution.py:332
  54.3 1.8 %collective-permute-start.10 = (bf16[4,3,100,128]{3,2,1,0:T(8,128)(2,1)S(1)}, bf16[4,3,100,128]{3,2,1,0:T(8,128)(2,1)S(1)}, u32[]{:S(2)}, u32[]{:S(2)}) collective-permute-start(bf16[4,3,100,128]{3,2,1,0:T(8,128)(2,1)S(1)} %get-tuple-element.58.rest_0_), channel_id=1, source_target_pairs={{0,2},{2,0},{4,6},{6,4},{8,10},{10,8},{12,14},{14,12},{1,3},{3,1},... | collective-permute-start | bytes 921608 | tf_op jit(solution)/shard_map/ppermute | solution.py:458
  56.1 1.7 %sums.4 = (bf16[4,3,100,128]{3,2,1,0:T(8,128)(2,1)S(1)}, f32[4,3,100,128]{3,2,1,0:T(8,128)S(1)}) custom-call(bf16[2,112,384]{2,1,0:T(8,128)(2,1)S(1)} %weights.1, bf16[128,192,128]{2,1,0:T(8,128)(2,1)S(1)} %get-tuple-element.49.plain, bf16[128,192,128]{2,1,0:T(8,128)(2,1)S(1)} %get-tuple-element.56.turned, bf16[4,3,100,128]{3,2,1,0:T(8,128)(2,1)S(1)} %get-tuple-element.58.rest_0_), custom_call_target="tpu_custom_call" | custom-call | flops 240000000 | bytes 720000 | tf_op jit(solution)/shard_map/sums/pallas_call | solution.py:332
  57.8 0.4 collective-permute-start.14
  58.2 1.5 %sums.5 = (bf16[4,2,100,128]{3,2,1,0:T(8,128)(2,1)S(1)}, f32[4,2,100,128]{3,2,1,0:T(8,128)S(1)}) custom-call(bf16[2,112,384]{2,1,0:T(8,128)(2,1)S(1)} %weights.1, bf16[128,192,128]{2,1,0:T(8,128)(2,1)S(1)} %get-tuple-element.49.plain, bf16[128,192,128]{2,1,0:T(8,128)(2,1)S(1)} %get-tuple-element.56.turned, bf16[4,3,100,128]{3,2,1,0:T(8,128)(2,1)S(1)} %get-tuple-element.64.rest_0_), custom_call_target="tpu_custom_call" | custom-call | flops 160000000 | bytes 480000 | tf_op jit(solution)/shard_map/sums/pallas_call | solution.py:332
  59.7 1.8 %collective-permute-start.18 = (bf16[4,2,100,128]{3,2,1,0:T(8,128)(2,1)S(1)}, bf16[4,2,100,128]{3,2,1,0:T(8,128)(2,1)S(1)}, u32[]{:S(2)}, u32[]{:S(2)}) collective-permute-start(bf16[4,2,100,128]{3,2,1,0:T(8,128)(2,1)S(1)} %get-tuple-element.70), channel_id=1, source_target_pairs={{0,2},{2,0},{4,6},{6,4},{8,10},{10,8},{12,14},{14,12},{1,3},{3,1},... | collective-permute-start | bytes 614408 | tf_op jit(solution)/shard_map/ppermute | solution.py:458
  61.4 3.4 %collective-permute-done.10.got = bf16[4,3,100,128]{3,2,1,0:T(8,128)(2,1)S(1)} collective-permute-done((bf16[4,3,100,128]{3,2,1,0:T(8,128)(2,1)S(1)}, bf16[4,3,100,128]{3,2,1,0:T(8,128)(2,1)S(1)}, u32[]{:S(2)}, u32[]{:S(2)}) %collective-permute-start.10) | collective-permute-done | bytes 307232 | tf_op jit(solution)/shard_map/ppermute | solution.py:458
  64.9 0.1 fold.3
  64.9 1.9 %collective-permute-start.11 = (bf16[1,3,100,128]{3,2,1,0:T(8,128)(2,1)S(1)}, bf16[1,3,100,128]{3,2,1,0:T(8,128)(2,1)S(1)}, u32[]{:S(2)}, u32[]{:S(2)}) collective-permute-start(bf16[1,3,100,128]{3,2,1,0:T(8,128)(2,1)S(1)} %get-tuple-element.60), channel_id=1, source_target_pairs={{0,4},{2,6},{4,0},{6,2},{8,12},{10,14},{12,8},{14,10},{1,5},{3,7},... | collective-permute-start | bytes 230408 | tf_op jit(solution)/shard_map/ppermute | solution.py:466
  66.8 2.6 %collective-permute-start.12 = (bf16[1,3,100,128]{3,2,1,0:T(8,128)(2,1)S(1)}, bf16[1,3,100,128]{3,2,1,0:T(8,128)(2,1)S(1)}, u32[]{:S(2)}, u32[]{:S(2)}) collective-permute-start(bf16[1,3,100,128]{3,2,1,0:T(8,128)(2,1)S(1)} %get-tuple-element.61), channel_id=1, source_target_pairs={{0,8},{2,10},{4,12},{6,14},{8,0},{10,2},{12,4},{14,6},{1,9},{3,11}... | collective-permute-start | bytes 230408 | tf_op jit(solution)/shard_map/ppermute | solution.py:466
  69.4 0.0 collective-permute-start.13
  69.4 2.3 %collective-permute-done.14.got = bf16[4,3,100,128]{3,2,1,0:T(8,128)(2,1)S(1)} collective-permute-done((bf16[4,3,100,128]{3,2,1,0:T(8,128)(2,1)S(1)}, bf16[4,3,100,128]{3,2,1,0:T(8,128)(2,1)S(1)}, u32[]{:S(2)}, u32[]{:S(2)}) %collective-permute-start.14) | collective-permute-done | bytes 307232 | tf_op jit(solution)/shard_map/ppermute | solution.py:458
  71.7 0.0 collective-permute-done.11.outs_0_.args_1_
  71.7 1.3 %collective-permute-done.12.outs_1_.args_2_ = bf16[1,3,100,128]{3,2,1,0:T(8,128)(2,1)S(1)} collective-permute-done((bf16[1,3,100,128]{3,2,1,0:T(8,128)(2,1)S(1)}, bf16[1,3,100,128]{3,2,1,0:T(8,128)(2,1)S(1)}, u32[]{:S(2)}, u32[]{:S(2)}) %collective-permute-start.12) | collective-permute-done | bytes 76832 | tf_op jit(solution)/shard_map/ppermute | solution.py:466
  73.0 3.5 %collective-permute-done.13.outs_2_.args_3_ = bf16[1,3,100,128]{3,2,1,0:T(8,128)(2,1)S(1)} collective-permute-done((bf16[1,3,100,128]{3,2,1,0:T(8,128)(2,1)S(1)}, bf16[1,3,100,128]{3,2,1,0:T(8,128)(2,1)S(1)}, u32[]{:S(2)}, u32[]{:S(2)}) %collective-permute-start.13) | collective-permute-done | bytes 76832 | tf_op jit(solution)/shard_map/ppermute | solution.py:466
  76.5 0.1 fold.4
  76.6 0.1 collective-permute-start.15
  76.6 2.2 %collective-permute-start.16 = (bf16[1,3,100,128]{3,2,1,0:T(8,128)(2,1)S(1)}, bf16[1,3,100,128]{3,2,1,0:T(8,128)(2,1)S(1)}, u32[]{:S(2)}, u32[]{:S(2)}) collective-permute-start(bf16[1,3,100,128]{3,2,1,0:T(8,128)(2,1)S(1)} %get-tuple-element.67), channel_id=1, source_target_pairs={{0,8},{2,10},{4,12},{6,14},{8,0},{10,2},{12,4},{14,6},{1,9},{3,11}... | collective-permute-start | bytes 230408 | tf_op jit(solution)/shard_map/ppermute | solution.py:466
  78.8 2.2 %collective-permute-start.17 = (bf16[1,3,100,128]{3,2,1,0:T(8,128)(2,1)S(1)}, bf16[1,3,100,128]{3,2,1,0:T(8,128)(2,1)S(1)}, u32[]{:S(2)}, u32[]{:S(2)}) collective-permute-start(bf16[1,3,100,128]{3,2,1,0:T(8,128)(2,1)S(1)} %get-tuple-element.68), channel_id=1, source_target_pairs={{0,12},{2,14},{4,8},{6,10},{8,4},{10,6},{12,0},{14,2},{1,13},{3,15... | collective-permute-start | bytes 230408 | tf_op jit(solution)/shard_map/ppermute | solution.py:466
  81.0 0.0 collective-permute-done.18.got
  81.0 1.4 %collective-permute-done.15.outs_0_.args_5_ = bf16[1,3,100,128]{3,2,1,0:T(8,128)(2,1)S(1)} collective-permute-done((bf16[1,3,100,128]{3,2,1,0:T(8,128)(2,1)S(1)}, bf16[1,3,100,128]{3,2,1,0:T(8,128)(2,1)S(1)}, u32[]{:S(2)}, u32[]{:S(2)}) %collective-permute-start.15) | collective-permute-done | bytes 76832 | tf_op jit(solution)/shard_map/ppermute | solution.py:466
  82.5 0.0 collective-permute-done.16.outs_1_.args_6_
  82.5 3.0 %collective-permute-done.17.outs_2_.args_7_ = bf16[1,3,100,128]{3,2,1,0:T(8,128)(2,1)S(1)} collective-permute-done((bf16[1,3,100,128]{3,2,1,0:T(8,128)(2,1)S(1)}, bf16[1,3,100,128]{3,2,1,0:T(8,128)(2,1)S(1)}, u32[]{:S(2)}, u32[]{:S(2)}) %collective-permute-start.17) | collective-permute-done | bytes 76832 | tf_op jit(solution)/shard_map/ppermute | solution.py:466
  85.6 1.9 %collective-permute-start.19 = (bf16[1,2,100,128]{3,2,1,0:T(8,128)(2,1)S(1)}, bf16[1,2,100,128]{3,2,1,0:T(8,128)(2,1)S(1)}, u32[]{:S(2)}, u32[]{:S(2)}) collective-permute-start(bf16[1,2,100,128]{3,2,1,0:T(8,128)(2,1)S(1)} %get-tuple-element.72), channel_id=1, source_target_pairs={{0,4},{2,6},{4,0},{6,2},{8,12},{10,14},{12,8},{14,10},{1,5},{3,7},... | collective-permute-start | bytes 153608 | tf_op jit(solution)/shard_map/ppermute | solution.py:466
  87.5 0.5 collective-permute-start.20
  87.9 2.1 %collective-permute-start.21 = (bf16[1,2,100,128]{3,2,1,0:T(8,128)(2,1)S(1)}, bf16[1,2,100,128]{3,2,1,0:T(8,128)(2,1)S(1)}, u32[]{:S(2)}, u32[]{:S(2)}) collective-permute-start(bf16[1,2,100,128]{3,2,1,0:T(8,128)(2,1)S(1)} %get-tuple-element.74), channel_id=1, source_target_pairs={{0,12},{2,14},{4,8},{6,10},{8,4},{10,6},{12,0},{14,2},{1,13},{3,15... | collective-permute-start | bytes 153608 | tf_op jit(solution)/shard_map/ppermute | solution.py:466
  90.0 0.0 collective-permute-done.19.args_9_
  90.0 2.7 %collective-permute-done.20.args_10_ = bf16[1,2,100,128]{3,2,1,0:T(8,128)(2,1)S(1)} collective-permute-done((bf16[1,2,100,128]{3,2,1,0:T(8,128)(2,1)S(1)}, bf16[1,2,100,128]{3,2,1,0:T(8,128)(2,1)S(1)}, u32[]{:S(2)}, u32[]{:S(2)}) %collective-permute-start.20) | collective-permute-done | bytes 51232 | tf_op jit(solution)/shard_map/ppermute | solution.py:466
  92.7 1.2 %collective-permute-done.21.args_11_ = bf16[1,2,100,128]{3,2,1,0:T(8,128)(2,1)S(1)} collective-permute-done((bf16[1,2,100,128]{3,2,1,0:T(8,128)(2,1)S(1)}, bf16[1,2,100,128]{3,2,1,0:T(8,128)(2,1)S(1)}, u32[]{:S(2)}, u32[]{:S(2)}) %collective-permute-start.21) | collective-permute-done | bytes 51232 | tf_op jit(solution)/shard_map/ppermute | solution.py:466
  93.9 0.9 finish.1
  (13 shorter events, 0.1 us)
Async XLA Ops:
  0.0 16.5 %copy-start.6 = (f32[128]{0:T(128)S(1)}, f32[128]{0:T(128)}, u32[]{:S(2)}) copy-start(f32[128]{0:T(128)} %param.11) | copy-start | bytes 1540
  0.0 16.5 %copy-start.5 = (f32[192]{0:T(256)S(1)}, f32[192]{0:T(256)}, u32[]{:S(2)}) copy-start(f32[192]{0:T(256)} %param.15) | copy-start | bytes 2308
  0.0 16.5 %copy-start.4 = (s32[100,3]{0,1:T(4,128)S(1)}, s32[100,3]{0,1:T(4,128)}, u32[]{:S(2)}) copy-start(s32[100,3]{0,1:T(4,128)} %param.13) | copy-start | bytes 3604
  0.0 16.5 %copy-start.3 = (f32[16,128]{1,0:T(8,128)S(1)}, f32[16,128]{1,0:T(8,128)}, u32[]{:S(2)}) copy-start(f32[16,128]{1,0:T(8,128)} %ctf.1) | copy-start | bytes 24580
  0.0 16.5 %copy-start.2 = (s32[192,100]{1,0:T(8,128)S(1)}, s32[192,100]{1,0:T(8,128)}, u32[]{:S(2)}) copy-start(s32[192,100]{1,0:T(8,128)} %mask.1) | copy-start | bytes 230404
  0.0 17.3 %collective-permute-start.3 = (bf16[96,64,128]{2,1,0:T(8,128)(2,1)}, bf16[96,64,128]{2,1,0:T(8,128)(2,1)S(1)}, u32[]{:S(2)}, u32[]{:S(2)}) collective-permute-start(bf16[96,64,128]{2,1,0:T(8,128)(2,1)} %mine.1), channel_id=1, source_target_pairs={{0,16},{16,0},{1,17},{17,1},{2,18},{18,2},{3,19},{19,3},{4,20},{20... | collective-permute-start | bytes 4718600 | tf_op jit(solution)/shard_map/ppermute | solution.py:427
  1.8 15.5 %copy-start = (bf16[96,64,128]{2,1,0:T(8,128)(2,1)S(1)}, bf16[96,64,128]{2,1,0:T(8,128)(2,1)}, u32[]{:S(2)}) copy-start(bf16[96,64,128]{2,1,0:T(8,128)(2,1)} %mine.1) | copy-start | bytes 4718596
  1.9 15.5 %copy-start.1 = (s32[96]{0:T(128)S(1)}, s32[96]{0:T(128)}, u32[]{:S(2)}) copy-start(s32[96]{0:T(128)} %bins.1) | copy-start | bytes 1156
  1.9 26.7 %collective-permute-start.2 = (bf16[64,64,128]{2,1,0:T(8,128)(2,1)S(1)}, bf16[64,64,128]{2,1,0:T(8,128)(2,1)S(1)}, u32[]{:S(2)}, u32[]{:S(2)}) collective-permute-start(bf16[64,64,128]{2,1,0:T(8,128)(2,1)S(1)} %slice.19), channel_id=1, source_target_pairs={{0,1},{1,0},{2,3},{3,2},{4,5},{5,4},{6,7},{7,6},{8,9},{9,8},{10,11... | collective-permute-start | bytes 3145736 | tf_op jit(solution)/shard_map/ppermute | solution.py:425
  4.5 24.1 %collective-permute-start = (s32[96]{0:T(128)}, s32[96]{0:T(128)S(1)}, u32[]{:S(2)}, u32[]{:S(2)}) collective-permute-start(s32[96]{0:T(128)} %bins.1), channel_id=1, source_target_pairs={{0,1},{1,0},{2,3},{3,2},{4,5},{5,4},{6,7},{7,6},{8,9},{9,8},{10,11... | collective-permute-start | bytes 1160 | tf_op jit(solution)/shard_map/ppermute | solution.py:426
  5.6 33.9 %collective-permute-start.1 = (bf16[32,64,128]{2,1,0:T(8,128)(2,1)S(1)}, bf16[32,64,128]{2,1,0:T(8,128)(2,1)S(1)}, u32[]{:S(2)}, u32[]{:S(2)}) collective-permute-start(bf16[32,64,128]{2,1,0:T(8,128)(2,1)S(1)} %slice.18), channel_id=1, source_target_pairs={{0,1},{1,0},{2,3},{3,2},{4,5},{5,4},{6,7},{7,6},{8,9},{9,8},{10,11... | collective-permute-start | bytes 1572872 | tf_op jit(solution)/shard_map/ppermute | solution.py:425
  28.6 1.6 %collective-permute-start.4 = (bf16[16,64,128]{2,1,0:T(8,128)(2,1)S(1)}, bf16[16,64,128]{2,1,0:T(8,128)(2,1)S(1)}, u32[]{:S(2)}, u32[]{:S(2)}) collective-permute-start(bf16[16,64,128]{2,1,0:T(8,128)(2,1)S(1)} %get-tuple-element.78), channel_id=1, source_target_pairs={{0,16},{16,0},{1,17},{17,1},{2,18},{18,2},{3,19},{19,3},{4,20},{20... | collective-permute-start | bytes 786440 | tf_op jit(solution)/shard_map/ppermute | solution.py:441
  28.7 1.9 %collective-permute-start.5 = (bf16[16,64,128]{2,1,0:T(8,128)(2,1)S(1)}, bf16[16,64,128]{2,1,0:T(8,128)(2,1)S(1)}, u32[]{:S(2)}, u32[]{:S(2)}) collective-permute-start(bf16[16,64,128]{2,1,0:T(8,128)(2,1)S(1)} %get-tuple-element.77), channel_id=1, source_target_pairs={{0,16},{16,0},{1,17},{17,1},{2,18},{18,2},{3,19},{19,3},{4,20},{20... | collective-permute-start | bytes 786440 | tf_op jit(solution)/shard_map/ppermute | solution.py:441
  29.2 1.8 %collective-permute-start.6 = (bf16[16,64,128]{2,1,0:T(8,128)(2,1)S(1)}, bf16[16,64,128]{2,1,0:T(8,128)(2,1)S(1)}, u32[]{:S(2)}, u32[]{:S(2)}) collective-permute-start(bf16[16,64,128]{2,1,0:T(8,128)(2,1)S(1)} %get-tuple-element.76), channel_id=1, source_target_pairs={{0,16},{16,0},{1,17},{17,1},{2,18},{18,2},{3,19},{19,3},{4,20},{20... | collective-permute-start | bytes 786440 | tf_op jit(solution)/shard_map/ppermute | solution.py:441
  29.3 2.1 %collective-permute-start.7 = (bf16[16,64,128]{2,1,0:T(8,128)(2,1)S(1)}, bf16[16,64,128]{2,1,0:T(8,128)(2,1)S(1)}, u32[]{:S(2)}, u32[]{:S(2)}) collective-permute-start(bf16[16,64,128]{2,1,0:T(8,128)(2,1)S(1)} %get-tuple-element.75), channel_id=1, source_target_pairs={{0,16},{16,0},{1,17},{17,1},{2,18},{18,2},{3,19},{19,3},{4,20},{20... | collective-permute-start | bytes 786440 | tf_op jit(solution)/shard_map/ppermute | solution.py:441
  39.5 1.9 %collective-permute-start.8 = (bf16[32,64,128]{2,1,0:T(8,128)(2,1)S(1)}, bf16[32,64,128]{2,1,0:T(8,128)(2,1)S(1)}, u32[]{:S(2)}, u32[]{:S(2)}) collective-permute-start(bf16[32,64,128]{2,1,0:T(8,128)(2,1)S(1)} %gate.3.mine), channel_id=1, source_target_pairs={{0,16},{16,0},{1,17},{17,1},{2,18},{18,2},{3,19},{19,3},{4,20},{20... | collective-permute-start | bytes 1572872 | tf_op jit(solution)/shard_map/ppermute | solution.py:441
  48.5 3.7 %collective-permute-start.9 = (f32[8,192]{1,0:T(8,128)S(1)}, f32[8,192]{1,0:T(8,128)S(1)}, u32[]{:S(2)}, u32[]{:S(2)}) collective-permute-start(f32[8,192]{1,0:T(8,128)S(1)} %get-tuple-element.54.mine), channel_id=1, source_target_pairs={{0,1},{1,0},{2,3},{3,2},{4,5},{5,4},{6,7},{7,6},{8,9},{9,8},{10,11... | collective-permute-start | bytes 18440 | tf_op jit(solution)/shard_map/ppermute | solution.py:449
  54.3 10.5 %collective-permute-start.10 = (bf16[4,3,100,128]{3,2,1,0:T(8,128)(2,1)S(1)}, bf16[4,3,100,128]{3,2,1,0:T(8,128)(2,1)S(1)}, u32[]{:S(2)}, u32[]{:S(2)}) collective-permute-start(bf16[4,3,100,128]{3,2,1,0:T(8,128)(2,1)S(1)} %get-tuple-element.58.rest_0_), channel_id=1, source_target_pairs={{0,2},{2,0},{4,6},{6,4},{8,10},{10,8},{12,14},{14,12},{1,3},{3,1},... | collective-permute-start | bytes 921608 | tf_op jit(solution)/shard_map/ppermute | solution.py:458
  57.8 13.9 %collective-permute-start.14 = (bf16[4,3,100,128]{3,2,1,0:T(8,128)(2,1)S(1)}, bf16[4,3,100,128]{3,2,1,0:T(8,128)(2,1)S(1)}, u32[]{:S(2)}, u32[]{:S(2)}) collective-permute-start(bf16[4,3,100,128]{3,2,1,0:T(8,128)(2,1)S(1)} %get-tuple-element.64.rest_0_), channel_id=1, source_target_pairs={{0,2},{2,0},{4,6},{6,4},{8,10},{10,8},{12,14},{14,12},{1,3},{3,1},... | collective-permute-start | bytes 921608 | tf_op jit(solution)/shard_map/ppermute | solution.py:458
  59.7 21.4 %collective-permute-start.18 = (bf16[4,2,100,128]{3,2,1,0:T(8,128)(2,1)S(1)}, bf16[4,2,100,128]{3,2,1,0:T(8,128)(2,1)S(1)}, u32[]{:S(2)}, u32[]{:S(2)}) collective-permute-start(bf16[4,2,100,128]{3,2,1,0:T(8,128)(2,1)S(1)} %get-tuple-element.70), channel_id=1, source_target_pairs={{0,2},{2,0},{4,6},{6,4},{8,10},{10,8},{12,14},{14,12},{1,3},{3,1},... | collective-permute-start | bytes 614408 | tf_op jit(solution)/shard_map/ppermute | solution.py:458
  64.9 6.8 %collective-permute-start.11 = (bf16[1,3,100,128]{3,2,1,0:T(8,128)(2,1)S(1)}, bf16[1,3,100,128]{3,2,1,0:T(8,128)(2,1)S(1)}, u32[]{:S(2)}, u32[]{:S(2)}) collective-permute-start(bf16[1,3,100,128]{3,2,1,0:T(8,128)(2,1)S(1)} %get-tuple-element.60), channel_id=1, source_target_pairs={{0,4},{2,6},{4,0},{6,2},{8,12},{10,14},{12,8},{14,10},{1,5},{3,7},... | collective-permute-start | bytes 230408 | tf_op jit(solution)/shard_map/ppermute | solution.py:466
  66.8 6.2 %collective-permute-start.12 = (bf16[1,3,100,128]{3,2,1,0:T(8,128)(2,1)S(1)}, bf16[1,3,100,128]{3,2,1,0:T(8,128)(2,1)S(1)}, u32[]{:S(2)}, u32[]{:S(2)}) collective-permute-start(bf16[1,3,100,128]{3,2,1,0:T(8,128)(2,1)S(1)} %get-tuple-element.61), channel_id=1, source_target_pairs={{0,8},{2,10},{4,12},{6,14},{8,0},{10,2},{12,4},{14,6},{1,9},{3,11}... | collective-permute-start | bytes 230408 | tf_op jit(solution)/shard_map/ppermute | solution.py:466
  69.4 7.1 %collective-permute-start.13 = (bf16[1,3,100,128]{3,2,1,0:T(8,128)(2,1)S(1)}, bf16[1,3,100,128]{3,2,1,0:T(8,128)(2,1)S(1)}, u32[]{:S(2)}, u32[]{:S(2)}) collective-permute-start(bf16[1,3,100,128]{3,2,1,0:T(8,128)(2,1)S(1)} %get-tuple-element.62), channel_id=1, source_target_pairs={{0,12},{2,14},{4,8},{6,10},{8,4},{10,6},{12,0},{14,2},{1,13},{3,15... | collective-permute-start | bytes 230408 | tf_op jit(solution)/shard_map/ppermute | solution.py:466
  76.6 5.9 %collective-permute-start.15 = (bf16[1,3,100,128]{3,2,1,0:T(8,128)(2,1)S(1)}, bf16[1,3,100,128]{3,2,1,0:T(8,128)(2,1)S(1)}, u32[]{:S(2)}, u32[]{:S(2)}) collective-permute-start(bf16[1,3,100,128]{3,2,1,0:T(8,128)(2,1)S(1)} %get-tuple-element.66), channel_id=1, source_target_pairs={{0,4},{2,6},{4,0},{6,2},{8,12},{10,14},{12,8},{14,10},{1,5},{3,7},... | collective-permute-start | bytes 230408 | tf_op jit(solution)/shard_map/ppermute | solution.py:466
  76.6 5.8 %collective-permute-start.16 = (bf16[1,3,100,128]{3,2,1,0:T(8,128)(2,1)S(1)}, bf16[1,3,100,128]{3,2,1,0:T(8,128)(2,1)S(1)}, u32[]{:S(2)}, u32[]{:S(2)}) collective-permute-start(bf16[1,3,100,128]{3,2,1,0:T(8,128)(2,1)S(1)} %get-tuple-element.67), channel_id=1, source_target_pairs={{0,8},{2,10},{4,12},{6,14},{8,0},{10,2},{12,4},{14,6},{1,9},{3,11}... | collective-permute-start | bytes 230408 | tf_op jit(solution)/shard_map/ppermute | solution.py:466
  78.8 6.7 %collective-permute-start.17 = (bf16[1,3,100,128]{3,2,1,0:T(8,128)(2,1)S(1)}, bf16[1,3,100,128]{3,2,1,0:T(8,128)(2,1)S(1)}, u32[]{:S(2)}, u32[]{:S(2)}) collective-permute-start(bf16[1,3,100,128]{3,2,1,0:T(8,128)(2,1)S(1)} %get-tuple-element.68), channel_id=1, source_target_pairs={{0,12},{2,14},{4,8},{6,10},{8,4},{10,6},{12,0},{14,2},{1,13},{3,15... | collective-permute-start | bytes 230408 | tf_op jit(solution)/shard_map/ppermute | solution.py:466
  85.6 4.5 %collective-permute-start.19 = (bf16[1,2,100,128]{3,2,1,0:T(8,128)(2,1)S(1)}, bf16[1,2,100,128]{3,2,1,0:T(8,128)(2,1)S(1)}, u32[]{:S(2)}, u32[]{:S(2)}) collective-permute-start(bf16[1,2,100,128]{3,2,1,0:T(8,128)(2,1)S(1)} %get-tuple-element.72), channel_id=1, source_target_pairs={{0,4},{2,6},{4,0},{6,2},{8,12},{10,14},{12,8},{14,10},{1,5},{3,7},... | collective-permute-start | bytes 153608 | tf_op jit(solution)/shard_map/ppermute | solution.py:466
  87.5 5.2 %collective-permute-start.20 = (bf16[1,2,100,128]{3,2,1,0:T(8,128)(2,1)S(1)}, bf16[1,2,100,128]{3,2,1,0:T(8,128)(2,1)S(1)}, u32[]{:S(2)}, u32[]{:S(2)}) collective-permute-start(bf16[1,2,100,128]{3,2,1,0:T(8,128)(2,1)S(1)} %get-tuple-element.73), channel_id=1, source_target_pairs={{0,8},{2,10},{4,12},{6,14},{8,0},{10,2},{12,4},{14,6},{1,9},{3,11}... | collective-permute-start | bytes 153608 | tf_op jit(solution)/shard_map/ppermute | solution.py:466
  87.9 6.0 %collective-permute-start.21 = (bf16[1,2,100,128]{3,2,1,0:T(8,128)(2,1)S(1)}, bf16[1,2,100,128]{3,2,1,0:T(8,128)(2,1)S(1)}, u32[]{:S(2)}, u32[]{:S(2)}) collective-permute-start(bf16[1,2,100,128]{3,2,1,0:T(8,128)(2,1)S(1)} %get-tuple-element.74), channel_id=1, source_target_pairs={{0,12},{2,14},{4,8},{6,10},{8,4},{10,6},{12,0},{14,2},{1,13},{3,15... | collective-permute-start | bytes 153608 | tf_op jit(solution)/shard_map/ppermute | solution.py:466

commit v5 on v4

--- a/solution.py
+++ b/solution.py
@@ -294,52 +294,91 @@
     )(held(scaled), held(mine), other, held(rot))
 
 
-def sums_kernel(weights, plain, turned, *rest, dom, start, classes):
-    send, keep = rest[-2:]
-    _, rows, _, width = send.shape
+def sums_kernel(weights, plain, turned, *rest, outer, dom, start, rows, classes):
+    outs = rest[-(dom // 2 if outer else 2) :]
+    width = outs[0].shape[2]
     height = plain.shape[0]
     block = height // 2 // dom
     first = lax.axis_index("section") * (height // 2) + start
-    parity = lax.axis_index("dom") % 2
+    own = lax.axis_index("dom")
+    parity = own % 2
     straight = weights[0]
     mirrored = weights[1]
     flip = width - 1 - lax.broadcasted_iota(jnp.int32, (straight.shape[0], width), 1)
 
-    @pl.loop(0, dom // 2)
-    def _(g):
-        for r in range(rows):
-            both = [first + (2 * g + side) * block + r for side in (1 - parity, parity)]
-            direct = jnp.concatenate(
-                [jnp.concatenate([plain[i], turned[height - 1 - i]], axis=0) for i in both], axis=1
-            )
-            mirror = jnp.concatenate(
-                [jnp.concatenate([plain[height - 1 - i], turned[i]], axis=0) for i in both], axis=1
-            )
-            direct = nn(straight, direct)
-            mirror = nn(mirrored, mirror)
-            away, here = [
+    def pair(g, sides, r):
+        both = [first + (2 * g + side) * block + r for side in sides]
+        direct = jnp.concatenate(
+            [jnp.concatenate([plain[i], turned[height - 1 - i]], axis=0) for i in both], axis=1
+        )
+        mirror = jnp.concatenate(
+            [jnp.concatenate([plain[height - 1 - i], turned[i]], axis=0) for i in both], axis=1
+        )
+        direct = nn(straight, direct)
+        mirror = nn(mirrored, mirror)
+        return [
+            (
                 direct[:, at : at + width]
                 + jnp.take_along_axis(mirror[:, at : at + width], flip, axis=1)
-                for at in (0, width)
-            ]
-            send[g, r] = away[:classes].astype(BF16)
-            keep[g, r] = here[:classes]
-
-
-def sums(weights, plain, turned, after, dom, start, rows, classes):
+            )[:classes]
+            for at in (0, width)
+        ]
+
+    if outer:
+        for m, out in enumerate(outs):
+            for r in range(rows):
+                for side, value in enumerate(pair(jnp.bitwise_xor(own // 2, m), (0, 1), r)):
+                    out[side, r * classes : (r + 1) * classes] = value.astype(out.dtype)
+    else:
+        keep, send = outs
+
+        @pl.loop(0, dom // 2)
+        def _(g):
+            for r in range(rows):
+                away, here = pair(g, (1 - parity, parity), r)
+                at = slice(r * classes, (r + 1) * classes)
+                send[g, at] = away.astype(BF16)
+                keep[g, at] = here
+
+
+def sums(weights, plain, turned, after, outer, dom, start, rows, classes):
     width = plain.shape[2]
     vmem = pl.BlockSpec(memory_space=pltpu.VMEM)
-    return pl.pallas_call(
-        functools.partial(sums_kernel, dom=dom, start=start, classes=classes),
+    count = 2 if outer else dom // 2
+    shape = (count, rows * classes, width)
+    return pl.pallas_call(
+        functools.partial(
+            sums_kernel, outer=outer, dom=dom, start=start, rows=rows, classes=classes
+        ),
         in_specs=[vmem] * 3 + [pl.BlockSpec(memory_space=pl.ANY)] * len(after),
-        out_shape=(
-            jax.ShapeDtypeStruct((dom // 2, rows, classes, width), BF16),
-            pinned((dom // 2, rows, classes, width), F32),
-        ),
+        out_shape=(pinned(shape, F32),)
+        + (pltpu.HBM(shape, BF16),) * (dom // 2 - 1 if outer else 1),
         compiler_params=pltpu.CompilerParams(vmem_limit_bytes=8 * MIB),
         cost_estimate=cost(SUMS * rows),
         name="sums",
     )(held(weights), held(plain), held(turned), *after)
+
+
+def gather_kernel(keep, *rest, came):
+    got = rest[:came]
+    here, away = rest[-2:]
+    parity = lax.axis_index("dom") % 2
+    for out, side in ((here, parity), (away, 1 - parity)):
+        value = keep[side]
+        for other in got:
+            value = value + other[side].astype(F32)
+        out[0] = value.astype(out.dtype)
+
+
+def gather(keep, got):
+    shape = (1,) + keep.shape[1:]
+    return pl.pallas_call(
+        functools.partial(gather_kernel, came=len(got)),
+        out_shape=(pinned(shape, F32), jax.ShapeDtypeStruct(shape, BF16)),
+        compiler_params=pltpu.CompilerParams(vmem_limit_bytes=8 * MIB),
+        cost_estimate=cost(FOLD),
+        name="gather",
+    )(held(keep), *got)
 
 
 def fold_kernel(keep, got, *outs, fan, bit):
@@ -366,29 +405,29 @@
     )(held(keep), got, *after)
 
 
-def finish_kernel(*args, counts):
+def finish_kernel(*args, counts, classes):
     out = args[-1]
     block_rows = sum(rows for rows, _ in counts)
-    classes = args[0].shape[2]
     at = 0
     row = 0
     for rows, pieces in counts:
         for r in range(rows):
-            value = args[at][0, r]
+            cut = slice(r * classes, (r + 1) * classes)
+            value = args[at][0, cut]
             for other in args[at + 1 : at + pieces]:
-                value = value + other[0, r].astype(F32)
+                value = value + other[0, cut].astype(F32)
             out[pl.ds(row, classes, stride=block_rows)] = value
             row += 1
         at += pieces
 
 
-def finish(done):
-    counts = tuple((pieces[0].shape[1], len(pieces)) for pieces in done)
-    _, _, classes, width = done[0][0].shape
+def finish(done, classes):
+    counts = tuple((pieces[0].shape[1] // classes, len(pieces)) for pieces in done)
+    width = done[0][0].shape[2]
     block_rows = sum(rows for rows, _ in counts)
     flat = [held(p) if i == 0 else p for pieces in done for i, p in enumerate(pieces)]
     out = pl.pallas_call(
-        functools.partial(finish_kernel, counts=counts),
+        functools.partial(finish_kernel, counts=counts, classes=classes),
         out_shape=jax.ShapeDtypeStruct((classes * block_rows, width), F32),
         compiler_params=pltpu.CompilerParams(vmem_limit_bytes=8 * MIB),
         cost_estimate=cost(1),
@@ -402,11 +441,11 @@
     return (particles - last, last)
 
 
-def row_pieces(rows):
-    if rows < 4:
-        return (rows,)
-    part = -(-rows // 3)
-    return (part, part, rows - 2 * part)
+def row_pieces(rows, dom):
+    if rows < 4 or dom > 8:
+        return (rows, 0)
+    outer = rows * 3 // 8
+    return (rows - outer, outer)
 
 
 def local(
@@ -448,26 +487,28 @@
     scaled, stats = score(plain, refs, norm, mask, noise)
     weights = make_weights(scaled, stats, over_cls(stats), rot)
 
-    start = 0
-    done = []
-    summed, folded = (), ()
-    for rows in row_pieces(half // dom):
-        send, keep = sums(weights, plain, turned, summed, dom, start, rows, classes)
-        summed = (send,)
-        start += rows
-        got = lax.ppermute(send, "dom", [(i, i ^ 1) for i in range(dom)])
-        bit = 1
-        while keep.shape[0] > 4:
-            keep, send = fold(keep, got, folded, 2, bit)
-            got = lax.ppermute(send, "dom", [(i, i ^ (1 << bit)) for i in range(dom)])
-            bit += 1
-        keep, *sends = fold(keep, got, folded, keep.shape[0], bit)
-        folded = tuple(
-            lax.ppermute(s, "dom", [(i, i ^ ((m + 1) << bit)) for i in range(dom)])
-            for m, s in enumerate(sends)
+    def along(x, mask):
+        return lax.ppermute(x, "dom", [(i, i ^ mask) for i in range(dom)])
+
+    inner, outer = row_pieces(half // dom, dom)
+    keep, send = sums(weights, plain, turned, (), False, dom, 0, inner, classes)
+    got = along(send, 1)
+    if outer:
+        keep_b, *sends_b = sums(
+            weights, plain, turned, (send,), True, dom, inner, outer, classes
         )
-        done.append((keep,) + folded)
-    return finish(done)
+        got_b = [along(s, (m + 1) << 1) for m, s in enumerate(sends_b)]
+    bit = 1
+    while keep.shape[0] > 4:
+        keep, send = fold(keep, got, (), 2, bit)
+        got = along(send, 1 << bit)
+        bit += 1
+    keep, *sends = fold(keep, got, (), keep.shape[0], bit)
+    done = [[keep] + [along(s, (m + 1) << bit) for m, s in enumerate(sends)]]
+    if outer:
+        keep_b, send_b = gather(keep_b, got_b)
+        done.append([keep_b, along(send_b, 1)])
+    return finish(done, classes)
 
 
 def solution(mesh):

time: 95 us -> 88 us (0.926)
  starting transfers between devices: 25.4 us -> 19 us
  waiting for transfers between devices: 33.7 us -> 32.1 us
  local copies, waits for them, and re-layouts: 2.47 us -> 3.55 us
    ppermute x12 -> x8, starting transfers between devices: 17.3 us -> 10.9 us  [along(): return lax.ppermute(x, 'dom', [(i, i ^ mask) for i in range(dom)])]
    ppermute x12 -> x8, waiting for transfers between devices: 18.9 us -> 17.3 us  [along(): return lax.ppermute(x, 'dom', [(i, i ^ mask) for i in range(dom)])]
    unnamed x14 -> x16, local copies, waits for them, and re-layouts: 0.03 us -> 1.1 us
  transfers between devices with their start and end apart: 22 -> 18, of which waited for: 16 -> 12; matrix products, arithmetic and copies ran while one was open for 3% -> 3% of each run, Pallas kernels for 24% -> 25%
where the time goes in v5:
time: 88 us; the launch traced here: 87.8 us
  Pallas kernels  32.9 us (37%)
  waiting for transfers between devices  32.1 us (36%)
  starting transfers between devices  19 us (22%)
  local copies, waits for them, and re-layouts  3.55 us (4%)
    ppermute x8, waiting for transfers between devices, along(): return lax.ppermute(x, 'dom', [(i, i ^ mask) for i in range(dom)])  17.3 us
    pallas_call x3, Pallas kernels, filter_chunk(): pl.pallas_call(functools.partial(filter_kernel, parts=parts, skip=skip, a...  12.5 us
    ppermute x8, starting transfers between devices, along(): return lax.ppermute(x, 'dom', [(i, i ^ mask) for i in range(dom)])  10.9 us
    pallas_call x1, Pallas kernels, lay_refs(): pl.pallas_call(functools.partial(refs_kernel, padded=padded), grid=(rots,...  8.81 us
    ppermute x1, waiting for transfers between devices, local(): other_bins = over_cls(defocus_bin)  4.8 us
    pallas_call x2, Pallas kernels, sums(): pl.pallas_call(functools.partial(sums_kernel, outer=outer, dom=dom, start...  4.73 us
    ppermute x2, starting transfers between devices, local(): remote = [over_cls(images[a:a + n]) for a, n in zip(starts, sizes)]  4.61 us
    pallas_call x1, Pallas kernels, score(): pl.pallas_call(score_kernel, out_shape=(pinned((height, count), F32), pin...  4.6 us
  transfers between devices with their start and end apart: 18, of which 12 were waited for; matrix products, arithmetic and copies ran while one was open for 3% of the time, Pallas kernels for 25%

profile of v5, /device:TPU:0, one launch (start us, length us, event | category | flops | bytes accessed | tf_op | source)
XLA Modules:
  0.0 87.8 jit_solution(673495201797732709)
XLA Ops:
  0.0 0.0 copy-start.7
  0.0 0.0 copy-start.6
  0.0 0.0 copy-start.5
  0.0 0.5 collective-permute-start.3
  0.5 1.3 %slice.19 = bf16[64,64,128]{2,1,0:T(8,128)(2,1)S(1)} slice(bf16[96,64,128]{2,1,0:T(8,128)(2,1)} %mine.1), slice={[0:64], [0:64], [0:128]} | slice | bytes 2097152 | tf_op jit(solution)/shard_map/slice | solution.py:464
  1.8 0.0 copy-start
  1.9 0.0 copy-start.2
  1.9 2.6 %collective-permute-start.2 = (bf16[64,64,128]{2,1,0:T(8,128)(2,1)S(1)}, bf16[64,64,128]{2,1,0:T(8,128)(2,1)S(1)}, u32[]{:S(2)}, u32[]{:S(2)}) collective-permute-start(bf16[64,64,128]{2,1,0:T(8,128)(2,1)S(1)} %slice.19), channel_id=1, source_target_pairs={{0,1},{1,0},{2,3},{3,2},{4,5},{5,4},{6,7},{7,6},{8,9},{9,8},{10,11... | collective-permute-start | bytes 3145736 | tf_op jit(solution)/shard_map/ppermute | solution.py:464
  4.5 0.1 collective-permute-start
  4.5 1.1 %slice.18 = bf16[32,64,128]{2,1,0:T(8,128)(2,1)S(1)} slice(bf16[96,64,128]{2,1,0:T(8,128)(2,1)} %mine.1), slice={[64:96], [0:64], [0:128]} | slice | bytes 1048576 | tf_op jit(solution)/shard_map/slice | solution.py:464
  5.6 2.0 %collective-permute-start.1 = (bf16[32,64,128]{2,1,0:T(8,128)(2,1)S(1)}, bf16[32,64,128]{2,1,0:T(8,128)(2,1)S(1)}, u32[]{:S(2)}, u32[]{:S(2)}) collective-permute-start(bf16[32,64,128]{2,1,0:T(8,128)(2,1)S(1)} %slice.18), channel_id=1, source_target_pairs={{0,1},{1,0},{2,3},{3,2},{4,5},{5,4},{6,7},{7,6},{8,9},{9,8},{10,11... | collective-permute-start | bytes 1572872 | tf_op jit(solution)/shard_map/ppermute | solution.py:464
  7.6 8.8 %refs.2 = (bf16[128,336,128]{2,1,0:T(8,128)(2,1)S(1)}, f32[336,128]{1,0:T(8,128)S(1)}) custom-call(bf16[100,3,128,128]{3,2,1,0:T(8,128)(2,1)} %refs.3), custom_call_target="tpu_custom_call" | custom-call | flops 900000000 | bytes 2700000 | tf_op jit(solution)/shard_map/refs/pallas_call | solution.py:165
  16.4 0.0 copy-done.7
  16.5 0.0 copy-done.6
  16.5 0.0 copy-done.5
  16.5 0.0 copy-done.4
  16.5 0.0 copy-done.3
  16.5 0.8 prepare.1
  17.3 0.0 collective-permute-done.3.rest_0_
  17.3 0.0 copy-done
  17.3 0.0 copy-done.2
  17.3 6.4 %filter.3 = (bf16[128,192,128]{2,1,0:T(8,128)(2,1)S(1)}, bf16[128,192,128]{2,1,0:T(8,128)(2,1)S(1)}, f32[8,128]{1,0:T(8,128)S(1)}) custom-call(s32[96]{0:T(128)S(1)} %copy-done.2, bf16[96,64,128]{2,1,0:T(8,128)(2,1)S(1)} %copy-done, bf16[16,128,128]{2,1,0:T(8,128)(2,1)S(1)} %get-tuple-element.35.left, bf16[16,128,128]{2,1,0:T(8,128)(2,1)S(1)} %get-tuple-element.36.right, ...), custom_call_target="tpu_custom_call" | custom-call | flops 960000000 | bytes 2880000 | tf_op jit(solution)/shard_map/filter/pallas_call | solution.py:217
  23.7 4.8 %collective-permute-done.refs_2_.bins = s32[96]{0:T(128)S(1)} collective-permute-done((s32[96]{0:T(128)}, s32[96]{0:T(128)S(1)}, u32[]{:S(2)}, u32[]{:S(2)}) %collective-permute-start) | collective-permute-done | bytes 416 | tf_op jit(solution)/shard_map/ppermute | solution.py:465
  28.5 0.0 collective-permute-done.2.refs_0_
  28.5 0.1 fusion
  28.6 0.1 collective-permute-start.4
  28.7 0.5 collective-permute-start.5
  29.2 0.1 collective-permute-start.6
  29.3 0.4 collective-permute-start.7
  29.7 0.5 collective-permute-done.4.rest_0_
  30.2 0.4 collective-permute-done.5.rest_1_
  30.6 0.4 collective-permute-done.6.rest_2_
  31.0 0.4 collective-permute-done.7.rest_3_
  31.4 3.6 %filter.4 = (bf16[128,192,128]{2,1,0:T(8,128)(2,1)S(1)}, bf16[128,192,128]{2,1,0:T(8,128)(2,1)S(1)}, f32[8,128]{1,0:T(8,128)S(1)}) custom-call(s32[96]{0:T(128)S(1)} %collective-permute-done.refs_2_.bins, bf16[64,64,128]{2,1,0:T(8,128)(2,1)S(1)} %gate.2.mine, ...), custom_call_target="tpu_custom_call", output_to_operand_aliasing={{0}: (8, {}), {1}: (9, {})} | custom-call | flops 640000000 | bytes 1920000 | tf_op jit(solution)/shard_map/filter/pallas_call | solution.py:217
  35.0 4.5 %collective-permute-done.1.refs_0_ = bf16[32,64,128]{2,1,0:T(8,128)(2,1)S(1)} collective-permute-done((bf16[32,64,128]{2,1,0:T(8,128)(2,1)S(1)}, bf16[32,64,128]{2,1,0:T(8,128)(2,1)S(1)}, u32[]{:S(2)}, u32[]{:S(2)}) %collective-permute-start.1) | collective-permute-done | bytes 524320 | tf_op jit(solution)/shard_map/ppermute | solution.py:464
  39.5 0.0 collective-permute-start.8
  39.5 1.9 %collective-permute-done.8.rest_0_ = bf16[32,64,128]{2,1,0:T(8,128)(2,1)S(1)} collective-permute-done((bf16[32,64,128]{2,1,0:T(8,128)(2,1)S(1)}, bf16[32,64,128]{2,1,0:T(8,128)(2,1)S(1)}, u32[]{:S(2)}, u32[]{:S(2)}) %collective-permute-start.8) | collective-permute-done | bytes 524320 | tf_op jit(solution)/shard_map/ppermute | solution.py:480
  41.4 2.5 %filter.5 = (bf16[128,192,128]{2,1,0:T(8,128)(2,1)S(1)}, bf16[128,192,128]{2,1,0:T(8,128)(2,1)S(1)}, f32[8,128]{1,0:T(8,128)}) custom-call(s32[96]{0:T(128)S(1)} %collective-permute-done.refs_2_.bins, bf16[32,64,128]{2,1,0:T(8,128)(2,1)S(1)} %gate.3.mine, ...), custom_call_target="tpu_custom_call", output_to_operand_aliasing={{0}: (5, {}), {1}: (6, {})} | custom-call | flops 320000000 | bytes 960000 | tf_op jit(solution)/shard_map/filter/pallas_call | solution.py:217
  44.0 4.6 %score.1 = (f32[336,192]{1,0:T(8,128)S(1)}, f32[8,192]{1,0:T(8,128)S(1)}) custom-call(bf16[128,192,128]{2,1,0:T(8,128)(2,1)S(1)} %get-tuple-element.43.plain, bf16[128,336,128]{2,1,0:T(8,128)(2,1)S(1)} %get-tuple-element.44.refs, f32[336,128]{1,0:T(8,128)S(1)} %get-tuple-element.34.after.norm, f32[112,192]{1,0:T(8,128)S(1)} %get-tuple-element.45.mask, ...), custom_call_target="tpu_custom_call" | custom-call | flops 500000000 | bytes 1500000 | tf_op jit(solution)/shard_map/score/pallas_call | solution.py:256
  48.5 1.8 %collective-permute-start.9 = (f32[8,192]{1,0:T(8,128)S(1)}, f32[8,192]{1,0:T(8,128)S(1)}, u32[]{:S(2)}, u32[]{:S(2)}) collective-permute-start(f32[8,192]{1,0:T(8,128)S(1)} %get-tuple-element.48.mine), channel_id=1, source_target_pairs={{0,1},{1,0},{2,3},{3,2},{4,5},{5,4},{6,7},{7,6},{8,9},{9,8},{10,11... | collective-permute-start | bytes 18440 | tf_op jit(solution)/shard_map/ppermute | solution.py:488
  50.4 1.9 %collective-permute-done.9.other = f32[8,192]{1,0:T(8,128)S(1)} collective-permute-done((f32[8,192]{1,0:T(8,128)S(1)}, f32[8,192]{1,0:T(8,128)S(1)}, u32[]{:S(2)}, u32[]{:S(2)}) %collective-permute-start.9) | collective-permute-done | bytes 6176 | tf_op jit(solution)/shard_map/ppermute | solution.py:488
  52.3 0.4 weights.1
  52.6 3.0 %sums.2 = (f32[4,500,128]{2,1,0:T(8,128)S(1)}, bf16[4,500,128]{2,1,0:T(8,128)(2,1)}) custom-call(bf16[2,112,384]{2,1,0:T(8,128)(2,1)S(1)} %weights.1, bf16[128,192,128]{2,1,0:T(8,128)(2,1)S(1)} %get-tuple-element.43.plain, bf16[128,192,128]{2,1,0:T(8,128)(2,1)S(1)} %get-tuple-element.50.turned), custom_call_target="tpu_custom_call" | custom-call | flops 400000000 | bytes 1200000 | tf_op jit(solution)/shard_map/sums/pallas_call | solution.py:349
  55.7 1.7 %collective-permute-start.10 = (bf16[4,500,128]{2,1,0:T(8,128)(2,1)}, bf16[4,500,128]{2,1,0:T(8,128)(2,1)S(1)}, u32[]{:S(2)}, u32[]{:S(2)}) collective-permute-start(bf16[4,500,128]{2,1,0:T(8,128)(2,1)} %get-tuple-element.52.rest_0_), channel_id=1, source_target_pairs={{0,2},{2,0},{4,6},{6,4},{8,10},{10,8},{12,14},{14,12},{1,3},{3,1},... | collective-permute-start | bytes 1536008 | tf_op jit(solution)/shard_map/ppermute | solution.py:491
  57.4 1.1 %copy-done.1 = bf16[4,500,128]{2,1,0:T(8,128)(2,1)S(1)} copy-done((bf16[4,500,128]{2,1,0:T(8,128)(2,1)S(1)}, bf16[4,500,128]{2,1,0:T(8,128)(2,1)}, u32[]{:S(2)}) %copy-start.1) | copy-done | bytes 512024
  58.4 1.7 %sums.3 = (f32[2,300,128]{2,1,0:T(8,128)S(1)}, bf16[2,300,128]{2,1,0:T(8,128)(2,1)}, bf16[2,300,128]{2,1,0:T(8,128)(2,1)}, bf16[2,300,128]{2,1,0:T(8,128)(2,1)}) custom-call(bf16[2,112,384]{2,1,0:T(8,128)(2,1)S(1)} %weights.1, bf16[128,192,128]{2,1,0:T(8,128)(2,1)S(1)} %get-tuple-element.43.plain, bf16[128,192,128]{2,1,0:T(8,128)(2,1)S(1)} %get-tuple-element.50.turned, ...), custom_call_target="tpu_custom_call" | custom-call | flops 240000000 | bytes 720000 | tf_op jit(solution)/shard_map/sums/pallas_call | solution.py:349
  60.1 1.6 %collective-permute-start.14 = (bf16[2,300,128]{2,1,0:T(8,128)(2,1)}, bf16[2,300,128]{2,1,0:T(8,128)(2,1)S(1)}, u32[]{:S(2)}, u32[]{:S(2)}) collective-permute-start(bf16[2,300,128]{2,1,0:T(8,128)(2,1)} %get-tuple-element.58), channel_id=1, source_target_pairs={{0,4},{2,6},{4,0},{6,2},{8,12},{10,14},{12,8},{14,10},{1,5},{3,7},... | collective-permute-start | bytes 460808 | tf_op jit(solution)/shard_map/ppermute | solution.py:491
  61.7 2.6 %collective-permute-start.15 = (bf16[2,300,128]{2,1,0:T(8,128)(2,1)}, bf16[2,300,128]{2,1,0:T(8,128)(2,1)S(1)}, u32[]{:S(2)}, u32[]{:S(2)}) collective-permute-start(bf16[2,300,128]{2,1,0:T(8,128)(2,1)} %get-tuple-element.59), channel_id=1, source_target_pairs={{0,8},{2,10},{4,12},{6,14},{8,0},{10,2},{12,4},{14,6},{1,9},{3,11}... | collective-permute-start | bytes 460808 | tf_op jit(solution)/shard_map/ppermute | solution.py:491
  64.3 0.2 collective-permute-start.16
  64.5 4.0 %collective-permute-done.10.got = bf16[4,500,128]{2,1,0:T(8,128)(2,1)S(1)} collective-permute-done((bf16[4,500,128]{2,1,0:T(8,128)(2,1)}, bf16[4,500,128]{2,1,0:T(8,128)(2,1)S(1)}, u32[]{:S(2)}, u32[]{:S(2)}) %collective-permute-start.10) | collective-permute-done | bytes 512032 | tf_op jit(solution)/shard_map/ppermute | solution.py:491
  68.5 0.1 fold.1
  68.6 1.9 %collective-permute-start.11 = (bf16[1,500,128]{2,1,0:T(8,128)(2,1)S(1)}, bf16[1,500,128]{2,1,0:T(8,128)(2,1)S(1)}, u32[]{:S(2)}, u32[]{:S(2)}) collective-permute-start(bf16[1,500,128]{2,1,0:T(8,128)(2,1)S(1)} %get-tuple-element.54), channel_id=1, source_target_pairs={{0,4},{2,6},{4,0},{6,2},{8,12},{10,14},{12,8},{14,10},{1,5},{3,7},... | collective-permute-start | bytes 384008 | tf_op jit(solution)/shard_map/ppermute | solution.py:491
  70.5 2.6 %collective-permute-start.12 = (bf16[1,500,128]{2,1,0:T(8,128)(2,1)S(1)}, bf16[1,500,128]{2,1,0:T(8,128)(2,1)S(1)}, u32[]{:S(2)}, u32[]{:S(2)}) collective-permute-start(bf16[1,500,128]{2,1,0:T(8,128)(2,1)S(1)} %get-tuple-element.55), channel_id=1, source_target_pairs={{0,8},{2,10},{4,12},{6,14},{8,0},{10,2},{12,4},{14,6},{1,9},{3,11}... | collective-permute-start | bytes 384008 | tf_op jit(solution)/shard_map/ppermute | solution.py:491
  73.1 0.0 collective-permute-done.14.rest_0_
  73.1 0.0 collective-permute-start.13
  73.1 3.7 %collective-permute-done.15.rest_1_ = bf16[2,300,128]{2,1,0:T(8,128)(2,1)S(1)} collective-permute-done((bf16[2,300,128]{2,1,0:T(8,128)(2,1)}, bf16[2,300,128]{2,1,0:T(8,128)(2,1)S(1)}, u32[]{:S(2)}, u32[]{:S(2)}) %collective-permute-start.15) | collective-permute-done | bytes 153632 | tf_op jit(solution)/shard_map/ppermute | solution.py:491
  76.8 0.0 collective-permute-done.16.rest_2_
  76.8 0.1 gather.1
  76.9 0.4 collective-permute-start.17
  77.3 4.1 %collective-permute-done.17.args_5_ = bf16[1,300,128]{2,1,0:T(8,128)(2,1)S(1)} collective-permute-done((bf16[1,300,128]{2,1,0:T(8,128)(2,1)S(1)}, bf16[1,300,128]{2,1,0:T(8,128)(2,1)S(1)}, u32[]{:S(2)}, u32[]{:S(2)}) %collective-permute-start.17) | collective-permute-done | bytes 76832 | tf_op jit(solution)/shard_map/ppermute | solution.py:491
  81.4 0.0 collective-permute-done.11.args_1_
  81.4 5.5 %collective-permute-done.12.args_2_ = bf16[1,500,128]{2,1,0:T(8,128)(2,1)S(1)} collective-permute-done((bf16[1,500,128]{2,1,0:T(8,128)(2,1)S(1)}, bf16[1,500,128]{2,1,0:T(8,128)(2,1)S(1)}, u32[]{:S(2)}, u32[]{:S(2)}) %collective-permute-start.12) | collective-permute-done | bytes 128032 | tf_op jit(solution)/shard_map/ppermute | solution.py:491
  86.9 0.0 collective-permute-done.13.args_3_
  86.9 0.9 %finish.1 = f32[800,128]{1,0:T(8,128)} custom-call(f32[1,500,128]{2,1,0:T(8,128)S(1)} %get-tuple-element.53.args_0_, bf16[1,500,128]{2,1,0:T(8,128)(2,1)S(1)} %collective-permute-done.11.args_1_, bf16[1,500,128]{2,1,0:T(8,128)(2,1)S(1)} %collective-permute-done.12.args_2_, bf16[1,500,128]{2,1,0:T(8,128)(2,1)S(1)} %collective-permute-done.13.args_3_, ...), custom_call_target="tpu_custom_call" | custom-call | flops 100000000 | bytes 300000 | tf_op jit(solution)/shard_map/finish/pallas_call | solution.py:429
  (5 shorter events, 0.0 us)
Async XLA Ops:
  0.0 16.5 %copy-start.7 = (f32[128]{0:T(128)S(1)}, f32[128]{0:T(128)}, u32[]{:S(2)}) copy-start(f32[128]{0:T(128)} %param.11) | copy-start | bytes 1540
  0.0 16.5 %copy-start.6 = (f32[192]{0:T(256)S(1)}, f32[192]{0:T(256)}, u32[]{:S(2)}) copy-start(f32[192]{0:T(256)} %param.15) | copy-start | bytes 2308
  0.0 16.5 %copy-start.5 = (s32[100,3]{0,1:T(4,128)S(1)}, s32[100,3]{0,1:T(4,128)}, u32[]{:S(2)}) copy-start(s32[100,3]{0,1:T(4,128)} %param.13) | copy-start | bytes 3604
  0.0 16.5 %copy-start.4 = (f32[16,128]{1,0:T(8,128)S(1)}, f32[16,128]{1,0:T(8,128)}, u32[]{:S(2)}) copy-start(f32[16,128]{1,0:T(8,128)} %ctf.1) | copy-start | bytes 24580
  0.0 16.5 %copy-start.3 = (s32[192,100]{1,0:T(8,128)S(1)}, s32[192,100]{1,0:T(8,128)}, u32[]{:S(2)}) copy-start(s32[192,100]{1,0:T(8,128)} %mask.1) | copy-start | bytes 230404
  0.0 17.3 %collective-permute-start.3 = (bf16[96,64,128]{2,1,0:T(8,128)(2,1)}, bf16[96,64,128]{2,1,0:T(8,128)(2,1)S(1)}, u32[]{:S(2)}, u32[]{:S(2)}) collective-permute-start(bf16[96,64,128]{2,1,0:T(8,128)(2,1)} %mine.1), channel_id=1, source_target_pairs={{0,16},{16,0},{1,17},{17,1},{2,18},{18,2},{3,19},{19,3},{4,20},{20... | collective-permute-start | bytes 4718600 | tf_op jit(solution)/shard_map/ppermute | solution.py:466
  1.8 15.5 %copy-start = (bf16[96,64,128]{2,1,0:T(8,128)(2,1)S(1)}, bf16[96,64,128]{2,1,0:T(8,128)(2,1)}, u32[]{:S(2)}) copy-start(bf16[96,64,128]{2,1,0:T(8,128)(2,1)} %mine.1) | copy-start | bytes 4718596
  1.9 15.5 %copy-start.2 = (s32[96]{0:T(128)S(1)}, s32[96]{0:T(128)}, u32[]{:S(2)}) copy-start(s32[96]{0:T(128)} %bins.1) | copy-start | bytes 1156
  1.9 26.7 %collective-permute-start.2 = (bf16[64,64,128]{2,1,0:T(8,128)(2,1)S(1)}, bf16[64,64,128]{2,1,0:T(8,128)(2,1)S(1)}, u32[]{:S(2)}, u32[]{:S(2)}) collective-permute-start(bf16[64,64,128]{2,1,0:T(8,128)(2,1)S(1)} %slice.19), channel_id=1, source_target_pairs={{0,1},{1,0},{2,3},{3,2},{4,5},{5,4},{6,7},{7,6},{8,9},{9,8},{10,11... | collective-permute-start | bytes 3145736 | tf_op jit(solution)/shard_map/ppermute | solution.py:464
  4.5 24.1 %collective-permute-start = (s32[96]{0:T(128)}, s32[96]{0:T(128)S(1)}, u32[]{:S(2)}, u32[]{:S(2)}) collective-permute-start(s32[96]{0:T(128)} %bins.1), channel_id=1, source_target_pairs={{0,1},{1,0},{2,3},{3,2},{4,5},{5,4},{6,7},{7,6},{8,9},{9,8},{10,11... | collective-permute-start | bytes 1160 | tf_op jit(solution)/shard_map/ppermute | solution.py:465
  5.6 33.9 %collective-permute-start.1 = (bf16[32,64,128]{2,1,0:T(8,128)(2,1)S(1)}, bf16[32,64,128]{2,1,0:T(8,128)(2,1)S(1)}, u32[]{:S(2)}, u32[]{:S(2)}) collective-permute-start(bf16[32,64,128]{2,1,0:T(8,128)(2,1)S(1)} %slice.18), channel_id=1, source_target_pairs={{0,1},{1,0},{2,3},{3,2},{4,5},{5,4},{6,7},{7,6},{8,9},{9,8},{10,11... | collective-permute-start | bytes 1572872 | tf_op jit(solution)/shard_map/ppermute | solution.py:464
  28.6 1.6 %collective-permute-start.4 = (bf16[16,64,128]{2,1,0:T(8,128)(2,1)S(1)}, bf16[16,64,128]{2,1,0:T(8,128)(2,1)S(1)}, u32[]{:S(2)}, u32[]{:S(2)}) collective-permute-start(bf16[16,64,128]{2,1,0:T(8,128)(2,1)S(1)} %get-tuple-element.66), channel_id=1, source_target_pairs={{0,16},{16,0},{1,17},{17,1},{2,18},{18,2},{3,19},{19,3},{4,20},{20... | collective-permute-start | bytes 786440 | tf_op jit(solution)/shard_map/ppermute | solution.py:480
  28.7 1.9 %collective-permute-start.5 = (bf16[16,64,128]{2,1,0:T(8,128)(2,1)S(1)}, bf16[16,64,128]{2,1,0:T(8,128)(2,1)S(1)}, u32[]{:S(2)}, u32[]{:S(2)}) collective-permute-start(bf16[16,64,128]{2,1,0:T(8,128)(2,1)S(1)} %get-tuple-element.65), channel_id=1, source_target_pairs={{0,16},{16,0},{1,17},{17,1},{2,18},{18,2},{3,19},{19,3},{4,20},{20... | collective-permute-start | bytes 786440 | tf_op jit(solution)/shard_map/ppermute | solution.py:480
  29.2 1.8 %collective-permute-start.6 = (bf16[16,64,128]{2,1,0:T(8,128)(2,1)S(1)}, bf16[16,64,128]{2,1,0:T(8,128)(2,1)S(1)}, u32[]{:S(2)}, u32[]{:S(2)}) collective-permute-start(bf16[16,64,128]{2,1,0:T(8,128)(2,1)S(1)} %get-tuple-element.64), channel_id=1, source_target_pairs={{0,16},{16,0},{1,17},{17,1},{2,18},{18,2},{3,19},{19,3},{4,20},{20... | collective-permute-start | bytes 786440 | tf_op jit(solution)/shard_map/ppermute | solution.py:480
  29.3 2.1 %collective-permute-start.7 = (bf16[16,64,128]{2,1,0:T(8,128)(2,1)S(1)}, bf16[16,64,128]{2,1,0:T(8,128)(2,1)S(1)}, u32[]{:S(2)}, u32[]{:S(2)}) collective-permute-start(bf16[16,64,128]{2,1,0:T(8,128)(2,1)S(1)} %get-tuple-element.63), channel_id=1, source_target_pairs={{0,16},{16,0},{1,17},{17,1},{2,18},{18,2},{3,19},{19,3},{4,20},{20... | collective-permute-start | bytes 786440 | tf_op jit(solution)/shard_map/ppermute | solution.py:480
  39.5 1.9 %collective-permute-start.8 = (bf16[32,64,128]{2,1,0:T(8,128)(2,1)S(1)}, bf16[32,64,128]{2,1,0:T(8,128)(2,1)S(1)}, u32[]{:S(2)}, u32[]{:S(2)}) collective-permute-start(bf16[32,64,128]{2,1,0:T(8,128)(2,1)S(1)} %gate.3.mine), channel_id=1, source_target_pairs={{0,16},{16,0},{1,17},{17,1},{2,18},{18,2},{3,19},{19,3},{4,20},{20... | collective-permute-start | bytes 1572872 | tf_op jit(solution)/shard_map/ppermute | solution.py:480
  48.5 3.7 %collective-permute-start.9 = (f32[8,192]{1,0:T(8,128)S(1)}, f32[8,192]{1,0:T(8,128)S(1)}, u32[]{:S(2)}, u32[]{:S(2)}) collective-permute-start(f32[8,192]{1,0:T(8,128)S(1)} %get-tuple-element.48.mine), channel_id=1, source_target_pairs={{0,1},{1,0},{2,3},{3,2},{4,5},{5,4},{6,7},{7,6},{8,9},{9,8},{10,11... | collective-permute-start | bytes 18440 | tf_op jit(solution)/shard_map/ppermute | solution.py:488
  55.7 12.9 %collective-permute-start.10 = (bf16[4,500,128]{2,1,0:T(8,128)(2,1)}, bf16[4,500,128]{2,1,0:T(8,128)(2,1)S(1)}, u32[]{:S(2)}, u32[]{:S(2)}) collective-permute-start(bf16[4,500,128]{2,1,0:T(8,128)(2,1)} %get-tuple-element.52.rest_0_), channel_id=1, source_target_pairs={{0,2},{2,0},{4,6},{6,4},{8,10},{10,8},{12,14},{14,12},{1,3},{3,1},... | collective-permute-start | bytes 1536008 | tf_op jit(solution)/shard_map/ppermute | solution.py:491
  57.4 1.1 %copy-start.1 = (bf16[4,500,128]{2,1,0:T(8,128)(2,1)S(1)}, bf16[4,500,128]{2,1,0:T(8,128)(2,1)}, u32[]{:S(2)}) copy-start(bf16[4,500,128]{2,1,0:T(8,128)(2,1)} %get-tuple-element.52.rest_0_) | copy-start | bytes 1536004
  60.1 12.9 %collective-permute-start.14 = (bf16[2,300,128]{2,1,0:T(8,128)(2,1)}, bf16[2,300,128]{2,1,0:T(8,128)(2,1)S(1)}, u32[]{:S(2)}, u32[]{:S(2)}) collective-permute-start(bf16[2,300,128]{2,1,0:T(8,128)(2,1)} %get-tuple-element.58), channel_id=1, source_target_pairs={{0,4},{2,6},{4,0},{6,2},{8,12},{10,14},{12,8},{14,10},{1,5},{3,7},... | collective-permute-start | bytes 460808 | tf_op jit(solution)/shard_map/ppermute | solution.py:491
  61.7 15.1 %collective-permute-start.15 = (bf16[2,300,128]{2,1,0:T(8,128)(2,1)}, bf16[2,300,128]{2,1,0:T(8,128)(2,1)S(1)}, u32[]{:S(2)}, u32[]{:S(2)}) collective-permute-start(bf16[2,300,128]{2,1,0:T(8,128)(2,1)} %get-tuple-element.59), channel_id=1, source_target_pairs={{0,8},{2,10},{4,12},{6,14},{8,0},{10,2},{12,4},{14,6},{1,9},{3,11}... | collective-permute-start | bytes 460808 | tf_op jit(solution)/shard_map/ppermute | solution.py:491
  64.3 12.5 %collective-permute-start.16 = (bf16[2,300,128]{2,1,0:T(8,128)(2,1)}, bf16[2,300,128]{2,1,0:T(8,128)(2,1)S(1)}, u32[]{:S(2)}, u32[]{:S(2)}) collective-permute-start(bf16[2,300,128]{2,1,0:T(8,128)(2,1)} %get-tuple-element.60), channel_id=1, source_target_pairs={{0,12},{2,14},{4,8},{6,10},{8,4},{10,6},{12,0},{14,2},{1,13},{3,15... | collective-permute-start | bytes 460808 | tf_op jit(solution)/shard_map/ppermute | solution.py:491
  68.6 12.7 %collective-permute-start.11 = (bf16[1,500,128]{2,1,0:T(8,128)(2,1)S(1)}, bf16[1,500,128]{2,1,0:T(8,128)(2,1)S(1)}, u32[]{:S(2)}, u32[]{:S(2)}) collective-permute-start(bf16[1,500,128]{2,1,0:T(8,128)(2,1)S(1)} %get-tuple-element.54), channel_id=1, source_target_pairs={{0,4},{2,6},{4,0},{6,2},{8,12},{10,14},{12,8},{14,10},{1,5},{3,7},... | collective-permute-start | bytes 384008 | tf_op jit(solution)/shard_map/ppermute | solution.py:491
  70.5 16.4 %collective-permute-start.12 = (bf16[1,500,128]{2,1,0:T(8,128)(2,1)S(1)}, bf16[1,500,128]{2,1,0:T(8,128)(2,1)S(1)}, u32[]{:S(2)}, u32[]{:S(2)}) collective-permute-start(bf16[1,500,128]{2,1,0:T(8,128)(2,1)S(1)} %get-tuple-element.55), channel_id=1, source_target_pairs={{0,8},{2,10},{4,12},{6,14},{8,0},{10,2},{12,4},{14,6},{1,9},{3,11}... | collective-permute-start | bytes 384008 | tf_op jit(solution)/shard_map/ppermute | solution.py:491
  73.1 13.8 %collective-permute-start.13 = (bf16[1,500,128]{2,1,0:T(8,128)(2,1)S(1)}, bf16[1,500,128]{2,1,0:T(8,128)(2,1)S(1)}, u32[]{:S(2)}, u32[]{:S(2)}) collective-permute-start(bf16[1,500,128]{2,1,0:T(8,128)(2,1)S(1)} %get-tuple-element.56), channel_id=1, source_target_pairs={{0,12},{2,14},{4,8},{6,10},{8,4},{10,6},{12,0},{14,2},{1,13},{3,15... | collective-permute-start | bytes 384008 | tf_op jit(solution)/shard_map/ppermute | solution.py:491
  76.9 4.5 %collective-permute-start.17 = (bf16[1,300,128]{2,1,0:T(8,128)(2,1)S(1)}, bf16[1,300,128]{2,1,0:T(8,128)(2,1)S(1)}, u32[]{:S(2)}, u32[]{:S(2)}) collective-permute-start(bf16[1,300,128]{2,1,0:T(8,128)(2,1)S(1)} %get-tuple-element.62), channel_id=1, source_target_pairs={{0,2},{2,0},{4,6},{6,4},{8,10},{10,8},{12,14},{14,12},{1,3},{3,1},... | collective-permute-start | bytes 230408 | tf_op jit(solution)/shard_map/ppermute | solution.py:491

commit v6 on v5

--- a/solution.py
+++ b/solution.py
@@ -12,7 +12,7 @@
 LOW = -1e30
 GROUP = 16
 PAD = 8
-DEEP = 16
+DEEP = 64
 SUMS = 0.8
 SCALE = 0.1
 FOLD = 1
@@ -180,33 +180,41 @@
 
 def filter_kernel(bins, mine, left, right, *rest, parts, skip, at):
     sibs = rest[:parts]
-    plain, turned, token, scr, scr_t = rest[-5:]
+    plain, turned, token = rest[-7:-4]
+    scratch = rest[-4:]
     token[...] = jnp.zeros_like(token)
     width = mine.shape[2]
     top = lax.axis_index("section") == 0
     pitch = width + PAD
 
-    def part(sib, first):
-        @pl.loop(0, sib.shape[0] // GROUP)
-        def _(g):
-            base = pl.multiple_of(g * GROUP, GROUP)
-            for i in range(GROUP):
-                b = bins[skip + first + base + i]
-                a = mine[first + base + i]
-                o = sib[base + i]
-                x = jnp.concatenate([jnp.where(top, a, o), jnp.where(top, o, a)], axis=0)
-                f = nn(left[b], nn(x, right[b]).astype(BF16))
-                scr[pl.ds(i * pitch, width)] = f
-                scr_t[pl.ds(i * pitch, width)] = f.T
-            to = pl.multiple_of(at + first + base, GROUP)
-            for r in range(width):
-                plain[r, pl.ds(to, GROUP)] = scr[pl.ds(r, GROUP, stride=pitch)].astype(BF16)
-                turned[r, pl.ds(to, GROUP)] = scr_t[pl.ds(r, GROUP, stride=pitch)].astype(BF16)
+    def group(sib, base, first, turn):
+        scr, scr_t = scratch[2 * turn : 2 * turn + 2]
+        for i in range(GROUP):
+            b = bins[skip + first + base + i]
+            a = mine[first + base + i]
+            o = sib[base + i]
+            x = jnp.concatenate([jnp.where(top, a, o), jnp.where(top, o, a)], axis=0)
+            f = nn(left[b], nn(x, right[b]).astype(BF16))
+            scr[pl.ds(i * pitch, width)] = f
+            scr_t[pl.ds(i * pitch, width)] = f.T
+        to = pl.multiple_of(at + first + base, GROUP)
+        for r in range(width):
+            plain[r, pl.ds(to, GROUP)] = scr[pl.ds(r, GROUP, stride=pitch)].astype(BF16)
+            turned[r, pl.ds(to, GROUP)] = scr_t[pl.ds(r, GROUP, stride=pitch)].astype(BF16)
 
     first = 0
-    for sib in sibs:
-        part(sib, first)
-        first += sib.shape[0]
+    for n, sib in enumerate(sibs):
+        count = sib.shape[0]
+        if count <= 2 * GROUP:
+            for g in range(count // GROUP):
+                group(sib, g * GROUP, first, (n + g) % 2)
+        else:
+
+            @pl.loop(0, count // GROUP)
+            def _(g):
+                group(sib, pl.multiple_of(g * GROUP, GROUP), first, 0)
+
+        first += count
 
 
 def filter_chunk(bins, mine, sibs, left, right, buffers, total, skip, at):
@@ -220,7 +228,7 @@
         out_specs=(vmem, vmem, vmem),
         out_shape=(pinned((2 * half, total, width), BF16),) * 2
         + (jax.ShapeDtypeStruct((8, width), F32),),
-        scratch_shapes=[pltpu.VMEM((GROUP * (2 * half + PAD), width), F32)] * 2,
+        scratch_shapes=[pltpu.VMEM((GROUP * (2 * half + PAD), width), F32)] * 4,
         input_output_aliases={4 + parts + i: i for i in range(len(buffers))},
         compiler_params=pltpu.CompilerParams(vmem_limit_bytes=8 * MIB),
         cost_estimate=cost(count * 0.1),
@@ -352,7 +360,7 @@
         ),
         in_specs=[vmem] * 3 + [pl.BlockSpec(memory_space=pl.ANY)] * len(after),
         out_shape=(pinned(shape, F32),)
-        + (pltpu.HBM(shape, BF16),) * (dom // 2 - 1 if outer else 1),
+        + (jax.ShapeDtypeStruct(shape, BF16),) * (dom // 2 - 1 if outer else 1),
         compiler_params=pltpu.CompilerParams(vmem_limit_bytes=8 * MIB),
         cost_estimate=cost(SUMS * rows),
         name="sums",
@@ -490,6 +498,10 @@
     def along(x, mask):
         return lax.ppermute(x, "dom", [(i, i ^ mask) for i in range(dom)])
 
+    def spread(sends, bit):
+        far_first = sorted(range(len(sends)), key=lambda m: m == 0)
+        return [along(sends[m], (m + 1) << bit) for m in far_first]
+
     inner, outer = row_pieces(half // dom, dom)
     keep, send = sums(weights, plain, turned, (), False, dom, 0, inner, classes)
     got = along(send, 1)
@@ -497,14 +509,14 @@
         keep_b, *sends_b = sums(
             weights, plain, turned, (send,), True, dom, inner, outer, classes
         )
-        got_b = [along(s, (m + 1) << 1) for m, s in enumerate(sends_b)]
+        got_b = spread(sends_b, 1)
     bit = 1
     while keep.shape[0] > 4:
         keep, send = fold(keep, got, (), 2, bit)
         got = along(send, 1 << bit)
         bit += 1
     keep, *sends = fold(keep, got, (), keep.shape[0], bit)
-    done = [[keep] + [along(s, (m + 1) << bit) for m, s in enumerate(sends)]]
+    done = [[keep] + spread(sends, bit)]
     if outer:
         keep_b, send_b = gather(keep_b, got_b)
         done.append([keep_b, along(send_b, 1)])

time: 88 us -> 83 us (0.943)
  Pallas kernels: 32.9 us -> 30.2 us
  waiting for transfers between devices: 32.1 us -> 29.5 us
  starting transfers between devices: 19 us -> 20.1 us
  local copies, waits for them, and re-layouts: 3.55 us -> 2.47 us
    ppermute x8, waiting for transfers between devices: 17.3 us -> 14.6 us  [along(): return lax.ppermute(x, 'dom', [(i, i ^ mask) for i in range(dom)])]
    pallas_call x2, Pallas kernels: 4.73 us -> 3.27 us  [sums(): pl.pallas_call(functools.partial(sums_kernel, outer=outer, dom=dom, start...]
    pallas_call x1, Pallas kernels: 4.6 us -> 3.43 us  [score(): pl.pallas_call(score_kernel, out_shape=(pinned((height, count), F32), pin...]
    ppermute x8, starting transfers between devices: 10.9 us -> 12 us  [along(): return lax.ppermute(x, 'dom', [(i, i ^ mask) for i in range(dom)])]
    unnamed x16 -> x14, local copies, waits for them, and re-layouts: 1.1 us -> 0.03 us
  transfers between devices with their start and end apart: 18 -> 18, of which waited for: 12 -> 11; matrix products, arithmetic and copies ran while one was open for 3% -> 3% of each run, Pallas kernels for 25% -> 25%
where the time goes in v6:
time: 83 us; the launch traced here: 82.5 us
  Pallas kernels  30.2 us (36%)
  waiting for transfers between devices  29.5 us (36%)
  starting transfers between devices  20.1 us (24%)
  local copies, waits for them, and re-layouts  2.47 us (3%)
    ppermute x8, waiting for transfers between devices, along(): return lax.ppermute(x, 'dom', [(i, i ^ mask) for i in range(dom)])  14.6 us
    pallas_call x3, Pallas kernels, filter_chunk(): pl.pallas_call(functools.partial(filter_kernel, parts=parts, skip=skip, a...  12.4 us
    ppermute x8, starting transfers between devices, along(): return lax.ppermute(x, 'dom', [(i, i ^ mask) for i in range(dom)])  12 us
    pallas_call x1, Pallas kernels, lay_refs(): pl.pallas_call(functools.partial(refs_kernel, padded=padded), grid=(rots,...  8.81 us
    ppermute x1, waiting for transfers between devices, local(): other_bins = over_cls(defocus_bin)  4.8 us
    ppermute x2, waiting for transfers between devices, local(): remote = [over_cls(images[a:a + n]) for a, n in zip(starts, sizes)]  4.64 us
    ppermute x2, starting transfers between devices, local(): remote = [over_cls(images[a:a + n]) for a, n in zip(starts, sizes)]  4.61 us
    ppermute x5, waiting for transfers between devices, local(): sibs = [over_section(piece[b:b + step]) for b in range(0, sizes[i], step)]  3.54 us
  transfers between devices with their start and end apart: 18, of which 11 were waited for; matrix products, arithmetic and copies ran while one was open for 3% of the time, Pallas kernels for 25%

profile of v6, /device:TPU:0, one launch (start us, length us, event | category | flops | bytes accessed | tf_op | source)
XLA Modules:
  0.0 82.5 jit_solution(4318657042430777819)
XLA Ops:
  0.0 0.0 copy-start.6
  0.0 0.0 copy-start.5
  0.0 0.0 copy-start.4
  0.0 0.0 copy-start.3
  0.0 0.5 collective-permute-start.3
  0.5 1.3 %slice.19 = bf16[64,64,128]{2,1,0:T(8,128)(2,1)S(1)} slice(bf16[96,64,128]{2,1,0:T(8,128)(2,1)} %mine.1), slice={[0:64], [0:64], [0:128]} | slice | bytes 2097152 | tf_op jit(solution)/shard_map/slice | solution.py:472
  1.8 0.0 copy-start
  1.9 0.0 copy-start.1
  1.9 2.6 %collective-permute-start.2 = (bf16[64,64,128]{2,1,0:T(8,128)(2,1)S(1)}, bf16[64,64,128]{2,1,0:T(8,128)(2,1)S(1)}, u32[]{:S(2)}, u32[]{:S(2)}) collective-permute-start(bf16[64,64,128]{2,1,0:T(8,128)(2,1)S(1)} %slice.19), channel_id=1, source_target_pairs={{0,1},{1,0},{2,3},{3,2},{4,5},{5,4},{6,7},{7,6},{8,9},{9,8},{10,11... | collective-permute-start | bytes 3145736 | tf_op jit(solution)/shard_map/ppermute | solution.py:472
  4.5 0.1 collective-permute-start
  4.5 1.1 %slice.18 = bf16[32,64,128]{2,1,0:T(8,128)(2,1)S(1)} slice(bf16[96,64,128]{2,1,0:T(8,128)(2,1)} %mine.1), slice={[64:96], [0:64], [0:128]} | slice | bytes 1048576 | tf_op jit(solution)/shard_map/slice | solution.py:472
  5.6 2.0 %collective-permute-start.1 = (bf16[32,64,128]{2,1,0:T(8,128)(2,1)S(1)}, bf16[32,64,128]{2,1,0:T(8,128)(2,1)S(1)}, u32[]{:S(2)}, u32[]{:S(2)}) collective-permute-start(bf16[32,64,128]{2,1,0:T(8,128)(2,1)S(1)} %slice.18), channel_id=1, source_target_pairs={{0,1},{1,0},{2,3},{3,2},{4,5},{5,4},{6,7},{7,6},{8,9},{9,8},{10,11... | collective-permute-start | bytes 1572872 | tf_op jit(solution)/shard_map/ppermute | solution.py:472
  7.6 8.8 %refs.2 = (bf16[128,336,128]{2,1,0:T(8,128)(2,1)S(1)}, f32[336,128]{1,0:T(8,128)S(1)}) custom-call(bf16[100,3,128,128]{3,2,1,0:T(8,128)(2,1)} %refs.3), custom_call_target="tpu_custom_call" | custom-call | flops 900000000 | bytes 2700000 | tf_op jit(solution)/shard_map/refs/pallas_call | solution.py:165
  16.4 0.0 copy-done.6
  16.5 0.0 copy-done.5
  16.5 0.0 copy-done.4
  16.5 0.0 copy-done.3
  16.5 0.0 copy-done.2
  16.5 0.8 prepare.1
  17.3 0.0 collective-permute-done.3.rest_0_
  17.3 0.0 copy-done
  17.3 0.0 copy-done.1
  17.3 6.4 %filter.3 = (bf16[128,192,128]{2,1,0:T(8,128)(2,1)S(1)}, bf16[128,192,128]{2,1,0:T(8,128)(2,1)S(1)}, f32[8,128]{1,0:T(8,128)S(1)}) custom-call(s32[96]{0:T(128)S(1)} %copy-done.1, bf16[96,64,128]{2,1,0:T(8,128)(2,1)S(1)} %copy-done, bf16[16,128,128]{2,1,0:T(8,128)(2,1)S(1)} %get-tuple-element.35.left, bf16[16,128,128]{2,1,0:T(8,128)(2,1)S(1)} %get-tuple-element.36.right, ...), custom_call_target="tpu_custom_call" | custom-call | flops 960000000 | bytes 2880000 | tf_op jit(solution)/shard_map/filter/pallas_call | solution.py:225
  23.7 4.8 %collective-permute-done.refs_2_.bins = s32[96]{0:T(128)S(1)} collective-permute-done((s32[96]{0:T(128)}, s32[96]{0:T(128)S(1)}, u32[]{:S(2)}, u32[]{:S(2)}) %collective-permute-start) | collective-permute-done | bytes 416 | tf_op jit(solution)/shard_map/ppermute | solution.py:473
  28.5 0.0 collective-permute-done.2.refs_0_
  28.5 0.1 fusion
  28.6 0.1 collective-permute-start.4
  28.7 0.5 collective-permute-start.5
  29.2 0.1 collective-permute-start.6
  29.3 0.4 collective-permute-start.7
  29.7 0.5 collective-permute-done.4.rest_0_
  30.2 0.4 collective-permute-done.5.rest_1_
  30.6 0.4 collective-permute-done.6.rest_2_
  31.0 0.4 collective-permute-done.7.rest_3_
  31.3 3.5 %filter.4 = (bf16[128,192,128]{2,1,0:T(8,128)(2,1)S(1)}, bf16[128,192,128]{2,1,0:T(8,128)(2,1)S(1)}, f32[8,128]{1,0:T(8,128)S(1)}) custom-call(s32[96]{0:T(128)S(1)} %collective-permute-done.refs_2_.bins, bf16[64,64,128]{2,1,0:T(8,128)(2,1)S(1)} %gate.2.mine, ...), custom_call_target="tpu_custom_call", output_to_operand_aliasing={{0}: (8, {}), {1}: (9, {})} | custom-call | flops 640000000 | bytes 1920000 | tf_op jit(solution)/shard_map/filter/pallas_call | solution.py:225
  34.9 4.6 %collective-permute-done.1.refs_0_ = bf16[32,64,128]{2,1,0:T(8,128)(2,1)S(1)} collective-permute-done((bf16[32,64,128]{2,1,0:T(8,128)(2,1)S(1)}, bf16[32,64,128]{2,1,0:T(8,128)(2,1)S(1)}, u32[]{:S(2)}, u32[]{:S(2)}) %collective-permute-start.1) | collective-permute-done | bytes 524320 | tf_op jit(solution)/shard_map/ppermute | solution.py:472
  39.5 0.0 collective-permute-start.8
  39.5 1.9 %collective-permute-done.8.rest_0_ = bf16[32,64,128]{2,1,0:T(8,128)(2,1)S(1)} collective-permute-done((bf16[32,64,128]{2,1,0:T(8,128)(2,1)S(1)}, bf16[32,64,128]{2,1,0:T(8,128)(2,1)S(1)}, u32[]{:S(2)}, u32[]{:S(2)}) %collective-permute-start.8) | collective-permute-done | bytes 524320 | tf_op jit(solution)/shard_map/ppermute | solution.py:488
  41.4 2.5 %filter.5 = (bf16[128,192,128]{2,1,0:T(8,128)(2,1)S(1)}, bf16[128,192,128]{2,1,0:T(8,128)(2,1)S(1)}, f32[8,128]{1,0:T(8,128)}) custom-call(s32[96]{0:T(128)S(1)} %collective-permute-done.refs_2_.bins, bf16[32,64,128]{2,1,0:T(8,128)(2,1)S(1)} %gate.3.mine, ...), custom_call_target="tpu_custom_call", output_to_operand_aliasing={{0}: (5, {}), {1}: (6, {})} | custom-call | flops 320000000 | bytes 960000 | tf_op jit(solution)/shard_map/filter/pallas_call | solution.py:225
  43.9 3.4 %score.1 = (f32[336,192]{1,0:T(8,128)S(1)}, f32[8,192]{1,0:T(8,128)S(1)}) custom-call(bf16[128,192,128]{2,1,0:T(8,128)(2,1)S(1)} %get-tuple-element.43.plain, bf16[128,336,128]{2,1,0:T(8,128)(2,1)S(1)} %get-tuple-element.44.refs, f32[336,128]{1,0:T(8,128)S(1)} %get-tuple-element.34.after.norm, f32[112,192]{1,0:T(8,128)S(1)} %get-tuple-element.45.mask, ...), custom_call_target="tpu_custom_call" | custom-call | flops 500000000 | bytes 1500000 | tf_op jit(solution)/shard_map/score/pallas_call | solution.py:264
  47.4 1.8 %collective-permute-start.9 = (f32[8,192]{1,0:T(8,128)S(1)}, f32[8,192]{1,0:T(8,128)S(1)}, u32[]{:S(2)}, u32[]{:S(2)}) collective-permute-start(f32[8,192]{1,0:T(8,128)S(1)} %get-tuple-element.48.mine), channel_id=1, source_target_pairs={{0,1},{1,0},{2,3},{3,2},{4,5},{5,4},{6,7},{7,6},{8,9},{9,8},{10,11... | collective-permute-start | bytes 18440 | tf_op jit(solution)/shard_map/ppermute | solution.py:496
  49.2 1.9 %collective-permute-done.9.other = f32[8,192]{1,0:T(8,128)S(1)} collective-permute-done((f32[8,192]{1,0:T(8,128)S(1)}, f32[8,192]{1,0:T(8,128)S(1)}, u32[]{:S(2)}, u32[]{:S(2)}) %collective-permute-start.9) | collective-permute-done | bytes 6176 | tf_op jit(solution)/shard_map/ppermute | solution.py:496
  51.1 0.4 weights.1
  51.5 2.2 %sums.2 = (f32[4,500,128]{2,1,0:T(8,128)S(1)}, bf16[4,500,128]{2,1,0:T(8,128)(2,1)S(1)}) custom-call(bf16[2,112,384]{2,1,0:T(8,128)(2,1)S(1)} %weights.1, bf16[128,192,128]{2,1,0:T(8,128)(2,1)S(1)} %get-tuple-element.43.plain, bf16[128,192,128]{2,1,0:T(8,128)(2,1)S(1)} %get-tuple-element.50.turned), custom_call_target="tpu_custom_call" | custom-call | flops 400000000 | bytes 1200000 | tf_op jit(solution)/shard_map/sums/pallas_call | solution.py:357
  53.7 1.8 %collective-permute-start.10 = (bf16[4,500,128]{2,1,0:T(8,128)(2,1)S(1)}, bf16[4,500,128]{2,1,0:T(8,128)(2,1)S(1)}, u32[]{:S(2)}, u32[]{:S(2)}) collective-permute-start(bf16[4,500,128]{2,1,0:T(8,128)(2,1)S(1)} %get-tuple-element.52.rest_0_), channel_id=1, source_target_pairs={{0,2},{2,0},{4,6},{6,4},{8,10},{10,8},{12,14},{14,12},{1,3},{3,1},... | collective-permute-start | bytes 1536008 | tf_op jit(solution)/shard_map/ppermute | solution.py:499
  55.5 1.1 %sums.3 = (f32[2,300,128]{2,1,0:T(8,128)S(1)}, bf16[2,300,128]{2,1,0:T(8,128)(2,1)S(1)}, bf16[2,300,128]{2,1,0:T(8,128)(2,1)S(1)}, bf16[2,300,128]{2,1,0:T(8,128)(2,1)S(1)}) custom-call(bf16[2,112,384]{2,1,0:T(8,128)(2,1)S(1)} %weights.1, bf16[128,192,128]{2,1,0:T(8,128)(2,1)S(1)} %get-tuple-element.43.plain, ...), custom_call_target="tpu_custom_call" | custom-call | flops 240000000 | bytes 720000 | tf_op jit(solution)/shard_map/sums/pallas_call | solution.py:357
  56.5 2.6 %collective-permute-start.14 = (bf16[2,300,128]{2,1,0:T(8,128)(2,1)S(1)}, bf16[2,300,128]{2,1,0:T(8,128)(2,1)S(1)}, u32[]{:S(2)}, u32[]{:S(2)}) collective-permute-start(bf16[2,300,128]{2,1,0:T(8,128)(2,1)S(1)} %get-tuple-element.58), channel_id=1, source_target_pairs={{0,8},{2,10},{4,12},{6,14},{8,0},{10,2},{12,4},{14,6},{1,9},{3,11}... | collective-permute-start | bytes 460808 | tf_op jit(solution)/shard_map/ppermute | solution.py:499
  59.2 1.4 %collective-permute-start.15 = (bf16[2,300,128]{2,1,0:T(8,128)(2,1)S(1)}, bf16[2,300,128]{2,1,0:T(8,128)(2,1)S(1)}, u32[]{:S(2)}, u32[]{:S(2)}) collective-permute-start(bf16[2,300,128]{2,1,0:T(8,128)(2,1)S(1)} %get-tuple-element.59), channel_id=1, source_target_pairs={{0,12},{2,14},{4,8},{6,10},{8,4},{10,6},{12,0},{14,2},{1,13},{3,15... | collective-permute-start | bytes 460808 | tf_op jit(solution)/shard_map/ppermute | solution.py:499
  60.5 0.2 collective-permute-start.16
  60.8 5.6 %collective-permute-done.10.got = bf16[4,500,128]{2,1,0:T(8,128)(2,1)S(1)} collective-permute-done((bf16[4,500,128]{2,1,0:T(8,128)(2,1)S(1)}, bf16[4,500,128]{2,1,0:T(8,128)(2,1)S(1)}, u32[]{:S(2)}, u32[]{:S(2)}) %collective-permute-start.10) | collective-permute-done | bytes 512032 | tf_op jit(solution)/shard_map/ppermute | solution.py:499
  66.4 0.1 fold.1
  66.5 2.9 %collective-permute-start.11 = (bf16[1,500,128]{2,1,0:T(8,128)(2,1)S(1)}, bf16[1,500,128]{2,1,0:T(8,128)(2,1)S(1)}, u32[]{:S(2)}, u32[]{:S(2)}) collective-permute-start(bf16[1,500,128]{2,1,0:T(8,128)(2,1)S(1)} %get-tuple-element.54), channel_id=1, source_target_pairs={{0,8},{2,10},{4,12},{6,14},{8,0},{10,2},{12,4},{14,6},{1,9},{3,11}... | collective-permute-start | bytes 384008 | tf_op jit(solution)/shard_map/ppermute | solution.py:499
  69.4 1.3 %collective-permute-start.12 = (bf16[1,500,128]{2,1,0:T(8,128)(2,1)S(1)}, bf16[1,500,128]{2,1,0:T(8,128)(2,1)S(1)}, u32[]{:S(2)}, u32[]{:S(2)}) collective-permute-start(bf16[1,500,128]{2,1,0:T(8,128)(2,1)S(1)} %get-tuple-element.55), channel_id=1, source_target_pairs={{0,12},{2,14},{4,8},{6,10},{8,4},{10,6},{12,0},{14,2},{1,13},{3,15... | collective-permute-start | bytes 384008 | tf_op jit(solution)/shard_map/ppermute | solution.py:499
  70.7 0.0 collective-permute-done.14.rest_0_
  70.7 0.2 collective-permute-start.13
  71.0 0.0 collective-permute-done.15.rest_1_
  71.0 0.0 collective-permute-done.16.rest_2_
  71.0 0.1 gather.1
  71.1 1.6 %collective-permute-start.17 = (bf16[1,300,128]{2,1,0:T(8,128)(2,1)S(1)}, bf16[1,300,128]{2,1,0:T(8,128)(2,1)S(1)}, u32[]{:S(2)}, u32[]{:S(2)}) collective-permute-start(bf16[1,300,128]{2,1,0:T(8,128)(2,1)S(1)} %get-tuple-element.62), channel_id=1, source_target_pairs={{0,2},{2,0},{4,6},{6,4},{8,10},{10,8},{12,14},{14,12},{1,3},{3,1},... | collective-permute-start | bytes 230408 | tf_op jit(solution)/shard_map/ppermute | solution.py:499
  72.6 2.9 %collective-permute-done.17.args_5_ = bf16[1,300,128]{2,1,0:T(8,128)(2,1)S(1)} collective-permute-done((bf16[1,300,128]{2,1,0:T(8,128)(2,1)S(1)}, bf16[1,300,128]{2,1,0:T(8,128)(2,1)S(1)}, u32[]{:S(2)}, u32[]{:S(2)}) %collective-permute-start.17) | collective-permute-done | bytes 76832 | tf_op jit(solution)/shard_map/ppermute | solution.py:499
  75.5 6.1 %collective-permute-done.11.args_1_ = bf16[1,500,128]{2,1,0:T(8,128)(2,1)S(1)} collective-permute-done((bf16[1,500,128]{2,1,0:T(8,128)(2,1)S(1)}, bf16[1,500,128]{2,1,0:T(8,128)(2,1)S(1)}, u32[]{:S(2)}, u32[]{:S(2)}) %collective-permute-start.11) | collective-permute-done | bytes 128032 | tf_op jit(solution)/shard_map/ppermute | solution.py:499
  81.6 0.0 collective-permute-done.12.args_2_
  81.6 0.0 collective-permute-done.13.args_3_
  81.6 0.9 %finish.1 = f32[800,128]{1,0:T(8,128)} custom-call(f32[1,500,128]{2,1,0:T(8,128)S(1)} %get-tuple-element.53.args_0_, bf16[1,500,128]{2,1,0:T(8,128)(2,1)S(1)} %collective-permute-done.11.args_1_, bf16[1,500,128]{2,1,0:T(8,128)(2,1)S(1)} %collective-permute-done.12.args_2_, bf16[1,500,128]{2,1,0:T(8,128)(2,1)S(1)} %collective-permute-done.13.args_3_, ...), custom_call_target="tpu_custom_call" | custom-call | flops 100000000 | bytes 300000 | tf_op jit(solution)/shard_map/finish/pallas_call | solution.py:437
  (3 shorter events, 0.0 us)
Async XLA Ops:
  0.0 16.5 %copy-start.6 = (f32[128]{0:T(128)S(1)}, f32[128]{0:T(128)}, u32[]{:S(2)}) copy-start(f32[128]{0:T(128)} %param.11) | copy-start | bytes 1540
  0.0 16.5 %copy-start.5 = (f32[192]{0:T(256)S(1)}, f32[192]{0:T(256)}, u32[]{:S(2)}) copy-start(f32[192]{0:T(256)} %param.15) | copy-start | bytes 2308
  0.0 16.5 %copy-start.4 = (s32[100,3]{0,1:T(4,128)S(1)}, s32[100,3]{0,1:T(4,128)}, u32[]{:S(2)}) copy-start(s32[100,3]{0,1:T(4,128)} %param.13) | copy-start | bytes 3604
  0.0 16.5 %copy-start.3 = (f32[16,128]{1,0:T(8,128)S(1)}, f32[16,128]{1,0:T(8,128)}, u32[]{:S(2)}) copy-start(f32[16,128]{1,0:T(8,128)} %ctf.1) | copy-start | bytes 24580
  0.0 16.5 %copy-start.2 = (s32[192,100]{1,0:T(8,128)S(1)}, s32[192,100]{1,0:T(8,128)}, u32[]{:S(2)}) copy-start(s32[192,100]{1,0:T(8,128)} %mask.1) | copy-start | bytes 230404
  0.0 17.3 %collective-permute-start.3 = (bf16[96,64,128]{2,1,0:T(8,128)(2,1)}, bf16[96,64,128]{2,1,0:T(8,128)(2,1)S(1)}, u32[]{:S(2)}, u32[]{:S(2)}) collective-permute-start(bf16[96,64,128]{2,1,0:T(8,128)(2,1)} %mine.1), channel_id=1, source_target_pairs={{0,16},{16,0},{1,17},{17,1},{2,18},{18,2},{3,19},{19,3},{4,20},{20... | collective-permute-start | bytes 4718600 | tf_op jit(solution)/shard_map/ppermute | solution.py:474
  1.8 15.5 %copy-start = (bf16[96,64,128]{2,1,0:T(8,128)(2,1)S(1)}, bf16[96,64,128]{2,1,0:T(8,128)(2,1)}, u32[]{:S(2)}) copy-start(bf16[96,64,128]{2,1,0:T(8,128)(2,1)} %mine.1) | copy-start | bytes 4718596
  1.9 15.5 %copy-start.1 = (s32[96]{0:T(128)S(1)}, s32[96]{0:T(128)}, u32[]{:S(2)}) copy-start(s32[96]{0:T(128)} %bins.1) | copy-start | bytes 1156
  1.9 26.7 %collective-permute-start.2 = (bf16[64,64,128]{2,1,0:T(8,128)(2,1)S(1)}, bf16[64,64,128]{2,1,0:T(8,128)(2,1)S(1)}, u32[]{:S(2)}, u32[]{:S(2)}) collective-permute-start(bf16[64,64,128]{2,1,0:T(8,128)(2,1)S(1)} %slice.19), channel_id=1, source_target_pairs={{0,1},{1,0},{2,3},{3,2},{4,5},{5,4},{6,7},{7,6},{8,9},{9,8},{10,11... | collective-permute-start | bytes 3145736 | tf_op jit(solution)/shard_map/ppermute | solution.py:472
  4.5 24.1 %collective-permute-start = (s32[96]{0:T(128)}, s32[96]{0:T(128)S(1)}, u32[]{:S(2)}, u32[]{:S(2)}) collective-permute-start(s32[96]{0:T(128)} %bins.1), channel_id=1, source_target_pairs={{0,1},{1,0},{2,3},{3,2},{4,5},{5,4},{6,7},{7,6},{8,9},{9,8},{10,11... | collective-permute-start | bytes 1160 | tf_op jit(solution)/shard_map/ppermute | solution.py:473
  5.6 33.9 %collective-permute-start.1 = (bf16[32,64,128]{2,1,0:T(8,128)(2,1)S(1)}, bf16[32,64,128]{2,1,0:T(8,128)(2,1)S(1)}, u32[]{:S(2)}, u32[]{:S(2)}) collective-permute-start(bf16[32,64,128]{2,1,0:T(8,128)(2,1)S(1)} %slice.18), channel_id=1, source_target_pairs={{0,1},{1,0},{2,3},{3,2},{4,5},{5,4},{6,7},{7,6},{8,9},{9,8},{10,11... | collective-permute-start | bytes 1572872 | tf_op jit(solution)/shard_map/ppermute | solution.py:472
  28.6 1.6 %collective-permute-start.4 = (bf16[16,64,128]{2,1,0:T(8,128)(2,1)S(1)}, bf16[16,64,128]{2,1,0:T(8,128)(2,1)S(1)}, u32[]{:S(2)}, u32[]{:S(2)}) collective-permute-start(bf16[16,64,128]{2,1,0:T(8,128)(2,1)S(1)} %get-tuple-element.66), channel_id=1, source_target_pairs={{0,16},{16,0},{1,17},{17,1},{2,18},{18,2},{3,19},{19,3},{4,20},{20... | collective-permute-start | bytes 786440 | tf_op jit(solution)/shard_map/ppermute | solution.py:488
  28.7 1.9 %collective-permute-start.5 = (bf16[16,64,128]{2,1,0:T(8,128)(2,1)S(1)}, bf16[16,64,128]{2,1,0:T(8,128)(2,1)S(1)}, u32[]{:S(2)}, u32[]{:S(2)}) collective-permute-start(bf16[16,64,128]{2,1,0:T(8,128)(2,1)S(1)} %get-tuple-element.65), channel_id=1, source_target_pairs={{0,16},{16,0},{1,17},{17,1},{2,18},{18,2},{3,19},{19,3},{4,20},{20... | collective-permute-start | bytes 786440 | tf_op jit(solution)/shard_map/ppermute | solution.py:488
  29.2 1.8 %collective-permute-start.6 = (bf16[16,64,128]{2,1,0:T(8,128)(2,1)S(1)}, bf16[16,64,128]{2,1,0:T(8,128)(2,1)S(1)}, u32[]{:S(2)}, u32[]{:S(2)}) collective-permute-start(bf16[16,64,128]{2,1,0:T(8,128)(2,1)S(1)} %get-tuple-element.64), channel_id=1, source_target_pairs={{0,16},{16,0},{1,17},{17,1},{2,18},{18,2},{3,19},{19,3},{4,20},{20... | collective-permute-start | bytes 786440 | tf_op jit(solution)/shard_map/ppermute | solution.py:488
  29.3 2.1 %collective-permute-start.7 = (bf16[16,64,128]{2,1,0:T(8,128)(2,1)S(1)}, bf16[16,64,128]{2,1,0:T(8,128)(2,1)S(1)}, u32[]{:S(2)}, u32[]{:S(2)}) collective-permute-start(bf16[16,64,128]{2,1,0:T(8,128)(2,1)S(1)} %get-tuple-element.63), channel_id=1, source_target_pairs={{0,16},{16,0},{1,17},{17,1},{2,18},{18,2},{3,19},{19,3},{4,20},{20... | collective-permute-start | bytes 786440 | tf_op jit(solution)/shard_map/ppermute | solution.py:488
  39.5 1.9 %collective-permute-start.8 = (bf16[32,64,128]{2,1,0:T(8,128)(2,1)S(1)}, bf16[32,64,128]{2,1,0:T(8,128)(2,1)S(1)}, u32[]{:S(2)}, u32[]{:S(2)}) collective-permute-start(bf16[32,64,128]{2,1,0:T(8,128)(2,1)S(1)} %gate.3.mine), channel_id=1, source_target_pairs={{0,16},{16,0},{1,17},{17,1},{2,18},{18,2},{3,19},{19,3},{4,20},{20... | collective-permute-start | bytes 1572872 | tf_op jit(solution)/shard_map/ppermute | solution.py:488
  47.4 3.7 %collective-permute-start.9 = (f32[8,192]{1,0:T(8,128)S(1)}, f32[8,192]{1,0:T(8,128)S(1)}, u32[]{:S(2)}, u32[]{:S(2)}) collective-permute-start(f32[8,192]{1,0:T(8,128)S(1)} %get-tuple-element.48.mine), channel_id=1, source_target_pairs={{0,1},{1,0},{2,3},{3,2},{4,5},{5,4},{6,7},{7,6},{8,9},{9,8},{10,11... | collective-permute-start | bytes 18440 | tf_op jit(solution)/shard_map/ppermute | solution.py:496
  53.7 12.7 %collective-permute-start.10 = (bf16[4,500,128]{2,1,0:T(8,128)(2,1)S(1)}, bf16[4,500,128]{2,1,0:T(8,128)(2,1)S(1)}, u32[]{:S(2)}, u32[]{:S(2)}) collective-permute-start(bf16[4,500,128]{2,1,0:T(8,128)(2,1)S(1)} %get-tuple-element.52.rest_0_), channel_id=1, source_target_pairs={{0,2},{2,0},{4,6},{6,4},{8,10},{10,8},{12,14},{14,12},{1,3},{3,1},... | collective-permute-start | bytes 1536008 | tf_op jit(solution)/shard_map/ppermute | solution.py:499
  56.5 14.2 %collective-permute-start.14 = (bf16[2,300,128]{2,1,0:T(8,128)(2,1)S(1)}, bf16[2,300,128]{2,1,0:T(8,128)(2,1)S(1)}, u32[]{:S(2)}, u32[]{:S(2)}) collective-permute-start(bf16[2,300,128]{2,1,0:T(8,128)(2,1)S(1)} %get-tuple-element.58), channel_id=1, source_target_pairs={{0,8},{2,10},{4,12},{6,14},{8,0},{10,2},{12,4},{14,6},{1,9},{3,11}... | collective-permute-start | bytes 460808 | tf_op jit(solution)/shard_map/ppermute | solution.py:499
  59.2 11.8 %collective-permute-start.15 = (bf16[2,300,128]{2,1,0:T(8,128)(2,1)S(1)}, bf16[2,300,128]{2,1,0:T(8,128)(2,1)S(1)}, u32[]{:S(2)}, u32[]{:S(2)}) collective-permute-start(bf16[2,300,128]{2,1,0:T(8,128)(2,1)S(1)} %get-tuple-element.59), channel_id=1, source_target_pairs={{0,12},{2,14},{4,8},{6,10},{8,4},{10,6},{12,0},{14,2},{1,13},{3,15... | collective-permute-start | bytes 460808 | tf_op jit(solution)/shard_map/ppermute | solution.py:499
  60.5 10.4 %collective-permute-start.16 = (bf16[2,300,128]{2,1,0:T(8,128)(2,1)S(1)}, bf16[2,300,128]{2,1,0:T(8,128)(2,1)S(1)}, u32[]{:S(2)}, u32[]{:S(2)}) collective-permute-start(bf16[2,300,128]{2,1,0:T(8,128)(2,1)S(1)} %get-tuple-element.60), channel_id=1, source_target_pairs={{0,4},{2,6},{4,0},{6,2},{8,12},{10,14},{12,8},{14,10},{1,5},{3,7},... | collective-permute-start | bytes 460808 | tf_op jit(solution)/shard_map/ppermute | solution.py:499
  66.5 15.1 %collective-permute-start.11 = (bf16[1,500,128]{2,1,0:T(8,128)(2,1)S(1)}, bf16[1,500,128]{2,1,0:T(8,128)(2,1)S(1)}, u32[]{:S(2)}, u32[]{:S(2)}) collective-permute-start(bf16[1,500,128]{2,1,0:T(8,128)(2,1)S(1)} %get-tuple-element.54), channel_id=1, source_target_pairs={{0,8},{2,10},{4,12},{6,14},{8,0},{10,2},{12,4},{14,6},{1,9},{3,11}... | collective-permute-start | bytes 384008 | tf_op jit(solution)/shard_map/ppermute | solution.py:499
  69.4 12.2 %collective-permute-start.12 = (bf16[1,500,128]{2,1,0:T(8,128)(2,1)S(1)}, bf16[1,500,128]{2,1,0:T(8,128)(2,1)S(1)}, u32[]{:S(2)}, u32[]{:S(2)}) collective-permute-start(bf16[1,500,128]{2,1,0:T(8,128)(2,1)S(1)} %get-tuple-element.55), channel_id=1, source_target_pairs={{0,12},{2,14},{4,8},{6,10},{8,4},{10,6},{12,0},{14,2},{1,13},{3,15... | collective-permute-start | bytes 384008 | tf_op jit(solution)/shard_map/ppermute | solution.py:499
  70.7 10.9 %collective-permute-start.13 = (bf16[1,500,128]{2,1,0:T(8,128)(2,1)S(1)}, bf16[1,500,128]{2,1,0:T(8,128)(2,1)S(1)}, u32[]{:S(2)}, u32[]{:S(2)}) collective-permute-start(bf16[1,500,128]{2,1,0:T(8,128)(2,1)S(1)} %get-tuple-element.56), channel_id=1, source_target_pairs={{0,4},{2,6},{4,0},{6,2},{8,12},{10,14},{12,8},{14,10},{1,5},{3,7},... | collective-permute-start | bytes 384008 | tf_op jit(solution)/shard_map/ppermute | solution.py:499
  71.1 4.5 %collective-permute-start.17 = (bf16[1,300,128]{2,1,0:T(8,128)(2,1)S(1)}, bf16[1,300,128]{2,1,0:T(8,128)(2,1)S(1)}, u32[]{:S(2)}, u32[]{:S(2)}) collective-permute-start(bf16[1,300,128]{2,1,0:T(8,128)(2,1)S(1)} %get-tuple-element.62), channel_id=1, source_target_pairs={{0,2},{2,0},{4,6},{6,4},{8,10},{10,8},{12,14},{14,12},{1,3},{3,1},... | collective-permute-start | bytes 230408 | tf_op jit(solution)/shard_map/ppermute | solution.py:499

commit v7 on v6

--- a/solution.py
+++ b/solution.py
@@ -12,7 +12,7 @@
 LOW = -1e30
 GROUP = 16
 PAD = 8
-DEEP = 64
+DEEP = 128
 SUMS = 0.8
 SCALE = 0.1
 FOLD = 1
@@ -187,34 +187,37 @@
     top = lax.axis_index("section") == 0
     pitch = width + PAD
 
-    def group(sib, base, first, turn):
+    def group(base, source, turn):
         scr, scr_t = scratch[2 * turn : 2 * turn + 2]
         for i in range(GROUP):
-            b = bins[skip + first + base + i]
-            a = mine[first + base + i]
-            o = sib[base + i]
+            b = bins[skip + base + i]
+            a = mine[base + i]
+            o = source(i)
             x = jnp.concatenate([jnp.where(top, a, o), jnp.where(top, o, a)], axis=0)
             f = nn(left[b], nn(x, right[b]).astype(BF16))
             scr[pl.ds(i * pitch, width)] = f
             scr_t[pl.ds(i * pitch, width)] = f.T
-        to = pl.multiple_of(at + first + base, GROUP)
+        to = pl.multiple_of(at + base, GROUP)
         for r in range(width):
             plain[r, pl.ds(to, GROUP)] = scr[pl.ds(r, GROUP, stride=pitch)].astype(BF16)
             turned[r, pl.ds(to, GROUP)] = scr_t[pl.ds(r, GROUP, stride=pitch)].astype(BF16)
 
-    first = 0
-    for n, sib in enumerate(sibs):
-        count = sib.shape[0]
-        if count <= 2 * GROUP:
-            for g in range(count // GROUP):
-                group(sib, g * GROUP, first, (n + g) % 2)
-        else:
-
-            @pl.loop(0, count // GROUP)
-            def _(g):
-                group(sib, pl.multiple_of(g * GROUP, GROUP), first, 0)
-
-        first += count
+    groups = mine.shape[0] // GROUP
+    if parts > 1 or groups <= 2:
+        places = [(sib, i) for sib in sibs for i in range(sib.shape[0])]
+        for g in range(groups):
+
+            def source(i, g=g):
+                sib, place = places[g * GROUP + i]
+                return sib[place]
+
+            group(g * GROUP, source, g % 2)
+    else:
+
+        @pl.loop(0, groups)
+        def _(g):
+            base = pl.multiple_of(g * GROUP, GROUP)
+            group(base, lambda i: sibs[0][base + i], 0)
 
 
 def filter_chunk(bins, mine, sibs, left, right, buffers, total, skip, at):
@@ -273,7 +276,7 @@
     )(held(plain), held(refs), held(norm), held(mask), held(noise))
 
 
-def weights_kernel(scaled, mine, other, rot, out):
+def weigh(scaled, mine, other, rot, out):
     rots, padded, _ = rot.shape
     count = scaled.shape[1]
     theirs = jnp.concatenate([other[:, count // 2 :], other[:, : count // 2]], axis=1)
@@ -290,20 +293,14 @@
         out[row] = jnp.concatenate([quarters[q] for q in pair], axis=1).astype(BF16)
 
 
-def make_weights(scaled, mine, other, rot):
-    _, padded, _ = rot.shape
-    count = scaled.shape[1]
-    return pl.pallas_call(
-        weights_kernel,
-        out_shape=pinned((2, padded, 2 * count), BF16),
-        compiler_params=pltpu.CompilerParams(vmem_limit_bytes=8 * MIB),
-        cost_estimate=cost(2),
-        name="weights",
-    )(held(scaled), held(mine), other, held(rot))
-
-
-def sums_kernel(weights, plain, turned, *rest, outer, dom, start, rows, classes):
-    outs = rest[-(dom // 2 if outer else 2) :]
+def sums_kernel(plain, turned, *rest, outer, dom, start, rows, classes):
+    if outer:
+        weights = rest[0]
+        outs = rest[-(dom // 2) :]
+    else:
+        weights = rest[-1]
+        outs = rest[-3:-1]
+        weigh(*rest[:4], weights)
     width = outs[0].shape[2]
     height = plain.shape[0]
     block = height // 2 // dom
@@ -349,22 +346,26 @@
                 keep[g, at] = here
 
 
-def sums(weights, plain, turned, after, outer, dom, start, rows, classes):
+def sums(inputs, plain, turned, after, outer, dom, start, rows, classes):
     width = plain.shape[2]
     vmem = pl.BlockSpec(memory_space=pltpu.VMEM)
     count = 2 if outer else dom // 2
     shape = (count, rows * classes, width)
+    out_shape = [pinned(shape, F32)]
+    out_shape += [jax.ShapeDtypeStruct(shape, BF16)] * (dom // 2 - 1 if outer else 1)
+    if not outer:
+        rot = inputs[3]
+        out_shape.append(pinned((2, rot.shape[1], 2 * plain.shape[1]), BF16))
     return pl.pallas_call(
         functools.partial(
             sums_kernel, outer=outer, dom=dom, start=start, rows=rows, classes=classes
         ),
-        in_specs=[vmem] * 3 + [pl.BlockSpec(memory_space=pl.ANY)] * len(after),
-        out_shape=(pinned(shape, F32),)
-        + (jax.ShapeDtypeStruct(shape, BF16),) * (dom // 2 - 1 if outer else 1),
+        in_specs=[vmem] * (2 + len(inputs)) + [pl.BlockSpec(memory_space=pl.ANY)] * len(after),
+        out_shape=tuple(out_shape),
         compiler_params=pltpu.CompilerParams(vmem_limit_bytes=8 * MIB),
         cost_estimate=cost(SUMS * rows),
         name="sums",
-    )(held(weights), held(plain), held(turned), *after)
+    )(held(plain), held(turned), *inputs, *after)
 
 
 def gather_kernel(keep, *rest, came):
@@ -445,8 +446,9 @@
 
 
 def y_pieces(particles):
-    last = particles // 3 // GROUP * GROUP
-    return (particles - last, last)
+    last = GROUP
+    middle = particles // 3 // GROUP * GROUP
+    return ((particles - middle - last, GROUP), (middle, GROUP // 2), (last, last))
 
 
 def row_pieces(rows, dom):
@@ -467,7 +469,7 @@
     over_cls = functools.partial(lax.ppermute, axis_name="cls", perm=swap)
     over_section = functools.partial(lax.ppermute, axis_name="section", perm=swap)
 
-    sizes = y_pieces(particles)
+    sizes, steps = zip(*y_pieces(particles))
     starts = [sum(sizes[:i]) for i in range(len(sizes))]
     remote = [over_cls(images[a : a + n]) for a, n in zip(starts, sizes)]
     other_bins = over_cls(defocus_bin)
@@ -484,7 +486,7 @@
     tokens = (token, other_bins)
     for i, a in enumerate(starts):
         piece = gate(remote[i], *tokens)
-        step = GROUP if i + 1 < len(starts) else sizes[i]
+        step = steps[i]
         sibs = [over_section(piece[b : b + step]) for b in range(0, sizes[i], step)]
         *buffers, token = filter_chunk(
             other_bins, piece, sibs, left, right, buffers, total, a, particles + a
@@ -493,7 +495,7 @@
     plain, turned = buffers
 
     scaled, stats = score(plain, refs, norm, mask, noise)
-    weights = make_weights(scaled, stats, over_cls(stats), rot)
+    inputs = (held(scaled), held(stats), over_cls(stats), held(rot))
 
     def along(x, mask):
         return lax.ppermute(x, "dom", [(i, i ^ mask) for i in range(dom)])
@@ -503,11 +505,11 @@
         return [along(sends[m], (m + 1) << bit) for m in far_first]
 
     inner, outer = row_pieces(half // dom, dom)
-    keep, send = sums(weights, plain, turned, (), False, dom, 0, inner, classes)
+    keep, send, weights = sums(inputs, plain, turned, (), False, dom, 0, inner, classes)
     got = along(send, 1)
     if outer:
         keep_b, *sends_b = sums(
-            weights, plain, turned, (send,), True, dom, inner, outer, classes
+            (held(weights),), plain, turned, (send,), True, dom, inner, outer, classes
         )
         got_b = spread(sends_b, 1)
     bit = 1

time: 83 us -> 81.5 us (0.982)
  waiting for transfers between devices: 29.5 us -> 25.8 us
  starting transfers between devices: 20.1 us -> 21.9 us
    ppermute x1, waiting for transfers between devices: 4.8 us -> 0.01 us  [local(): other_bins = over_cls(defocus_bin)]
    ppermute x2 -> x3, waiting for transfers between devices: 4.64 us -> 6.23 us  [local(): remote = [over_cls(images[a:a + n]) for a, n in zip(starts, sizes)]]
    ppermute x2 -> x3, starting transfers between devices: 4.61 us -> 5.8 us  [local(): remote = [over_cls(images[a:a + n]) for a, n in zip(starts, sizes)]]
    pallas_call x3 -> x4, Pallas kernels: 12.4 us -> 13.2 us  [filter_chunk(): pl.pallas_call(functools.partial(filter_kernel, parts=parts, skip=skip, a...]
    ppermute x5 -> x8, starting transfers between devices: 1.08 us -> 1.73 us  [local(): sibs = [over_section(piece[b:b + step]) for b in range(0, sizes[i], step)]]
    ppermute x5 -> x8, waiting for transfers between devices: 3.54 us -> 3.03 us  [local(): sibs = [over_section(piece[b:b + step]) for b in range(0, sizes[i], step)]]
    slice x2 -> x3, local copies, waits for them, and re-layouts: 2.37 us -> 2.28 us  [local(): remote = [over_cls(images[a:a + n]) for a, n in zip(starts, sizes)]]
  transfers between devices with their start and end apart: 18 -> 22, of which waited for: 11 -> 13; matrix products, arithmetic and copies ran while one was open for 3% -> 3% of each run, Pallas kernels for 25% -> 27%
where the time goes in v7:
time: 81.5 us; the launch traced here: 81 us
  Pallas kernels  30.6 us (38%)
  waiting for transfers between devices  25.8 us (32%)
  starting transfers between devices  21.9 us (27%)
  local copies, waits for them, and re-layouts  2.4 us (3%)
    ppermute x8, waiting for transfers between devices, along(): return lax.ppermute(x, 'dom', [(i, i ^ mask) for i in range(dom)])  14.7 us
    pallas_call x4, Pallas kernels, filter_chunk(): pl.pallas_call(functools.partial(filter_kernel, parts=parts, skip=skip, a...  13.2 us
    ppermute x8, starting transfers between devices, along(): return lax.ppermute(x, 'dom', [(i, i ^ mask) for i in range(dom)])  12 us
    pallas_call x1, Pallas kernels, lay_refs(): pl.pallas_call(functools.partial(refs_kernel, padded=padded), grid=(rots,...  8.81 us
    ppermute x3, waiting for transfers between devices, local(): remote = [over_cls(images[a:a + n]) for a, n in zip(starts, sizes)]  6.23 us
    ppermute x3, starting transfers between devices, local(): remote = [over_cls(images[a:a + n]) for a, n in zip(starts, sizes)]  5.8 us
    pallas_call x2, Pallas kernels, sums(): pl.pallas_call(functools.partial(sums_kernel, outer=outer, dom=dom, start...  3.62 us
    pallas_call x1, Pallas kernels, score(): pl.pallas_call(score_kernel, out_shape=(pinned((height, count), F32), pin...  3.1 us
  transfers between devices with their start and end apart: 22, of which 13 were waited for; matrix products, arithmetic and copies ran while one was open for 3% of the time, Pallas kernels for 27%

profile of v7, /device:TPU:0, one launch (start us, length us, event | category | flops | bytes accessed | tf_op | source)
XLA Modules:
  0.0 81.0 jit_solution(8958812637407679965)
XLA Ops:
  0.0 0.5 collective-permute-start.4
  0.5 1.2 %slice.32 = bf16[48,64,128]{2,1,0:T(8,128)(2,1)S(1)} slice(bf16[96,64,128]{2,1,0:T(8,128)(2,1)} %mine.1), slice={[0:48], [0:64], [0:128]} | slice | bytes 1572864 | tf_op jit(solution)/shard_map/slice | solution.py:474
  1.7 0.0 copy-start
  1.7 0.0 copy-start.1
  1.8 2.6 %collective-permute-start.3 = (bf16[48,64,128]{2,1,0:T(8,128)(2,1)S(1)}, bf16[48,64,128]{2,1,0:T(8,128)(2,1)S(1)}, u32[]{:S(2)}, u32[]{:S(2)}) collective-permute-start(bf16[48,64,128]{2,1,0:T(8,128)(2,1)S(1)} %slice.32), channel_id=1, source_target_pairs={{0,1},{1,0},{2,3},{3,2},{4,5},{5,4},{6,7},{7,6},{8,9},{9,8},{10,11... | collective-permute-start | bytes 2359304 | tf_op jit(solution)/shard_map/ppermute | solution.py:474
  4.4 0.1 collective-permute-start
  4.4 1.1 %slice.31 = bf16[32,64,128]{2,1,0:T(8,128)(2,1)S(1)} slice(bf16[96,64,128]{2,1,0:T(8,128)(2,1)} %mine.1), slice={[48:80], [0:64], [0:128]} | slice | bytes 1048576 | tf_op jit(solution)/shard_map/slice | solution.py:474
  5.5 2.0 %collective-permute-start.2 = (bf16[32,64,128]{2,1,0:T(8,128)(2,1)S(1)}, bf16[32,64,128]{2,1,0:T(8,128)(2,1)S(1)}, u32[]{:S(2)}, u32[]{:S(2)}) collective-permute-start(bf16[32,64,128]{2,1,0:T(8,128)(2,1)S(1)} %slice.31), channel_id=1, source_target_pairs={{0,1},{1,0},{2,3},{3,2},{4,5},{5,4},{6,7},{7,6},{8,9},{9,8},{10,11... | collective-permute-start | bytes 1572872 | tf_op jit(solution)/shard_map/ppermute | solution.py:474
  7.5 8.8 %refs.2 = (bf16[128,336,128]{2,1,0:T(8,128)(2,1)S(1)}, f32[336,128]{1,0:T(8,128)S(1)}) custom-call(bf16[100,3,128,128]{3,2,1,0:T(8,128)(2,1)} %refs.3), custom_call_target="tpu_custom_call" | custom-call | flops 900000000 | bytes 2700000 | tf_op jit(solution)/shard_map/refs/pallas_call | solution.py:165
  16.3 0.0 copy-done.4
  16.4 0.0 copy-done.3
  16.4 0.0 copy-done.2
  16.4 0.8 %prepare.1 = (bf16[16,128,128]{2,1,0:T(8,128)(2,1)S(1)}, bf16[16,128,128]{2,1,0:T(8,128)(2,1)S(1)}, f32[112,192]{1,0:T(8,128)S(1)}, f32[1,192]{1,0:T(1,128)S(1)}, f32[3,112,128]{2,1,0:T(8,128)S(1)}) custom-call(f32[16,128]{1,0:T(8,128)S(1)} %copy-done.3, f32[1,128]{1,0:T(1,128)S(1)} %bitcast.6, s32[192,100]{1,0:T(8,128)S(1)} %copy-done.2, ...), custom_call_target="tpu_custom_call" | custom-call | flops 300000000 | bytes 900000 | tf_op jit(solution)/shard_map/prepare/pallas_call | solution.py:96
  17.2 0.0 collective-permute-done.4.rest_0_
  17.2 6.4 %filter.4 = (bf16[128,192,128]{2,1,0:T(8,128)(2,1)S(1)}, bf16[128,192,128]{2,1,0:T(8,128)(2,1)S(1)}, f32[8,128]{1,0:T(8,128)S(1)}) custom-call(s32[96]{0:T(128)S(1)} %copy-done.1, bf16[96,64,128]{2,1,0:T(8,128)(2,1)S(1)} %copy-done, bf16[16,128,128]{2,1,0:T(8,128)(2,1)S(1)} %get-tuple-element.39.left, bf16[16,128,128]{2,1,0:T(8,128)(2,1)S(1)} %get-tuple-element.40.right, ...), custom_call_target="tpu_custom_call" | custom-call | flops 960000000 | bytes 2880000 | tf_op jit(solution)/shard_map/filter/pallas_call | solution.py:228
  23.6 0.0 collective-permute-done.refs_2_.bins
  23.6 0.0 collective-permute-done.3.refs_0_
  23.6 0.1 fusion
  23.7 0.1 collective-permute-start.5
  23.8 0.5 collective-permute-start.6
  24.3 0.1 collective-permute-start.7
  24.4 1.2 %collective-permute-start.1 = (bf16[16,64,128]{2,1,0:T(8,128)(2,1)S(1)}, bf16[16,64,128]{2,1,0:T(8,128)(2,1)S(1)}, u32[]{:S(2)}, u32[]{:S(2)}) collective-permute-start(bf16[16,64,128]{2,1,0:T(8,128)(2,1)S(1)} %slice.30), channel_id=1, source_target_pairs={{0,1},{1,0},{2,3},{3,2},{4,5},{5,4},{6,7},{7,6},{8,9},{9,8},{10,11... | collective-permute-start | bytes 786440 | tf_op jit(solution)/shard_map/ppermute | solution.py:474
  25.6 0.0 collective-permute-done.5.rest_0_
  25.6 0.1 collective-permute-done.6.rest_1_
  25.7 0.4 collective-permute-done.7.rest_2_
  26.0 2.8 %filter.5 = (bf16[128,192,128]{2,1,0:T(8,128)(2,1)S(1)}, bf16[128,192,128]{2,1,0:T(8,128)(2,1)S(1)}, f32[8,128]{1,0:T(8,128)S(1)}) custom-call(s32[96]{0:T(128)S(1)} %collective-permute-done.refs_2_.bins, bf16[48,64,128]{2,1,0:T(8,128)(2,1)S(1)} %gate.3.mine, ...), custom_call_target="tpu_custom_call", output_to_operand_aliasing={{0}: (7, {}), {1}: (8, {})} | custom-call | flops 480000000 | bytes 1440000 | tf_op jit(solution)/shard_map/filter/pallas_call | solution.py:228
  28.9 5.1 %collective-permute-done.2.refs_0_ = bf16[32,64,128]{2,1,0:T(8,128)(2,1)S(1)} collective-permute-done((bf16[32,64,128]{2,1,0:T(8,128)(2,1)S(1)}, bf16[32,64,128]{2,1,0:T(8,128)(2,1)S(1)}, u32[]{:S(2)}, u32[]{:S(2)}) %collective-permute-start.2) | collective-permute-done | bytes 524320 | tf_op jit(solution)/shard_map/ppermute | solution.py:474
  34.0 0.1 collective-permute-start.10
  34.1 0.5 collective-permute-start.11
  34.6 0.1 collective-permute-start.8
  34.7 0.4 collective-permute-start.9
  35.1 0.3 collective-permute-done.10.rest_2_
  35.4 0.2 collective-permute-done.11.rest_3_
  35.6 0.3 collective-permute-done.8.rest_0_
  36.0 0.2 collective-permute-done.9.rest_1_
  36.1 2.1 %filter.6 = (bf16[128,192,128]{2,1,0:T(8,128)(2,1)S(1)}, bf16[128,192,128]{2,1,0:T(8,128)(2,1)S(1)}, f32[8,128]{1,0:T(8,128)S(1)}) custom-call(s32[96]{0:T(128)S(1)} %collective-permute-done.refs_2_.bins, bf16[32,64,128]{2,1,0:T(8,128)(2,1)S(1)} %gate.4.mine, ...), custom_call_target="tpu_custom_call", output_to_operand_aliasing={{0}: (8, {}), {1}: (9, {})} | custom-call | flops 320000000 | bytes 960000 | tf_op jit(solution)/shard_map/filter/pallas_call | solution.py:228
  38.3 1.1 %collective-permute-done.1.refs_0_ = bf16[16,64,128]{2,1,0:T(8,128)(2,1)S(1)} collective-permute-done((bf16[16,64,128]{2,1,0:T(8,128)(2,1)S(1)}, bf16[16,64,128]{2,1,0:T(8,128)(2,1)S(1)}, u32[]{:S(2)}, u32[]{:S(2)}) %collective-permute-start.1) | collective-permute-done | bytes 262176 | tf_op jit(solution)/shard_map/ppermute | solution.py:474
  39.4 0.0 collective-permute-start.12
  39.4 1.5 %collective-permute-done.12.rest_0_ = bf16[16,64,128]{2,1,0:T(8,128)(2,1)S(1)} collective-permute-done((bf16[16,64,128]{2,1,0:T(8,128)(2,1)S(1)}, bf16[16,64,128]{2,1,0:T(8,128)(2,1)S(1)}, u32[]{:S(2)}, u32[]{:S(2)}) %collective-permute-start.12) | collective-permute-done | bytes 262176 | tf_op jit(solution)/shard_map/ppermute | solution.py:490
  41.0 1.9 %filter.7 = (bf16[128,192,128]{2,1,0:T(8,128)(2,1)S(1)}, bf16[128,192,128]{2,1,0:T(8,128)(2,1)S(1)}, f32[8,128]{1,0:T(8,128)}) custom-call(s32[96]{0:T(128)S(1)} %collective-permute-done.refs_2_.bins, bf16[16,64,128]{2,1,0:T(8,128)(2,1)S(1)} %gate.5.mine, ...), custom_call_target="tpu_custom_call", output_to_operand_aliasing={{0}: (5, {}), {1}: (6, {})} | custom-call | flops 160000000 | bytes 480000 | tf_op jit(solution)/shard_map/filter/pallas_call | solution.py:228
  42.8 3.1 %score.1 = (f32[336,192]{1,0:T(8,128)S(1)}, f32[8,192]{1,0:T(8,128)S(1)}) custom-call(bf16[128,192,128]{2,1,0:T(8,128)(2,1)S(1)} %get-tuple-element.50.plain, bf16[128,336,128]{2,1,0:T(8,128)(2,1)S(1)} %get-tuple-element.52.refs, f32[336,128]{1,0:T(8,128)S(1)} %get-tuple-element.38.after.norm, f32[112,192]{1,0:T(8,128)S(1)} %get-tuple-element.53.mask, ...), custom_call_target="tpu_custom_call" | custom-call | flops 500000000 | bytes 1500000 | tf_op jit(solution)/shard_map/score/pallas_call | solution.py:267
  45.9 1.8 %collective-permute-start.13 = (f32[8,192]{1,0:T(8,128)S(1)}, f32[8,192]{1,0:T(8,128)S(1)}, u32[]{:S(2)}, u32[]{:S(2)}) collective-permute-start(f32[8,192]{1,0:T(8,128)S(1)} %get-tuple-element.56.rest_1_), channel_id=1, source_target_pairs={{0,1},{1,0},{2,3},{3,2},{4,5},{5,4},{6,7},{7,6},{8,9},{9,8},{10,11... | collective-permute-start | bytes 18440 | tf_op jit(solution)/shard_map/ppermute | solution.py:498
  47.7 1.9 %collective-permute-done.13.rest_2_ = f32[8,192]{1,0:T(8,128)S(1)} collective-permute-done((f32[8,192]{1,0:T(8,128)S(1)}, f32[8,192]{1,0:T(8,128)S(1)}, u32[]{:S(2)}, u32[]{:S(2)}) %collective-permute-start.13) | collective-permute-done | bytes 6176 | tf_op jit(solution)/shard_map/ppermute | solution.py:498
  49.6 2.6 %sums.2 = (f32[4,500,128]{2,1,0:T(8,128)S(1)}, bf16[4,500,128]{2,1,0:T(8,128)(2,1)S(1)}, bf16[2,112,384]{2,1,0:T(8,128)(2,1)S(1)}) custom-call(bf16[128,192,128]{2,1,0:T(8,128)(2,1)S(1)} %get-tuple-element.50.plain, bf16[128,192,128]{2,1,0:T(8,128)(2,1)S(1)} %get-tuple-element.51.turned, f32[336,192]{1,0:T(8,128)S(1)} %get-tuple-element.55.rest_0_, ...), custom_call_target="tpu_custom_call" | custom-call | flops 400000000 | bytes 1200000 | tf_op jit(solution)/shard_map/sums/pallas_call | solution.py:359
  52.2 1.8 %collective-permute-start.14 = (bf16[4,500,128]{2,1,0:T(8,128)(2,1)S(1)}, bf16[4,500,128]{2,1,0:T(8,128)(2,1)S(1)}, u32[]{:S(2)}, u32[]{:S(2)}) collective-permute-start(bf16[4,500,128]{2,1,0:T(8,128)(2,1)S(1)} %get-tuple-element.59.rest_1_), channel_id=1, source_target_pairs={{0,2},{2,0},{4,6},{6,4},{8,10},{10,8},{12,14},{14,12},{1,3},{3,1},... | collective-permute-start | bytes 1536008 | tf_op jit(solution)/shard_map/ppermute | solution.py:501
  54.0 1.1 %sums.3 = (f32[2,300,128]{2,1,0:T(8,128)S(1)}, bf16[2,300,128]{2,1,0:T(8,128)(2,1)S(1)}, bf16[2,300,128]{2,1,0:T(8,128)(2,1)S(1)}, bf16[2,300,128]{2,1,0:T(8,128)(2,1)S(1)}) custom-call(bf16[128,192,128]{2,1,0:T(8,128)(2,1)S(1)} %get-tuple-element.50.plain, bf16[128,192,128]{2,1,0:T(8,128)(2,1)S(1)} %get-tuple-element.51.turned, ...), custom_call_target="tpu_custom_call" | custom-call | flops 240000000 | bytes 720000 | tf_op jit(solution)/shard_map/sums/pallas_call | solution.py:359
  55.0 2.7 %collective-permute-start.18 = (bf16[2,300,128]{2,1,0:T(8,128)(2,1)S(1)}, bf16[2,300,128]{2,1,0:T(8,128)(2,1)S(1)}, u32[]{:S(2)}, u32[]{:S(2)}) collective-permute-start(bf16[2,300,128]{2,1,0:T(8,128)(2,1)S(1)} %get-tuple-element.66), channel_id=1, source_target_pairs={{0,8},{2,10},{4,12},{6,14},{8,0},{10,2},{12,4},{14,6},{1,9},{3,11}... | collective-permute-start | bytes 460808 | tf_op jit(solution)/shard_map/ppermute | solution.py:501
  57.7 1.3 %collective-permute-start.19 = (bf16[2,300,128]{2,1,0:T(8,128)(2,1)S(1)}, bf16[2,300,128]{2,1,0:T(8,128)(2,1)S(1)}, u32[]{:S(2)}, u32[]{:S(2)}) collective-permute-start(bf16[2,300,128]{2,1,0:T(8,128)(2,1)S(1)} %get-tuple-element.67), channel_id=1, source_target_pairs={{0,12},{2,14},{4,8},{6,10},{8,4},{10,6},{12,0},{14,2},{1,13},{3,15... | collective-permute-start | bytes 460808 | tf_op jit(solution)/shard_map/ppermute | solution.py:501
  59.0 0.2 collective-permute-start.20
  59.3 5.6 %collective-permute-done.14.got = bf16[4,500,128]{2,1,0:T(8,128)(2,1)S(1)} collective-permute-done((bf16[4,500,128]{2,1,0:T(8,128)(2,1)S(1)}, bf16[4,500,128]{2,1,0:T(8,128)(2,1)S(1)}, u32[]{:S(2)}, u32[]{:S(2)}) %collective-permute-start.14) | collective-permute-done | bytes 512032 | tf_op jit(solution)/shard_map/ppermute | solution.py:501
  64.9 0.1 fold.1
  65.1 2.9 %collective-permute-start.15 = (bf16[1,500,128]{2,1,0:T(8,128)(2,1)S(1)}, bf16[1,500,128]{2,1,0:T(8,128)(2,1)S(1)}, u32[]{:S(2)}, u32[]{:S(2)}) collective-permute-start(bf16[1,500,128]{2,1,0:T(8,128)(2,1)S(1)} %get-tuple-element.61), channel_id=1, source_target_pairs={{0,8},{2,10},{4,12},{6,14},{8,0},{10,2},{12,4},{14,6},{1,9},{3,11}... | collective-permute-start | bytes 384008 | tf_op jit(solution)/shard_map/ppermute | solution.py:501
  67.9 1.4 %collective-permute-start.16 = (bf16[1,500,128]{2,1,0:T(8,128)(2,1)S(1)}, bf16[1,500,128]{2,1,0:T(8,128)(2,1)S(1)}, u32[]{:S(2)}, u32[]{:S(2)}) collective-permute-start(bf16[1,500,128]{2,1,0:T(8,128)(2,1)S(1)} %get-tuple-element.62), channel_id=1, source_target_pairs={{0,12},{2,14},{4,8},{6,10},{8,4},{10,6},{12,0},{14,2},{1,13},{3,15... | collective-permute-start | bytes 384008 | tf_op jit(solution)/shard_map/ppermute | solution.py:501
  69.3 0.0 collective-permute-done.18.rest_0_
  69.3 0.2 collective-permute-start.17
  69.5 0.0 collective-permute-done.19.rest_1_
  69.5 0.0 collective-permute-done.20.rest_2_
  69.5 0.1 gather.1
  69.6 1.6 %collective-permute-start.21 = (bf16[1,300,128]{2,1,0:T(8,128)(2,1)S(1)}, bf16[1,300,128]{2,1,0:T(8,128)(2,1)S(1)}, u32[]{:S(2)}, u32[]{:S(2)}) collective-permute-start(bf16[1,300,128]{2,1,0:T(8,128)(2,1)S(1)} %get-tuple-element.70), channel_id=1, source_target_pairs={{0,2},{2,0},{4,6},{6,4},{8,10},{10,8},{12,14},{14,12},{1,3},{3,1},... | collective-permute-start | bytes 230408 | tf_op jit(solution)/shard_map/ppermute | solution.py:501
  71.1 2.9 %collective-permute-done.21.args_5_ = bf16[1,300,128]{2,1,0:T(8,128)(2,1)S(1)} collective-permute-done((bf16[1,300,128]{2,1,0:T(8,128)(2,1)S(1)}, bf16[1,300,128]{2,1,0:T(8,128)(2,1)S(1)}, u32[]{:S(2)}, u32[]{:S(2)}) %collective-permute-start.21) | collective-permute-done | bytes 76832 | tf_op jit(solution)/shard_map/ppermute | solution.py:501
  74.0 6.1 %collective-permute-done.15.args_1_ = bf16[1,500,128]{2,1,0:T(8,128)(2,1)S(1)} collective-permute-done((bf16[1,500,128]{2,1,0:T(8,128)(2,1)S(1)}, bf16[1,500,128]{2,1,0:T(8,128)(2,1)S(1)}, u32[]{:S(2)}, u32[]{:S(2)}) %collective-permute-start.15) | collective-permute-done | bytes 128032 | tf_op jit(solution)/shard_map/ppermute | solution.py:501
  80.1 0.0 collective-permute-done.16.args_2_
  80.1 0.0 collective-permute-done.17.args_3_
  80.1 0.9 %finish.1 = f32[800,128]{1,0:T(8,128)} custom-call(f32[1,500,128]{2,1,0:T(8,128)S(1)} %get-tuple-element.60.args_0_, bf16[1,500,128]{2,1,0:T(8,128)(2,1)S(1)} %collective-permute-done.15.args_1_, bf16[1,500,128]{2,1,0:T(8,128)(2,1)S(1)} %collective-permute-done.16.args_2_, bf16[1,500,128]{2,1,0:T(8,128)(2,1)S(1)} %collective-permute-done.17.args_3_, ...), custom_call_target="tpu_custom_call" | custom-call | flops 100000000 | bytes 300000 | tf_op jit(solution)/shard_map/finish/pallas_call | solution.py:438
  (14 shorter events, 0.1 us)
Async XLA Ops:
  0.0 16.3 %copy-start.6 = (f32[128]{0:T(128)S(1)}, f32[128]{0:T(128)}, u32[]{:S(2)}) copy-start(f32[128]{0:T(128)} %param.11) | copy-start | bytes 1540
  0.0 16.3 %copy-start.5 = (f32[192]{0:T(256)S(1)}, f32[192]{0:T(256)}, u32[]{:S(2)}) copy-start(f32[192]{0:T(256)} %param.15) | copy-start | bytes 2308
  0.0 16.3 %copy-start.4 = (s32[100,3]{0,1:T(4,128)S(1)}, s32[100,3]{0,1:T(4,128)}, u32[]{:S(2)}) copy-start(s32[100,3]{0,1:T(4,128)} %param.13) | copy-start | bytes 3604
  0.0 16.3 %copy-start.3 = (f32[16,128]{1,0:T(8,128)S(1)}, f32[16,128]{1,0:T(8,128)}, u32[]{:S(2)}) copy-start(f32[16,128]{1,0:T(8,128)} %ctf.1) | copy-start | bytes 24580
  0.0 16.4 %copy-start.2 = (s32[192,100]{1,0:T(8,128)S(1)}, s32[192,100]{1,0:T(8,128)}, u32[]{:S(2)}) copy-start(s32[192,100]{1,0:T(8,128)} %mask.1) | copy-start | bytes 230404
  0.0 17.2 %collective-permute-start.4 = (bf16[96,64,128]{2,1,0:T(8,128)(2,1)}, bf16[96,64,128]{2,1,0:T(8,128)(2,1)S(1)}, u32[]{:S(2)}, u32[]{:S(2)}) collective-permute-start(bf16[96,64,128]{2,1,0:T(8,128)(2,1)} %mine.1), channel_id=1, source_target_pairs={{0,16},{16,0},{1,17},{17,1},{2,18},{18,2},{3,19},{19,3},{4,20},{20... | collective-permute-start | bytes 4718600 | tf_op jit(solution)/shard_map/ppermute | solution.py:476
  1.7 15.5 %copy-start = (bf16[96,64,128]{2,1,0:T(8,128)(2,1)S(1)}, bf16[96,64,128]{2,1,0:T(8,128)(2,1)}, u32[]{:S(2)}) copy-start(bf16[96,64,128]{2,1,0:T(8,128)(2,1)} %mine.1) | copy-start | bytes 4718596
  1.7 15.5 %copy-start.1 = (s32[96]{0:T(128)S(1)}, s32[96]{0:T(128)}, u32[]{:S(2)}) copy-start(s32[96]{0:T(128)} %bins.1) | copy-start | bytes 1156
  1.8 21.9 %collective-permute-start.3 = (bf16[48,64,128]{2,1,0:T(8,128)(2,1)S(1)}, bf16[48,64,128]{2,1,0:T(8,128)(2,1)S(1)}, u32[]{:S(2)}, u32[]{:S(2)}) collective-permute-start(bf16[48,64,128]{2,1,0:T(8,128)(2,1)S(1)} %slice.32), channel_id=1, source_target_pairs={{0,1},{1,0},{2,3},{3,2},{4,5},{5,4},{6,7},{7,6},{8,9},{9,8},{10,11... | collective-permute-start | bytes 2359304 | tf_op jit(solution)/shard_map/ppermute | solution.py:474
  4.4 19.2 %collective-permute-start = (s32[96]{0:T(128)}, s32[96]{0:T(128)S(1)}, u32[]{:S(2)}, u32[]{:S(2)}) collective-permute-start(s32[96]{0:T(128)} %bins.1), channel_id=1, source_target_pairs={{0,1},{1,0},{2,3},{3,2},{4,5},{5,4},{6,7},{7,6},{8,9},{9,8},{10,11... | collective-permute-start | bytes 1160 | tf_op jit(solution)/shard_map/ppermute | solution.py:475
  5.5 28.5 %collective-permute-start.2 = (bf16[32,64,128]{2,1,0:T(8,128)(2,1)S(1)}, bf16[32,64,128]{2,1,0:T(8,128)(2,1)S(1)}, u32[]{:S(2)}, u32[]{:S(2)}) collective-permute-start(bf16[32,64,128]{2,1,0:T(8,128)(2,1)S(1)} %slice.31), channel_id=1, source_target_pairs={{0,1},{1,0},{2,3},{3,2},{4,5},{5,4},{6,7},{7,6},{8,9},{9,8},{10,11... | collective-permute-start | bytes 1572872 | tf_op jit(solution)/shard_map/ppermute | solution.py:474
  23.7 1.9 %collective-permute-start.5 = (bf16[16,64,128]{2,1,0:T(8,128)(2,1)S(1)}, bf16[16,64,128]{2,1,0:T(8,128)(2,1)S(1)}, u32[]{:S(2)}, u32[]{:S(2)}) collective-permute-start(bf16[16,64,128]{2,1,0:T(8,128)(2,1)S(1)} %get-tuple-element.73), channel_id=1, source_target_pairs={{0,16},{16,0},{1,17},{17,1},{2,18},{18,2},{3,19},{19,3},{4,20},{20... | collective-permute-start | bytes 786440 | tf_op jit(solution)/shard_map/ppermute | solution.py:490
  23.8 1.9 %collective-permute-start.6 = (bf16[16,64,128]{2,1,0:T(8,128)(2,1)S(1)}, bf16[16,64,128]{2,1,0:T(8,128)(2,1)S(1)}, u32[]{:S(2)}, u32[]{:S(2)}) collective-permute-start(bf16[16,64,128]{2,1,0:T(8,128)(2,1)S(1)} %get-tuple-element.72), channel_id=1, source_target_pairs={{0,16},{16,0},{1,17},{17,1},{2,18},{18,2},{3,19},{19,3},{4,20},{20... | collective-permute-start | bytes 786440 | tf_op jit(solution)/shard_map/ppermute | solution.py:490
  24.3 1.8 %collective-permute-start.7 = (bf16[16,64,128]{2,1,0:T(8,128)(2,1)S(1)}, bf16[16,64,128]{2,1,0:T(8,128)(2,1)S(1)}, u32[]{:S(2)}, u32[]{:S(2)}) collective-permute-start(bf16[16,64,128]{2,1,0:T(8,128)(2,1)S(1)} %get-tuple-element.71), channel_id=1, source_target_pairs={{0,16},{16,0},{1,17},{17,1},{2,18},{18,2},{3,19},{19,3},{4,20},{20... | collective-permute-start | bytes 786440 | tf_op jit(solution)/shard_map/ppermute | solution.py:490
  24.4 15.1 %collective-permute-start.1 = (bf16[16,64,128]{2,1,0:T(8,128)(2,1)S(1)}, bf16[16,64,128]{2,1,0:T(8,128)(2,1)S(1)}, u32[]{:S(2)}, u32[]{:S(2)}) collective-permute-start(bf16[16,64,128]{2,1,0:T(8,128)(2,1)S(1)} %slice.30), channel_id=1, source_target_pairs={{0,1},{1,0},{2,3},{3,2},{4,5},{5,4},{6,7},{7,6},{8,9},{9,8},{10,11... | collective-permute-start | bytes 786440 | tf_op jit(solution)/shard_map/ppermute | solution.py:474
  34.0 1.4 %collective-permute-start.10 = (bf16[8,64,128]{2,1,0:T(8,128)(2,1)S(1)}, bf16[8,64,128]{2,1,0:T(8,128)(2,1)S(1)}, u32[]{:S(2)}, u32[]{:S(2)}) collective-permute-start(bf16[8,64,128]{2,1,0:T(8,128)(2,1)S(1)} %get-tuple-element.75), channel_id=1, source_target_pairs={{0,16},{16,0},{1,17},{17,1},{2,18},{18,2},{3,19},{19,3},{4,20},{20... | collective-permute-start | bytes 393224 | tf_op jit(solution)/shard_map/ppermute | solution.py:490
  34.1 1.5 %collective-permute-start.11 = (bf16[8,64,128]{2,1,0:T(8,128)(2,1)S(1)}, bf16[8,64,128]{2,1,0:T(8,128)(2,1)S(1)}, u32[]{:S(2)}, u32[]{:S(2)}) collective-permute-start(bf16[8,64,128]{2,1,0:T(8,128)(2,1)S(1)} %get-tuple-element.74), channel_id=1, source_target_pairs={{0,16},{16,0},{1,17},{17,1},{2,18},{18,2},{3,19},{19,3},{4,20},{20... | collective-permute-start | bytes 393224 | tf_op jit(solution)/shard_map/ppermute | solution.py:490
  34.6 1.3 %collective-permute-start.8 = (bf16[8,64,128]{2,1,0:T(8,128)(2,1)S(1)}, bf16[8,64,128]{2,1,0:T(8,128)(2,1)S(1)}, u32[]{:S(2)}, u32[]{:S(2)}) collective-permute-start(bf16[8,64,128]{2,1,0:T(8,128)(2,1)S(1)} %get-tuple-element.77), channel_id=1, source_target_pairs={{0,16},{16,0},{1,17},{17,1},{2,18},{18,2},{3,19},{19,3},{4,20},{20... | collective-permute-start | bytes 393224 | tf_op jit(solution)/shard_map/ppermute | solution.py:490
  34.7 1.5 %collective-permute-start.9 = (bf16[8,64,128]{2,1,0:T(8,128)(2,1)S(1)}, bf16[8,64,128]{2,1,0:T(8,128)(2,1)S(1)}, u32[]{:S(2)}, u32[]{:S(2)}) collective-permute-start(bf16[8,64,128]{2,1,0:T(8,128)(2,1)S(1)} %get-tuple-element.76), channel_id=1, source_target_pairs={{0,16},{16,0},{1,17},{17,1},{2,18},{18,2},{3,19},{19,3},{4,20},{20... | collective-permute-start | bytes 393224 | tf_op jit(solution)/shard_map/ppermute | solution.py:490
  39.4 1.5 %collective-permute-start.12 = (bf16[16,64,128]{2,1,0:T(8,128)(2,1)S(1)}, bf16[16,64,128]{2,1,0:T(8,128)(2,1)S(1)}, u32[]{:S(2)}, u32[]{:S(2)}) collective-permute-start(bf16[16,64,128]{2,1,0:T(8,128)(2,1)S(1)} %gate.5.mine), channel_id=1, source_target_pairs={{0,16},{16,0},{1,17},{17,1},{2,18},{18,2},{3,19},{19,3},{4,20},{20... | collective-permute-start | bytes 786440 | tf_op jit(solution)/shard_map/ppermute | solution.py:490
  45.9 3.7 %collective-permute-start.13 = (f32[8,192]{1,0:T(8,128)S(1)}, f32[8,192]{1,0:T(8,128)S(1)}, u32[]{:S(2)}, u32[]{:S(2)}) collective-permute-start(f32[8,192]{1,0:T(8,128)S(1)} %get-tuple-element.56.rest_1_), channel_id=1, source_target_pairs={{0,1},{1,0},{2,3},{3,2},{4,5},{5,4},{6,7},{7,6},{8,9},{9,8},{10,11... | collective-permute-start | bytes 18440 | tf_op jit(solution)/shard_map/ppermute | solution.py:498
  52.2 12.7 %collective-permute-start.14 = (bf16[4,500,128]{2,1,0:T(8,128)(2,1)S(1)}, bf16[4,500,128]{2,1,0:T(8,128)(2,1)S(1)}, u32[]{:S(2)}, u32[]{:S(2)}) collective-permute-start(bf16[4,500,128]{2,1,0:T(8,128)(2,1)S(1)} %get-tuple-element.59.rest_1_), channel_id=1, source_target_pairs={{0,2},{2,0},{4,6},{6,4},{8,10},{10,8},{12,14},{14,12},{1,3},{3,1},... | collective-permute-start | bytes 1536008 | tf_op jit(solution)/shard_map/ppermute | solution.py:501
  55.0 14.2 %collective-permute-start.18 = (bf16[2,300,128]{2,1,0:T(8,128)(2,1)S(1)}, bf16[2,300,128]{2,1,0:T(8,128)(2,1)S(1)}, u32[]{:S(2)}, u32[]{:S(2)}) collective-permute-start(bf16[2,300,128]{2,1,0:T(8,128)(2,1)S(1)} %get-tuple-element.66), channel_id=1, source_target_pairs={{0,8},{2,10},{4,12},{6,14},{8,0},{10,2},{12,4},{14,6},{1,9},{3,11}... | collective-permute-start | bytes 460808 | tf_op jit(solution)/shard_map/ppermute | solution.py:501
  57.7 11.8 %collective-permute-start.19 = (bf16[2,300,128]{2,1,0:T(8,128)(2,1)S(1)}, bf16[2,300,128]{2,1,0:T(8,128)(2,1)S(1)}, u32[]{:S(2)}, u32[]{:S(2)}) collective-permute-start(bf16[2,300,128]{2,1,0:T(8,128)(2,1)S(1)} %get-tuple-element.67), channel_id=1, source_target_pairs={{0,12},{2,14},{4,8},{6,10},{8,4},{10,6},{12,0},{14,2},{1,13},{3,15... | collective-permute-start | bytes 460808 | tf_op jit(solution)/shard_map/ppermute | solution.py:501
  59.0 10.4 %collective-permute-start.20 = (bf16[2,300,128]{2,1,0:T(8,128)(2,1)S(1)}, bf16[2,300,128]{2,1,0:T(8,128)(2,1)S(1)}, u32[]{:S(2)}, u32[]{:S(2)}) collective-permute-start(bf16[2,300,128]{2,1,0:T(8,128)(2,1)S(1)} %get-tuple-element.68), channel_id=1, source_target_pairs={{0,4},{2,6},{4,0},{6,2},{8,12},{10,14},{12,8},{14,10},{1,5},{3,7},... | collective-permute-start | bytes 460808 | tf_op jit(solution)/shard_map/ppermute | solution.py:501
  65.1 15.1 %collective-permute-start.15 = (bf16[1,500,128]{2,1,0:T(8,128)(2,1)S(1)}, bf16[1,500,128]{2,1,0:T(8,128)(2,1)S(1)}, u32[]{:S(2)}, u32[]{:S(2)}) collective-permute-start(bf16[1,500,128]{2,1,0:T(8,128)(2,1)S(1)} %get-tuple-element.61), channel_id=1, source_target_pairs={{0,8},{2,10},{4,12},{6,14},{8,0},{10,2},{12,4},{14,6},{1,9},{3,11}... | collective-permute-start | bytes 384008 | tf_op jit(solution)/shard_map/ppermute | solution.py:501
  67.9 12.2 %collective-permute-start.16 = (bf16[1,500,128]{2,1,0:T(8,128)(2,1)S(1)}, bf16[1,500,128]{2,1,0:T(8,128)(2,1)S(1)}, u32[]{:S(2)}, u32[]{:S(2)}) collective-permute-start(bf16[1,500,128]{2,1,0:T(8,128)(2,1)S(1)} %get-tuple-element.62), channel_id=1, source_target_pairs={{0,12},{2,14},{4,8},{6,10},{8,4},{10,6},{12,0},{14,2},{1,13},{3,15... | collective-permute-start | bytes 384008 | tf_op jit(solution)/shard_map/ppermute | solution.py:501
  69.3 10.9 %collective-permute-start.17 = (bf16[1,500,128]{2,1,0:T(8,128)(2,1)S(1)}, bf16[1,500,128]{2,1,0:T(8,128)(2,1)S(1)}, u32[]{:S(2)}, u32[]{:S(2)}) collective-permute-start(bf16[1,500,128]{2,1,0:T(8,128)(2,1)S(1)} %get-tuple-element.63), channel_id=1, source_target_pairs={{0,4},{2,6},{4,0},{6,2},{8,12},{10,14},{12,8},{14,10},{1,5},{3,7},... | collective-permute-start | bytes 384008 | tf_op jit(solution)/shard_map/ppermute | solution.py:501
  69.6 4.5 %collective-permute-start.21 = (bf16[1,300,128]{2,1,0:T(8,128)(2,1)S(1)}, bf16[1,300,128]{2,1,0:T(8,128)(2,1)S(1)}, u32[]{:S(2)}, u32[]{:S(2)}) collective-permute-start(bf16[1,300,128]{2,1,0:T(8,128)(2,1)S(1)} %get-tuple-element.70), channel_id=1, source_target_pairs={{0,2},{2,0},{4,6},{6,4},{8,10},{10,8},{12,14},{14,12},{1,3},{3,1},... | collective-permute-start | bytes 230408 | tf_op jit(solution)/shard_map/ppermute | solution.py:501

commit v8 on v7

--- a/solution.py
+++ b/solution.py
@@ -178,11 +178,14 @@
     )(pltpu.with_memory_space_constraint(refs, pltpu.HBM))
 
 
-def filter_kernel(bins, mine, left, right, *rest, parts, skip, at):
+def filter_kernel(*args, picked, parts, skip, at, chained):
+    bins = None if picked else args[0]
+    mine, left, right, *rest = args[0 if picked else 1 :]
     sibs = rest[:parts]
-    plain, turned, token = rest[-7:-4]
+    plain, turned, *token = rest[-6 - chained : -4]
     scratch = rest[-4:]
-    token[...] = jnp.zeros_like(token)
+    for t in token:
+        t[...] = jnp.zeros_like(t)
     width = mine.shape[2]
     top = lax.axis_index("section") == 0
     pitch = width + PAD
@@ -190,7 +193,7 @@
     def group(base, source, turn):
         scr, scr_t = scratch[2 * turn : 2 * turn + 2]
         for i in range(GROUP):
-            b = bins[skip + base + i]
+            b = base + i if picked else bins[skip + base + i]
             a = mine[base + i]
             o = source(i)
             x = jnp.concatenate([jnp.where(top, a, o), jnp.where(top, o, a)], axis=0)
@@ -220,23 +223,46 @@
             group(base, lambda i: sibs[0][base + i], 0)
 
 
-def filter_chunk(bins, mine, sibs, left, right, buffers, total, skip, at):
+def filter_chunk(bins, mine, sibs, left, right, buffers, total, skip, at, chained):
     count, half, width = mine.shape
     smem = pl.BlockSpec(memory_space=pltpu.SMEM)
     vmem = pl.BlockSpec(memory_space=pltpu.VMEM)
     parts = len(sibs)
-    return pl.pallas_call(
-        functools.partial(filter_kernel, parts=parts, skip=skip, at=at),
-        in_specs=[smem] + [vmem] * (3 + parts + len(buffers)),
-        out_specs=(vmem, vmem, vmem),
+    picked = bins is None
+    head = [] if picked else [bins]
+    return pl.pallas_call(
+        functools.partial(
+            filter_kernel, picked=picked, parts=parts, skip=skip, at=at, chained=chained
+        ),
+        in_specs=[smem] * len(head) + [vmem] * (3 + parts + len(buffers)),
+        out_specs=(vmem,) * (2 + chained),
         out_shape=(pinned((2 * half, total, width), BF16),) * 2
-        + (jax.ShapeDtypeStruct((8, width), F32),),
+        + (pinned((8, width), F32),) * chained,
         scratch_shapes=[pltpu.VMEM((GROUP * (2 * half + PAD), width), F32)] * 4,
-        input_output_aliases={4 + parts + i: i for i in range(len(buffers))},
+        input_output_aliases={len(head) + 3 + parts + i: i for i in range(len(buffers))},
         compiler_params=pltpu.CompilerParams(vmem_limit_bytes=8 * MIB),
         cost_estimate=cost(count * 0.1),
         name="filter",
-    )(bins, mine, held(left), held(right), *sibs, *[held(b) for b in buffers])
+    )(*head, mine, held(left), held(right), *sibs, *[held(b) for b in buffers])
+
+
+def pick_kernel(bins, left, right, after, left_out, right_out, *, skip):
+    del after
+    for i in range(left_out.shape[0]):
+        left_out[i] = left[bins[skip + i]]
+        right_out[i] = right[bins[skip + i]]
+
+
+def pick(bins, left, right, after, skip, count):
+    vmem = pl.BlockSpec(memory_space=pltpu.VMEM)
+    return pl.pallas_call(
+        functools.partial(pick_kernel, skip=skip),
+        in_specs=[pl.BlockSpec(memory_space=pltpu.SMEM), vmem, vmem, vmem],
+        out_shape=(pinned((count,) + left.shape[1:], BF16),) * 2,
+        compiler_params=pltpu.CompilerParams(vmem_limit_bytes=4 * MIB),
+        cost_estimate=cost(1),
+        name="pick",
+    )(bins, held(left), held(right), held(after))
 
 
 def score_kernel(plain, refs, norm, mask, noise, scaled, stats):
@@ -481,17 +507,19 @@
     )
     total = 2 * particles
     *buffers, token = filter_chunk(
-        defocus_bin, images, [own_sib], left, right, (), total, 0, 0
+        defocus_bin, images, [own_sib], left, right, (), total, 0, 0, 1
     )
-    tokens = (token, other_bins)
+    chosen = pick(other_bins, left, right, token, starts[-1], sizes[-1])
+    tokens = [chosen[0]]
     for i, a in enumerate(starts):
         piece = gate(remote[i], *tokens)
         step = steps[i]
         sibs = [over_section(piece[b : b + step]) for b in range(0, sizes[i], step)]
-        *buffers, token = filter_chunk(
-            other_bins, piece, sibs, left, right, buffers, total, a, particles + a
-        )
-        tokens = (token,)
+        last = i + 1 == len(starts)
+        filters = (None, piece, sibs, *chosen) if last else (other_bins, piece, sibs, left, right)
+        made = filter_chunk(*filters, buffers, total, a, particles + a, int(not last))
+        buffers = made[:2]
+        tokens = made[2:]
     plain, turned = buffers
 
     scaled, stats = score(plain, refs, norm, mask, noise)

time: 81.5 us -> 80.6 us (0.989)
    pallas_call x4 -> x5, Pallas kernels: 13.2 us -> 12.9 us  [the longest x4 12.3 us: filter_chunk(): pl.pallas_call(functools.partial(filter_kernel, picked=picked, parts=part...]
  transfers between devices with their start and end apart: 22 -> 22, of which waited for: 13 -> 13; matrix products, arithmetic and copies ran while one was open for 3% -> 3% of each run, Pallas kernels for 27% -> 29%
where the time goes in v8:
time: 80.6 us; the launch traced here: 80.1 us
  Pallas kernels  30.4 us (38%)
  waiting for transfers between devices  25.2 us (31%)
  starting transfers between devices  22 us (27%)
  local copies, waits for them, and re-layouts  2.4 us (3%)
    ppermute x8, waiting for transfers between devices, along(): return lax.ppermute(x, 'dom', [(i, i ^ mask) for i in range(dom)])  14.6 us
    pallas_call x4, Pallas kernels, filter_chunk(): pl.pallas_call(functools.partial(filter_kernel, picked=picked, parts=part...  12.3 us
    ppermute x8, starting transfers between devices, along(): return lax.ppermute(x, 'dom', [(i, i ^ mask) for i in range(dom)])  12 us
    pallas_call x1, Pallas kernels, lay_refs(): pl.pallas_call(functools.partial(refs_kernel, padded=padded), grid=(rots,...  8.81 us
    ppermute x3, starting transfers between devices, local(): remote = [over_cls(images[a:a + n]) for a, n in zip(starts, sizes)]  5.82 us
    ppermute x3, waiting for transfers between devices, local(): remote = [over_cls(images[a:a + n]) for a, n in zip(starts, sizes)]  5.61 us
    pallas_call x2, Pallas kernels, sums(): pl.pallas_call(functools.partial(sums_kernel, outer=outer, dom=dom, start...  3.62 us
    pallas_call x1, Pallas kernels, score(): pl.pallas_call(score_kernel, out_shape=(pinned((height, count), F32), pin...  3.11 us
  transfers between devices with their start and end apart: 22, of which 13 were waited for; matrix products, arithmetic and copies ran while one was open for 3% of the time, Pallas kernels for 29%

profile of v8, /device:TPU:0, one launch (start us, length us, event | category | flops | bytes accessed | tf_op | source)
XLA Modules:
  0.0 80.1 jit_solution(10755387152394061342)
XLA Ops:
  0.0 0.5 collective-permute-start.4
  0.5 1.2 %slice.32 = bf16[48,64,128]{2,1,0:T(8,128)(2,1)S(1)} slice(bf16[96,64,128]{2,1,0:T(8,128)(2,1)} %args_1_.4), slice={[0:48], [0:64], [0:128]} | slice | bytes 1572864 | tf_op jit(solution)/shard_map/slice | solution.py:500
  1.7 0.0 copy-start
  1.7 0.0 copy-start.1
  1.8 2.6 %collective-permute-start.3 = (bf16[48,64,128]{2,1,0:T(8,128)(2,1)S(1)}, bf16[48,64,128]{2,1,0:T(8,128)(2,1)S(1)}, u32[]{:S(2)}, u32[]{:S(2)}) collective-permute-start(bf16[48,64,128]{2,1,0:T(8,128)(2,1)S(1)} %slice.32), channel_id=1, source_target_pairs={{0,1},{1,0},{2,3},{3,2},{4,5},{5,4},{6,7},{7,6},{8,9},{9,8},{10,11... | collective-permute-start | bytes 2359304 | tf_op jit(solution)/shard_map/ppermute | solution.py:500
  4.4 0.1 collective-permute-start.1
  4.4 1.1 %slice.31 = bf16[32,64,128]{2,1,0:T(8,128)(2,1)S(1)} slice(bf16[96,64,128]{2,1,0:T(8,128)(2,1)} %args_1_.4), slice={[48:80], [0:64], [0:128]} | slice | bytes 1048576 | tf_op jit(solution)/shard_map/slice | solution.py:500
  5.5 2.0 %collective-permute-start.2 = (bf16[32,64,128]{2,1,0:T(8,128)(2,1)S(1)}, bf16[32,64,128]{2,1,0:T(8,128)(2,1)S(1)}, u32[]{:S(2)}, u32[]{:S(2)}) collective-permute-start(bf16[32,64,128]{2,1,0:T(8,128)(2,1)S(1)} %slice.31), channel_id=1, source_target_pairs={{0,1},{1,0},{2,3},{3,2},{4,5},{5,4},{6,7},{7,6},{8,9},{9,8},{10,11... | collective-permute-start | bytes 1572872 | tf_op jit(solution)/shard_map/ppermute | solution.py:500
  7.5 8.8 %refs.2 = (bf16[128,336,128]{2,1,0:T(8,128)(2,1)S(1)}, f32[336,128]{1,0:T(8,128)S(1)}) custom-call(bf16[100,3,128,128]{3,2,1,0:T(8,128)(2,1)} %refs.3), custom_call_target="tpu_custom_call" | custom-call | flops 900000000 | bytes 2700000 | tf_op jit(solution)/shard_map/refs/pallas_call | solution.py:165
  16.3 0.0 copy-done.4
  16.4 0.0 copy-done.3
  16.4 0.8 %prepare.1 = (bf16[16,128,128]{2,1,0:T(8,128)(2,1)S(1)}, bf16[16,128,128]{2,1,0:T(8,128)(2,1)S(1)}, f32[112,192]{1,0:T(8,128)S(1)}, f32[1,192]{1,0:T(1,128)S(1)}, f32[3,112,128]{2,1,0:T(8,128)S(1)}) custom-call(f32[16,128]{1,0:T(8,128)S(1)} %copy-done.3, f32[1,128]{1,0:T(1,128)S(1)} %bitcast.6, s32[192,100]{1,0:T(8,128)S(1)} %copy-done.2, ...), custom_call_target="tpu_custom_call" | custom-call | flops 300000000 | bytes 900000 | tf_op jit(solution)/shard_map/prepare/pallas_call | solution.py:96
  17.2 0.0 collective-permute-done.4.args_4_
  17.2 6.4 %filter.4 = (bf16[128,192,128]{2,1,0:T(8,128)(2,1)S(1)}, bf16[128,192,128]{2,1,0:T(8,128)(2,1)S(1)}, f32[8,128]{1,0:T(8,128)S(1)}) custom-call(s32[96]{0:T(128)S(1)} %copy-done.1, bf16[96,64,128]{2,1,0:T(8,128)(2,1)S(1)} %copy-done, bf16[16,128,128]{2,1,0:T(8,128)(2,1)S(1)} %get-tuple-element.41.args_2_.left, ...), custom_call_target="tpu_custom_call" | custom-call | flops 960000000 | bytes 2880000 | tf_op jit(solution)/shard_map/filter/pallas_call | solution.py:233
  23.6 0.0 collective-permute-done.1.bins.args_0_
  23.6 0.6 pick.1
  24.2 0.0 collective-permute-done.3.refs_0_
  24.3 0.1 fusion
  24.3 0.1 collective-permute-start.5
  24.4 0.5 collective-permute-start.6
  24.9 0.1 collective-permute-start.7
  25.0 1.2 %collective-permute-start = (bf16[16,64,128]{2,1,0:T(8,128)(2,1)S(1)}, bf16[16,64,128]{2,1,0:T(8,128)(2,1)S(1)}, u32[]{:S(2)}, u32[]{:S(2)}) collective-permute-start(bf16[16,64,128]{2,1,0:T(8,128)(2,1)S(1)} %slice.30), channel_id=1, source_target_pairs={{0,1},{1,0},{2,3},{3,2},{4,5},{5,4},{6,7},{7,6},{8,9},{9,8},{10,11... | collective-permute-start | bytes 786440 | tf_op jit(solution)/shard_map/ppermute | solution.py:500
  26.2 0.0 collective-permute-done.5.args_4_
  26.2 0.1 collective-permute-done.6.args_5_
  26.3 0.4 collective-permute-done.7.args_6_
  26.7 2.8 %filter.5 = (bf16[128,192,128]{2,1,0:T(8,128)(2,1)S(1)}, bf16[128,192,128]{2,1,0:T(8,128)(2,1)S(1)}, f32[8,128]{1,0:T(8,128)S(1)}) custom-call(s32[96]{0:T(128)S(1)} %collective-permute-done.1.bins.args_0_, bf16[48,64,128]{2,1,0:T(8,128)(2,1)S(1)} %gate.3.args_1_, ...), custom_call_target="tpu_custom_call", output_to_operand_aliasing={{0}: (7, {}), {1}: (8, {})} | custom-call | flops 480000000 | bytes 1440000 | tf_op jit(solution)/shard_map/filter/pallas_call | solution.py:233
  29.5 4.5 %collective-permute-done.2.refs_0_ = bf16[32,64,128]{2,1,0:T(8,128)(2,1)S(1)} collective-permute-done((bf16[32,64,128]{2,1,0:T(8,128)(2,1)S(1)}, bf16[32,64,128]{2,1,0:T(8,128)(2,1)S(1)}, u32[]{:S(2)}, u32[]{:S(2)}) %collective-permute-start.2) | collective-permute-done | bytes 524320 | tf_op jit(solution)/shard_map/ppermute | solution.py:500
  34.0 0.1 collective-permute-start.10
  34.1 0.5 collective-permute-start.11
  34.6 0.1 collective-permute-start.8
  34.7 0.4 collective-permute-start.9
  35.1 0.3 collective-permute-done.10.args_6_
  35.4 0.2 collective-permute-done.11.args_7_
  35.6 0.3 collective-permute-done.8.args_4_
  36.0 0.2 collective-permute-done.9.args_5_
  36.1 2.1 %filter.6 = (bf16[128,192,128]{2,1,0:T(8,128)(2,1)S(1)}, bf16[128,192,128]{2,1,0:T(8,128)(2,1)S(1)}, f32[8,128]{1,0:T(8,128)S(1)}) custom-call(s32[96]{0:T(128)S(1)} %collective-permute-done.1.bins.args_0_, bf16[32,64,128]{2,1,0:T(8,128)(2,1)S(1)} %gate.4.args_1_, ...), custom_call_target="tpu_custom_call", output_to_operand_aliasing={{0}: (8, {}), {1}: (9, {})} | custom-call | flops 320000000 | bytes 960000 | tf_op jit(solution)/shard_map/filter/pallas_call | solution.py:233
  38.3 1.1 %collective-permute-done.refs_0_ = bf16[16,64,128]{2,1,0:T(8,128)(2,1)S(1)} collective-permute-done((bf16[16,64,128]{2,1,0:T(8,128)(2,1)S(1)}, bf16[16,64,128]{2,1,0:T(8,128)(2,1)S(1)}, u32[]{:S(2)}, u32[]{:S(2)}) %collective-permute-start) | collective-permute-done | bytes 262176 | tf_op jit(solution)/shard_map/ppermute | solution.py:500
  39.4 0.0 collective-permute-start.12
  39.4 1.5 %collective-permute-done.12.args_3_ = bf16[16,64,128]{2,1,0:T(8,128)(2,1)S(1)} collective-permute-done((bf16[16,64,128]{2,1,0:T(8,128)(2,1)S(1)}, bf16[16,64,128]{2,1,0:T(8,128)(2,1)S(1)}, u32[]{:S(2)}, u32[]{:S(2)}) %collective-permute-start.12) | collective-permute-done | bytes 262176 | tf_op jit(solution)/shard_map/ppermute | solution.py:517
  41.0 1.0 %filter.7 = (bf16[128,192,128]{2,1,0:T(8,128)(2,1)S(1)}, bf16[128,192,128]{2,1,0:T(8,128)(2,1)S(1)}) custom-call(bf16[16,64,128]{2,1,0:T(8,128)(2,1)S(1)} %gate.5.args_0_, bf16[16,128,128]{2,1,0:T(8,128)(2,1)S(1)} %get-tuple-element.44.refs_1_.args_1_, ...), custom_call_target="tpu_custom_call", output_to_operand_aliasing={{0}: (4, {}), {1}: (5, {})} | custom-call | flops 160000000 | bytes 480000 | tf_op jit(solution)/shard_map/filter/pallas_call | solution.py:233
  41.9 3.1 %score.1 = (f32[336,192]{1,0:T(8,128)S(1)}, f32[8,192]{1,0:T(8,128)S(1)}) custom-call(bf16[128,192,128]{2,1,0:T(8,128)(2,1)S(1)} %get-tuple-element.54.plain, bf16[128,336,128]{2,1,0:T(8,128)(2,1)S(1)} %get-tuple-element.56.refs, f32[336,128]{1,0:T(8,128)S(1)} %get-tuple-element.40.after.norm, f32[112,192]{1,0:T(8,128)S(1)} %get-tuple-element.57.mask, ...), custom_call_target="tpu_custom_call" | custom-call | flops 500000000 | bytes 1500000 | tf_op jit(solution)/shard_map/score/pallas_call | solution.py:293
  45.0 1.8 %collective-permute-start.13 = (f32[8,192]{1,0:T(8,128)S(1)}, f32[8,192]{1,0:T(8,128)S(1)}, u32[]{:S(2)}, u32[]{:S(2)}) collective-permute-start(f32[8,192]{1,0:T(8,128)S(1)} %get-tuple-element.60.rest_1_), channel_id=1, source_target_pairs={{0,1},{1,0},{2,3},{3,2},{4,5},{5,4},{6,7},{7,6},{8,9},{9,8},{10,11... | collective-permute-start | bytes 18440 | tf_op jit(solution)/shard_map/ppermute | solution.py:526
  46.8 1.9 %collective-permute-done.13.rest_2_ = f32[8,192]{1,0:T(8,128)S(1)} collective-permute-done((f32[8,192]{1,0:T(8,128)S(1)}, f32[8,192]{1,0:T(8,128)S(1)}, u32[]{:S(2)}, u32[]{:S(2)}) %collective-permute-start.13) | collective-permute-done | bytes 6176 | tf_op jit(solution)/shard_map/ppermute | solution.py:526
  48.7 2.6 %sums.2 = (f32[4,500,128]{2,1,0:T(8,128)S(1)}, bf16[4,500,128]{2,1,0:T(8,128)(2,1)S(1)}, bf16[2,112,384]{2,1,0:T(8,128)(2,1)S(1)}) custom-call(bf16[128,192,128]{2,1,0:T(8,128)(2,1)S(1)} %get-tuple-element.54.plain, bf16[128,192,128]{2,1,0:T(8,128)(2,1)S(1)} %get-tuple-element.55.turned, f32[336,192]{1,0:T(8,128)S(1)} %get-tuple-element.59.rest_0_, ...), custom_call_target="tpu_custom_call" | custom-call | flops 400000000 | bytes 1200000 | tf_op jit(solution)/shard_map/sums/pallas_call | solution.py:385
  51.3 1.8 %collective-permute-start.14 = (bf16[4,500,128]{2,1,0:T(8,128)(2,1)S(1)}, bf16[4,500,128]{2,1,0:T(8,128)(2,1)S(1)}, u32[]{:S(2)}, u32[]{:S(2)}) collective-permute-start(bf16[4,500,128]{2,1,0:T(8,128)(2,1)S(1)} %get-tuple-element.63.rest_1_), channel_id=1, source_target_pairs={{0,2},{2,0},{4,6},{6,4},{8,10},{10,8},{12,14},{14,12},{1,3},{3,1},... | collective-permute-start | bytes 1536008 | tf_op jit(solution)/shard_map/ppermute | solution.py:529
  53.1 1.1 %sums.3 = (f32[2,300,128]{2,1,0:T(8,128)S(1)}, bf16[2,300,128]{2,1,0:T(8,128)(2,1)S(1)}, bf16[2,300,128]{2,1,0:T(8,128)(2,1)S(1)}, bf16[2,300,128]{2,1,0:T(8,128)(2,1)S(1)}) custom-call(bf16[128,192,128]{2,1,0:T(8,128)(2,1)S(1)} %get-tuple-element.54.plain, bf16[128,192,128]{2,1,0:T(8,128)(2,1)S(1)} %get-tuple-element.55.turned, ...), custom_call_target="tpu_custom_call" | custom-call | flops 240000000 | bytes 720000 | tf_op jit(solution)/shard_map/sums/pallas_call | solution.py:385
  54.2 2.7 %collective-permute-start.18 = (bf16[2,300,128]{2,1,0:T(8,128)(2,1)S(1)}, bf16[2,300,128]{2,1,0:T(8,128)(2,1)S(1)}, u32[]{:S(2)}, u32[]{:S(2)}) collective-permute-start(bf16[2,300,128]{2,1,0:T(8,128)(2,1)S(1)} %get-tuple-element.70), channel_id=1, source_target_pairs={{0,8},{2,10},{4,12},{6,14},{8,0},{10,2},{12,4},{14,6},{1,9},{3,11}... | collective-permute-start | bytes 460808 | tf_op jit(solution)/shard_map/ppermute | solution.py:529
  56.8 1.3 %collective-permute-start.19 = (bf16[2,300,128]{2,1,0:T(8,128)(2,1)S(1)}, bf16[2,300,128]{2,1,0:T(8,128)(2,1)S(1)}, u32[]{:S(2)}, u32[]{:S(2)}) collective-permute-start(bf16[2,300,128]{2,1,0:T(8,128)(2,1)S(1)} %get-tuple-element.71), channel_id=1, source_target_pairs={{0,12},{2,14},{4,8},{6,10},{8,4},{10,6},{12,0},{14,2},{1,13},{3,15... | collective-permute-start | bytes 460808 | tf_op jit(solution)/shard_map/ppermute | solution.py:529
  58.2 0.2 collective-permute-start.20
  58.4 5.6 %collective-permute-done.14.got = bf16[4,500,128]{2,1,0:T(8,128)(2,1)S(1)} collective-permute-done((bf16[4,500,128]{2,1,0:T(8,128)(2,1)S(1)}, bf16[4,500,128]{2,1,0:T(8,128)(2,1)S(1)}, u32[]{:S(2)}, u32[]{:S(2)}) %collective-permute-start.14) | collective-permute-done | bytes 512032 | tf_op jit(solution)/shard_map/ppermute | solution.py:529
  64.0 0.1 fold.1
  64.2 2.9 %collective-permute-start.15 = (bf16[1,500,128]{2,1,0:T(8,128)(2,1)S(1)}, bf16[1,500,128]{2,1,0:T(8,128)(2,1)S(1)}, u32[]{:S(2)}, u32[]{:S(2)}) collective-permute-start(bf16[1,500,128]{2,1,0:T(8,128)(2,1)S(1)} %get-tuple-element.65), channel_id=1, source_target_pairs={{0,8},{2,10},{4,12},{6,14},{8,0},{10,2},{12,4},{14,6},{1,9},{3,11}... | collective-permute-start | bytes 384008 | tf_op jit(solution)/shard_map/ppermute | solution.py:529
  67.0 1.4 %collective-permute-start.16 = (bf16[1,500,128]{2,1,0:T(8,128)(2,1)S(1)}, bf16[1,500,128]{2,1,0:T(8,128)(2,1)S(1)}, u32[]{:S(2)}, u32[]{:S(2)}) collective-permute-start(bf16[1,500,128]{2,1,0:T(8,128)(2,1)S(1)} %get-tuple-element.66), channel_id=1, source_target_pairs={{0,12},{2,14},{4,8},{6,10},{8,4},{10,6},{12,0},{14,2},{1,13},{3,15... | collective-permute-start | bytes 384008 | tf_op jit(solution)/shard_map/ppermute | solution.py:529
  68.4 0.0 collective-permute-done.18.rest_0_
  68.4 0.2 collective-permute-start.17
  68.6 0.0 collective-permute-done.19.rest_1_
  68.6 0.0 collective-permute-done.20.rest_2_
  68.6 0.1 gather.1
  68.7 1.6 %collective-permute-start.21 = (bf16[1,300,128]{2,1,0:T(8,128)(2,1)S(1)}, bf16[1,300,128]{2,1,0:T(8,128)(2,1)S(1)}, u32[]{:S(2)}, u32[]{:S(2)}) collective-permute-start(bf16[1,300,128]{2,1,0:T(8,128)(2,1)S(1)} %get-tuple-element.74), channel_id=1, source_target_pairs={{0,2},{2,0},{4,6},{6,4},{8,10},{10,8},{12,14},{14,12},{1,3},{3,1},... | collective-permute-start | bytes 230408 | tf_op jit(solution)/shard_map/ppermute | solution.py:529
  70.2 2.9 %collective-permute-done.21.args_5_ = bf16[1,300,128]{2,1,0:T(8,128)(2,1)S(1)} collective-permute-done((bf16[1,300,128]{2,1,0:T(8,128)(2,1)S(1)}, bf16[1,300,128]{2,1,0:T(8,128)(2,1)S(1)}, u32[]{:S(2)}, u32[]{:S(2)}) %collective-permute-start.21) | collective-permute-done | bytes 76832 | tf_op jit(solution)/shard_map/ppermute | solution.py:529
  73.2 6.1 %collective-permute-done.15.args_1_ = bf16[1,500,128]{2,1,0:T(8,128)(2,1)S(1)} collective-permute-done((bf16[1,500,128]{2,1,0:T(8,128)(2,1)S(1)}, bf16[1,500,128]{2,1,0:T(8,128)(2,1)S(1)}, u32[]{:S(2)}, u32[]{:S(2)}) %collective-permute-start.15) | collective-permute-done | bytes 128032 | tf_op jit(solution)/shard_map/ppermute | solution.py:529
  79.2 0.0 collective-permute-done.16.args_2_
  79.2 0.0 collective-permute-done.17.args_3_
  79.2 0.9 %finish.1 = f32[800,128]{1,0:T(8,128)} custom-call(f32[1,500,128]{2,1,0:T(8,128)S(1)} %get-tuple-element.64.args_0_, bf16[1,500,128]{2,1,0:T(8,128)(2,1)S(1)} %collective-permute-done.15.args_1_, bf16[1,500,128]{2,1,0:T(8,128)(2,1)S(1)} %collective-permute-done.16.args_2_, bf16[1,500,128]{2,1,0:T(8,128)(2,1)S(1)} %collective-permute-done.17.args_3_, ...), custom_call_target="tpu_custom_call" | custom-call | flops 100000000 | bytes 300000 | tf_op jit(solution)/shard_map/finish/pallas_call | solution.py:464
  (15 shorter events, 0.1 us)
Async XLA Ops:
  0.0 16.3 %copy-start.6 = (f32[128]{0:T(128)S(1)}, f32[128]{0:T(128)}, u32[]{:S(2)}) copy-start(f32[128]{0:T(128)} %param.11) | copy-start | bytes 1540
  0.0 16.3 %copy-start.5 = (f32[192]{0:T(256)S(1)}, f32[192]{0:T(256)}, u32[]{:S(2)}) copy-start(f32[192]{0:T(256)} %param.15) | copy-start | bytes 2308
  0.0 16.3 %copy-start.4 = (s32[100,3]{0,1:T(4,128)S(1)}, s32[100,3]{0,1:T(4,128)}, u32[]{:S(2)}) copy-start(s32[100,3]{0,1:T(4,128)} %param.13) | copy-start | bytes 3604
  0.0 16.3 %copy-start.3 = (f32[16,128]{1,0:T(8,128)S(1)}, f32[16,128]{1,0:T(8,128)}, u32[]{:S(2)}) copy-start(f32[16,128]{1,0:T(8,128)} %ctf.1) | copy-start | bytes 24580
  0.0 16.4 %copy-start.2 = (s32[192,100]{1,0:T(8,128)S(1)}, s32[192,100]{1,0:T(8,128)}, u32[]{:S(2)}) copy-start(s32[192,100]{1,0:T(8,128)} %mask.1) | copy-start | bytes 230404
  0.0 17.2 %collective-permute-start.4 = (bf16[96,64,128]{2,1,0:T(8,128)(2,1)}, bf16[96,64,128]{2,1,0:T(8,128)(2,1)S(1)}, u32[]{:S(2)}, u32[]{:S(2)}) collective-permute-start(bf16[96,64,128]{2,1,0:T(8,128)(2,1)} %args_1_.4), channel_id=1, source_target_pairs={{0,16},{16,0},{1,17},{17,1},{2,18},{18,2},{3,19},{19,3},{4,20},{20... | collective-permute-start | bytes 4718600 | tf_op jit(solution)/shard_map/ppermute | solution.py:502
  1.7 15.5 %copy-start = (bf16[96,64,128]{2,1,0:T(8,128)(2,1)S(1)}, bf16[96,64,128]{2,1,0:T(8,128)(2,1)}, u32[]{:S(2)}) copy-start(bf16[96,64,128]{2,1,0:T(8,128)(2,1)} %args_1_.4) | copy-start | bytes 4718596
  1.7 15.5 %copy-start.1 = (s32[96]{0:T(128)S(1)}, s32[96]{0:T(128)}, u32[]{:S(2)}) copy-start(s32[96]{0:T(128)} %args_0_.4) | copy-start | bytes 1156
  1.8 22.5 %collective-permute-start.3 = (bf16[48,64,128]{2,1,0:T(8,128)(2,1)S(1)}, bf16[48,64,128]{2,1,0:T(8,128)(2,1)S(1)}, u32[]{:S(2)}, u32[]{:S(2)}) collective-permute-start(bf16[48,64,128]{2,1,0:T(8,128)(2,1)S(1)} %slice.32), channel_id=1, source_target_pairs={{0,1},{1,0},{2,3},{3,2},{4,5},{5,4},{6,7},{7,6},{8,9},{9,8},{10,11... | collective-permute-start | bytes 2359304 | tf_op jit(solution)/shard_map/ppermute | solution.py:500
  4.4 19.2 %collective-permute-start.1 = (s32[96]{0:T(128)}, s32[96]{0:T(128)S(1)}, u32[]{:S(2)}, u32[]{:S(2)}) collective-permute-start(s32[96]{0:T(128)} %args_0_.4), channel_id=1, source_target_pairs={{0,1},{1,0},{2,3},{3,2},{4,5},{5,4},{6,7},{7,6},{8,9},{9,8},{10,11... | collective-permute-start | bytes 1160 | tf_op jit(solution)/shard_map/ppermute | solution.py:501
  5.5 28.5 %collective-permute-start.2 = (bf16[32,64,128]{2,1,0:T(8,128)(2,1)S(1)}, bf16[32,64,128]{2,1,0:T(8,128)(2,1)S(1)}, u32[]{:S(2)}, u32[]{:S(2)}) collective-permute-start(bf16[32,64,128]{2,1,0:T(8,128)(2,1)S(1)} %slice.31), channel_id=1, source_target_pairs={{0,1},{1,0},{2,3},{3,2},{4,5},{5,4},{6,7},{7,6},{8,9},{9,8},{10,11... | collective-permute-start | bytes 1572872 | tf_op jit(solution)/shard_map/ppermute | solution.py:500
  24.3 1.9 %collective-permute-start.5 = (bf16[16,64,128]{2,1,0:T(8,128)(2,1)S(1)}, bf16[16,64,128]{2,1,0:T(8,128)(2,1)S(1)}, u32[]{:S(2)}, u32[]{:S(2)}) collective-permute-start(bf16[16,64,128]{2,1,0:T(8,128)(2,1)S(1)} %get-tuple-element.77), channel_id=1, source_target_pairs={{0,16},{16,0},{1,17},{17,1},{2,18},{18,2},{3,19},{19,3},{4,20},{20... | collective-permute-start | bytes 786440 | tf_op jit(solution)/shard_map/ppermute | solution.py:517
  24.4 1.9 %collective-permute-start.6 = (bf16[16,64,128]{2,1,0:T(8,128)(2,1)S(1)}, bf16[16,64,128]{2,1,0:T(8,128)(2,1)S(1)}, u32[]{:S(2)}, u32[]{:S(2)}) collective-permute-start(bf16[16,64,128]{2,1,0:T(8,128)(2,1)S(1)} %get-tuple-element.76), channel_id=1, source_target_pairs={{0,16},{16,0},{1,17},{17,1},{2,18},{18,2},{3,19},{19,3},{4,20},{20... | collective-permute-start | bytes 786440 | tf_op jit(solution)/shard_map/ppermute | solution.py:517
  24.9 1.8 %collective-permute-start.7 = (bf16[16,64,128]{2,1,0:T(8,128)(2,1)S(1)}, bf16[16,64,128]{2,1,0:T(8,128)(2,1)S(1)}, u32[]{:S(2)}, u32[]{:S(2)}) collective-permute-start(bf16[16,64,128]{2,1,0:T(8,128)(2,1)S(1)} %get-tuple-element.75), channel_id=1, source_target_pairs={{0,16},{16,0},{1,17},{17,1},{2,18},{18,2},{3,19},{19,3},{4,20},{20... | collective-permute-start | bytes 786440 | tf_op jit(solution)/shard_map/ppermute | solution.py:517
  25.0 14.4 %collective-permute-start = (bf16[16,64,128]{2,1,0:T(8,128)(2,1)S(1)}, bf16[16,64,128]{2,1,0:T(8,128)(2,1)S(1)}, u32[]{:S(2)}, u32[]{:S(2)}) collective-permute-start(bf16[16,64,128]{2,1,0:T(8,128)(2,1)S(1)} %slice.30), channel_id=1, source_target_pairs={{0,1},{1,0},{2,3},{3,2},{4,5},{5,4},{6,7},{7,6},{8,9},{9,8},{10,11... | collective-permute-start | bytes 786440 | tf_op jit(solution)/shard_map/ppermute | solution.py:500
  34.0 1.4 %collective-permute-start.10 = (bf16[8,64,128]{2,1,0:T(8,128)(2,1)S(1)}, bf16[8,64,128]{2,1,0:T(8,128)(2,1)S(1)}, u32[]{:S(2)}, u32[]{:S(2)}) collective-permute-start(bf16[8,64,128]{2,1,0:T(8,128)(2,1)S(1)} %get-tuple-element.79), channel_id=1, source_target_pairs={{0,16},{16,0},{1,17},{17,1},{2,18},{18,2},{3,19},{19,3},{4,20},{20... | collective-permute-start | bytes 393224 | tf_op jit(solution)/shard_map/ppermute | solution.py:517
  34.1 1.5 %collective-permute-start.11 = (bf16[8,64,128]{2,1,0:T(8,128)(2,1)S(1)}, bf16[8,64,128]{2,1,0:T(8,128)(2,1)S(1)}, u32[]{:S(2)}, u32[]{:S(2)}) collective-permute-start(bf16[8,64,128]{2,1,0:T(8,128)(2,1)S(1)} %get-tuple-element.78), channel_id=1, source_target_pairs={{0,16},{16,0},{1,17},{17,1},{2,18},{18,2},{3,19},{19,3},{4,20},{20... | collective-permute-start | bytes 393224 | tf_op jit(solution)/shard_map/ppermute | solution.py:517
  34.6 1.3 %collective-permute-start.8 = (bf16[8,64,128]{2,1,0:T(8,128)(2,1)S(1)}, bf16[8,64,128]{2,1,0:T(8,128)(2,1)S(1)}, u32[]{:S(2)}, u32[]{:S(2)}) collective-permute-start(bf16[8,64,128]{2,1,0:T(8,128)(2,1)S(1)} %get-tuple-element.81), channel_id=1, source_target_pairs={{0,16},{16,0},{1,17},{17,1},{2,18},{18,2},{3,19},{19,3},{4,20},{20... | collective-permute-start | bytes 393224 | tf_op jit(solution)/shard_map/ppermute | solution.py:517
  34.7 1.5 %collective-permute-start.9 = (bf16[8,64,128]{2,1,0:T(8,128)(2,1)S(1)}, bf16[8,64,128]{2,1,0:T(8,128)(2,1)S(1)}, u32[]{:S(2)}, u32[]{:S(2)}) collective-permute-start(bf16[8,64,128]{2,1,0:T(8,128)(2,1)S(1)} %get-tuple-element.80), channel_id=1, source_target_pairs={{0,16},{16,0},{1,17},{17,1},{2,18},{18,2},{3,19},{19,3},{4,20},{20... | collective-permute-start | bytes 393224 | tf_op jit(solution)/shard_map/ppermute | solution.py:517
  39.4 1.5 %collective-permute-start.12 = (bf16[16,64,128]{2,1,0:T(8,128)(2,1)S(1)}, bf16[16,64,128]{2,1,0:T(8,128)(2,1)S(1)}, u32[]{:S(2)}, u32[]{:S(2)}) collective-permute-start(bf16[16,64,128]{2,1,0:T(8,128)(2,1)S(1)} %gate.5.args_0_), channel_id=1, source_target_pairs={{0,16},{16,0},{1,17},{17,1},{2,18},{18,2},{3,19},{19,3},{4,20},{20... | collective-permute-start | bytes 786440 | tf_op jit(solution)/shard_map/ppermute | solution.py:517
  45.0 3.7 %collective-permute-start.13 = (f32[8,192]{1,0:T(8,128)S(1)}, f32[8,192]{1,0:T(8,128)S(1)}, u32[]{:S(2)}, u32[]{:S(2)}) collective-permute-start(f32[8,192]{1,0:T(8,128)S(1)} %get-tuple-element.60.rest_1_), channel_id=1, source_target_pairs={{0,1},{1,0},{2,3},{3,2},{4,5},{5,4},{6,7},{7,6},{8,9},{9,8},{10,11... | collective-permute-start | bytes 18440 | tf_op jit(solution)/shard_map/ppermute | solution.py:526
  51.3 12.7 %collective-permute-start.14 = (bf16[4,500,128]{2,1,0:T(8,128)(2,1)S(1)}, bf16[4,500,128]{2,1,0:T(8,128)(2,1)S(1)}, u32[]{:S(2)}, u32[]{:S(2)}) collective-permute-start(bf16[4,500,128]{2,1,0:T(8,128)(2,1)S(1)} %get-tuple-element.63.rest_1_), channel_id=1, source_target_pairs={{0,2},{2,0},{4,6},{6,4},{8,10},{10,8},{12,14},{14,12},{1,3},{3,1},... | collective-permute-start | bytes 1536008 | tf_op jit(solution)/shard_map/ppermute | solution.py:529
  54.2 14.2 %collective-permute-start.18 = (bf16[2,300,128]{2,1,0:T(8,128)(2,1)S(1)}, bf16[2,300,128]{2,1,0:T(8,128)(2,1)S(1)}, u32[]{:S(2)}, u32[]{:S(2)}) collective-permute-start(bf16[2,300,128]{2,1,0:T(8,128)(2,1)S(1)} %get-tuple-element.70), channel_id=1, source_target_pairs={{0,8},{2,10},{4,12},{6,14},{8,0},{10,2},{12,4},{14,6},{1,9},{3,11}... | collective-permute-start | bytes 460808 | tf_op jit(solution)/shard_map/ppermute | solution.py:529
  56.8 11.8 %collective-permute-start.19 = (bf16[2,300,128]{2,1,0:T(8,128)(2,1)S(1)}, bf16[2,300,128]{2,1,0:T(8,128)(2,1)S(1)}, u32[]{:S(2)}, u32[]{:S(2)}) collective-permute-start(bf16[2,300,128]{2,1,0:T(8,128)(2,1)S(1)} %get-tuple-element.71), channel_id=1, source_target_pairs={{0,12},{2,14},{4,8},{6,10},{8,4},{10,6},{12,0},{14,2},{1,13},{3,15... | collective-permute-start | bytes 460808 | tf_op jit(solution)/shard_map/ppermute | solution.py:529
  58.2 10.5 %collective-permute-start.20 = (bf16[2,300,128]{2,1,0:T(8,128)(2,1)S(1)}, bf16[2,300,128]{2,1,0:T(8,128)(2,1)S(1)}, u32[]{:S(2)}, u32[]{:S(2)}) collective-permute-start(bf16[2,300,128]{2,1,0:T(8,128)(2,1)S(1)} %get-tuple-element.72), channel_id=1, source_target_pairs={{0,4},{2,6},{4,0},{6,2},{8,12},{10,14},{12,8},{14,10},{1,5},{3,7},... | collective-permute-start | bytes 460808 | tf_op jit(solution)/shard_map/ppermute | solution.py:529
  64.2 15.1 %collective-permute-start.15 = (bf16[1,500,128]{2,1,0:T(8,128)(2,1)S(1)}, bf16[1,500,128]{2,1,0:T(8,128)(2,1)S(1)}, u32[]{:S(2)}, u32[]{:S(2)}) collective-permute-start(bf16[1,500,128]{2,1,0:T(8,128)(2,1)S(1)} %get-tuple-element.65), channel_id=1, source_target_pairs={{0,8},{2,10},{4,12},{6,14},{8,0},{10,2},{12,4},{14,6},{1,9},{3,11}... | collective-permute-start | bytes 384008 | tf_op jit(solution)/shard_map/ppermute | solution.py:529
  67.0 12.2 %collective-permute-start.16 = (bf16[1,500,128]{2,1,0:T(8,128)(2,1)S(1)}, bf16[1,500,128]{2,1,0:T(8,128)(2,1)S(1)}, u32[]{:S(2)}, u32[]{:S(2)}) collective-permute-start(bf16[1,500,128]{2,1,0:T(8,128)(2,1)S(1)} %get-tuple-element.66), channel_id=1, source_target_pairs={{0,12},{2,14},{4,8},{6,10},{8,4},{10,6},{12,0},{14,2},{1,13},{3,15... | collective-permute-start | bytes 384008 | tf_op jit(solution)/shard_map/ppermute | solution.py:529
  68.4 10.9 %collective-permute-start.17 = (bf16[1,500,128]{2,1,0:T(8,128)(2,1)S(1)}, bf16[1,500,128]{2,1,0:T(8,128)(2,1)S(1)}, u32[]{:S(2)}, u32[]{:S(2)}) collective-permute-start(bf16[1,500,128]{2,1,0:T(8,128)(2,1)S(1)} %get-tuple-element.67), channel_id=1, source_target_pairs={{0,4},{2,6},{4,0},{6,2},{8,12},{10,14},{12,8},{14,10},{1,5},{3,7},... | collective-permute-start | bytes 384008 | tf_op jit(solution)/shard_map/ppermute | solution.py:529
  68.7 4.5 %collective-permute-start.21 = (bf16[1,300,128]{2,1,0:T(8,128)(2,1)S(1)}, bf16[1,300,128]{2,1,0:T(8,128)(2,1)S(1)}, u32[]{:S(2)}, u32[]{:S(2)}) collective-permute-start(bf16[1,300,128]{2,1,0:T(8,128)(2,1)S(1)} %get-tuple-element.74), channel_id=1, source_target_pairs={{0,2},{2,0},{4,6},{6,4},{8,10},{10,8},{12,14},{14,12},{1,3},{3,1},... | collective-permute-start | bytes 230408 | tf_op jit(solution)/shard_map/ppermute | solution.py:529

commit v9 on v8

--- a/solution.py
+++ b/solution.py
@@ -319,14 +319,17 @@
         out[row] = jnp.concatenate([quarters[q] for q in pair], axis=1).astype(BF16)
 
 
-def sums_kernel(plain, turned, *rest, outer, dom, start, rows, classes):
+def sums_kernel(plain, turned, *rest, first_call, outer, dom, start, rows, classes):
     if outer:
         weights = rest[0]
         outs = rest[-(dom // 2) :]
-    else:
+    elif first_call:
         weights = rest[-1]
         outs = rest[-3:-1]
         weigh(*rest[:4], weights)
+    else:
+        weights = rest[0]
+        outs = rest[-2:]
     width = outs[0].shape[2]
     height = plain.shape[0]
     block = height // 2 // dom
@@ -379,12 +382,13 @@
     shape = (count, rows * classes, width)
     out_shape = [pinned(shape, F32)]
     out_shape += [jax.ShapeDtypeStruct(shape, BF16)] * (dom // 2 - 1 if outer else 1)
-    if not outer:
+    first_call = len(inputs) > 1
+    if first_call:
         rot = inputs[3]
         out_shape.append(pinned((2, rot.shape[1], 2 * plain.shape[1]), BF16))
     return pl.pallas_call(
         functools.partial(
-            sums_kernel, outer=outer, dom=dom, start=start, rows=rows, classes=classes
+            sums_kernel, first_call=first_call, outer=outer, dom=dom, start=start, rows=rows, classes=classes
         ),
         in_specs=[vmem] * (2 + len(inputs)) + [pl.BlockSpec(memory_space=pl.ANY)] * len(after),
         out_shape=tuple(out_shape),
@@ -405,15 +409,17 @@
         out[0] = value.astype(out.dtype)
 
 
-def gather(keep, got):
+def gather(keep, got, after):
     shape = (1,) + keep.shape[1:]
     return pl.pallas_call(
         functools.partial(gather_kernel, came=len(got)),
+        in_specs=[pl.BlockSpec(memory_space=pltpu.VMEM)] * (1 + len(got))
+        + [pl.BlockSpec(memory_space=pl.ANY)] * len(after),
         out_shape=(pinned(shape, F32), jax.ShapeDtypeStruct(shape, BF16)),
         compiler_params=pltpu.CompilerParams(vmem_limit_bytes=8 * MIB),
         cost_estimate=cost(FOLD),
         name="gather",
-    )(held(keep), *got)
+    )(held(keep), *got, *after)
 
 
 def fold_kernel(keep, got, *outs, fan, bit):
@@ -478,10 +484,10 @@
 
 
 def row_pieces(rows, dom):
-    if rows < 4 or dom > 8:
-        return (rows, 0)
-    outer = rows * 3 // 8
-    return (rows - outer, outer)
+    if rows < 8 or dom > 8:
+        return (rows,), 0
+    part = rows * 3 // 8
+    return (part, part), rows - 2 * part
 
 
 def local(
@@ -532,23 +538,37 @@
         far_first = sorted(range(len(sends)), key=lambda m: m == 0)
         return [along(sends[m], (m + 1) << bit) for m in far_first]
 
-    inner, outer = row_pieces(half // dom, dom)
-    keep, send, weights = sums(inputs, plain, turned, (), False, dom, 0, inner, classes)
-    got = along(send, 1)
+    firsts, outer = row_pieces(half // dom, dom)
+    start = 0
+    weights = None
+    after = ()
+    parts = []
+    for rows in firsts:
+        args = inputs if weights is None else (held(weights),)
+        keep, send, *made = sums(args, plain, turned, after, False, dom, start, rows, classes)
+        weights = made[0] if made else weights
+        start += rows
+        after = (send,)
+        parts.append((keep, along(send, 1)))
+    got_b = []
     if outer:
         keep_b, *sends_b = sums(
-            (held(weights),), plain, turned, (send,), True, dom, inner, outer, classes
+            (held(weights),), plain, turned, after, True, dom, start, outer, classes
         )
         got_b = spread(sends_b, 1)
-    bit = 1
-    while keep.shape[0] > 4:
-        keep, send = fold(keep, got, (), 2, bit)
-        got = along(send, 1 << bit)
-        bit += 1
-    keep, *sends = fold(keep, got, (), keep.shape[0], bit)
-    done = [[keep] + spread(sends, bit)]
+    done = []
+    after = ()
+    for keep, got in parts:
+        bit = 1
+        while keep.shape[0] > 4:
+            keep, send = fold(keep, got, after, 2, bit)
+            got = along(send, 1 << bit)
+            bit += 1
+        keep, *sends = fold(keep, got, after, keep.shape[0], bit)
+        done.append([keep] + spread(sends, bit))
+        after = tuple(got_b)
     if outer:
-        keep_b, send_b = gather(keep_b, got_b)
+        keep_b, send_b = gather(keep_b, got_b, done[0][1:] if True else [])
         done.append([keep_b, along(send_b, 1)])
     return finish(done, classes)
 

time: 80.6 us -> 80.8 us (level)
  waiting for transfers between devices: 25.2 us -> 16.9 us
  starting transfers between devices: 22 us -> 29.5 us
  Pallas kernels: 30.4 us -> 31.3 us
    ppermute x8 -> x12, waiting for transfers between devices: 14.6 us -> 6.4 us  [along(): return lax.ppermute(x, 'dom', [(i, i ^ mask) for i in range(dom)])]
    ppermute x8 -> x12, starting transfers between devices: 12 us -> 19.5 us  [along(): return lax.ppermute(x, 'dom', [(i, i ^ mask) for i in range(dom)])]
    pallas_call x3 -> x4, Pallas kernels: 3.7 us -> 4.57 us  [the longest x3 4.51 us: sums(): pl.pallas_call(functools.partial(sums_kernel, first_call=first_call, oute...]
  transfers between devices with their start and end apart: 22 -> 26, of which waited for: 13 -> 14; matrix products, arithmetic and copies ran while one was open for 3% -> 3% of each run, Pallas kernels for 29% -> 30%
where the time goes in v9:
time: 80.8 us; the launch traced here: 80.3 us
  Pallas kernels  31.3 us (39%)
  starting transfers between devices  29.5 us (37%)
  waiting for transfers between devices  16.9 us (21%)
  local copies, waits for them, and re-layouts  2.4 us (3%)
    ppermute x12, starting transfers between devices, along(): return lax.ppermute(x, 'dom', [(i, i ^ mask) for i in range(dom)])  19.5 us
    pallas_call x4, Pallas kernels, filter_chunk(): pl.pallas_call(functools.partial(filter_kernel, picked=picked, parts=part...  12.3 us
    pallas_call x1, Pallas kernels, lay_refs(): pl.pallas_call(functools.partial(refs_kernel, padded=padded), grid=(rots,...  8.81 us
    ppermute x12, waiting for transfers between devices, along(): return lax.ppermute(x, 'dom', [(i, i ^ mask) for i in range(dom)])  6.4 us
    ppermute x3, starting transfers between devices, local(): remote = [over_cls(images[a:a + n]) for a, n in zip(starts, sizes)]  5.82 us
    ppermute x3, waiting for transfers between devices, local(): remote = [over_cls(images[a:a + n]) for a, n in zip(starts, sizes)]  5.61 us
    pallas_call x3, Pallas kernels, sums(): pl.pallas_call(functools.partial(sums_kernel, first_call=first_call, oute...  4.51 us
    pallas_call x1, Pallas kernels, score(): pl.pallas_call(score_kernel, out_shape=(pinned((height, count), F32), pin...  3.11 us
  transfers between devices with their start and end apart: 26, of which 14 were waited for; matrix products, arithmetic and copies ran while one was open for 3% of the time, Pallas kernels for 30%

profile of v9, /device:TPU:0, one launch (start us, length us, event | category | flops | bytes accessed | tf_op | source)
XLA Modules:
  0.0 80.3 jit_solution(6062930491018805486)
XLA Ops:
  0.0 0.5 collective-permute-start.4
  0.5 1.2 %slice.32 = bf16[48,64,128]{2,1,0:T(8,128)(2,1)S(1)} slice(bf16[96,64,128]{2,1,0:T(8,128)(2,1)} %args_1_.4), slice={[0:48], [0:64], [0:128]} | slice | bytes 1572864 | tf_op jit(solution)/shard_map/slice | solution.py:506
  1.7 0.0 copy-start
  1.7 0.0 copy-start.1
  1.8 2.6 %collective-permute-start.3 = (bf16[48,64,128]{2,1,0:T(8,128)(2,1)S(1)}, bf16[48,64,128]{2,1,0:T(8,128)(2,1)S(1)}, u32[]{:S(2)}, u32[]{:S(2)}) collective-permute-start(bf16[48,64,128]{2,1,0:T(8,128)(2,1)S(1)} %slice.32), channel_id=1, source_target_pairs={{0,1},{1,0},{2,3},{3,2},{4,5},{5,4},{6,7},{7,6},{8,9},{9,8},{10,11... | collective-permute-start | bytes 2359304 | tf_op jit(solution)/shard_map/ppermute | solution.py:506
  4.4 0.1 collective-permute-start.1
  4.4 1.1 %slice.31 = bf16[32,64,128]{2,1,0:T(8,128)(2,1)S(1)} slice(bf16[96,64,128]{2,1,0:T(8,128)(2,1)} %args_1_.4), slice={[48:80], [0:64], [0:128]} | slice | bytes 1048576 | tf_op jit(solution)/shard_map/slice | solution.py:506
  5.5 2.0 %collective-permute-start.2 = (bf16[32,64,128]{2,1,0:T(8,128)(2,1)S(1)}, bf16[32,64,128]{2,1,0:T(8,128)(2,1)S(1)}, u32[]{:S(2)}, u32[]{:S(2)}) collective-permute-start(bf16[32,64,128]{2,1,0:T(8,128)(2,1)S(1)} %slice.31), channel_id=1, source_target_pairs={{0,1},{1,0},{2,3},{3,2},{4,5},{5,4},{6,7},{7,6},{8,9},{9,8},{10,11... | collective-permute-start | bytes 1572872 | tf_op jit(solution)/shard_map/ppermute | solution.py:506
  7.5 8.8 %refs.2 = (bf16[128,336,128]{2,1,0:T(8,128)(2,1)S(1)}, f32[336,128]{1,0:T(8,128)S(1)}) custom-call(bf16[100,3,128,128]{3,2,1,0:T(8,128)(2,1)} %refs.3), custom_call_target="tpu_custom_call" | custom-call | flops 900000000 | bytes 2700000 | tf_op jit(solution)/shard_map/refs/pallas_call | solution.py:165
  16.4 0.8 %prepare.1 = (bf16[16,128,128]{2,1,0:T(8,128)(2,1)S(1)}, bf16[16,128,128]{2,1,0:T(8,128)(2,1)S(1)}, f32[112,192]{1,0:T(8,128)S(1)}, f32[1,192]{1,0:T(1,128)S(1)}, f32[3,112,128]{2,1,0:T(8,128)S(1)}) custom-call(f32[16,128]{1,0:T(8,128)S(1)} %copy-done.3, f32[1,128]{1,0:T(1,128)S(1)} %bitcast.6, s32[192,100]{1,0:T(8,128)S(1)} %copy-done.2, ...), custom_call_target="tpu_custom_call" | custom-call | flops 300000000 | bytes 900000 | tf_op jit(solution)/shard_map/prepare/pallas_call | solution.py:96
  17.2 0.0 collective-permute-done.4.args_4_
  17.2 6.4 %filter.4 = (bf16[128,192,128]{2,1,0:T(8,128)(2,1)S(1)}, bf16[128,192,128]{2,1,0:T(8,128)(2,1)S(1)}, f32[8,128]{1,0:T(8,128)S(1)}) custom-call(s32[96]{0:T(128)S(1)} %copy-done.1, bf16[96,64,128]{2,1,0:T(8,128)(2,1)S(1)} %copy-done, bf16[16,128,128]{2,1,0:T(8,128)(2,1)S(1)} %get-tuple-element.47.args_2_.left, ...), custom_call_target="tpu_custom_call" | custom-call | flops 960000000 | bytes 2880000 | tf_op jit(solution)/shard_map/filter/pallas_call | solution.py:233
  23.6 0.0 collective-permute-done.1.bins.args_0_
  23.6 0.6 pick.1
  24.3 0.1 fusion
  24.3 0.1 collective-permute-start.5
  24.4 0.5 collective-permute-start.6
  24.9 0.1 collective-permute-start.7
  25.0 1.2 %collective-permute-start = (bf16[16,64,128]{2,1,0:T(8,128)(2,1)S(1)}, bf16[16,64,128]{2,1,0:T(8,128)(2,1)S(1)}, u32[]{:S(2)}, u32[]{:S(2)}) collective-permute-start(bf16[16,64,128]{2,1,0:T(8,128)(2,1)S(1)} %slice.30), channel_id=1, source_target_pairs={{0,1},{1,0},{2,3},{3,2},{4,5},{5,4},{6,7},{7,6},{8,9},{9,8},{10,11... | collective-permute-start | bytes 786440 | tf_op jit(solution)/shard_map/ppermute | solution.py:506
  26.2 0.0 collective-permute-done.5.args_4_
  26.2 0.1 collective-permute-done.6.args_5_
  26.3 0.4 collective-permute-done.7.args_6_
  26.7 2.8 %filter.5 = (bf16[128,192,128]{2,1,0:T(8,128)(2,1)S(1)}, bf16[128,192,128]{2,1,0:T(8,128)(2,1)S(1)}, f32[8,128]{1,0:T(8,128)S(1)}) custom-call(s32[96]{0:T(128)S(1)} %collective-permute-done.1.bins.args_0_, bf16[48,64,128]{2,1,0:T(8,128)(2,1)S(1)} %gate.3.args_1_, ...), custom_call_target="tpu_custom_call", output_to_operand_aliasing={{0}: (7, {}), {1}: (8, {})} | custom-call | flops 480000000 | bytes 1440000 | tf_op jit(solution)/shard_map/filter/pallas_call | solution.py:233
  29.5 4.5 %collective-permute-done.2.refs_0_ = bf16[32,64,128]{2,1,0:T(8,128)(2,1)S(1)} collective-permute-done((bf16[32,64,128]{2,1,0:T(8,128)(2,1)S(1)}, bf16[32,64,128]{2,1,0:T(8,128)(2,1)S(1)}, u32[]{:S(2)}, u32[]{:S(2)}) %collective-permute-start.2) | collective-permute-done | bytes 524320 | tf_op jit(solution)/shard_map/ppermute | solution.py:506
  34.0 0.1 collective-permute-start.10
  34.1 0.5 collective-permute-start.11
  34.6 0.1 collective-permute-start.8
  34.7 0.4 collective-permute-start.9
  35.1 0.3 collective-permute-done.10.args_6_
  35.4 0.2 collective-permute-done.11.args_7_
  35.6 0.3 collective-permute-done.8.args_4_
  36.0 0.2 collective-permute-done.9.args_5_
  36.1 2.1 %filter.6 = (bf16[128,192,128]{2,1,0:T(8,128)(2,1)S(1)}, bf16[128,192,128]{2,1,0:T(8,128)(2,1)S(1)}, f32[8,128]{1,0:T(8,128)S(1)}) custom-call(s32[96]{0:T(128)S(1)} %collective-permute-done.1.bins.args_0_, bf16[32,64,128]{2,1,0:T(8,128)(2,1)S(1)} %gate.4.args_1_, ...), custom_call_target="tpu_custom_call", output_to_operand_aliasing={{0}: (8, {}), {1}: (9, {})} | custom-call | flops 320000000 | bytes 960000 | tf_op jit(solution)/shard_map/filter/pallas_call | solution.py:233
  38.3 1.1 %collective-permute-done.refs_0_ = bf16[16,64,128]{2,1,0:T(8,128)(2,1)S(1)} collective-permute-done((bf16[16,64,128]{2,1,0:T(8,128)(2,1)S(1)}, bf16[16,64,128]{2,1,0:T(8,128)(2,1)S(1)}, u32[]{:S(2)}, u32[]{:S(2)}) %collective-permute-start) | collective-permute-done | bytes 262176 | tf_op jit(solution)/shard_map/ppermute | solution.py:506
  39.4 1.5 %collective-permute-done.12.args_3_ = bf16[16,64,128]{2,1,0:T(8,128)(2,1)S(1)} collective-permute-done((bf16[16,64,128]{2,1,0:T(8,128)(2,1)S(1)}, bf16[16,64,128]{2,1,0:T(8,128)(2,1)S(1)}, u32[]{:S(2)}, u32[]{:S(2)}) %collective-permute-start.12) | collective-permute-done | bytes 262176 | tf_op jit(solution)/shard_map/ppermute | solution.py:523
  41.0 1.0 %filter.7 = (bf16[128,192,128]{2,1,0:T(8,128)(2,1)S(1)}, bf16[128,192,128]{2,1,0:T(8,128)(2,1)S(1)}) custom-call(bf16[16,64,128]{2,1,0:T(8,128)(2,1)S(1)} %gate.5.args_0_, bf16[16,128,128]{2,1,0:T(8,128)(2,1)S(1)} %get-tuple-element.50.refs_1_.args_1_, ...), custom_call_target="tpu_custom_call", output_to_operand_aliasing={{0}: (4, {}), {1}: (5, {})} | custom-call | flops 160000000 | bytes 480000 | tf_op jit(solution)/shard_map/filter/pallas_call | solution.py:233
  41.9 3.1 %score.1 = (f32[336,192]{1,0:T(8,128)S(1)}, f32[8,192]{1,0:T(8,128)S(1)}) custom-call(bf16[128,192,128]{2,1,0:T(8,128)(2,1)S(1)} %get-tuple-element.60.plain, bf16[128,336,128]{2,1,0:T(8,128)(2,1)S(1)} %get-tuple-element.62.refs, f32[336,128]{1,0:T(8,128)S(1)} %get-tuple-element.46.after.norm, f32[112,192]{1,0:T(8,128)S(1)} %get-tuple-element.63.mask, ...), custom_call_target="tpu_custom_call" | custom-call | flops 500000000 | bytes 1500000 | tf_op jit(solution)/shard_map/score/pallas_call | solution.py:293
  45.0 1.8 %collective-permute-start.13 = (f32[8,192]{1,0:T(8,128)S(1)}, f32[8,192]{1,0:T(8,128)S(1)}, u32[]{:S(2)}, u32[]{:S(2)}) collective-permute-start(f32[8,192]{1,0:T(8,128)S(1)} %get-tuple-element.66.rest_1_), channel_id=1, source_target_pairs={{0,1},{1,0},{2,3},{3,2},{4,5},{5,4},{6,7},{7,6},{8,9},{9,8},{10,11... | collective-permute-start | bytes 18440 | tf_op jit(solution)/shard_map/ppermute | solution.py:532
  46.8 1.9 %collective-permute-done.13.rest_2_ = f32[8,192]{1,0:T(8,128)S(1)} collective-permute-done((f32[8,192]{1,0:T(8,128)S(1)}, f32[8,192]{1,0:T(8,128)S(1)}, u32[]{:S(2)}, u32[]{:S(2)}) %collective-permute-start.13) | collective-permute-done | bytes 6176 | tf_op jit(solution)/shard_map/ppermute | solution.py:532
  48.7 2.0 %sums.3 = (f32[4,300,128]{2,1,0:T(8,128)S(1)}, bf16[4,300,128]{2,1,0:T(8,128)(2,1)S(1)}, bf16[2,112,384]{2,1,0:T(8,128)(2,1)S(1)}) custom-call(bf16[128,192,128]{2,1,0:T(8,128)(2,1)S(1)} %get-tuple-element.60.plain, bf16[128,192,128]{2,1,0:T(8,128)(2,1)S(1)} %get-tuple-element.61.turned, f32[336,192]{1,0:T(8,128)S(1)} %get-tuple-element.65.rest_0_, ...), custom_call_target="tpu_custom_call" | custom-call | flops 240000000 | bytes 720000 | tf_op jit(solution)/shard_map/sums/pallas_call | solution.py:389
  50.8 1.8 %collective-permute-start.14 = (bf16[4,300,128]{2,1,0:T(8,128)(2,1)S(1)}, bf16[4,300,128]{2,1,0:T(8,128)(2,1)S(1)}, u32[]{:S(2)}, u32[]{:S(2)}) collective-permute-start(bf16[4,300,128]{2,1,0:T(8,128)(2,1)S(1)} %get-tuple-element.69.rest_1_), channel_id=1, source_target_pairs={{0,2},{2,0},{4,6},{6,4},{8,10},{10,8},{12,14},{14,12},{1,3},{3,1},... | collective-permute-start | bytes 921608 | tf_op jit(solution)/shard_map/ppermute | solution.py:535
  52.6 1.7 %sums.4 = (f32[4,300,128]{2,1,0:T(8,128)S(1)}, bf16[4,300,128]{2,1,0:T(8,128)(2,1)S(1)}) custom-call(bf16[128,192,128]{2,1,0:T(8,128)(2,1)S(1)} %get-tuple-element.60.plain, bf16[128,192,128]{2,1,0:T(8,128)(2,1)S(1)} %get-tuple-element.61.turned, bf16[2,112,384]{2,1,0:T(8,128)(2,1)S(1)} %get-tuple-element.74.rest_0_, ...), custom_call_target="tpu_custom_call" | custom-call | flops 240000000 | bytes 720000 | tf_op jit(solution)/shard_map/sums/pallas_call | solution.py:389
  54.3 0.4 collective-permute-start.18
  54.7 0.8 sums.5
  55.4 2.9 %collective-permute-start.19 = (bf16[2,200,128]{2,1,0:T(8,128)(2,1)S(1)}, bf16[2,200,128]{2,1,0:T(8,128)(2,1)S(1)}, u32[]{:S(2)}, u32[]{:S(2)}) collective-permute-start(bf16[2,200,128]{2,1,0:T(8,128)(2,1)S(1)} %get-tuple-element.77), channel_id=1, source_target_pairs={{0,8},{2,10},{4,12},{6,14},{8,0},{10,2},{12,4},{14,6},{1,9},{3,11}... | collective-permute-start | bytes 307208 | tf_op jit(solution)/shard_map/ppermute | solution.py:535
  58.3 1.4 %collective-permute-start.20 = (bf16[2,200,128]{2,1,0:T(8,128)(2,1)S(1)}, bf16[2,200,128]{2,1,0:T(8,128)(2,1)S(1)}, u32[]{:S(2)}, u32[]{:S(2)}) collective-permute-start(bf16[2,200,128]{2,1,0:T(8,128)(2,1)S(1)} %get-tuple-element.78), channel_id=1, source_target_pairs={{0,12},{2,14},{4,8},{6,10},{8,4},{10,6},{12,0},{14,2},{1,13},{3,15... | collective-permute-start | bytes 307208 | tf_op jit(solution)/shard_map/ppermute | solution.py:535
  59.7 0.2 collective-permute-start.21
  59.9 1.3 %collective-permute-done.14.got = bf16[4,300,128]{2,1,0:T(8,128)(2,1)S(1)} collective-permute-done((bf16[4,300,128]{2,1,0:T(8,128)(2,1)S(1)}, bf16[4,300,128]{2,1,0:T(8,128)(2,1)S(1)}, u32[]{:S(2)}, u32[]{:S(2)}) %collective-permute-start.14) | collective-permute-done | bytes 307232 | tf_op jit(solution)/shard_map/ppermute | solution.py:535
  61.2 0.1 fold.2
  61.2 2.9 %collective-permute-start.15 = (bf16[1,300,128]{2,1,0:T(8,128)(2,1)S(1)}, bf16[1,300,128]{2,1,0:T(8,128)(2,1)S(1)}, u32[]{:S(2)}, u32[]{:S(2)}) collective-permute-start(bf16[1,300,128]{2,1,0:T(8,128)(2,1)S(1)} %get-tuple-element.71), channel_id=1, source_target_pairs={{0,8},{2,10},{4,12},{6,14},{8,0},{10,2},{12,4},{14,6},{1,9},{3,11}... | collective-permute-start | bytes 230408 | tf_op jit(solution)/shard_map/ppermute | solution.py:535
  64.1 1.9 %collective-permute-done.19.outs_0_.rest_0_ = bf16[2,200,128]{2,1,0:T(8,128)(2,1)S(1)} collective-permute-done((bf16[2,200,128]{2,1,0:T(8,128)(2,1)S(1)}, bf16[2,200,128]{2,1,0:T(8,128)(2,1)S(1)}, u32[]{:S(2)}, u32[]{:S(2)}) %collective-permute-start.19) | collective-permute-done | bytes 102432 | tf_op jit(solution)/shard_map/ppermute | solution.py:535
  66.1 3.0 %collective-permute-start.16 = (bf16[1,300,128]{2,1,0:T(8,128)(2,1)S(1)}, bf16[1,300,128]{2,1,0:T(8,128)(2,1)S(1)}, u32[]{:S(2)}, u32[]{:S(2)}) collective-permute-start(bf16[1,300,128]{2,1,0:T(8,128)(2,1)S(1)} %get-tuple-element.72), channel_id=1, source_target_pairs={{0,12},{2,14},{4,8},{6,10},{8,4},{10,6},{12,0},{14,2},{1,13},{3,15... | collective-permute-start | bytes 230408 | tf_op jit(solution)/shard_map/ppermute | solution.py:535
  69.1 1.5 %collective-permute-start.17 = (bf16[1,300,128]{2,1,0:T(8,128)(2,1)S(1)}, bf16[1,300,128]{2,1,0:T(8,128)(2,1)S(1)}, u32[]{:S(2)}, u32[]{:S(2)}) collective-permute-start(bf16[1,300,128]{2,1,0:T(8,128)(2,1)S(1)} %get-tuple-element.73), channel_id=1, source_target_pairs={{0,4},{2,6},{4,0},{6,2},{8,12},{10,14},{12,8},{14,10},{1,5},{3,7},... | collective-permute-start | bytes 230408 | tf_op jit(solution)/shard_map/ppermute | solution.py:535
  70.6 0.0 collective-permute-done.21.outs_2_.rest_2_
  70.6 0.0 collective-permute-done.18.got
  70.6 0.1 fold.3
  70.7 0.7 collective-permute-start.22
  71.4 2.2 %collective-permute-start.23 = (bf16[1,300,128]{2,1,0:T(8,128)(2,1)S(1)}, bf16[1,300,128]{2,1,0:T(8,128)(2,1)S(1)}, u32[]{:S(2)}, u32[]{:S(2)}) collective-permute-start(bf16[1,300,128]{2,1,0:T(8,128)(2,1)S(1)} %get-tuple-element.82), channel_id=1, source_target_pairs={{0,12},{2,14},{4,8},{6,10},{8,4},{10,6},{12,0},{14,2},{1,13},{3,15... | collective-permute-start | bytes 230408 | tf_op jit(solution)/shard_map/ppermute | solution.py:535
  73.6 0.6 collective-permute-start.24
  74.3 0.1 gather.1
  74.3 1.9 %collective-permute-start.25 = (bf16[1,200,128]{2,1,0:T(8,128)(2,1)S(1)}, bf16[1,200,128]{2,1,0:T(8,128)(2,1)S(1)}, u32[]{:S(2)}, u32[]{:S(2)}) collective-permute-start(bf16[1,200,128]{2,1,0:T(8,128)(2,1)S(1)} %get-tuple-element.86), channel_id=1, source_target_pairs={{0,2},{2,0},{4,6},{6,4},{8,10},{10,8},{12,14},{14,12},{1,3},{3,1},... | collective-permute-start | bytes 153608 | tf_op jit(solution)/shard_map/ppermute | solution.py:535
  76.2 2.9 %collective-permute-done.22.args_5_ = bf16[1,300,128]{2,1,0:T(8,128)(2,1)S(1)} collective-permute-done((bf16[1,300,128]{2,1,0:T(8,128)(2,1)S(1)}, bf16[1,300,128]{2,1,0:T(8,128)(2,1)S(1)}, u32[]{:S(2)}, u32[]{:S(2)}) %collective-permute-start.22) | collective-permute-done | bytes 76832 | tf_op jit(solution)/shard_map/ppermute | solution.py:535
  79.1 0.3 collective-permute-done.24.args_7_
  79.4 0.9 %finish.1 = f32[800,128]{1,0:T(8,128)} custom-call(f32[1,300,128]{2,1,0:T(8,128)S(1)} %get-tuple-element.70.args_0_, bf16[1,300,128]{2,1,0:T(8,128)(2,1)S(1)} %collective-permute-done.15.rest_3_.args_1_, bf16[1,300,128]{2,1,0:T(8,128)(2,1)S(1)} %collective-permute-done.16.rest_4_.args_2_, bf16[1,300,128]{2,1,0:T(8,128)(2,1)S(1)} %collective-permute-done.17.rest_5_.args_3_, ...), custom_call_target="tpu_custom_call" | custom-call | flops 100000000 | bytes 300000 | tf_op jit(solution)/shard_map/finish/pallas_call | solution.py:470
  (25 shorter events, 0.1 us)
Async XLA Ops:
  0.0 16.3 %copy-start.6 = (f32[128]{0:T(128)S(1)}, f32[128]{0:T(128)}, u32[]{:S(2)}) copy-start(f32[128]{0:T(128)} %param.11) | copy-start | bytes 1540
  0.0 16.3 %copy-start.5 = (f32[192]{0:T(256)S(1)}, f32[192]{0:T(256)}, u32[]{:S(2)}) copy-start(f32[192]{0:T(256)} %param.15) | copy-start | bytes 2308
  0.0 16.3 %copy-start.4 = (s32[100,3]{0,1:T(4,128)S(1)}, s32[100,3]{0,1:T(4,128)}, u32[]{:S(2)}) copy-start(s32[100,3]{0,1:T(4,128)} %param.13) | copy-start | bytes 3604
  0.0 16.3 %copy-start.3 = (f32[16,128]{1,0:T(8,128)S(1)}, f32[16,128]{1,0:T(8,128)}, u32[]{:S(2)}) copy-start(f32[16,128]{1,0:T(8,128)} %ctf.1) | copy-start | bytes 24580
  0.0 16.4 %copy-start.2 = (s32[192,100]{1,0:T(8,128)S(1)}, s32[192,100]{1,0:T(8,128)}, u32[]{:S(2)}) copy-start(s32[192,100]{1,0:T(8,128)} %mask.1) | copy-start | bytes 230404
  0.0 17.2 %collective-permute-start.4 = (bf16[96,64,128]{2,1,0:T(8,128)(2,1)}, bf16[96,64,128]{2,1,0:T(8,128)(2,1)S(1)}, u32[]{:S(2)}, u32[]{:S(2)}) collective-permute-start(bf16[96,64,128]{2,1,0:T(8,128)(2,1)} %args_1_.4), channel_id=1, source_target_pairs={{0,16},{16,0},{1,17},{17,1},{2,18},{18,2},{3,19},{19,3},{4,20},{20... | collective-permute-start | bytes 4718600 | tf_op jit(solution)/shard_map/ppermute | solution.py:508
  1.7 15.5 %copy-start = (bf16[96,64,128]{2,1,0:T(8,128)(2,1)S(1)}, bf16[96,64,128]{2,1,0:T(8,128)(2,1)}, u32[]{:S(2)}) copy-start(bf16[96,64,128]{2,1,0:T(8,128)(2,1)} %args_1_.4) | copy-start | bytes 4718596
  1.7 15.5 %copy-start.1 = (s32[96]{0:T(128)S(1)}, s32[96]{0:T(128)}, u32[]{:S(2)}) copy-start(s32[96]{0:T(128)} %args_0_.4) | copy-start | bytes 1156
  1.8 22.5 %collective-permute-start.3 = (bf16[48,64,128]{2,1,0:T(8,128)(2,1)S(1)}, bf16[48,64,128]{2,1,0:T(8,128)(2,1)S(1)}, u32[]{:S(2)}, u32[]{:S(2)}) collective-permute-start(bf16[48,64,128]{2,1,0:T(8,128)(2,1)S(1)} %slice.32), channel_id=1, source_target_pairs={{0,1},{1,0},{2,3},{3,2},{4,5},{5,4},{6,7},{7,6},{8,9},{9,8},{10,11... | collective-permute-start | bytes 2359304 | tf_op jit(solution)/shard_map/ppermute | solution.py:506
  4.4 19.2 %collective-permute-start.1 = (s32[96]{0:T(128)}, s32[96]{0:T(128)S(1)}, u32[]{:S(2)}, u32[]{:S(2)}) collective-permute-start(s32[96]{0:T(128)} %args_0_.4), channel_id=1, source_target_pairs={{0,1},{1,0},{2,3},{3,2},{4,5},{5,4},{6,7},{7,6},{8,9},{9,8},{10,11... | collective-permute-start | bytes 1160 | tf_op jit(solution)/shard_map/ppermute | solution.py:507
  5.5 28.5 %collective-permute-start.2 = (bf16[32,64,128]{2,1,0:T(8,128)(2,1)S(1)}, bf16[32,64,128]{2,1,0:T(8,128)(2,1)S(1)}, u32[]{:S(2)}, u32[]{:S(2)}) collective-permute-start(bf16[32,64,128]{2,1,0:T(8,128)(2,1)S(1)} %slice.31), channel_id=1, source_target_pairs={{0,1},{1,0},{2,3},{3,2},{4,5},{5,4},{6,7},{7,6},{8,9},{9,8},{10,11... | collective-permute-start | bytes 1572872 | tf_op jit(solution)/shard_map/ppermute | solution.py:506
  24.3 1.9 %collective-permute-start.5 = (bf16[16,64,128]{2,1,0:T(8,128)(2,1)S(1)}, bf16[16,64,128]{2,1,0:T(8,128)(2,1)S(1)}, u32[]{:S(2)}, u32[]{:S(2)}) collective-permute-start(bf16[16,64,128]{2,1,0:T(8,128)(2,1)S(1)} %get-tuple-element.89), channel_id=1, source_target_pairs={{0,16},{16,0},{1,17},{17,1},{2,18},{18,2},{3,19},{19,3},{4,20},{20... | collective-permute-start | bytes 786440 | tf_op jit(solution)/shard_map/ppermute | solution.py:523
  24.4 1.9 %collective-permute-start.6 = (bf16[16,64,128]{2,1,0:T(8,128)(2,1)S(1)}, bf16[16,64,128]{2,1,0:T(8,128)(2,1)S(1)}, u32[]{:S(2)}, u32[]{:S(2)}) collective-permute-start(bf16[16,64,128]{2,1,0:T(8,128)(2,1)S(1)} %get-tuple-element.88), channel_id=1, source_target_pairs={{0,16},{16,0},{1,17},{17,1},{2,18},{18,2},{3,19},{19,3},{4,20},{20... | collective-permute-start | bytes 786440 | tf_op jit(solution)/shard_map/ppermute | solution.py:523
  24.9 1.8 %collective-permute-start.7 = (bf16[16,64,128]{2,1,0:T(8,128)(2,1)S(1)}, bf16[16,64,128]{2,1,0:T(8,128)(2,1)S(1)}, u32[]{:S(2)}, u32[]{:S(2)}) collective-permute-start(bf16[16,64,128]{2,1,0:T(8,128)(2,1)S(1)} %get-tuple-element.87), channel_id=1, source_target_pairs={{0,16},{16,0},{1,17},{17,1},{2,18},{18,2},{3,19},{19,3},{4,20},{20... | collective-permute-start | bytes 786440 | tf_op jit(solution)/shard_map/ppermute | solution.py:523
  25.0 14.4 %collective-permute-start = (bf16[16,64,128]{2,1,0:T(8,128)(2,1)S(1)}, bf16[16,64,128]{2,1,0:T(8,128)(2,1)S(1)}, u32[]{:S(2)}, u32[]{:S(2)}) collective-permute-start(bf16[16,64,128]{2,1,0:T(8,128)(2,1)S(1)} %slice.30), channel_id=1, source_target_pairs={{0,1},{1,0},{2,3},{3,2},{4,5},{5,4},{6,7},{7,6},{8,9},{9,8},{10,11... | collective-permute-start | bytes 786440 | tf_op jit(solution)/shard_map/ppermute | solution.py:506
  34.0 1.4 %collective-permute-start.10 = (bf16[8,64,128]{2,1,0:T(8,128)(2,1)S(1)}, bf16[8,64,128]{2,1,0:T(8,128)(2,1)S(1)}, u32[]{:S(2)}, u32[]{:S(2)}) collective-permute-start(bf16[8,64,128]{2,1,0:T(8,128)(2,1)S(1)} %get-tuple-element.91), channel_id=1, source_target_pairs={{0,16},{16,0},{1,17},{17,1},{2,18},{18,2},{3,19},{19,3},{4,20},{20... | collective-permute-start | bytes 393224 | tf_op jit(solution)/shard_map/ppermute | solution.py:523
  34.1 1.5 %collective-permute-start.11 = (bf16[8,64,128]{2,1,0:T(8,128)(2,1)S(1)}, bf16[8,64,128]{2,1,0:T(8,128)(2,1)S(1)}, u32[]{:S(2)}, u32[]{:S(2)}) collective-permute-start(bf16[8,64,128]{2,1,0:T(8,128)(2,1)S(1)} %get-tuple-element.90), channel_id=1, source_target_pairs={{0,16},{16,0},{1,17},{17,1},{2,18},{18,2},{3,19},{19,3},{4,20},{20... | collective-permute-start | bytes 393224 | tf_op jit(solution)/shard_map/ppermute | solution.py:523
  34.6 1.3 %collective-permute-start.8 = (bf16[8,64,128]{2,1,0:T(8,128)(2,1)S(1)}, bf16[8,64,128]{2,1,0:T(8,128)(2,1)S(1)}, u32[]{:S(2)}, u32[]{:S(2)}) collective-permute-start(bf16[8,64,128]{2,1,0:T(8,128)(2,1)S(1)} %get-tuple-element.93), channel_id=1, source_target_pairs={{0,16},{16,0},{1,17},{17,1},{2,18},{18,2},{3,19},{19,3},{4,20},{20... | collective-permute-start | bytes 393224 | tf_op jit(solution)/shard_map/ppermute | solution.py:523
  34.7 1.5 %collective-permute-start.9 = (bf16[8,64,128]{2,1,0:T(8,128)(2,1)S(1)}, bf16[8,64,128]{2,1,0:T(8,128)(2,1)S(1)}, u32[]{:S(2)}, u32[]{:S(2)}) collective-permute-start(bf16[8,64,128]{2,1,0:T(8,128)(2,1)S(1)} %get-tuple-element.92), channel_id=1, source_target_pairs={{0,16},{16,0},{1,17},{17,1},{2,18},{18,2},{3,19},{19,3},{4,20},{20... | collective-permute-start | bytes 393224 | tf_op jit(solution)/shard_map/ppermute | solution.py:523
  39.4 1.5 %collective-permute-start.12 = (bf16[16,64,128]{2,1,0:T(8,128)(2,1)S(1)}, bf16[16,64,128]{2,1,0:T(8,128)(2,1)S(1)}, u32[]{:S(2)}, u32[]{:S(2)}) collective-permute-start(bf16[16,64,128]{2,1,0:T(8,128)(2,1)S(1)} %gate.5.args_0_), channel_id=1, source_target_pairs={{0,16},{16,0},{1,17},{17,1},{2,18},{18,2},{3,19},{19,3},{4,20},{20... | collective-permute-start | bytes 786440 | tf_op jit(solution)/shard_map/ppermute | solution.py:523
  45.0 3.7 %collective-permute-start.13 = (f32[8,192]{1,0:T(8,128)S(1)}, f32[8,192]{1,0:T(8,128)S(1)}, u32[]{:S(2)}, u32[]{:S(2)}) collective-permute-start(f32[8,192]{1,0:T(8,128)S(1)} %get-tuple-element.66.rest_1_), channel_id=1, source_target_pairs={{0,1},{1,0},{2,3},{3,2},{4,5},{5,4},{6,7},{7,6},{8,9},{9,8},{10,11... | collective-permute-start | bytes 18440 | tf_op jit(solution)/shard_map/ppermute | solution.py:532
  50.8 10.4 %collective-permute-start.14 = (bf16[4,300,128]{2,1,0:T(8,128)(2,1)S(1)}, bf16[4,300,128]{2,1,0:T(8,128)(2,1)S(1)}, u32[]{:S(2)}, u32[]{:S(2)}) collective-permute-start(bf16[4,300,128]{2,1,0:T(8,128)(2,1)S(1)} %get-tuple-element.69.rest_1_), channel_id=1, source_target_pairs={{0,2},{2,0},{4,6},{6,4},{8,10},{10,8},{12,14},{14,12},{1,3},{3,1},... | collective-permute-start | bytes 921608 | tf_op jit(solution)/shard_map/ppermute | solution.py:535
  54.3 16.3 %collective-permute-start.18 = (bf16[4,300,128]{2,1,0:T(8,128)(2,1)S(1)}, bf16[4,300,128]{2,1,0:T(8,128)(2,1)S(1)}, u32[]{:S(2)}, u32[]{:S(2)}) collective-permute-start(bf16[4,300,128]{2,1,0:T(8,128)(2,1)S(1)} %get-tuple-element.76.rest_1_), channel_id=1, source_target_pairs={{0,2},{2,0},{4,6},{6,4},{8,10},{10,8},{12,14},{14,12},{1,3},{3,1},... | collective-permute-start | bytes 921608 | tf_op jit(solution)/shard_map/ppermute | solution.py:535
  55.4 10.6 %collective-permute-start.19 = (bf16[2,200,128]{2,1,0:T(8,128)(2,1)S(1)}, bf16[2,200,128]{2,1,0:T(8,128)(2,1)S(1)}, u32[]{:S(2)}, u32[]{:S(2)}) collective-permute-start(bf16[2,200,128]{2,1,0:T(8,128)(2,1)S(1)} %get-tuple-element.77), channel_id=1, source_target_pairs={{0,8},{2,10},{4,12},{6,14},{8,0},{10,2},{12,4},{14,6},{1,9},{3,11}... | collective-permute-start | bytes 307208 | tf_op jit(solution)/shard_map/ppermute | solution.py:535
  58.3 10.8 %collective-permute-start.20 = (bf16[2,200,128]{2,1,0:T(8,128)(2,1)S(1)}, bf16[2,200,128]{2,1,0:T(8,128)(2,1)S(1)}, u32[]{:S(2)}, u32[]{:S(2)}) collective-permute-start(bf16[2,200,128]{2,1,0:T(8,128)(2,1)S(1)} %get-tuple-element.78), channel_id=1, source_target_pairs={{0,12},{2,14},{4,8},{6,10},{8,4},{10,6},{12,0},{14,2},{1,13},{3,15... | collective-permute-start | bytes 307208 | tf_op jit(solution)/shard_map/ppermute | solution.py:535
  59.7 10.9 %collective-permute-start.21 = (bf16[2,200,128]{2,1,0:T(8,128)(2,1)S(1)}, bf16[2,200,128]{2,1,0:T(8,128)(2,1)S(1)}, u32[]{:S(2)}, u32[]{:S(2)}) collective-permute-start(bf16[2,200,128]{2,1,0:T(8,128)(2,1)S(1)} %get-tuple-element.79), channel_id=1, source_target_pairs={{0,4},{2,6},{4,0},{6,2},{8,12},{10,14},{12,8},{14,10},{1,5},{3,7},... | collective-permute-start | bytes 307208 | tf_op jit(solution)/shard_map/ppermute | solution.py:535
  61.2 12.4 %collective-permute-start.15 = (bf16[1,300,128]{2,1,0:T(8,128)(2,1)S(1)}, bf16[1,300,128]{2,1,0:T(8,128)(2,1)S(1)}, u32[]{:S(2)}, u32[]{:S(2)}) collective-permute-start(bf16[1,300,128]{2,1,0:T(8,128)(2,1)S(1)} %get-tuple-element.71), channel_id=1, source_target_pairs={{0,8},{2,10},{4,12},{6,14},{8,0},{10,2},{12,4},{14,6},{1,9},{3,11}... | collective-permute-start | bytes 230408 | tf_op jit(solution)/shard_map/ppermute | solution.py:535
  66.1 8.2 %collective-permute-start.16 = (bf16[1,300,128]{2,1,0:T(8,128)(2,1)S(1)}, bf16[1,300,128]{2,1,0:T(8,128)(2,1)S(1)}, u32[]{:S(2)}, u32[]{:S(2)}) collective-permute-start(bf16[1,300,128]{2,1,0:T(8,128)(2,1)S(1)} %get-tuple-element.72), channel_id=1, source_target_pairs={{0,12},{2,14},{4,8},{6,10},{8,4},{10,6},{12,0},{14,2},{1,13},{3,15... | collective-permute-start | bytes 230408 | tf_op jit(solution)/shard_map/ppermute | solution.py:535
  69.1 5.2 %collective-permute-start.17 = (bf16[1,300,128]{2,1,0:T(8,128)(2,1)S(1)}, bf16[1,300,128]{2,1,0:T(8,128)(2,1)S(1)}, u32[]{:S(2)}, u32[]{:S(2)}) collective-permute-start(bf16[1,300,128]{2,1,0:T(8,128)(2,1)S(1)} %get-tuple-element.73), channel_id=1, source_target_pairs={{0,4},{2,6},{4,0},{6,2},{8,12},{10,14},{12,8},{14,10},{1,5},{3,7},... | collective-permute-start | bytes 230408 | tf_op jit(solution)/shard_map/ppermute | solution.py:535
  70.7 8.4 %collective-permute-start.22 = (bf16[1,300,128]{2,1,0:T(8,128)(2,1)S(1)}, bf16[1,300,128]{2,1,0:T(8,128)(2,1)S(1)}, u32[]{:S(2)}, u32[]{:S(2)}) collective-permute-start(bf16[1,300,128]{2,1,0:T(8,128)(2,1)S(1)} %get-tuple-element.81), channel_id=1, source_target_pairs={{0,8},{2,10},{4,12},{6,14},{8,0},{10,2},{12,4},{14,6},{1,9},{3,11}... | collective-permute-start | bytes 230408 | tf_op jit(solution)/shard_map/ppermute | solution.py:535
  71.4 7.7 %collective-permute-start.23 = (bf16[1,300,128]{2,1,0:T(8,128)(2,1)S(1)}, bf16[1,300,128]{2,1,0:T(8,128)(2,1)S(1)}, u32[]{:S(2)}, u32[]{:S(2)}) collective-permute-start(bf16[1,300,128]{2,1,0:T(8,128)(2,1)S(1)} %get-tuple-element.82), channel_id=1, source_target_pairs={{0,12},{2,14},{4,8},{6,10},{8,4},{10,6},{12,0},{14,2},{1,13},{3,15... | collective-permute-start | bytes 230408 | tf_op jit(solution)/shard_map/ppermute | solution.py:535
  73.6 5.7 %collective-permute-start.24 = (bf16[1,300,128]{2,1,0:T(8,128)(2,1)S(1)}, bf16[1,300,128]{2,1,0:T(8,128)(2,1)S(1)}, u32[]{:S(2)}, u32[]{:S(2)}) collective-permute-start(bf16[1,300,128]{2,1,0:T(8,128)(2,1)S(1)} %get-tuple-element.83), channel_id=1, source_target_pairs={{0,4},{2,6},{4,0},{6,2},{8,12},{10,14},{12,8},{14,10},{1,5},{3,7},... | collective-permute-start | bytes 230408 | tf_op jit(solution)/shard_map/ppermute | solution.py:535
  74.3 5.1 %collective-permute-start.25 = (bf16[1,200,128]{2,1,0:T(8,128)(2,1)S(1)}, bf16[1,200,128]{2,1,0:T(8,128)(2,1)S(1)}, u32[]{:S(2)}, u32[]{:S(2)}) collective-permute-start(bf16[1,200,128]{2,1,0:T(8,128)(2,1)S(1)} %get-tuple-element.86), channel_id=1, source_target_pairs={{0,2},{2,0},{4,6},{6,4},{8,10},{10,8},{12,14},{14,12},{1,3},{3,1},... | collective-permute-start | bytes 153608 | tf_op jit(solution)/shard_map/ppermute | solution.py:535

commit v10 on v8

--- a/solution.py
+++ b/solution.py
@@ -109,6 +109,25 @@
     )(ctf, band.reshape(1, width), mask, noise.reshape(1, total), rot, held(after))
 
 
+def cut_kernel(images, out, done):
+    copy = pltpu.make_async_copy(images.at[pl.ds(0, out.shape[0])], out, done)
+    copy.start()
+    copy.wait()
+
+
+def cut(images, count):
+    return pl.pallas_call(
+        cut_kernel,
+        in_specs=[pl.BlockSpec(memory_space=pl.ANY)],
+        out_specs=pl.BlockSpec(memory_space=pltpu.VMEM),
+        out_shape=pinned((count,) + images.shape[1:], images.dtype),
+        scratch_shapes=[pltpu.SemaphoreType.DMA(())],
+        compiler_params=pltpu.CompilerParams(vmem_limit_bytes=2 * MIB),
+        cost_estimate=cost(1),
+        name="cut",
+    )(pltpu.with_memory_space_constraint(images, pltpu.HBM))
+
+
 def gate_kernel(*refs):
     del refs
 
@@ -206,7 +225,18 @@
             turned[r, pl.ds(to, GROUP)] = scr_t[pl.ds(r, GROUP, stride=pitch)].astype(BF16)
 
     groups = mine.shape[0] // GROUP
-    if parts > 1 or groups <= 2:
+    if groups > 3:
+        base = 0
+        for sib in sibs:
+            sib_groups = sib.shape[0] // GROUP
+
+            @pl.loop(0, sib_groups)
+            def _(g, sib=sib, base=base):
+                at = pl.multiple_of(g * GROUP, GROUP)
+                group(base + at, lambda i: sib[at + i], 0)
+
+            base += sib.shape[0]
+    else:
         places = [(sib, i) for sib in sibs for i in range(sib.shape[0])]
         for g in range(groups):
 
@@ -215,12 +245,6 @@
                 return sib[place]
 
             group(g * GROUP, source, g % 2)
-    else:
-
-        @pl.loop(0, groups)
-        def _(g):
-            base = pl.multiple_of(g * GROUP, GROUP)
-            group(base, lambda i: sibs[0][base + i], 0)
 
 
 def filter_chunk(bins, mine, sibs, left, right, buffers, total, skip, at, chained):
@@ -497,9 +521,11 @@
 
     sizes, steps = zip(*y_pieces(particles))
     starts = [sum(sizes[:i]) for i in range(len(sizes))]
-    remote = [over_cls(images[a : a + n]) for a, n in zip(starts, sizes)]
+    slices = [images[a : a + n] for a, n in zip(starts, sizes)]
+    slices[0] = cut(images, sizes[0])
+    remote = [over_cls(x) for x in slices]
     other_bins = over_cls(defocus_bin)
-    own_sib = over_section(images)
+    own_sibs = [over_section(images)]
 
     refs, norm = lay_refs(references, padded)
     left, right, mask, noise, rot = prepare(
@@ -507,7 +533,7 @@
     )
     total = 2 * particles
     *buffers, token = filter_chunk(
-        defocus_bin, images, [own_sib], left, right, (), total, 0, 0, 1
+        defocus_bin, images, own_sibs, left, right, (), total, 0, 0, 1
     )
     chosen = pick(other_bins, left, right, token, starts[-1], sizes[-1])
     tokens = [chosen[0]]

time: 80.6 us -> 80.6 us (level)
  local copies, waits for them, and re-layouts: 2.4 us -> 1.21 us
  Pallas kernels: 30.4 us -> 31.5 us
    slice x3 -> x2, local copies, waits for them, and re-layouts: 2.28 us -> 1.09 us  [local(): slices = [images[a:a + n] for a, n in zip(starts, sizes)]]
    pallas_call x0 -> x1, Pallas kernels: none -> 1.14 us  [cut(): pl.pallas_call(cut_kernel, in_specs=[pl.BlockSpec(memory_space=pl.ANY)],...]
  transfers between devices with their start and end apart: 22 -> 22, of which waited for: 13 -> 13; matrix products, arithmetic and copies ran while one was open for 3% -> 1% of each run, Pallas kernels for 29% -> 30%
where the time goes in v10:
time: 80.6 us; the launch traced here: 80.1 us
  Pallas kernels  31.5 us (39%)
  waiting for transfers between devices  25.2 us (31%)
  starting transfers between devices  21.9 us (27%)
  local copies, waits for them, and re-layouts  1.21 us (2%)
    ppermute x8, waiting for transfers between devices, along(): return lax.ppermute(x, 'dom', [(i, i ^ mask) for i in range(dom)])  14.6 us
    pallas_call x4, Pallas kernels, filter_chunk(): pl.pallas_call(functools.partial(filter_kernel, picked=picked, parts=part...  12.3 us
    ppermute x8, starting transfers between devices, along(): return lax.ppermute(x, 'dom', [(i, i ^ mask) for i in range(dom)])  12 us
    pallas_call x1, Pallas kernels, lay_refs(): pl.pallas_call(functools.partial(refs_kernel, padded=padded), grid=(rots,...  8.81 us
    ppermute x3, starting transfers between devices, local(): remote = [over_cls(x) for x in slices]  5.8 us
    ppermute x3, waiting for transfers between devices, local(): remote = [over_cls(x) for x in slices]  5.58 us
    pallas_call x2, Pallas kernels, sums(): pl.pallas_call(functools.partial(sums_kernel, outer=outer, dom=dom, start...  3.62 us
    pallas_call x1, Pallas kernels, score(): pl.pallas_call(score_kernel, out_shape=(pinned((height, count), F32), pin...  3.1 us
  transfers between devices with their start and end apart: 22, of which 13 were waited for; matrix products, arithmetic and copies ran while one was open for 1% of the time, Pallas kernels for 30%

profile of v10, /device:TPU:0, one launch (start us, length us, event | category | flops | bytes accessed | tf_op | source)
XLA Modules:
  0.0 80.1 jit_solution(11723827310668520074)
XLA Ops:
  0.0 0.5 collective-permute-start.4
  0.5 1.1 %cut.1 = bf16[48,64,128]{2,1,0:T(8,128)(2,1)S(1)} custom-call(bf16[96,64,128]{2,1,0:T(8,128)(2,1)} %args_1_.4), custom_call_target="tpu_custom_call" | custom-call | flops 100000000 | bytes 300000 | tf_op jit(solution)/shard_map/cut/pallas_call | solution.py:119
  1.7 0.0 copy-start
  1.7 0.0 copy-start.1
  1.7 2.6 %collective-permute-start.3 = (bf16[48,64,128]{2,1,0:T(8,128)(2,1)S(1)}, bf16[48,64,128]{2,1,0:T(8,128)(2,1)S(1)}, u32[]{:S(2)}, u32[]{:S(2)}) collective-permute-start(bf16[48,64,128]{2,1,0:T(8,128)(2,1)S(1)} %cut.1), channel_id=1, source_target_pairs={{0,1},{1,0},{2,3},{3,2},{4,5},{5,4},{6,7},{7,6},{8,9},{9,8},{10,11... | collective-permute-start | bytes 2359304 | tf_op jit(solution)/shard_map/ppermute | solution.py:526
  4.3 0.1 collective-permute-start.1
  4.4 1.1 %slice.28 = bf16[32,64,128]{2,1,0:T(8,128)(2,1)S(1)} slice(bf16[96,64,128]{2,1,0:T(8,128)(2,1)} %args_1_.4), slice={[48:80], [0:64], [0:128]} | slice | bytes 1048576 | tf_op jit(solution)/shard_map/slice | solution.py:524
  5.5 2.0 %collective-permute-start.2 = (bf16[32,64,128]{2,1,0:T(8,128)(2,1)S(1)}, bf16[32,64,128]{2,1,0:T(8,128)(2,1)S(1)}, u32[]{:S(2)}, u32[]{:S(2)}) collective-permute-start(bf16[32,64,128]{2,1,0:T(8,128)(2,1)S(1)} %slice.28), channel_id=1, source_target_pairs={{0,1},{1,0},{2,3},{3,2},{4,5},{5,4},{6,7},{7,6},{8,9},{9,8},{10,11... | collective-permute-start | bytes 1572872 | tf_op jit(solution)/shard_map/ppermute | solution.py:526
  7.5 8.8 %refs.2 = (bf16[128,336,128]{2,1,0:T(8,128)(2,1)S(1)}, f32[336,128]{1,0:T(8,128)S(1)}) custom-call(bf16[100,3,128,128]{3,2,1,0:T(8,128)(2,1)} %refs.3), custom_call_target="tpu_custom_call" | custom-call | flops 900000000 | bytes 2700000 | tf_op jit(solution)/shard_map/refs/pallas_call | solution.py:184
  16.3 0.0 copy-done.4
  16.3 0.0 copy-done.3
  16.3 0.8 %prepare.1 = (bf16[16,128,128]{2,1,0:T(8,128)(2,1)S(1)}, bf16[16,128,128]{2,1,0:T(8,128)(2,1)S(1)}, f32[112,192]{1,0:T(8,128)S(1)}, f32[1,192]{1,0:T(1,128)S(1)}, f32[3,112,128]{2,1,0:T(8,128)S(1)}) custom-call(f32[16,128]{1,0:T(8,128)S(1)} %copy-done.3, f32[1,128]{1,0:T(1,128)S(1)} %bitcast.6, s32[192,100]{1,0:T(8,128)S(1)} %copy-done.2, ...), custom_call_target="tpu_custom_call" | custom-call | flops 300000000 | bytes 900000 | tf_op jit(solution)/shard_map/prepare/pallas_call | solution.py:96
  17.2 0.0 collective-permute-done.4.args_4_
  17.2 6.4 %filter.4 = (bf16[128,192,128]{2,1,0:T(8,128)(2,1)S(1)}, bf16[128,192,128]{2,1,0:T(8,128)(2,1)S(1)}, f32[8,128]{1,0:T(8,128)S(1)}) custom-call(s32[96]{0:T(128)S(1)} %copy-done.1, bf16[96,64,128]{2,1,0:T(8,128)(2,1)S(1)} %copy-done, bf16[16,128,128]{2,1,0:T(8,128)(2,1)S(1)} %get-tuple-element.41.args_2_.left, ...), custom_call_target="tpu_custom_call" | custom-call | flops 960000000 | bytes 2880000 | tf_op jit(solution)/shard_map/filter/pallas_call | solution.py:257
  23.6 0.0 collective-permute-done.1.bins.args_0_
  23.6 0.6 pick.1
  24.2 0.0 collective-permute-done.3.refs_0_
  24.2 0.1 fusion
  24.3 0.1 collective-permute-start.5
  24.4 0.5 collective-permute-start.6
  24.9 0.1 collective-permute-start.7
  25.0 1.2 %collective-permute-start = (bf16[16,64,128]{2,1,0:T(8,128)(2,1)S(1)}, bf16[16,64,128]{2,1,0:T(8,128)(2,1)S(1)}, u32[]{:S(2)}, u32[]{:S(2)}) collective-permute-start(bf16[16,64,128]{2,1,0:T(8,128)(2,1)S(1)} %slice.27), channel_id=1, source_target_pairs={{0,1},{1,0},{2,3},{3,2},{4,5},{5,4},{6,7},{7,6},{8,9},{9,8},{10,11... | collective-permute-start | bytes 786440 | tf_op jit(solution)/shard_map/ppermute | solution.py:526
  26.2 0.0 collective-permute-done.5.args_4_
  26.2 0.1 collective-permute-done.6.args_5_
  26.3 0.4 collective-permute-done.7.args_6_
  26.7 2.8 %filter.5 = (bf16[128,192,128]{2,1,0:T(8,128)(2,1)S(1)}, bf16[128,192,128]{2,1,0:T(8,128)(2,1)S(1)}, f32[8,128]{1,0:T(8,128)S(1)}) custom-call(s32[96]{0:T(128)S(1)} %collective-permute-done.1.bins.args_0_, bf16[48,64,128]{2,1,0:T(8,128)(2,1)S(1)} %gate.3.args_1_, ...), custom_call_target="tpu_custom_call", output_to_operand_aliasing={{0}: (7, {}), {1}: (8, {})} | custom-call | flops 480000000 | bytes 1440000 | tf_op jit(solution)/shard_map/filter/pallas_call | solution.py:257
  29.5 4.5 %collective-permute-done.2.refs_0_ = bf16[32,64,128]{2,1,0:T(8,128)(2,1)S(1)} collective-permute-done((bf16[32,64,128]{2,1,0:T(8,128)(2,1)S(1)}, bf16[32,64,128]{2,1,0:T(8,128)(2,1)S(1)}, u32[]{:S(2)}, u32[]{:S(2)}) %collective-permute-start.2) | collective-permute-done | bytes 524320 | tf_op jit(solution)/shard_map/ppermute | solution.py:526
  34.0 0.1 collective-permute-start.10
  34.1 0.5 collective-permute-start.11
  34.6 0.1 collective-permute-start.8
  34.6 0.4 collective-permute-start.9
  35.1 0.3 collective-permute-done.10.args_6_
  35.4 0.2 collective-permute-done.11.args_7_
  35.6 0.3 collective-permute-done.8.args_4_
  35.9 0.2 collective-permute-done.9.args_5_
  36.1 2.1 %filter.6 = (bf16[128,192,128]{2,1,0:T(8,128)(2,1)S(1)}, bf16[128,192,128]{2,1,0:T(8,128)(2,1)S(1)}, f32[8,128]{1,0:T(8,128)S(1)}) custom-call(s32[96]{0:T(128)S(1)} %collective-permute-done.1.bins.args_0_, bf16[32,64,128]{2,1,0:T(8,128)(2,1)S(1)} %gate.4.args_1_, ...), custom_call_target="tpu_custom_call", output_to_operand_aliasing={{0}: (8, {}), {1}: (9, {})} | custom-call | flops 320000000 | bytes 960000 | tf_op jit(solution)/shard_map/filter/pallas_call | solution.py:257
  38.3 1.1 %collective-permute-done.refs_0_ = bf16[16,64,128]{2,1,0:T(8,128)(2,1)S(1)} collective-permute-done((bf16[16,64,128]{2,1,0:T(8,128)(2,1)S(1)}, bf16[16,64,128]{2,1,0:T(8,128)(2,1)S(1)}, u32[]{:S(2)}, u32[]{:S(2)}) %collective-permute-start) | collective-permute-done | bytes 262176 | tf_op jit(solution)/shard_map/ppermute | solution.py:526
  39.4 0.0 collective-permute-start.12
  39.4 1.5 %collective-permute-done.12.args_3_ = bf16[16,64,128]{2,1,0:T(8,128)(2,1)S(1)} collective-permute-done((bf16[16,64,128]{2,1,0:T(8,128)(2,1)S(1)}, bf16[16,64,128]{2,1,0:T(8,128)(2,1)S(1)}, u32[]{:S(2)}, u32[]{:S(2)}) %collective-permute-start.12) | collective-permute-done | bytes 262176 | tf_op jit(solution)/shard_map/ppermute | solution.py:543
  40.9 1.0 %filter.7 = (bf16[128,192,128]{2,1,0:T(8,128)(2,1)S(1)}, bf16[128,192,128]{2,1,0:T(8,128)(2,1)S(1)}) custom-call(bf16[16,64,128]{2,1,0:T(8,128)(2,1)S(1)} %gate.5.args_0_, bf16[16,128,128]{2,1,0:T(8,128)(2,1)S(1)} %get-tuple-element.44.refs_1_.args_1_, ...), custom_call_target="tpu_custom_call", output_to_operand_aliasing={{0}: (4, {}), {1}: (5, {})} | custom-call | flops 160000000 | bytes 480000 | tf_op jit(solution)/shard_map/filter/pallas_call | solution.py:257
  41.9 3.1 %score.1 = (f32[336,192]{1,0:T(8,128)S(1)}, f32[8,192]{1,0:T(8,128)S(1)}) custom-call(bf16[128,192,128]{2,1,0:T(8,128)(2,1)S(1)} %get-tuple-element.54.plain, bf16[128,336,128]{2,1,0:T(8,128)(2,1)S(1)} %get-tuple-element.56.refs, f32[336,128]{1,0:T(8,128)S(1)} %get-tuple-element.40.after.norm, f32[112,192]{1,0:T(8,128)S(1)} %get-tuple-element.57.mask, ...), custom_call_target="tpu_custom_call" | custom-call | flops 500000000 | bytes 1500000 | tf_op jit(solution)/shard_map/score/pallas_call | solution.py:317
  45.0 1.8 %collective-permute-start.13 = (f32[8,192]{1,0:T(8,128)S(1)}, f32[8,192]{1,0:T(8,128)S(1)}, u32[]{:S(2)}, u32[]{:S(2)}) collective-permute-start(f32[8,192]{1,0:T(8,128)S(1)} %get-tuple-element.60.rest_1_), channel_id=1, source_target_pairs={{0,1},{1,0},{2,3},{3,2},{4,5},{5,4},{6,7},{7,6},{8,9},{9,8},{10,11... | collective-permute-start | bytes 18440 | tf_op jit(solution)/shard_map/ppermute | solution.py:552
  46.8 1.9 %collective-permute-done.13.rest_2_ = f32[8,192]{1,0:T(8,128)S(1)} collective-permute-done((f32[8,192]{1,0:T(8,128)S(1)}, f32[8,192]{1,0:T(8,128)S(1)}, u32[]{:S(2)}, u32[]{:S(2)}) %collective-permute-start.13) | collective-permute-done | bytes 6176 | tf_op jit(solution)/shard_map/ppermute | solution.py:552
  48.7 2.6 %sums.2 = (f32[4,500,128]{2,1,0:T(8,128)S(1)}, bf16[4,500,128]{2,1,0:T(8,128)(2,1)S(1)}, bf16[2,112,384]{2,1,0:T(8,128)(2,1)S(1)}) custom-call(bf16[128,192,128]{2,1,0:T(8,128)(2,1)S(1)} %get-tuple-element.54.plain, bf16[128,192,128]{2,1,0:T(8,128)(2,1)S(1)} %get-tuple-element.55.turned, f32[336,192]{1,0:T(8,128)S(1)} %get-tuple-element.59.rest_0_, ...), custom_call_target="tpu_custom_call" | custom-call | flops 400000000 | bytes 1200000 | tf_op jit(solution)/shard_map/sums/pallas_call | solution.py:409
  51.3 1.8 %collective-permute-start.14 = (bf16[4,500,128]{2,1,0:T(8,128)(2,1)S(1)}, bf16[4,500,128]{2,1,0:T(8,128)(2,1)S(1)}, u32[]{:S(2)}, u32[]{:S(2)}) collective-permute-start(bf16[4,500,128]{2,1,0:T(8,128)(2,1)S(1)} %get-tuple-element.63.rest_1_), channel_id=1, source_target_pairs={{0,2},{2,0},{4,6},{6,4},{8,10},{10,8},{12,14},{14,12},{1,3},{3,1},... | collective-permute-start | bytes 1536008 | tf_op jit(solution)/shard_map/ppermute | solution.py:555
  53.1 1.1 %sums.3 = (f32[2,300,128]{2,1,0:T(8,128)S(1)}, bf16[2,300,128]{2,1,0:T(8,128)(2,1)S(1)}, bf16[2,300,128]{2,1,0:T(8,128)(2,1)S(1)}, bf16[2,300,128]{2,1,0:T(8,128)(2,1)S(1)}) custom-call(bf16[128,192,128]{2,1,0:T(8,128)(2,1)S(1)} %get-tuple-element.54.plain, bf16[128,192,128]{2,1,0:T(8,128)(2,1)S(1)} %get-tuple-element.55.turned, ...), custom_call_target="tpu_custom_call" | custom-call | flops 240000000 | bytes 720000 | tf_op jit(solution)/shard_map/sums/pallas_call | solution.py:409
  54.1 2.6 %collective-permute-start.18 = (bf16[2,300,128]{2,1,0:T(8,128)(2,1)S(1)}, bf16[2,300,128]{2,1,0:T(8,128)(2,1)S(1)}, u32[]{:S(2)}, u32[]{:S(2)}) collective-permute-start(bf16[2,300,128]{2,1,0:T(8,128)(2,1)S(1)} %get-tuple-element.70), channel_id=1, source_target_pairs={{0,8},{2,10},{4,12},{6,14},{8,0},{10,2},{12,4},{14,6},{1,9},{3,11}... | collective-permute-start | bytes 460808 | tf_op jit(solution)/shard_map/ppermute | solution.py:555
  56.8 1.4 %collective-permute-start.19 = (bf16[2,300,128]{2,1,0:T(8,128)(2,1)S(1)}, bf16[2,300,128]{2,1,0:T(8,128)(2,1)S(1)}, u32[]{:S(2)}, u32[]{:S(2)}) collective-permute-start(bf16[2,300,128]{2,1,0:T(8,128)(2,1)S(1)} %get-tuple-element.71), channel_id=1, source_target_pairs={{0,12},{2,14},{4,8},{6,10},{8,4},{10,6},{12,0},{14,2},{1,13},{3,15... | collective-permute-start | bytes 460808 | tf_op jit(solution)/shard_map/ppermute | solution.py:555
  58.1 0.2 collective-permute-start.20
  58.3 5.6 %collective-permute-done.14.got = bf16[4,500,128]{2,1,0:T(8,128)(2,1)S(1)} collective-permute-done((bf16[4,500,128]{2,1,0:T(8,128)(2,1)S(1)}, bf16[4,500,128]{2,1,0:T(8,128)(2,1)S(1)}, u32[]{:S(2)}, u32[]{:S(2)}) %collective-permute-start.14) | collective-permute-done | bytes 512032 | tf_op jit(solution)/shard_map/ppermute | solution.py:555
  64.0 0.1 fold.1
  64.1 2.9 %collective-permute-start.15 = (bf16[1,500,128]{2,1,0:T(8,128)(2,1)S(1)}, bf16[1,500,128]{2,1,0:T(8,128)(2,1)S(1)}, u32[]{:S(2)}, u32[]{:S(2)}) collective-permute-start(bf16[1,500,128]{2,1,0:T(8,128)(2,1)S(1)} %get-tuple-element.65), channel_id=1, source_target_pairs={{0,8},{2,10},{4,12},{6,14},{8,0},{10,2},{12,4},{14,6},{1,9},{3,11}... | collective-permute-start | bytes 384008 | tf_op jit(solution)/shard_map/ppermute | solution.py:555
  67.0 1.4 %collective-permute-start.16 = (bf16[1,500,128]{2,1,0:T(8,128)(2,1)S(1)}, bf16[1,500,128]{2,1,0:T(8,128)(2,1)S(1)}, u32[]{:S(2)}, u32[]{:S(2)}) collective-permute-start(bf16[1,500,128]{2,1,0:T(8,128)(2,1)S(1)} %get-tuple-element.66), channel_id=1, source_target_pairs={{0,12},{2,14},{4,8},{6,10},{8,4},{10,6},{12,0},{14,2},{1,13},{3,15... | collective-permute-start | bytes 384008 | tf_op jit(solution)/shard_map/ppermute | solution.py:555
  68.3 0.0 collective-permute-done.18.rest_0_
  68.3 0.2 collective-permute-start.17
  68.6 0.0 collective-permute-done.19.rest_1_
  68.6 0.0 collective-permute-done.20.rest_2_
  68.6 0.1 gather.1
  68.7 1.6 %collective-permute-start.21 = (bf16[1,300,128]{2,1,0:T(8,128)(2,1)S(1)}, bf16[1,300,128]{2,1,0:T(8,128)(2,1)S(1)}, u32[]{:S(2)}, u32[]{:S(2)}) collective-permute-start(bf16[1,300,128]{2,1,0:T(8,128)(2,1)S(1)} %get-tuple-element.74), channel_id=1, source_target_pairs={{0,2},{2,0},{4,6},{6,4},{8,10},{10,8},{12,14},{14,12},{1,3},{3,1},... | collective-permute-start | bytes 230408 | tf_op jit(solution)/shard_map/ppermute | solution.py:555
  70.2 2.9 %collective-permute-done.21.args_5_ = bf16[1,300,128]{2,1,0:T(8,128)(2,1)S(1)} collective-permute-done((bf16[1,300,128]{2,1,0:T(8,128)(2,1)S(1)}, bf16[1,300,128]{2,1,0:T(8,128)(2,1)S(1)}, u32[]{:S(2)}, u32[]{:S(2)}) %collective-permute-start.21) | collective-permute-done | bytes 76832 | tf_op jit(solution)/shard_map/ppermute | solution.py:555
  73.1 6.1 %collective-permute-done.15.args_1_ = bf16[1,500,128]{2,1,0:T(8,128)(2,1)S(1)} collective-permute-done((bf16[1,500,128]{2,1,0:T(8,128)(2,1)S(1)}, bf16[1,500,128]{2,1,0:T(8,128)(2,1)S(1)}, u32[]{:S(2)}, u32[]{:S(2)}) %collective-permute-start.15) | collective-permute-done | bytes 128032 | tf_op jit(solution)/shard_map/ppermute | solution.py:555
  79.2 0.0 collective-permute-done.16.args_2_
  79.2 0.0 collective-permute-done.17.args_3_
  79.2 0.9 %finish.1 = f32[800,128]{1,0:T(8,128)} custom-call(f32[1,500,128]{2,1,0:T(8,128)S(1)} %get-tuple-element.64.args_0_, bf16[1,500,128]{2,1,0:T(8,128)(2,1)S(1)} %collective-permute-done.15.args_1_, bf16[1,500,128]{2,1,0:T(8,128)(2,1)S(1)} %collective-permute-done.16.args_2_, bf16[1,500,128]{2,1,0:T(8,128)(2,1)S(1)} %collective-permute-done.17.args_3_, ...), custom_call_target="tpu_custom_call" | custom-call | flops 100000000 | bytes 300000 | tf_op jit(solution)/shard_map/finish/pallas_call | solution.py:488
  (15 shorter events, 0.1 us)
Async XLA Ops:
  0.0 16.3 %copy-start.6 = (f32[128]{0:T(128)S(1)}, f32[128]{0:T(128)}, u32[]{:S(2)}) copy-start(f32[128]{0:T(128)} %param.11) | copy-start | bytes 1540
  0.0 16.3 %copy-start.5 = (f32[192]{0:T(256)S(1)}, f32[192]{0:T(256)}, u32[]{:S(2)}) copy-start(f32[192]{0:T(256)} %param.15) | copy-start | bytes 2308
  0.0 16.3 %copy-start.4 = (s32[100,3]{0,1:T(4,128)S(1)}, s32[100,3]{0,1:T(4,128)}, u32[]{:S(2)}) copy-start(s32[100,3]{0,1:T(4,128)} %param.13) | copy-start | bytes 3604
  0.0 16.3 %copy-start.3 = (f32[16,128]{1,0:T(8,128)S(1)}, f32[16,128]{1,0:T(8,128)}, u32[]{:S(2)}) copy-start(f32[16,128]{1,0:T(8,128)} %ctf.1) | copy-start | bytes 24580
  0.0 16.3 %copy-start.2 = (s32[192,100]{1,0:T(8,128)S(1)}, s32[192,100]{1,0:T(8,128)}, u32[]{:S(2)}) copy-start(s32[192,100]{1,0:T(8,128)} %mask.1) | copy-start | bytes 230404
  0.0 17.1 %collective-permute-start.4 = (bf16[96,64,128]{2,1,0:T(8,128)(2,1)}, bf16[96,64,128]{2,1,0:T(8,128)(2,1)S(1)}, u32[]{:S(2)}, u32[]{:S(2)}) collective-permute-start(bf16[96,64,128]{2,1,0:T(8,128)(2,1)} %args_1_.4), channel_id=1, source_target_pairs={{0,16},{16,0},{1,17},{17,1},{2,18},{18,2},{3,19},{19,3},{4,20},{20... | collective-permute-start | bytes 4718600 | tf_op jit(solution)/shard_map/ppermute | solution.py:528
  1.7 15.5 %copy-start = (bf16[96,64,128]{2,1,0:T(8,128)(2,1)S(1)}, bf16[96,64,128]{2,1,0:T(8,128)(2,1)}, u32[]{:S(2)}) copy-start(bf16[96,64,128]{2,1,0:T(8,128)(2,1)} %args_1_.4) | copy-start | bytes 4718596
  1.7 15.5 %copy-start.1 = (s32[96]{0:T(128)S(1)}, s32[96]{0:T(128)}, u32[]{:S(2)}) copy-start(s32[96]{0:T(128)} %args_0_.4) | copy-start | bytes 1156
  1.7 22.5 %collective-permute-start.3 = (bf16[48,64,128]{2,1,0:T(8,128)(2,1)S(1)}, bf16[48,64,128]{2,1,0:T(8,128)(2,1)S(1)}, u32[]{:S(2)}, u32[]{:S(2)}) collective-permute-start(bf16[48,64,128]{2,1,0:T(8,128)(2,1)S(1)} %cut.1), channel_id=1, source_target_pairs={{0,1},{1,0},{2,3},{3,2},{4,5},{5,4},{6,7},{7,6},{8,9},{9,8},{10,11... | collective-permute-start | bytes 2359304 | tf_op jit(solution)/shard_map/ppermute | solution.py:526
  4.3 19.3 %collective-permute-start.1 = (s32[96]{0:T(128)}, s32[96]{0:T(128)S(1)}, u32[]{:S(2)}, u32[]{:S(2)}) collective-permute-start(s32[96]{0:T(128)} %args_0_.4), channel_id=1, source_target_pairs={{0,1},{1,0},{2,3},{3,2},{4,5},{5,4},{6,7},{7,6},{8,9},{9,8},{10,11... | collective-permute-start | bytes 1160 | tf_op jit(solution)/shard_map/ppermute | solution.py:527
  5.5 28.5 %collective-permute-start.2 = (bf16[32,64,128]{2,1,0:T(8,128)(2,1)S(1)}, bf16[32,64,128]{2,1,0:T(8,128)(2,1)S(1)}, u32[]{:S(2)}, u32[]{:S(2)}) collective-permute-start(bf16[32,64,128]{2,1,0:T(8,128)(2,1)S(1)} %slice.28), channel_id=1, source_target_pairs={{0,1},{1,0},{2,3},{3,2},{4,5},{5,4},{6,7},{7,6},{8,9},{9,8},{10,11... | collective-permute-start | bytes 1572872 | tf_op jit(solution)/shard_map/ppermute | solution.py:526
  24.3 1.9 %collective-permute-start.5 = (bf16[16,64,128]{2,1,0:T(8,128)(2,1)S(1)}, bf16[16,64,128]{2,1,0:T(8,128)(2,1)S(1)}, u32[]{:S(2)}, u32[]{:S(2)}) collective-permute-start(bf16[16,64,128]{2,1,0:T(8,128)(2,1)S(1)} %get-tuple-element.77), channel_id=1, source_target_pairs={{0,16},{16,0},{1,17},{17,1},{2,18},{18,2},{3,19},{19,3},{4,20},{20... | collective-permute-start | bytes 786440 | tf_op jit(solution)/shard_map/ppermute | solution.py:543
  24.4 1.9 %collective-permute-start.6 = (bf16[16,64,128]{2,1,0:T(8,128)(2,1)S(1)}, bf16[16,64,128]{2,1,0:T(8,128)(2,1)S(1)}, u32[]{:S(2)}, u32[]{:S(2)}) collective-permute-start(bf16[16,64,128]{2,1,0:T(8,128)(2,1)S(1)} %get-tuple-element.76), channel_id=1, source_target_pairs={{0,16},{16,0},{1,17},{17,1},{2,18},{18,2},{3,19},{19,3},{4,20},{20... | collective-permute-start | bytes 786440 | tf_op jit(solution)/shard_map/ppermute | solution.py:543
  24.9 1.8 %collective-permute-start.7 = (bf16[16,64,128]{2,1,0:T(8,128)(2,1)S(1)}, bf16[16,64,128]{2,1,0:T(8,128)(2,1)S(1)}, u32[]{:S(2)}, u32[]{:S(2)}) collective-permute-start(bf16[16,64,128]{2,1,0:T(8,128)(2,1)S(1)} %get-tuple-element.75), channel_id=1, source_target_pairs={{0,16},{16,0},{1,17},{17,1},{2,18},{18,2},{3,19},{19,3},{4,20},{20... | collective-permute-start | bytes 786440 | tf_op jit(solution)/shard_map/ppermute | solution.py:543
  25.0 14.4 %collective-permute-start = (bf16[16,64,128]{2,1,0:T(8,128)(2,1)S(1)}, bf16[16,64,128]{2,1,0:T(8,128)(2,1)S(1)}, u32[]{:S(2)}, u32[]{:S(2)}) collective-permute-start(bf16[16,64,128]{2,1,0:T(8,128)(2,1)S(1)} %slice.27), channel_id=1, source_target_pairs={{0,1},{1,0},{2,3},{3,2},{4,5},{5,4},{6,7},{7,6},{8,9},{9,8},{10,11... | collective-permute-start | bytes 786440 | tf_op jit(solution)/shard_map/ppermute | solution.py:526
  34.0 1.4 %collective-permute-start.10 = (bf16[8,64,128]{2,1,0:T(8,128)(2,1)S(1)}, bf16[8,64,128]{2,1,0:T(8,128)(2,1)S(1)}, u32[]{:S(2)}, u32[]{:S(2)}) collective-permute-start(bf16[8,64,128]{2,1,0:T(8,128)(2,1)S(1)} %get-tuple-element.79), channel_id=1, source_target_pairs={{0,16},{16,0},{1,17},{17,1},{2,18},{18,2},{3,19},{19,3},{4,20},{20... | collective-permute-start | bytes 393224 | tf_op jit(solution)/shard_map/ppermute | solution.py:543
  34.1 1.5 %collective-permute-start.11 = (bf16[8,64,128]{2,1,0:T(8,128)(2,1)S(1)}, bf16[8,64,128]{2,1,0:T(8,128)(2,1)S(1)}, u32[]{:S(2)}, u32[]{:S(2)}) collective-permute-start(bf16[8,64,128]{2,1,0:T(8,128)(2,1)S(1)} %get-tuple-element.78), channel_id=1, source_target_pairs={{0,16},{16,0},{1,17},{17,1},{2,18},{18,2},{3,19},{19,3},{4,20},{20... | collective-permute-start | bytes 393224 | tf_op jit(solution)/shard_map/ppermute | solution.py:543
  34.6 1.3 %collective-permute-start.8 = (bf16[8,64,128]{2,1,0:T(8,128)(2,1)S(1)}, bf16[8,64,128]{2,1,0:T(8,128)(2,1)S(1)}, u32[]{:S(2)}, u32[]{:S(2)}) collective-permute-start(bf16[8,64,128]{2,1,0:T(8,128)(2,1)S(1)} %get-tuple-element.81), channel_id=1, source_target_pairs={{0,16},{16,0},{1,17},{17,1},{2,18},{18,2},{3,19},{19,3},{4,20},{20... | collective-permute-start | bytes 393224 | tf_op jit(solution)/shard_map/ppermute | solution.py:543
  34.6 1.5 %collective-permute-start.9 = (bf16[8,64,128]{2,1,0:T(8,128)(2,1)S(1)}, bf16[8,64,128]{2,1,0:T(8,128)(2,1)S(1)}, u32[]{:S(2)}, u32[]{:S(2)}) collective-permute-start(bf16[8,64,128]{2,1,0:T(8,128)(2,1)S(1)} %get-tuple-element.80), channel_id=1, source_target_pairs={{0,16},{16,0},{1,17},{17,1},{2,18},{18,2},{3,19},{19,3},{4,20},{20... | collective-permute-start | bytes 393224 | tf_op jit(solution)/shard_map/ppermute | solution.py:543
  39.4 1.5 %collective-permute-start.12 = (bf16[16,64,128]{2,1,0:T(8,128)(2,1)S(1)}, bf16[16,64,128]{2,1,0:T(8,128)(2,1)S(1)}, u32[]{:S(2)}, u32[]{:S(2)}) collective-permute-start(bf16[16,64,128]{2,1,0:T(8,128)(2,1)S(1)} %gate.5.args_0_), channel_id=1, source_target_pairs={{0,16},{16,0},{1,17},{17,1},{2,18},{18,2},{3,19},{19,3},{4,20},{20... | collective-permute-start | bytes 786440 | tf_op jit(solution)/shard_map/ppermute | solution.py:543
  45.0 3.7 %collective-permute-start.13 = (f32[8,192]{1,0:T(8,128)S(1)}, f32[8,192]{1,0:T(8,128)S(1)}, u32[]{:S(2)}, u32[]{:S(2)}) collective-permute-start(f32[8,192]{1,0:T(8,128)S(1)} %get-tuple-element.60.rest_1_), channel_id=1, source_target_pairs={{0,1},{1,0},{2,3},{3,2},{4,5},{5,4},{6,7},{7,6},{8,9},{9,8},{10,11... | collective-permute-start | bytes 18440 | tf_op jit(solution)/shard_map/ppermute | solution.py:552
  51.3 12.7 %collective-permute-start.14 = (bf16[4,500,128]{2,1,0:T(8,128)(2,1)S(1)}, bf16[4,500,128]{2,1,0:T(8,128)(2,1)S(1)}, u32[]{:S(2)}, u32[]{:S(2)}) collective-permute-start(bf16[4,500,128]{2,1,0:T(8,128)(2,1)S(1)} %get-tuple-element.63.rest_1_), channel_id=1, source_target_pairs={{0,2},{2,0},{4,6},{6,4},{8,10},{10,8},{12,14},{14,12},{1,3},{3,1},... | collective-permute-start | bytes 1536008 | tf_op jit(solution)/shard_map/ppermute | solution.py:555
  54.1 14.2 %collective-permute-start.18 = (bf16[2,300,128]{2,1,0:T(8,128)(2,1)S(1)}, bf16[2,300,128]{2,1,0:T(8,128)(2,1)S(1)}, u32[]{:S(2)}, u32[]{:S(2)}) collective-permute-start(bf16[2,300,128]{2,1,0:T(8,128)(2,1)S(1)} %get-tuple-element.70), channel_id=1, source_target_pairs={{0,8},{2,10},{4,12},{6,14},{8,0},{10,2},{12,4},{14,6},{1,9},{3,11}... | collective-permute-start | bytes 460808 | tf_op jit(solution)/shard_map/ppermute | solution.py:555
  56.8 11.8 %collective-permute-start.19 = (bf16[2,300,128]{2,1,0:T(8,128)(2,1)S(1)}, bf16[2,300,128]{2,1,0:T(8,128)(2,1)S(1)}, u32[]{:S(2)}, u32[]{:S(2)}) collective-permute-start(bf16[2,300,128]{2,1,0:T(8,128)(2,1)S(1)} %get-tuple-element.71), channel_id=1, source_target_pairs={{0,12},{2,14},{4,8},{6,10},{8,4},{10,6},{12,0},{14,2},{1,13},{3,15... | collective-permute-start | bytes 460808 | tf_op jit(solution)/shard_map/ppermute | solution.py:555
  58.1 10.4 %collective-permute-start.20 = (bf16[2,300,128]{2,1,0:T(8,128)(2,1)S(1)}, bf16[2,300,128]{2,1,0:T(8,128)(2,1)S(1)}, u32[]{:S(2)}, u32[]{:S(2)}) collective-permute-start(bf16[2,300,128]{2,1,0:T(8,128)(2,1)S(1)} %get-tuple-element.72), channel_id=1, source_target_pairs={{0,4},{2,6},{4,0},{6,2},{8,12},{10,14},{12,8},{14,10},{1,5},{3,7},... | collective-permute-start | bytes 460808 | tf_op jit(solution)/shard_map/ppermute | solution.py:555
  64.1 15.1 %collective-permute-start.15 = (bf16[1,500,128]{2,1,0:T(8,128)(2,1)S(1)}, bf16[1,500,128]{2,1,0:T(8,128)(2,1)S(1)}, u32[]{:S(2)}, u32[]{:S(2)}) collective-permute-start(bf16[1,500,128]{2,1,0:T(8,128)(2,1)S(1)} %get-tuple-element.65), channel_id=1, source_target_pairs={{0,8},{2,10},{4,12},{6,14},{8,0},{10,2},{12,4},{14,6},{1,9},{3,11}... | collective-permute-start | bytes 384008 | tf_op jit(solution)/shard_map/ppermute | solution.py:555
  67.0 12.2 %collective-permute-start.16 = (bf16[1,500,128]{2,1,0:T(8,128)(2,1)S(1)}, bf16[1,500,128]{2,1,0:T(8,128)(2,1)S(1)}, u32[]{:S(2)}, u32[]{:S(2)}) collective-permute-start(bf16[1,500,128]{2,1,0:T(8,128)(2,1)S(1)} %get-tuple-element.66), channel_id=1, source_target_pairs={{0,12},{2,14},{4,8},{6,10},{8,4},{10,6},{12,0},{14,2},{1,13},{3,15... | collective-permute-start | bytes 384008 | tf_op jit(solution)/shard_map/ppermute | solution.py:555
  68.3 10.9 %collective-permute-start.17 = (bf16[1,500,128]{2,1,0:T(8,128)(2,1)S(1)}, bf16[1,500,128]{2,1,0:T(8,128)(2,1)S(1)}, u32[]{:S(2)}, u32[]{:S(2)}) collective-permute-start(bf16[1,500,128]{2,1,0:T(8,128)(2,1)S(1)} %get-tuple-element.67), channel_id=1, source_target_pairs={{0,4},{2,6},{4,0},{6,2},{8,12},{10,14},{12,8},{14,10},{1,5},{3,7},... | collective-permute-start | bytes 384008 | tf_op jit(solution)/shard_map/ppermute | solution.py:555
  68.7 4.5 %collective-permute-start.21 = (bf16[1,300,128]{2,1,0:T(8,128)(2,1)S(1)}, bf16[1,300,128]{2,1,0:T(8,128)(2,1)S(1)}, u32[]{:S(2)}, u32[]{:S(2)}) collective-permute-start(bf16[1,300,128]{2,1,0:T(8,128)(2,1)S(1)} %get-tuple-element.74), channel_id=1, source_target_pairs={{0,2},{2,0},{4,6},{6,4},{8,10},{10,8},{12,14},{14,12},{1,3},{3,1},... | collective-permute-start | bytes 230408 | tf_op jit(solution)/shard_map/ppermute | solution.py:555

commit v11 on v8

--- a/solution.py
+++ b/solution.py
@@ -319,79 +319,91 @@
         out[row] = jnp.concatenate([quarters[q] for q in pair], axis=1).astype(BF16)
 
 
-def sums_kernel(plain, turned, *rest, outer, dom, start, rows, classes):
+def row_pair(weights, plain, turned, both, classes):
+    height, _, width = plain.shape
+    direct = jnp.concatenate(
+        [jnp.concatenate([plain[i], turned[height - 1 - i]], axis=0) for i in both], axis=1
+    )
+    mirror = jnp.concatenate(
+        [jnp.concatenate([plain[height - 1 - i], turned[i]], axis=0) for i in both], axis=1
+    )
+    direct = nn(weights[0], direct)
+    mirror = nn(weights[1], mirror)
+    padded = weights.shape[1]
+    flip = width - 1 - lax.broadcasted_iota(jnp.int32, (padded, width), 1)
+    return [
+        (
+            direct[:, at : at + width]
+            + jnp.take_along_axis(mirror[:, at : at + width], flip, axis=1)
+        )[:classes]
+        for at in (0, width)
+    ]
+
+
+def row_place(plain, dom, start):
+    half = plain.shape[0] // 2
+    first = lax.axis_index("section") * half + start
+    return lambda block, r: first + block * (half // dom) + r
+
+
+def one_side(weights, plain, turned, out, side, dom, start, rows, classes):
+    place = row_place(plain, dom, start)
+    count = dom // 2
+
+    def pair(g, h):
+        for r in range(rows):
+            both = [place(2 * k + side, r) for k in (g, h)]
+            for k, value in zip((g, h), row_pair(weights, plain, turned, both, classes)):
+                out[k, r * classes : (r + 1) * classes] = value.astype(out.dtype)
+
+    if count == 1:
+        pair(0, 0)
+    else:
+
+        @pl.loop(0, count // 2)
+        def _(g):
+            pair(2 * g, 2 * g + 1)
+
+
+def both_sides(weights, plain, turned, out, z, dom, start, rows, classes):
+    place = row_place(plain, dom, start)
+    for r in range(rows):
+        both = [place(2 * z + side, r) for side in range(2)]
+        for side, value in enumerate(row_pair(weights, plain, turned, both, classes)):
+            out[side, r * classes : (r + 1) * classes] = value.astype(out.dtype)
+
+
+def inner_kernel(scaled, mine, other, rot, plain, turned, send, weights, *, dom, **sizes):
+    weigh(scaled, mine, other, rot, weights)
+    away = 1 - lax.axis_index("dom") % 2
+    one_side(weights, plain, turned, send, away, dom, **sizes)
+
+
+def outer_kernel(weights, plain, turned, after, *outs, dom, **sizes):
+    del after
+    z = lax.axis_index("dom") // 2
+    for m, out in enumerate(outs):
+        both_sides(weights, plain, turned, out, jnp.bitwise_xor(z, m + 1), dom, **sizes)
+
+
+def keep_kernel(weights, plain, turned, after, *outs, dom, classes, inner, outer):
+    del after
+    own = lax.axis_index("dom")
+    one_side(weights, plain, turned, outs[0], own % 2, dom, 0, inner, classes)
     if outer:
-        weights = rest[0]
-        outs = rest[-(dom // 2) :]
-    else:
-        weights = rest[-1]
-        outs = rest[-3:-1]
-        weigh(*rest[:4], weights)
-    width = outs[0].shape[2]
-    height = plain.shape[0]
-    block = height // 2 // dom
-    first = lax.axis_index("section") * (height // 2) + start
-    own = lax.axis_index("dom")
-    parity = own % 2
-    straight = weights[0]
-    mirrored = weights[1]
-    flip = width - 1 - lax.broadcasted_iota(jnp.int32, (straight.shape[0], width), 1)
-
-    def pair(g, sides, r):
-        both = [first + (2 * g + side) * block + r for side in sides]
-        direct = jnp.concatenate(
-            [jnp.concatenate([plain[i], turned[height - 1 - i]], axis=0) for i in both], axis=1
-        )
-        mirror = jnp.concatenate(
-            [jnp.concatenate([plain[height - 1 - i], turned[i]], axis=0) for i in both], axis=1
-        )
-        direct = nn(straight, direct)
-        mirror = nn(mirrored, mirror)
-        return [
-            (
-                direct[:, at : at + width]
-                + jnp.take_along_axis(mirror[:, at : at + width], flip, axis=1)
-            )[:classes]
-            for at in (0, width)
-        ]
-
-    if outer:
-        for m, out in enumerate(outs):
-            for r in range(rows):
-                for side, value in enumerate(pair(jnp.bitwise_xor(own // 2, m), (0, 1), r)):
-                    out[side, r * classes : (r + 1) * classes] = value.astype(out.dtype)
-    else:
-        keep, send = outs
-
-        @pl.loop(0, dom // 2)
-        def _(g):
-            for r in range(rows):
-                away, here = pair(g, (1 - parity, parity), r)
-                at = slice(r * classes, (r + 1) * classes)
-                send[g, at] = away.astype(BF16)
-                keep[g, at] = here
-
-
-def sums(inputs, plain, turned, after, outer, dom, start, rows, classes):
-    width = plain.shape[2]
+        both_sides(weights, plain, turned, outs[1], own // 2, dom, inner, outer, classes)
+
+
+def call_sums(kernel, args, after, out_shape, rows):
     vmem = pl.BlockSpec(memory_space=pltpu.VMEM)
-    count = 2 if outer else dom // 2
-    shape = (count, rows * classes, width)
-    out_shape = [pinned(shape, F32)]
-    out_shape += [jax.ShapeDtypeStruct(shape, BF16)] * (dom // 2 - 1 if outer else 1)
-    if not outer:
-        rot = inputs[3]
-        out_shape.append(pinned((2, rot.shape[1], 2 * plain.shape[1]), BF16))
-    return pl.pallas_call(
-        functools.partial(
-            sums_kernel, outer=outer, dom=dom, start=start, rows=rows, classes=classes
-        ),
-        in_specs=[vmem] * (2 + len(inputs)) + [pl.BlockSpec(memory_space=pl.ANY)] * len(after),
-        out_shape=tuple(out_shape),
+    return pl.pallas_call(
+        kernel,
+        in_specs=[vmem] * len(args) + [pl.BlockSpec(memory_space=pl.ANY)] * len(after),
+        out_shape=out_shape,
         compiler_params=pltpu.CompilerParams(vmem_limit_bytes=8 * MIB),
         cost_estimate=cost(SUMS * rows),
         name="sums",
-    )(held(plain), held(turned), *inputs, *after)
+    )(*args, *after)
 
 
 def gather_kernel(keep, *rest, came):
@@ -533,13 +545,45 @@
         return [along(sends[m], (m + 1) << bit) for m in far_first]
 
     inner, outer = row_pieces(half // dom, dom)
-    keep, send, weights = sums(inputs, plain, turned, (), False, dom, 0, inner, classes)
+    images_in = (held(plain), held(turned))
+    count = dom // 2
+    send, weights = call_sums(
+        functools.partial(
+            inner_kernel, dom=dom, start=0, rows=inner, classes=classes
+        ),
+        inputs + images_in,
+        (),
+        (
+            jax.ShapeDtypeStruct((count, inner * classes, width), BF16),
+            pinned((2, rot.shape[1], 2 * total), BF16),
+        ),
+        inner,
+    )
     got = along(send, 1)
+    weighted = (held(weights),) + images_in
+    keep_shape = (pinned((count, inner * classes, width), F32),)
+    after = send
     if outer:
-        keep_b, *sends_b = sums(
-            (held(weights),), plain, turned, (send,), True, dom, inner, outer, classes
+        shape = (2, outer * classes, width)
+        sends_b = call_sums(
+            functools.partial(
+                outer_kernel, dom=dom, start=inner, rows=outer, classes=classes
+            ),
+            weighted,
+            (send,),
+            (jax.ShapeDtypeStruct(shape, BF16),) * (count - 1),
+            outer,
         )
         got_b = spread(sends_b, 1)
+        keep_shape += (pinned(shape, F32),)
+        after = sends_b[0]
+    keep, *keep_b = call_sums(
+        functools.partial(keep_kernel, dom=dom, classes=classes, inner=inner, outer=outer),
+        weighted,
+        (after,),
+        keep_shape,
+        inner,
+    )
     bit = 1
     while keep.shape[0] > 4:
         keep, send = fold(keep, got, (), 2, bit)
@@ -548,7 +592,7 @@
     keep, *sends = fold(keep, got, (), keep.shape[0], bit)
     done = [[keep] + spread(sends, bit)]
     if outer:
-        keep_b, send_b = gather(keep_b, got_b)
+        keep_b, send_b = gather(keep_b[0], got_b)
         done.append([keep_b, along(send_b, 1)])
     return finish(done, classes)
 

time: 80.6 us -> 79.3 us (0.984)
  waiting for transfers between devices: 25.2 us -> 23.6 us
    ppermute x8, waiting for transfers between devices: 14.6 us -> 13.1 us  [along(): return lax.ppermute(x, 'dom', [(i, i ^ mask) for i in range(dom)])]
    pallas_call x2 -> x3, Pallas kernels: 3.62 us -> 3.92 us  [call_sums(): pl.pallas_call(kernel, in_specs=[vmem] * len(args) + [pl.BlockSpec(memory...]
  transfers between devices with their start and end apart: 22 -> 22, of which waited for: 13 -> 13; matrix products, arithmetic and copies ran while one was open for 3% -> 3% of each run, Pallas kernels for 29% -> 31%
where the time goes in v11:
time: 79.3 us; the launch traced here: 78.8 us
  Pallas kernels  30.7 us (39%)
  waiting for transfers between devices  23.6 us (30%)
  starting transfers between devices  22 us (28%)
  local copies, waits for them, and re-layouts  2.4 us (3%)
    ppermute x8, waiting for transfers between devices, along(): return lax.ppermute(x, 'dom', [(i, i ^ mask) for i in range(dom)])  13.1 us
    pallas_call x4, Pallas kernels, filter_chunk(): pl.pallas_call(functools.partial(filter_kernel, picked=picked, parts=part...  12.3 us
    ppermute x8, starting transfers between devices, along(): return lax.ppermute(x, 'dom', [(i, i ^ mask) for i in range(dom)])  12 us
    pallas_call x1, Pallas kernels, lay_refs(): pl.pallas_call(functools.partial(refs_kernel, padded=padded), grid=(rots,...  8.81 us
    ppermute x3, starting transfers between devices, local(): remote = [over_cls(images[a:a + n]) for a, n in zip(starts, sizes)]  5.82 us
    ppermute x3, waiting for transfers between devices, local(): remote = [over_cls(images[a:a + n]) for a, n in zip(starts, sizes)]  5.61 us
    pallas_call x3, Pallas kernels, call_sums(): pl.pallas_call(kernel, in_specs=[vmem] * len(args) + [pl.BlockSpec(memory...  3.92 us
    pallas_call x1, Pallas kernels, score(): pl.pallas_call(score_kernel, out_shape=(pinned((height, count), F32), pin...  3.1 us
  transfers between devices with their start and end apart: 22, of which 13 were waited for; matrix products, arithmetic and copies ran while one was open for 3% of the time, Pallas kernels for 31%

profile of v11, /device:TPU:0, one launch (start us, length us, event | category | flops | bytes accessed | tf_op | source)
XLA Modules:
  0.0 78.8 jit_solution(14616179896309523142)
XLA Ops:
  0.0 0.5 collective-permute-start.4
  0.5 1.2 %slice.32 = bf16[48,64,128]{2,1,0:T(8,128)(2,1)S(1)} slice(bf16[96,64,128]{2,1,0:T(8,128)(2,1)} %args_1_.4), slice={[0:48], [0:64], [0:128]} | slice | bytes 1572864 | tf_op jit(solution)/shard_map/slice | solution.py:512
  1.7 0.0 copy-start
  1.7 0.0 copy-start.1
  1.8 2.6 %collective-permute-start.3 = (bf16[48,64,128]{2,1,0:T(8,128)(2,1)S(1)}, bf16[48,64,128]{2,1,0:T(8,128)(2,1)S(1)}, u32[]{:S(2)}, u32[]{:S(2)}) collective-permute-start(bf16[48,64,128]{2,1,0:T(8,128)(2,1)S(1)} %slice.32), channel_id=1, source_target_pairs={{0,1},{1,0},{2,3},{3,2},{4,5},{5,4},{6,7},{7,6},{8,9},{9,8},{10,11... | collective-permute-start | bytes 2359304 | tf_op jit(solution)/shard_map/ppermute | solution.py:512
  4.4 0.1 collective-permute-start.1
  4.4 1.1 %slice.31 = bf16[32,64,128]{2,1,0:T(8,128)(2,1)S(1)} slice(bf16[96,64,128]{2,1,0:T(8,128)(2,1)} %args_1_.4), slice={[48:80], [0:64], [0:128]} | slice | bytes 1048576 | tf_op jit(solution)/shard_map/slice | solution.py:512
  5.5 2.0 %collective-permute-start.2 = (bf16[32,64,128]{2,1,0:T(8,128)(2,1)S(1)}, bf16[32,64,128]{2,1,0:T(8,128)(2,1)S(1)}, u32[]{:S(2)}, u32[]{:S(2)}) collective-permute-start(bf16[32,64,128]{2,1,0:T(8,128)(2,1)S(1)} %slice.31), channel_id=1, source_target_pairs={{0,1},{1,0},{2,3},{3,2},{4,5},{5,4},{6,7},{7,6},{8,9},{9,8},{10,11... | collective-permute-start | bytes 1572872 | tf_op jit(solution)/shard_map/ppermute | solution.py:512
  7.5 8.8 %refs.2 = (bf16[128,336,128]{2,1,0:T(8,128)(2,1)S(1)}, f32[336,128]{1,0:T(8,128)S(1)}) custom-call(bf16[100,3,128,128]{3,2,1,0:T(8,128)(2,1)} %refs.3), custom_call_target="tpu_custom_call" | custom-call | flops 900000000 | bytes 2700000 | tf_op jit(solution)/shard_map/refs/pallas_call | solution.py:165
  16.4 0.8 %prepare.1 = (bf16[16,128,128]{2,1,0:T(8,128)(2,1)S(1)}, bf16[16,128,128]{2,1,0:T(8,128)(2,1)S(1)}, f32[112,192]{1,0:T(8,128)S(1)}, f32[1,192]{1,0:T(1,128)S(1)}, f32[3,112,128]{2,1,0:T(8,128)S(1)}) custom-call(f32[16,128]{1,0:T(8,128)S(1)} %copy-done.3, f32[1,128]{1,0:T(1,128)S(1)} %bitcast.6, s32[192,100]{1,0:T(8,128)S(1)} %copy-done.2, ...), custom_call_target="tpu_custom_call" | custom-call | flops 300000000 | bytes 900000 | tf_op jit(solution)/shard_map/prepare/pallas_call | solution.py:96
  17.2 0.0 collective-permute-done.4.args_4_
  17.2 0.0 copy-done
  17.2 6.4 %filter.4 = (bf16[128,192,128]{2,1,0:T(8,128)(2,1)S(1)}, bf16[128,192,128]{2,1,0:T(8,128)(2,1)S(1)}, f32[8,128]{1,0:T(8,128)S(1)}) custom-call(s32[96]{0:T(128)S(1)} %copy-done.1, bf16[96,64,128]{2,1,0:T(8,128)(2,1)S(1)} %copy-done, bf16[16,128,128]{2,1,0:T(8,128)(2,1)S(1)} %get-tuple-element.41.args_2_.left, ...), custom_call_target="tpu_custom_call" | custom-call | flops 960000000 | bytes 2880000 | tf_op jit(solution)/shard_map/filter/pallas_call | solution.py:233
  23.6 0.0 collective-permute-done.1.bins.args_0_
  23.6 0.6 pick.1
  24.2 0.0 collective-permute-done.3.refs_0_
  24.3 0.1 fusion
  24.3 0.1 collective-permute-start.5
  24.4 0.5 collective-permute-start.6
  24.9 0.1 collective-permute-start.7
  25.0 1.2 %collective-permute-start = (bf16[16,64,128]{2,1,0:T(8,128)(2,1)S(1)}, bf16[16,64,128]{2,1,0:T(8,128)(2,1)S(1)}, u32[]{:S(2)}, u32[]{:S(2)}) collective-permute-start(bf16[16,64,128]{2,1,0:T(8,128)(2,1)S(1)} %slice.30), channel_id=1, source_target_pairs={{0,1},{1,0},{2,3},{3,2},{4,5},{5,4},{6,7},{7,6},{8,9},{9,8},{10,11... | collective-permute-start | bytes 786440 | tf_op jit(solution)/shard_map/ppermute | solution.py:512
  26.2 0.0 collective-permute-done.5.args_4_
  26.2 0.1 collective-permute-done.6.args_5_
  26.3 0.4 collective-permute-done.7.args_6_
  26.7 2.8 %filter.5 = (bf16[128,192,128]{2,1,0:T(8,128)(2,1)S(1)}, bf16[128,192,128]{2,1,0:T(8,128)(2,1)S(1)}, f32[8,128]{1,0:T(8,128)S(1)}) custom-call(s32[96]{0:T(128)S(1)} %collective-permute-done.1.bins.args_0_, bf16[48,64,128]{2,1,0:T(8,128)(2,1)S(1)} %gate.3.args_1_, ...), custom_call_target="tpu_custom_call", output_to_operand_aliasing={{0}: (7, {}), {1}: (8, {})} | custom-call | flops 480000000 | bytes 1440000 | tf_op jit(solution)/shard_map/filter/pallas_call | solution.py:233
  29.5 4.5 %collective-permute-done.2.refs_0_ = bf16[32,64,128]{2,1,0:T(8,128)(2,1)S(1)} collective-permute-done((bf16[32,64,128]{2,1,0:T(8,128)(2,1)S(1)}, bf16[32,64,128]{2,1,0:T(8,128)(2,1)S(1)}, u32[]{:S(2)}, u32[]{:S(2)}) %collective-permute-start.2) | collective-permute-done | bytes 524320 | tf_op jit(solution)/shard_map/ppermute | solution.py:512
  34.0 0.1 collective-permute-start.10
  34.1 0.5 collective-permute-start.11
  34.6 0.1 collective-permute-start.8
  34.7 0.4 collective-permute-start.9
  35.1 0.3 collective-permute-done.10.args_6_
  35.4 0.2 collective-permute-done.11.args_7_
  35.6 0.3 collective-permute-done.8.args_4_
  36.0 0.2 collective-permute-done.9.args_5_
  36.1 2.1 %filter.6 = (bf16[128,192,128]{2,1,0:T(8,128)(2,1)S(1)}, bf16[128,192,128]{2,1,0:T(8,128)(2,1)S(1)}, f32[8,128]{1,0:T(8,128)S(1)}) custom-call(s32[96]{0:T(128)S(1)} %collective-permute-done.1.bins.args_0_, bf16[32,64,128]{2,1,0:T(8,128)(2,1)S(1)} %gate.4.args_1_, ...), custom_call_target="tpu_custom_call", output_to_operand_aliasing={{0}: (8, {}), {1}: (9, {})} | custom-call | flops 320000000 | bytes 960000 | tf_op jit(solution)/shard_map/filter/pallas_call | solution.py:233
  38.3 1.1 %collective-permute-done.refs_0_ = bf16[16,64,128]{2,1,0:T(8,128)(2,1)S(1)} collective-permute-done((bf16[16,64,128]{2,1,0:T(8,128)(2,1)S(1)}, bf16[16,64,128]{2,1,0:T(8,128)(2,1)S(1)}, u32[]{:S(2)}, u32[]{:S(2)}) %collective-permute-start) | collective-permute-done | bytes 262176 | tf_op jit(solution)/shard_map/ppermute | solution.py:512
  39.4 0.0 collective-permute-start.12
  39.4 1.5 %collective-permute-done.12.args_3_ = bf16[16,64,128]{2,1,0:T(8,128)(2,1)S(1)} collective-permute-done((bf16[16,64,128]{2,1,0:T(8,128)(2,1)S(1)}, bf16[16,64,128]{2,1,0:T(8,128)(2,1)S(1)}, u32[]{:S(2)}, u32[]{:S(2)}) %collective-permute-start.12) | collective-permute-done | bytes 262176 | tf_op jit(solution)/shard_map/ppermute | solution.py:529
  41.0 1.0 %filter.7 = (bf16[128,192,128]{2,1,0:T(8,128)(2,1)S(1)}, bf16[128,192,128]{2,1,0:T(8,128)(2,1)S(1)}) custom-call(bf16[16,64,128]{2,1,0:T(8,128)(2,1)S(1)} %gate.5.args_0_, bf16[16,128,128]{2,1,0:T(8,128)(2,1)S(1)} %get-tuple-element.44.refs_1_.args_1_, ...), custom_call_target="tpu_custom_call", output_to_operand_aliasing={{0}: (4, {}), {1}: (5, {})} | custom-call | flops 160000000 | bytes 480000 | tf_op jit(solution)/shard_map/filter/pallas_call | solution.py:233
  41.9 3.1 %score.1 = (f32[336,192]{1,0:T(8,128)S(1)}, f32[8,192]{1,0:T(8,128)S(1)}) custom-call(bf16[128,192,128]{2,1,0:T(8,128)(2,1)S(1)} %get-tuple-element.54.plain, bf16[128,336,128]{2,1,0:T(8,128)(2,1)S(1)} %get-tuple-element.55.refs, f32[336,128]{1,0:T(8,128)S(1)} %get-tuple-element.40.after.norm, f32[112,192]{1,0:T(8,128)S(1)} %get-tuple-element.56.mask, ...), custom_call_target="tpu_custom_call" | custom-call | flops 500000000 | bytes 1500000 | tf_op jit(solution)/shard_map/score/pallas_call | solution.py:293
  45.0 1.8 %collective-permute-start.13 = (f32[8,192]{1,0:T(8,128)S(1)}, f32[8,192]{1,0:T(8,128)S(1)}, u32[]{:S(2)}, u32[]{:S(2)}) collective-permute-start(f32[8,192]{1,0:T(8,128)S(1)} %get-tuple-element.59.mine), channel_id=1, source_target_pairs={{0,1},{1,0},{2,3},{3,2},{4,5},{5,4},{6,7},{7,6},{8,9},{9,8},{10,11... | collective-permute-start | bytes 18440 | tf_op jit(solution)/shard_map/ppermute | solution.py:538
  46.8 1.9 %collective-permute-done.13.other = f32[8,192]{1,0:T(8,128)S(1)} collective-permute-done((f32[8,192]{1,0:T(8,128)S(1)}, f32[8,192]{1,0:T(8,128)S(1)}, u32[]{:S(2)}, u32[]{:S(2)}) %collective-permute-start.13) | collective-permute-done | bytes 6176 | tf_op jit(solution)/shard_map/ppermute | solution.py:538
  48.7 1.5 %sums.3 = (bf16[4,500,128]{2,1,0:T(8,128)(2,1)S(1)}, bf16[2,112,384]{2,1,0:T(8,128)(2,1)S(1)}) custom-call(f32[336,192]{1,0:T(8,128)S(1)} %get-tuple-element.58.scaled, f32[8,192]{1,0:T(8,128)S(1)} %get-tuple-element.59.mine, f32[8,192]{1,0:T(8,128)S(1)} %collective-permute-done.13.other, f32[3,112,128]{2,1,0:T(8,128)S(1)} %get-tuple-element.60.rot, ...), custom_call_target="tpu_custom_call" | custom-call | flops 400000000 | bytes 1200000 | tf_op jit(solution)/shard_map/sums/pallas_call | solution.py:399
  50.3 1.8 %collective-permute-start.14 = (bf16[4,500,128]{2,1,0:T(8,128)(2,1)S(1)}, bf16[4,500,128]{2,1,0:T(8,128)(2,1)S(1)}, u32[]{:S(2)}, u32[]{:S(2)}) collective-permute-start(bf16[4,500,128]{2,1,0:T(8,128)(2,1)S(1)} %get-tuple-element.63.after), channel_id=1, source_target_pairs={{0,2},{2,0},{4,6},{6,4},{8,10},{10,8},{12,14},{14,12},{1,3},{3,1},... | collective-permute-start | bytes 1536008 | tf_op jit(solution)/shard_map/ppermute | solution.py:541
  52.0 0.8 %sums.4 = (bf16[2,300,128]{2,1,0:T(8,128)(2,1)S(1)}, bf16[2,300,128]{2,1,0:T(8,128)(2,1)S(1)}, bf16[2,300,128]{2,1,0:T(8,128)(2,1)S(1)}) custom-call(bf16[2,112,384]{2,1,0:T(8,128)(2,1)S(1)} %get-tuple-element.62.weights, bf16[128,192,128]{2,1,0:T(8,128)(2,1)S(1)} %get-tuple-element.54.plain, bf16[128,192,128]{2,1,0:T(8,128)(2,1)S(1)} %get-tuple-element.61.turned, ...), custom_call_target="tpu_custom_call" | custom-call | flops 240000000 | bytes 720000 | tf_op jit(solution)/shard_map/sums/pallas_call | solution.py:399
  52.9 2.7 %collective-permute-start.18 = (bf16[2,300,128]{2,1,0:T(8,128)(2,1)S(1)}, bf16[2,300,128]{2,1,0:T(8,128)(2,1)S(1)}, u32[]{:S(2)}, u32[]{:S(2)}) collective-permute-start(bf16[2,300,128]{2,1,0:T(8,128)(2,1)S(1)} %get-tuple-element.71), channel_id=1, source_target_pairs={{0,8},{2,10},{4,12},{6,14},{8,0},{10,2},{12,4},{14,6},{1,9},{3,11}... | collective-permute-start | bytes 460808 | tf_op jit(solution)/shard_map/ppermute | solution.py:541
  55.5 1.3 %collective-permute-start.19 = (bf16[2,300,128]{2,1,0:T(8,128)(2,1)S(1)}, bf16[2,300,128]{2,1,0:T(8,128)(2,1)S(1)}, u32[]{:S(2)}, u32[]{:S(2)}) collective-permute-start(bf16[2,300,128]{2,1,0:T(8,128)(2,1)S(1)} %get-tuple-element.72), channel_id=1, source_target_pairs={{0,12},{2,14},{4,8},{6,10},{8,4},{10,6},{12,0},{14,2},{1,13},{3,15... | collective-permute-start | bytes 460808 | tf_op jit(solution)/shard_map/ppermute | solution.py:541
  56.9 0.2 collective-permute-start.20
  57.1 1.6 %sums.5 = (f32[4,500,128]{2,1,0:T(8,128)S(1)}, f32[2,300,128]{2,1,0:T(8,128)S(1)}) custom-call(bf16[2,112,384]{2,1,0:T(8,128)(2,1)S(1)} %get-tuple-element.62.weights, bf16[128,192,128]{2,1,0:T(8,128)(2,1)S(1)} %get-tuple-element.54.plain, bf16[128,192,128]{2,1,0:T(8,128)(2,1)S(1)} %get-tuple-element.61.turned, bf16[2,300,128]{2,1,0:T(8,128)(2,1)S(1)} %get-tuple-element.64.after), custom_call_target="tpu_custom_call" | custom-call | flops 400000000 | bytes 1200000 | tf_op jit(solution)/shard_map/sums/pallas_call | solution.py:399
  58.7 4.3 %collective-permute-done.14.got = bf16[4,500,128]{2,1,0:T(8,128)(2,1)S(1)} collective-permute-done((bf16[4,500,128]{2,1,0:T(8,128)(2,1)S(1)}, bf16[4,500,128]{2,1,0:T(8,128)(2,1)S(1)}, u32[]{:S(2)}, u32[]{:S(2)}) %collective-permute-start.14) | collective-permute-done | bytes 512032 | tf_op jit(solution)/shard_map/ppermute | solution.py:541
  63.0 0.1 fold.1
  63.1 2.9 %collective-permute-start.15 = (bf16[1,500,128]{2,1,0:T(8,128)(2,1)S(1)}, bf16[1,500,128]{2,1,0:T(8,128)(2,1)S(1)}, u32[]{:S(2)}, u32[]{:S(2)}) collective-permute-start(bf16[1,500,128]{2,1,0:T(8,128)(2,1)S(1)} %get-tuple-element.67), channel_id=1, source_target_pairs={{0,8},{2,10},{4,12},{6,14},{8,0},{10,2},{12,4},{14,6},{1,9},{3,11}... | collective-permute-start | bytes 384008 | tf_op jit(solution)/shard_map/ppermute | solution.py:541
  66.0 1.4 %collective-permute-start.16 = (bf16[1,500,128]{2,1,0:T(8,128)(2,1)S(1)}, bf16[1,500,128]{2,1,0:T(8,128)(2,1)S(1)}, u32[]{:S(2)}, u32[]{:S(2)}) collective-permute-start(bf16[1,500,128]{2,1,0:T(8,128)(2,1)S(1)} %get-tuple-element.68), channel_id=1, source_target_pairs={{0,12},{2,14},{4,8},{6,10},{8,4},{10,6},{12,0},{14,2},{1,13},{3,15... | collective-permute-start | bytes 384008 | tf_op jit(solution)/shard_map/ppermute | solution.py:541
  67.3 0.0 collective-permute-done.18.rest_0_
  67.3 0.2 collective-permute-start.17
  67.5 0.0 collective-permute-done.19.rest_1_
  67.5 0.0 collective-permute-done.20.rest_2_
  67.6 0.1 gather.1
  67.6 1.5 %collective-permute-start.21 = (bf16[1,300,128]{2,1,0:T(8,128)(2,1)S(1)}, bf16[1,300,128]{2,1,0:T(8,128)(2,1)S(1)}, u32[]{:S(2)}, u32[]{:S(2)}) collective-permute-start(bf16[1,300,128]{2,1,0:T(8,128)(2,1)S(1)} %get-tuple-element.74), channel_id=1, source_target_pairs={{0,2},{2,0},{4,6},{6,4},{8,10},{10,8},{12,14},{14,12},{1,3},{3,1},... | collective-permute-start | bytes 230408 | tf_op jit(solution)/shard_map/ppermute | solution.py:541
  69.2 2.9 %collective-permute-done.21.args_5_ = bf16[1,300,128]{2,1,0:T(8,128)(2,1)S(1)} collective-permute-done((bf16[1,300,128]{2,1,0:T(8,128)(2,1)S(1)}, bf16[1,300,128]{2,1,0:T(8,128)(2,1)S(1)}, u32[]{:S(2)}, u32[]{:S(2)}) %collective-permute-start.21) | collective-permute-done | bytes 76832 | tf_op jit(solution)/shard_map/ppermute | solution.py:541
  72.1 5.9 %collective-permute-done.15.args_1_ = bf16[1,500,128]{2,1,0:T(8,128)(2,1)S(1)} collective-permute-done((bf16[1,500,128]{2,1,0:T(8,128)(2,1)S(1)}, bf16[1,500,128]{2,1,0:T(8,128)(2,1)S(1)}, u32[]{:S(2)}, u32[]{:S(2)}) %collective-permute-start.15) | collective-permute-done | bytes 128032 | tf_op jit(solution)/shard_map/ppermute | solution.py:541
  78.0 0.0 collective-permute-done.16.args_2_
  78.0 0.0 collective-permute-done.17.args_3_
  78.0 0.9 %finish.1 = f32[800,128]{1,0:T(8,128)} custom-call(f32[1,500,128]{2,1,0:T(8,128)S(1)} %get-tuple-element.66.args_0_, bf16[1,500,128]{2,1,0:T(8,128)(2,1)S(1)} %collective-permute-done.15.args_1_, bf16[1,500,128]{2,1,0:T(8,128)(2,1)S(1)} %collective-permute-done.16.args_2_, bf16[1,500,128]{2,1,0:T(8,128)(2,1)S(1)} %collective-permute-done.17.args_3_, ...), custom_call_target="tpu_custom_call" | custom-call | flops 100000000 | bytes 300000 | tf_op jit(solution)/shard_map/finish/pallas_call | solution.py:476
  (16 shorter events, 0.1 us)
Async XLA Ops:
  0.0 16.3 %copy-start.6 = (f32[128]{0:T(128)S(1)}, f32[128]{0:T(128)}, u32[]{:S(2)}) copy-start(f32[128]{0:T(128)} %param.11) | copy-start | bytes 1540
  0.0 16.3 %copy-start.5 = (f32[192]{0:T(256)S(1)}, f32[192]{0:T(256)}, u32[]{:S(2)}) copy-start(f32[192]{0:T(256)} %param.15) | copy-start | bytes 2308
  0.0 16.3 %copy-start.4 = (s32[100,3]{0,1:T(4,128)S(1)}, s32[100,3]{0,1:T(4,128)}, u32[]{:S(2)}) copy-start(s32[100,3]{0,1:T(4,128)} %param.13) | copy-start | bytes 3604
  0.0 16.3 %copy-start.3 = (f32[16,128]{1,0:T(8,128)S(1)}, f32[16,128]{1,0:T(8,128)}, u32[]{:S(2)}) copy-start(f32[16,128]{1,0:T(8,128)} %ctf.1) | copy-start | bytes 24580
  0.0 16.4 %copy-start.2 = (s32[192,100]{1,0:T(8,128)S(1)}, s32[192,100]{1,0:T(8,128)}, u32[]{:S(2)}) copy-start(s32[192,100]{1,0:T(8,128)} %mask.1) | copy-start | bytes 230404
  0.0 17.2 %collective-permute-start.4 = (bf16[96,64,128]{2,1,0:T(8,128)(2,1)}, bf16[96,64,128]{2,1,0:T(8,128)(2,1)S(1)}, u32[]{:S(2)}, u32[]{:S(2)}) collective-permute-start(bf16[96,64,128]{2,1,0:T(8,128)(2,1)} %args_1_.4), channel_id=1, source_target_pairs={{0,16},{16,0},{1,17},{17,1},{2,18},{18,2},{3,19},{19,3},{4,20},{20... | collective-permute-start | bytes 4718600 | tf_op jit(solution)/shard_map/ppermute | solution.py:514
  1.7 15.5 %copy-start = (bf16[96,64,128]{2,1,0:T(8,128)(2,1)S(1)}, bf16[96,64,128]{2,1,0:T(8,128)(2,1)}, u32[]{:S(2)}) copy-start(bf16[96,64,128]{2,1,0:T(8,128)(2,1)} %args_1_.4) | copy-start | bytes 4718596
  1.7 15.5 %copy-start.1 = (s32[96]{0:T(128)S(1)}, s32[96]{0:T(128)}, u32[]{:S(2)}) copy-start(s32[96]{0:T(128)} %args_0_.4) | copy-start | bytes 1156
  1.8 22.5 %collective-permute-start.3 = (bf16[48,64,128]{2,1,0:T(8,128)(2,1)S(1)}, bf16[48,64,128]{2,1,0:T(8,128)(2,1)S(1)}, u32[]{:S(2)}, u32[]{:S(2)}) collective-permute-start(bf16[48,64,128]{2,1,0:T(8,128)(2,1)S(1)} %slice.32), channel_id=1, source_target_pairs={{0,1},{1,0},{2,3},{3,2},{4,5},{5,4},{6,7},{7,6},{8,9},{9,8},{10,11... | collective-permute-start | bytes 2359304 | tf_op jit(solution)/shard_map/ppermute | solution.py:512
  4.4 19.2 %collective-permute-start.1 = (s32[96]{0:T(128)}, s32[96]{0:T(128)S(1)}, u32[]{:S(2)}, u32[]{:S(2)}) collective-permute-start(s32[96]{0:T(128)} %args_0_.4), channel_id=1, source_target_pairs={{0,1},{1,0},{2,3},{3,2},{4,5},{5,4},{6,7},{7,6},{8,9},{9,8},{10,11... | collective-permute-start | bytes 1160 | tf_op jit(solution)/shard_map/ppermute | solution.py:513
  5.5 28.5 %collective-permute-start.2 = (bf16[32,64,128]{2,1,0:T(8,128)(2,1)S(1)}, bf16[32,64,128]{2,1,0:T(8,128)(2,1)S(1)}, u32[]{:S(2)}, u32[]{:S(2)}) collective-permute-start(bf16[32,64,128]{2,1,0:T(8,128)(2,1)S(1)} %slice.31), channel_id=1, source_target_pairs={{0,1},{1,0},{2,3},{3,2},{4,5},{5,4},{6,7},{7,6},{8,9},{9,8},{10,11... | collective-permute-start | bytes 1572872 | tf_op jit(solution)/shard_map/ppermute | solution.py:512
  24.3 1.9 %collective-permute-start.5 = (bf16[16,64,128]{2,1,0:T(8,128)(2,1)S(1)}, bf16[16,64,128]{2,1,0:T(8,128)(2,1)S(1)}, u32[]{:S(2)}, u32[]{:S(2)}) collective-permute-start(bf16[16,64,128]{2,1,0:T(8,128)(2,1)S(1)} %get-tuple-element.77), channel_id=1, source_target_pairs={{0,16},{16,0},{1,17},{17,1},{2,18},{18,2},{3,19},{19,3},{4,20},{20... | collective-permute-start | bytes 786440 | tf_op jit(solution)/shard_map/ppermute | solution.py:529
  24.4 1.9 %collective-permute-start.6 = (bf16[16,64,128]{2,1,0:T(8,128)(2,1)S(1)}, bf16[16,64,128]{2,1,0:T(8,128)(2,1)S(1)}, u32[]{:S(2)}, u32[]{:S(2)}) collective-permute-start(bf16[16,64,128]{2,1,0:T(8,128)(2,1)S(1)} %get-tuple-element.76), channel_id=1, source_target_pairs={{0,16},{16,0},{1,17},{17,1},{2,18},{18,2},{3,19},{19,3},{4,20},{20... | collective-permute-start | bytes 786440 | tf_op jit(solution)/shard_map/ppermute | solution.py:529
  24.9 1.8 %collective-permute-start.7 = (bf16[16,64,128]{2,1,0:T(8,128)(2,1)S(1)}, bf16[16,64,128]{2,1,0:T(8,128)(2,1)S(1)}, u32[]{:S(2)}, u32[]{:S(2)}) collective-permute-start(bf16[16,64,128]{2,1,0:T(8,128)(2,1)S(1)} %get-tuple-element.75), channel_id=1, source_target_pairs={{0,16},{16,0},{1,17},{17,1},{2,18},{18,2},{3,19},{19,3},{4,20},{20... | collective-permute-start | bytes 786440 | tf_op jit(solution)/shard_map/ppermute | solution.py:529
  25.0 14.4 %collective-permute-start = (bf16[16,64,128]{2,1,0:T(8,128)(2,1)S(1)}, bf16[16,64,128]{2,1,0:T(8,128)(2,1)S(1)}, u32[]{:S(2)}, u32[]{:S(2)}) collective-permute-start(bf16[16,64,128]{2,1,0:T(8,128)(2,1)S(1)} %slice.30), channel_id=1, source_target_pairs={{0,1},{1,0},{2,3},{3,2},{4,5},{5,4},{6,7},{7,6},{8,9},{9,8},{10,11... | collective-permute-start | bytes 786440 | tf_op jit(solution)/shard_map/ppermute | solution.py:512
  34.0 1.4 %collective-permute-start.10 = (bf16[8,64,128]{2,1,0:T(8,128)(2,1)S(1)}, bf16[8,64,128]{2,1,0:T(8,128)(2,1)S(1)}, u32[]{:S(2)}, u32[]{:S(2)}) collective-permute-start(bf16[8,64,128]{2,1,0:T(8,128)(2,1)S(1)} %get-tuple-element.79), channel_id=1, source_target_pairs={{0,16},{16,0},{1,17},{17,1},{2,18},{18,2},{3,19},{19,3},{4,20},{20... | collective-permute-start | bytes 393224 | tf_op jit(solution)/shard_map/ppermute | solution.py:529
  34.1 1.5 %collective-permute-start.11 = (bf16[8,64,128]{2,1,0:T(8,128)(2,1)S(1)}, bf16[8,64,128]{2,1,0:T(8,128)(2,1)S(1)}, u32[]{:S(2)}, u32[]{:S(2)}) collective-permute-start(bf16[8,64,128]{2,1,0:T(8,128)(2,1)S(1)} %get-tuple-element.78), channel_id=1, source_target_pairs={{0,16},{16,0},{1,17},{17,1},{2,18},{18,2},{3,19},{19,3},{4,20},{20... | collective-permute-start | bytes 393224 | tf_op jit(solution)/shard_map/ppermute | solution.py:529
  34.6 1.3 %collective-permute-start.8 = (bf16[8,64,128]{2,1,0:T(8,128)(2,1)S(1)}, bf16[8,64,128]{2,1,0:T(8,128)(2,1)S(1)}, u32[]{:S(2)}, u32[]{:S(2)}) collective-permute-start(bf16[8,64,128]{2,1,0:T(8,128)(2,1)S(1)} %get-tuple-element.81), channel_id=1, source_target_pairs={{0,16},{16,0},{1,17},{17,1},{2,18},{18,2},{3,19},{19,3},{4,20},{20... | collective-permute-start | bytes 393224 | tf_op jit(solution)/shard_map/ppermute | solution.py:529
  34.7 1.5 %collective-permute-start.9 = (bf16[8,64,128]{2,1,0:T(8,128)(2,1)S(1)}, bf16[8,64,128]{2,1,0:T(8,128)(2,1)S(1)}, u32[]{:S(2)}, u32[]{:S(2)}) collective-permute-start(bf16[8,64,128]{2,1,0:T(8,128)(2,1)S(1)} %get-tuple-element.80), channel_id=1, source_target_pairs={{0,16},{16,0},{1,17},{17,1},{2,18},{18,2},{3,19},{19,3},{4,20},{20... | collective-permute-start | bytes 393224 | tf_op jit(solution)/shard_map/ppermute | solution.py:529
  39.4 1.5 %collective-permute-start.12 = (bf16[16,64,128]{2,1,0:T(8,128)(2,1)S(1)}, bf16[16,64,128]{2,1,0:T(8,128)(2,1)S(1)}, u32[]{:S(2)}, u32[]{:S(2)}) collective-permute-start(bf16[16,64,128]{2,1,0:T(8,128)(2,1)S(1)} %gate.5.args_0_), channel_id=1, source_target_pairs={{0,16},{16,0},{1,17},{17,1},{2,18},{18,2},{3,19},{19,3},{4,20},{20... | collective-permute-start | bytes 786440 | tf_op jit(solution)/shard_map/ppermute | solution.py:529
  45.0 3.7 %collective-permute-start.13 = (f32[8,192]{1,0:T(8,128)S(1)}, f32[8,192]{1,0:T(8,128)S(1)}, u32[]{:S(2)}, u32[]{:S(2)}) collective-permute-start(f32[8,192]{1,0:T(8,128)S(1)} %get-tuple-element.59.mine), channel_id=1, source_target_pairs={{0,1},{1,0},{2,3},{3,2},{4,5},{5,4},{6,7},{7,6},{8,9},{9,8},{10,11... | collective-permute-start | bytes 18440 | tf_op jit(solution)/shard_map/ppermute | solution.py:538
  50.3 12.7 %collective-permute-start.14 = (bf16[4,500,128]{2,1,0:T(8,128)(2,1)S(1)}, bf16[4,500,128]{2,1,0:T(8,128)(2,1)S(1)}, u32[]{:S(2)}, u32[]{:S(2)}) collective-permute-start(bf16[4,500,128]{2,1,0:T(8,128)(2,1)S(1)} %get-tuple-element.63.after), channel_id=1, source_target_pairs={{0,2},{2,0},{4,6},{6,4},{8,10},{10,8},{12,14},{14,12},{1,3},{3,1},... | collective-permute-start | bytes 1536008 | tf_op jit(solution)/shard_map/ppermute | solution.py:541
  52.9 14.4 %collective-permute-start.18 = (bf16[2,300,128]{2,1,0:T(8,128)(2,1)S(1)}, bf16[2,300,128]{2,1,0:T(8,128)(2,1)S(1)}, u32[]{:S(2)}, u32[]{:S(2)}) collective-permute-start(bf16[2,300,128]{2,1,0:T(8,128)(2,1)S(1)} %get-tuple-element.71), channel_id=1, source_target_pairs={{0,8},{2,10},{4,12},{6,14},{8,0},{10,2},{12,4},{14,6},{1,9},{3,11}... | collective-permute-start | bytes 460808 | tf_op jit(solution)/shard_map/ppermute | solution.py:541
  55.5 12.0 %collective-permute-start.19 = (bf16[2,300,128]{2,1,0:T(8,128)(2,1)S(1)}, bf16[2,300,128]{2,1,0:T(8,128)(2,1)S(1)}, u32[]{:S(2)}, u32[]{:S(2)}) collective-permute-start(bf16[2,300,128]{2,1,0:T(8,128)(2,1)S(1)} %get-tuple-element.72), channel_id=1, source_target_pairs={{0,12},{2,14},{4,8},{6,10},{8,4},{10,6},{12,0},{14,2},{1,13},{3,15... | collective-permute-start | bytes 460808 | tf_op jit(solution)/shard_map/ppermute | solution.py:541
  56.9 10.7 %collective-permute-start.20 = (bf16[2,300,128]{2,1,0:T(8,128)(2,1)S(1)}, bf16[2,300,128]{2,1,0:T(8,128)(2,1)S(1)}, u32[]{:S(2)}, u32[]{:S(2)}) collective-permute-start(bf16[2,300,128]{2,1,0:T(8,128)(2,1)S(1)} %get-tuple-element.64.after), channel_id=1, source_target_pairs={{0,4},{2,6},{4,0},{6,2},{8,12},{10,14},{12,8},{14,10},{1,5},{3,7},... | collective-permute-start | bytes 460808 | tf_op jit(solution)/shard_map/ppermute | solution.py:541
  63.1 14.8 %collective-permute-start.15 = (bf16[1,500,128]{2,1,0:T(8,128)(2,1)S(1)}, bf16[1,500,128]{2,1,0:T(8,128)(2,1)S(1)}, u32[]{:S(2)}, u32[]{:S(2)}) collective-permute-start(bf16[1,500,128]{2,1,0:T(8,128)(2,1)S(1)} %get-tuple-element.67), channel_id=1, source_target_pairs={{0,8},{2,10},{4,12},{6,14},{8,0},{10,2},{12,4},{14,6},{1,9},{3,11}... | collective-permute-start | bytes 384008 | tf_op jit(solution)/shard_map/ppermute | solution.py:541
  66.0 12.0 %collective-permute-start.16 = (bf16[1,500,128]{2,1,0:T(8,128)(2,1)S(1)}, bf16[1,500,128]{2,1,0:T(8,128)(2,1)S(1)}, u32[]{:S(2)}, u32[]{:S(2)}) collective-permute-start(bf16[1,500,128]{2,1,0:T(8,128)(2,1)S(1)} %get-tuple-element.68), channel_id=1, source_target_pairs={{0,12},{2,14},{4,8},{6,10},{8,4},{10,6},{12,0},{14,2},{1,13},{3,15... | collective-permute-start | bytes 384008 | tf_op jit(solution)/shard_map/ppermute | solution.py:541
  67.3 10.6 %collective-permute-start.17 = (bf16[1,500,128]{2,1,0:T(8,128)(2,1)S(1)}, bf16[1,500,128]{2,1,0:T(8,128)(2,1)S(1)}, u32[]{:S(2)}, u32[]{:S(2)}) collective-permute-start(bf16[1,500,128]{2,1,0:T(8,128)(2,1)S(1)} %get-tuple-element.69), channel_id=1, source_target_pairs={{0,4},{2,6},{4,0},{6,2},{8,12},{10,14},{12,8},{14,10},{1,5},{3,7},... | collective-permute-start | bytes 384008 | tf_op jit(solution)/shard_map/ppermute | solution.py:541
  67.6 4.5 %collective-permute-start.21 = (bf16[1,300,128]{2,1,0:T(8,128)(2,1)S(1)}, bf16[1,300,128]{2,1,0:T(8,128)(2,1)S(1)}, u32[]{:S(2)}, u32[]{:S(2)}) collective-permute-start(bf16[1,300,128]{2,1,0:T(8,128)(2,1)S(1)} %get-tuple-element.74), channel_id=1, source_target_pairs={{0,2},{2,0},{4,6},{6,4},{8,10},{10,8},{12,14},{14,12},{1,3},{3,1},... | collective-permute-start | bytes 230408 | tf_op jit(solution)/shard_map/ppermute | solution.py:541

commit v12 on v11

--- a/solution.py
+++ b/solution.py
@@ -302,21 +302,35 @@
     )(held(plain), held(refs), held(norm), held(mask), held(noise))
 
 
-def weigh(scaled, mine, other, rot, out):
+def shares_kernel(scaled, mine, rot, out):
     rots, padded, _ = rot.shape
-    count = scaled.shape[1]
+    e = jnp.exp(scaled[...] - mine[0:1])
+    for q in range(4):
+        acc = jnp.zeros((padded, scaled.shape[1]), F32)
+        for j in range(rots):
+            acc = acc + jnp.where(rot[j][:, :1] == q, e[j * padded : (j + 1) * padded], 0.0)
+        out[q] = acc
+
+
+def make_shares(scaled, mine, rot):
+    return pl.pallas_call(
+        shares_kernel,
+        out_shape=pinned((4, rot.shape[1], scaled.shape[1]), F32),
+        compiler_params=pltpu.CompilerParams(vmem_limit_bytes=8 * MIB),
+        cost_estimate=cost(1),
+        name="shares",
+    )(held(scaled), held(mine), held(rot))
+
+
+def weigh(shares, mine, other, out):
+    count = shares.shape[2]
     theirs = jnp.concatenate([other[:, count // 2 :], other[:, : count // 2]], axis=1)
     peak = jnp.maximum(mine[0:1], theirs[0:1])
-    total = mine[1:2] * jnp.exp(mine[0:1] - peak) + theirs[1:2] * jnp.exp(theirs[0:1] - peak)
-    w = (jnp.exp(scaled[...] - peak) / total).astype(BF16).astype(F32)
-    quarters = []
-    for q in range(4):
-        acc = jnp.zeros((padded, count), F32)
-        for j in range(rots):
-            acc = acc + jnp.where(rot[j][:, :1] == q, w[j * padded : (j + 1) * padded], 0.0)
-        quarters.append(acc)
+    near = jnp.exp(mine[0:1] - peak)
+    total = mine[1:2] * near + theirs[1:2] * jnp.exp(theirs[0:1] - peak)
+    factor = near / total
     for row, pair in enumerate(((0, 3), (2, 1))):
-        out[row] = jnp.concatenate([quarters[q] for q in pair], axis=1).astype(BF16)
+        out[row] = jnp.concatenate([shares[q] * factor for q in pair], axis=1).astype(BF16)
 
 
 def row_pair(weights, plain, turned, both, classes):
@@ -373,8 +387,8 @@
             out[side, r * classes : (r + 1) * classes] = value.astype(out.dtype)
 
 
-def inner_kernel(scaled, mine, other, rot, plain, turned, send, weights, *, dom, **sizes):
-    weigh(scaled, mine, other, rot, weights)
+def inner_kernel(shares, mine, other, plain, turned, send, weights, *, dom, **sizes):
+    weigh(shares, mine, other, weights)
     away = 1 - lax.axis_index("dom") % 2
     one_side(weights, plain, turned, send, away, dom, **sizes)
 
@@ -535,7 +549,8 @@
     plain, turned = buffers
 
     scaled, stats = score(plain, refs, norm, mask, noise)
-    inputs = (held(scaled), held(stats), over_cls(stats), held(rot))
+    theirs = over_cls(stats)
+    inputs = (held(make_shares(scaled, stats, rot)), held(stats), theirs)
 
     def along(x, mask):
         return lax.ppermute(x, "dom", [(i, i ^ mask) for i in range(dom)])

time: 79.3 us -> 79.2 us (level)
  no operation moved by 1% of the time
where the time goes in v12:
time: 79.2 us; the launch traced here: 78.7 us
  Pallas kernels  30.7 us (39%)
  waiting for transfers between devices  23.3 us (29%)
  starting transfers between devices  22 us (28%)
  local copies, waits for them, and re-layouts  2.4 us (3%)
    ppermute x8, waiting for transfers between devices, along(): return lax.ppermute(x, 'dom', [(i, i ^ mask) for i in range(dom)])  13.1 us
    pallas_call x4, Pallas kernels, filter_chunk(): pl.pallas_call(functools.partial(filter_kernel, picked=picked, parts=part...  12.3 us
    ppermute x8, starting transfers between devices, along(): return lax.ppermute(x, 'dom', [(i, i ^ mask) for i in range(dom)])  12 us
    pallas_call x1, Pallas kernels, lay_refs(): pl.pallas_call(functools.partial(refs_kernel, padded=padded), grid=(rots,...  8.81 us
    ppermute x3, starting transfers between devices, local(): remote = [over_cls(images[a:a + n]) for a, n in zip(starts, sizes)]  5.82 us
    ppermute x3, waiting for transfers between devices, local(): remote = [over_cls(images[a:a + n]) for a, n in zip(starts, sizes)]  5.61 us
    pallas_call x3, Pallas kernels, call_sums(): pl.pallas_call(kernel, in_specs=[vmem] * len(args) + [pl.BlockSpec(memory...  3.76 us
    pallas_call x1, Pallas kernels, score(): pl.pallas_call(score_kernel, out_shape=(pinned((height, count), F32), pin...  3.1 us
  transfers between devices with their start and end apart: 22, of which 13 were waited for; matrix products, arithmetic and copies ran while one was open for 3% of the time, Pallas kernels for 31%

profile of v12, /device:TPU:0, one launch (start us, length us, event | category | flops | bytes accessed | tf_op | source)
XLA Modules:
  0.0 78.7 jit_solution(6707675527538115767)
XLA Ops:
  0.0 0.5 collective-permute-start.4
  0.5 1.2 %slice.32 = bf16[48,64,128]{2,1,0:T(8,128)(2,1)S(1)} slice(bf16[96,64,128]{2,1,0:T(8,128)(2,1)} %args_1_.4), slice={[0:48], [0:64], [0:128]} | slice | bytes 1572864 | tf_op jit(solution)/shard_map/slice | solution.py:526
  1.7 0.0 copy-start
  1.7 0.0 copy-start.1
  1.8 2.6 %collective-permute-start.3 = (bf16[48,64,128]{2,1,0:T(8,128)(2,1)S(1)}, bf16[48,64,128]{2,1,0:T(8,128)(2,1)S(1)}, u32[]{:S(2)}, u32[]{:S(2)}) collective-permute-start(bf16[48,64,128]{2,1,0:T(8,128)(2,1)S(1)} %slice.32), channel_id=1, source_target_pairs={{0,1},{1,0},{2,3},{3,2},{4,5},{5,4},{6,7},{7,6},{8,9},{9,8},{10,11... | collective-permute-start | bytes 2359304 | tf_op jit(solution)/shard_map/ppermute | solution.py:526
  4.4 0.1 collective-permute-start.1
  4.4 1.1 %slice.31 = bf16[32,64,128]{2,1,0:T(8,128)(2,1)S(1)} slice(bf16[96,64,128]{2,1,0:T(8,128)(2,1)} %args_1_.4), slice={[48:80], [0:64], [0:128]} | slice | bytes 1048576 | tf_op jit(solution)/shard_map/slice | solution.py:526
  5.5 2.0 %collective-permute-start.2 = (bf16[32,64,128]{2,1,0:T(8,128)(2,1)S(1)}, bf16[32,64,128]{2,1,0:T(8,128)(2,1)S(1)}, u32[]{:S(2)}, u32[]{:S(2)}) collective-permute-start(bf16[32,64,128]{2,1,0:T(8,128)(2,1)S(1)} %slice.31), channel_id=1, source_target_pairs={{0,1},{1,0},{2,3},{3,2},{4,5},{5,4},{6,7},{7,6},{8,9},{9,8},{10,11... | collective-permute-start | bytes 1572872 | tf_op jit(solution)/shard_map/ppermute | solution.py:526
  7.5 8.8 %refs.2 = (bf16[128,336,128]{2,1,0:T(8,128)(2,1)S(1)}, f32[336,128]{1,0:T(8,128)S(1)}) custom-call(bf16[100,3,128,128]{3,2,1,0:T(8,128)(2,1)} %refs.3), custom_call_target="tpu_custom_call" | custom-call | flops 900000000 | bytes 2700000 | tf_op jit(solution)/shard_map/refs/pallas_call | solution.py:165
  16.4 0.8 %prepare.1 = (bf16[16,128,128]{2,1,0:T(8,128)(2,1)S(1)}, bf16[16,128,128]{2,1,0:T(8,128)(2,1)S(1)}, f32[112,192]{1,0:T(8,128)S(1)}, f32[1,192]{1,0:T(1,128)S(1)}, f32[3,112,128]{2,1,0:T(8,128)S(1)}) custom-call(f32[16,128]{1,0:T(8,128)S(1)} %copy-done.3, f32[1,128]{1,0:T(1,128)S(1)} %bitcast.6, s32[192,100]{1,0:T(8,128)S(1)} %copy-done.2, ...), custom_call_target="tpu_custom_call" | custom-call | flops 300000000 | bytes 900000 | tf_op jit(solution)/shard_map/prepare/pallas_call | solution.py:96
  17.2 0.0 collective-permute-done.4.args_4_
  17.2 6.4 %filter.4 = (bf16[128,192,128]{2,1,0:T(8,128)(2,1)S(1)}, bf16[128,192,128]{2,1,0:T(8,128)(2,1)S(1)}, f32[8,128]{1,0:T(8,128)S(1)}) custom-call(s32[96]{0:T(128)S(1)} %copy-done.1, bf16[96,64,128]{2,1,0:T(8,128)(2,1)S(1)} %copy-done, bf16[16,128,128]{2,1,0:T(8,128)(2,1)S(1)} %get-tuple-element.41.args_2_.left, ...), custom_call_target="tpu_custom_call" | custom-call | flops 960000000 | bytes 2880000 | tf_op jit(solution)/shard_map/filter/pallas_call | solution.py:233
  23.6 0.0 collective-permute-done.1.bins.args_0_
  23.6 0.6 pick.1
  24.2 0.0 collective-permute-done.3.refs_0_
  24.3 0.1 fusion
  24.3 0.1 collective-permute-start.5
  24.4 0.5 collective-permute-start.6
  24.9 0.1 collective-permute-start.7
  25.0 1.2 %collective-permute-start = (bf16[16,64,128]{2,1,0:T(8,128)(2,1)S(1)}, bf16[16,64,128]{2,1,0:T(8,128)(2,1)S(1)}, u32[]{:S(2)}, u32[]{:S(2)}) collective-permute-start(bf16[16,64,128]{2,1,0:T(8,128)(2,1)S(1)} %slice.30), channel_id=1, source_target_pairs={{0,1},{1,0},{2,3},{3,2},{4,5},{5,4},{6,7},{7,6},{8,9},{9,8},{10,11... | collective-permute-start | bytes 786440 | tf_op jit(solution)/shard_map/ppermute | solution.py:526
  26.2 0.0 collective-permute-done.5.args_4_
  26.2 0.1 collective-permute-done.6.args_5_
  26.3 0.4 collective-permute-done.7.args_6_
  26.7 2.8 %filter.5 = (bf16[128,192,128]{2,1,0:T(8,128)(2,1)S(1)}, bf16[128,192,128]{2,1,0:T(8,128)(2,1)S(1)}, f32[8,128]{1,0:T(8,128)S(1)}) custom-call(s32[96]{0:T(128)S(1)} %collective-permute-done.1.bins.args_0_, bf16[48,64,128]{2,1,0:T(8,128)(2,1)S(1)} %gate.3.args_1_, ...), custom_call_target="tpu_custom_call", output_to_operand_aliasing={{0}: (7, {}), {1}: (8, {})} | custom-call | flops 480000000 | bytes 1440000 | tf_op jit(solution)/shard_map/filter/pallas_call | solution.py:233
  29.5 4.5 %collective-permute-done.2.refs_0_ = bf16[32,64,128]{2,1,0:T(8,128)(2,1)S(1)} collective-permute-done((bf16[32,64,128]{2,1,0:T(8,128)(2,1)S(1)}, bf16[32,64,128]{2,1,0:T(8,128)(2,1)S(1)}, u32[]{:S(2)}, u32[]{:S(2)}) %collective-permute-start.2) | collective-permute-done | bytes 524320 | tf_op jit(solution)/shard_map/ppermute | solution.py:526
  34.0 0.1 collective-permute-start.10
  34.1 0.5 collective-permute-start.11
  34.6 0.1 collective-permute-start.8
  34.7 0.4 collective-permute-start.9
  35.1 0.3 collective-permute-done.10.args_6_
  35.5 0.2 collective-permute-done.11.args_7_
  35.6 0.3 collective-permute-done.8.args_4_
  36.0 0.2 collective-permute-done.9.args_5_
  36.1 2.1 %filter.6 = (bf16[128,192,128]{2,1,0:T(8,128)(2,1)S(1)}, bf16[128,192,128]{2,1,0:T(8,128)(2,1)S(1)}, f32[8,128]{1,0:T(8,128)S(1)}) custom-call(s32[96]{0:T(128)S(1)} %collective-permute-done.1.bins.args_0_, bf16[32,64,128]{2,1,0:T(8,128)(2,1)S(1)} %gate.4.args_1_, ...), custom_call_target="tpu_custom_call", output_to_operand_aliasing={{0}: (8, {}), {1}: (9, {})} | custom-call | flops 320000000 | bytes 960000 | tf_op jit(solution)/shard_map/filter/pallas_call | solution.py:233
  38.3 1.1 %collective-permute-done.refs_0_ = bf16[16,64,128]{2,1,0:T(8,128)(2,1)S(1)} collective-permute-done((bf16[16,64,128]{2,1,0:T(8,128)(2,1)S(1)}, bf16[16,64,128]{2,1,0:T(8,128)(2,1)S(1)}, u32[]{:S(2)}, u32[]{:S(2)}) %collective-permute-start) | collective-permute-done | bytes 262176 | tf_op jit(solution)/shard_map/ppermute | solution.py:526
  39.4 0.0 collective-permute-start.12
  39.4 1.5 %collective-permute-done.12.args_3_ = bf16[16,64,128]{2,1,0:T(8,128)(2,1)S(1)} collective-permute-done((bf16[16,64,128]{2,1,0:T(8,128)(2,1)S(1)}, bf16[16,64,128]{2,1,0:T(8,128)(2,1)S(1)}, u32[]{:S(2)}, u32[]{:S(2)}) %collective-permute-start.12) | collective-permute-done | bytes 262176 | tf_op jit(solution)/shard_map/ppermute | solution.py:543
  41.0 1.0 %filter.7 = (bf16[128,192,128]{2,1,0:T(8,128)(2,1)S(1)}, bf16[128,192,128]{2,1,0:T(8,128)(2,1)S(1)}) custom-call(bf16[16,64,128]{2,1,0:T(8,128)(2,1)S(1)} %gate.5.args_0_, bf16[16,128,128]{2,1,0:T(8,128)(2,1)S(1)} %get-tuple-element.44.refs_1_.args_1_, ...), custom_call_target="tpu_custom_call", output_to_operand_aliasing={{0}: (4, {}), {1}: (5, {})} | custom-call | flops 160000000 | bytes 480000 | tf_op jit(solution)/shard_map/filter/pallas_call | solution.py:233
  41.9 3.1 %score.1 = (f32[336,192]{1,0:T(8,128)S(1)}, f32[8,192]{1,0:T(8,128)S(1)}) custom-call(bf16[128,192,128]{2,1,0:T(8,128)(2,1)S(1)} %get-tuple-element.54.plain, bf16[128,336,128]{2,1,0:T(8,128)(2,1)S(1)} %get-tuple-element.55.refs, f32[336,128]{1,0:T(8,128)S(1)} %get-tuple-element.40.after.norm, f32[112,192]{1,0:T(8,128)S(1)} %get-tuple-element.56.mask, ...), custom_call_target="tpu_custom_call" | custom-call | flops 500000000 | bytes 1500000 | tf_op jit(solution)/shard_map/score/pallas_call | solution.py:293
  45.0 1.8 %collective-permute-start.13 = (f32[8,192]{1,0:T(8,128)S(1)}, f32[8,192]{1,0:T(8,128)S(1)}, u32[]{:S(2)}, u32[]{:S(2)}) collective-permute-start(f32[8,192]{1,0:T(8,128)S(1)} %get-tuple-element.59.mine), channel_id=1, source_target_pairs={{0,1},{1,0},{2,3},{3,2},{4,5},{5,4},{6,7},{7,6},{8,9},{9,8},{10,11... | collective-permute-start | bytes 18440 | tf_op jit(solution)/shard_map/ppermute | solution.py:552
  46.8 0.2 shares.1
  47.1 1.6 %collective-permute-done.13.other = f32[8,192]{1,0:T(8,128)S(1)} collective-permute-done((f32[8,192]{1,0:T(8,128)S(1)}, f32[8,192]{1,0:T(8,128)S(1)}, u32[]{:S(2)}, u32[]{:S(2)}) %collective-permute-start.13) | collective-permute-done | bytes 6176 | tf_op jit(solution)/shard_map/ppermute | solution.py:552
  48.7 1.3 %sums.3 = (bf16[4,500,128]{2,1,0:T(8,128)(2,1)S(1)}, bf16[2,112,384]{2,1,0:T(8,128)(2,1)S(1)}) custom-call(f32[4,112,192]{2,1,0:T(8,128)S(1)} %shares.1, f32[8,192]{1,0:T(8,128)S(1)} %get-tuple-element.59.mine, f32[8,192]{1,0:T(8,128)S(1)} %collective-permute-done.13.other, bf16[128,192,128]{2,1,0:T(8,128)(2,1)S(1)} %get-tuple-element.54.plain, ...), custom_call_target="tpu_custom_call" | custom-call | flops 400000000 | bytes 1200000 | tf_op jit(solution)/shard_map/sums/pallas_call | solution.py:413
  50.1 1.8 %collective-permute-start.14 = (bf16[4,500,128]{2,1,0:T(8,128)(2,1)S(1)}, bf16[4,500,128]{2,1,0:T(8,128)(2,1)S(1)}, u32[]{:S(2)}, u32[]{:S(2)}) collective-permute-start(bf16[4,500,128]{2,1,0:T(8,128)(2,1)S(1)} %get-tuple-element.63.after), channel_id=1, source_target_pairs={{0,2},{2,0},{4,6},{6,4},{8,10},{10,8},{12,14},{14,12},{1,3},{3,1},... | collective-permute-start | bytes 1536008 | tf_op jit(solution)/shard_map/ppermute | solution.py:556
  51.9 0.8 %sums.4 = (bf16[2,300,128]{2,1,0:T(8,128)(2,1)S(1)}, bf16[2,300,128]{2,1,0:T(8,128)(2,1)S(1)}, bf16[2,300,128]{2,1,0:T(8,128)(2,1)S(1)}) custom-call(bf16[2,112,384]{2,1,0:T(8,128)(2,1)S(1)} %get-tuple-element.62.weights, bf16[128,192,128]{2,1,0:T(8,128)(2,1)S(1)} %get-tuple-element.54.plain, bf16[128,192,128]{2,1,0:T(8,128)(2,1)S(1)} %get-tuple-element.61.turned, ...), custom_call_target="tpu_custom_call" | custom-call | flops 240000000 | bytes 720000 | tf_op jit(solution)/shard_map/sums/pallas_call | solution.py:413
  52.7 2.7 %collective-permute-start.18 = (bf16[2,300,128]{2,1,0:T(8,128)(2,1)S(1)}, bf16[2,300,128]{2,1,0:T(8,128)(2,1)S(1)}, u32[]{:S(2)}, u32[]{:S(2)}) collective-permute-start(bf16[2,300,128]{2,1,0:T(8,128)(2,1)S(1)} %get-tuple-element.71), channel_id=1, source_target_pairs={{0,8},{2,10},{4,12},{6,14},{8,0},{10,2},{12,4},{14,6},{1,9},{3,11}... | collective-permute-start | bytes 460808 | tf_op jit(solution)/shard_map/ppermute | solution.py:556
  55.4 1.4 %collective-permute-start.19 = (bf16[2,300,128]{2,1,0:T(8,128)(2,1)S(1)}, bf16[2,300,128]{2,1,0:T(8,128)(2,1)S(1)}, u32[]{:S(2)}, u32[]{:S(2)}) collective-permute-start(bf16[2,300,128]{2,1,0:T(8,128)(2,1)S(1)} %get-tuple-element.72), channel_id=1, source_target_pairs={{0,12},{2,14},{4,8},{6,10},{8,4},{10,6},{12,0},{14,2},{1,13},{3,15... | collective-permute-start | bytes 460808 | tf_op jit(solution)/shard_map/ppermute | solution.py:556
  56.7 0.2 collective-permute-start.20
  57.0 1.6 %sums.5 = (f32[4,500,128]{2,1,0:T(8,128)S(1)}, f32[2,300,128]{2,1,0:T(8,128)S(1)}) custom-call(bf16[2,112,384]{2,1,0:T(8,128)(2,1)S(1)} %get-tuple-element.62.weights, bf16[128,192,128]{2,1,0:T(8,128)(2,1)S(1)} %get-tuple-element.54.plain, bf16[128,192,128]{2,1,0:T(8,128)(2,1)S(1)} %get-tuple-element.61.turned, bf16[2,300,128]{2,1,0:T(8,128)(2,1)S(1)} %get-tuple-element.64.after), custom_call_target="tpu_custom_call" | custom-call | flops 400000000 | bytes 1200000 | tf_op jit(solution)/shard_map/sums/pallas_call | solution.py:413
  58.5 4.3 %collective-permute-done.14.got = bf16[4,500,128]{2,1,0:T(8,128)(2,1)S(1)} collective-permute-done((bf16[4,500,128]{2,1,0:T(8,128)(2,1)S(1)}, bf16[4,500,128]{2,1,0:T(8,128)(2,1)S(1)}, u32[]{:S(2)}, u32[]{:S(2)}) %collective-permute-start.14) | collective-permute-done | bytes 512032 | tf_op jit(solution)/shard_map/ppermute | solution.py:556
  62.8 0.1 fold.1
  62.9 2.9 %collective-permute-start.15 = (bf16[1,500,128]{2,1,0:T(8,128)(2,1)S(1)}, bf16[1,500,128]{2,1,0:T(8,128)(2,1)S(1)}, u32[]{:S(2)}, u32[]{:S(2)}) collective-permute-start(bf16[1,500,128]{2,1,0:T(8,128)(2,1)S(1)} %get-tuple-element.67), channel_id=1, source_target_pairs={{0,8},{2,10},{4,12},{6,14},{8,0},{10,2},{12,4},{14,6},{1,9},{3,11}... | collective-permute-start | bytes 384008 | tf_op jit(solution)/shard_map/ppermute | solution.py:556
  65.8 1.4 %collective-permute-start.16 = (bf16[1,500,128]{2,1,0:T(8,128)(2,1)S(1)}, bf16[1,500,128]{2,1,0:T(8,128)(2,1)S(1)}, u32[]{:S(2)}, u32[]{:S(2)}) collective-permute-start(bf16[1,500,128]{2,1,0:T(8,128)(2,1)S(1)} %get-tuple-element.68), channel_id=1, source_target_pairs={{0,12},{2,14},{4,8},{6,10},{8,4},{10,6},{12,0},{14,2},{1,13},{3,15... | collective-permute-start | bytes 384008 | tf_op jit(solution)/shard_map/ppermute | solution.py:556
  67.2 0.0 collective-permute-done.18.rest_0_
  67.2 0.2 collective-permute-start.17
  67.4 0.0 collective-permute-done.19.rest_1_
  67.4 0.0 collective-permute-done.20.rest_2_
  67.4 0.1 gather.1
  67.5 1.6 %collective-permute-start.21 = (bf16[1,300,128]{2,1,0:T(8,128)(2,1)S(1)}, bf16[1,300,128]{2,1,0:T(8,128)(2,1)S(1)}, u32[]{:S(2)}, u32[]{:S(2)}) collective-permute-start(bf16[1,300,128]{2,1,0:T(8,128)(2,1)S(1)} %get-tuple-element.74), channel_id=1, source_target_pairs={{0,2},{2,0},{4,6},{6,4},{8,10},{10,8},{12,14},{14,12},{1,3},{3,1},... | collective-permute-start | bytes 230408 | tf_op jit(solution)/shard_map/ppermute | solution.py:556
  69.0 2.9 %collective-permute-done.21.args_5_ = bf16[1,300,128]{2,1,0:T(8,128)(2,1)S(1)} collective-permute-done((bf16[1,300,128]{2,1,0:T(8,128)(2,1)S(1)}, bf16[1,300,128]{2,1,0:T(8,128)(2,1)S(1)}, u32[]{:S(2)}, u32[]{:S(2)}) %collective-permute-start.21) | collective-permute-done | bytes 76832 | tf_op jit(solution)/shard_map/ppermute | solution.py:556
  71.9 5.9 %collective-permute-done.15.args_1_ = bf16[1,500,128]{2,1,0:T(8,128)(2,1)S(1)} collective-permute-done((bf16[1,500,128]{2,1,0:T(8,128)(2,1)S(1)}, bf16[1,500,128]{2,1,0:T(8,128)(2,1)S(1)}, u32[]{:S(2)}, u32[]{:S(2)}) %collective-permute-start.15) | collective-permute-done | bytes 128032 | tf_op jit(solution)/shard_map/ppermute | solution.py:556
  77.8 0.0 collective-permute-done.16.args_2_
  77.8 0.0 collective-permute-done.17.args_3_
  77.8 0.9 %finish.1 = f32[800,128]{1,0:T(8,128)} custom-call(f32[1,500,128]{2,1,0:T(8,128)S(1)} %get-tuple-element.66.args_0_, bf16[1,500,128]{2,1,0:T(8,128)(2,1)S(1)} %collective-permute-done.15.args_1_, bf16[1,500,128]{2,1,0:T(8,128)(2,1)S(1)} %collective-permute-done.16.args_2_, bf16[1,500,128]{2,1,0:T(8,128)(2,1)S(1)} %collective-permute-done.17.args_3_, ...), custom_call_target="tpu_custom_call" | custom-call | flops 100000000 | bytes 300000 | tf_op jit(solution)/shard_map/finish/pallas_call | solution.py:490
  (17 shorter events, 0.1 us)
Async XLA Ops:
  0.0 16.3 %copy-start.6 = (f32[128]{0:T(128)S(1)}, f32[128]{0:T(128)}, u32[]{:S(2)}) copy-start(f32[128]{0:T(128)} %param.11) | copy-start | bytes 1540
  0.0 16.3 %copy-start.5 = (f32[192]{0:T(256)S(1)}, f32[192]{0:T(256)}, u32[]{:S(2)}) copy-start(f32[192]{0:T(256)} %param.15) | copy-start | bytes 2308
  0.0 16.3 %copy-start.4 = (s32[100,3]{0,1:T(4,128)S(1)}, s32[100,3]{0,1:T(4,128)}, u32[]{:S(2)}) copy-start(s32[100,3]{0,1:T(4,128)} %param.13) | copy-start | bytes 3604
  0.0 16.3 %copy-start.3 = (f32[16,128]{1,0:T(8,128)S(1)}, f32[16,128]{1,0:T(8,128)}, u32[]{:S(2)}) copy-start(f32[16,128]{1,0:T(8,128)} %ctf.1) | copy-start | bytes 24580
  0.0 16.4 %copy-start.2 = (s32[192,100]{1,0:T(8,128)S(1)}, s32[192,100]{1,0:T(8,128)}, u32[]{:S(2)}) copy-start(s32[192,100]{1,0:T(8,128)} %mask.1) | copy-start | bytes 230404
  0.0 17.2 %collective-permute-start.4 = (bf16[96,64,128]{2,1,0:T(8,128)(2,1)}, bf16[96,64,128]{2,1,0:T(8,128)(2,1)S(1)}, u32[]{:S(2)}, u32[]{:S(2)}) collective-permute-start(bf16[96,64,128]{2,1,0:T(8,128)(2,1)} %args_1_.4), channel_id=1, source_target_pairs={{0,16},{16,0},{1,17},{17,1},{2,18},{18,2},{3,19},{19,3},{4,20},{20... | collective-permute-start | bytes 4718600 | tf_op jit(solution)/shard_map/ppermute | solution.py:528
  1.7 15.5 %copy-start = (bf16[96,64,128]{2,1,0:T(8,128)(2,1)S(1)}, bf16[96,64,128]{2,1,0:T(8,128)(2,1)}, u32[]{:S(2)}) copy-start(bf16[96,64,128]{2,1,0:T(8,128)(2,1)} %args_1_.4) | copy-start | bytes 4718596
  1.7 15.5 %copy-start.1 = (s32[96]{0:T(128)S(1)}, s32[96]{0:T(128)}, u32[]{:S(2)}) copy-start(s32[96]{0:T(128)} %args_0_.4) | copy-start | bytes 1156
  1.8 22.5 %collective-permute-start.3 = (bf16[48,64,128]{2,1,0:T(8,128)(2,1)S(1)}, bf16[48,64,128]{2,1,0:T(8,128)(2,1)S(1)}, u32[]{:S(2)}, u32[]{:S(2)}) collective-permute-start(bf16[48,64,128]{2,1,0:T(8,128)(2,1)S(1)} %slice.32), channel_id=1, source_target_pairs={{0,1},{1,0},{2,3},{3,2},{4,5},{5,4},{6,7},{7,6},{8,9},{9,8},{10,11... | collective-permute-start | bytes 2359304 | tf_op jit(solution)/shard_map/ppermute | solution.py:526
  4.4 19.2 %collective-permute-start.1 = (s32[96]{0:T(128)}, s32[96]{0:T(128)S(1)}, u32[]{:S(2)}, u32[]{:S(2)}) collective-permute-start(s32[96]{0:T(128)} %args_0_.4), channel_id=1, source_target_pairs={{0,1},{1,0},{2,3},{3,2},{4,5},{5,4},{6,7},{7,6},{8,9},{9,8},{10,11... | collective-permute-start | bytes 1160 | tf_op jit(solution)/shard_map/ppermute | solution.py:527
  5.5 28.5 %collective-permute-start.2 = (bf16[32,64,128]{2,1,0:T(8,128)(2,1)S(1)}, bf16[32,64,128]{2,1,0:T(8,128)(2,1)S(1)}, u32[]{:S(2)}, u32[]{:S(2)}) collective-permute-start(bf16[32,64,128]{2,1,0:T(8,128)(2,1)S(1)} %slice.31), channel_id=1, source_target_pairs={{0,1},{1,0},{2,3},{3,2},{4,5},{5,4},{6,7},{7,6},{8,9},{9,8},{10,11... | collective-permute-start | bytes 1572872 | tf_op jit(solution)/shard_map/ppermute | solution.py:526
  24.3 1.9 %collective-permute-start.5 = (bf16[16,64,128]{2,1,0:T(8,128)(2,1)S(1)}, bf16[16,64,128]{2,1,0:T(8,128)(2,1)S(1)}, u32[]{:S(2)}, u32[]{:S(2)}) collective-permute-start(bf16[16,64,128]{2,1,0:T(8,128)(2,1)S(1)} %get-tuple-element.77), channel_id=1, source_target_pairs={{0,16},{16,0},{1,17},{17,1},{2,18},{18,2},{3,19},{19,3},{4,20},{20... | collective-permute-start | bytes 786440 | tf_op jit(solution)/shard_map/ppermute | solution.py:543
  24.4 1.9 %collective-permute-start.6 = (bf16[16,64,128]{2,1,0:T(8,128)(2,1)S(1)}, bf16[16,64,128]{2,1,0:T(8,128)(2,1)S(1)}, u32[]{:S(2)}, u32[]{:S(2)}) collective-permute-start(bf16[16,64,128]{2,1,0:T(8,128)(2,1)S(1)} %get-tuple-element.76), channel_id=1, source_target_pairs={{0,16},{16,0},{1,17},{17,1},{2,18},{18,2},{3,19},{19,3},{4,20},{20... | collective-permute-start | bytes 786440 | tf_op jit(solution)/shard_map/ppermute | solution.py:543
  24.9 1.8 %collective-permute-start.7 = (bf16[16,64,128]{2,1,0:T(8,128)(2,1)S(1)}, bf16[16,64,128]{2,1,0:T(8,128)(2,1)S(1)}, u32[]{:S(2)}, u32[]{:S(2)}) collective-permute-start(bf16[16,64,128]{2,1,0:T(8,128)(2,1)S(1)} %get-tuple-element.75), channel_id=1, source_target_pairs={{0,16},{16,0},{1,17},{17,1},{2,18},{18,2},{3,19},{19,3},{4,20},{20... | collective-permute-start | bytes 786440 | tf_op jit(solution)/shard_map/ppermute | solution.py:543
  25.0 14.4 %collective-permute-start = (bf16[16,64,128]{2,1,0:T(8,128)(2,1)S(1)}, bf16[16,64,128]{2,1,0:T(8,128)(2,1)S(1)}, u32[]{:S(2)}, u32[]{:S(2)}) collective-permute-start(bf16[16,64,128]{2,1,0:T(8,128)(2,1)S(1)} %slice.30), channel_id=1, source_target_pairs={{0,1},{1,0},{2,3},{3,2},{4,5},{5,4},{6,7},{7,6},{8,9},{9,8},{10,11... | collective-permute-start | bytes 786440 | tf_op jit(solution)/shard_map/ppermute | solution.py:526
  34.0 1.4 %collective-permute-start.10 = (bf16[8,64,128]{2,1,0:T(8,128)(2,1)S(1)}, bf16[8,64,128]{2,1,0:T(8,128)(2,1)S(1)}, u32[]{:S(2)}, u32[]{:S(2)}) collective-permute-start(bf16[8,64,128]{2,1,0:T(8,128)(2,1)S(1)} %get-tuple-element.79), channel_id=1, source_target_pairs={{0,16},{16,0},{1,17},{17,1},{2,18},{18,2},{3,19},{19,3},{4,20},{20... | collective-permute-start | bytes 393224 | tf_op jit(solution)/shard_map/ppermute | solution.py:543
  34.1 1.5 %collective-permute-start.11 = (bf16[8,64,128]{2,1,0:T(8,128)(2,1)S(1)}, bf16[8,64,128]{2,1,0:T(8,128)(2,1)S(1)}, u32[]{:S(2)}, u32[]{:S(2)}) collective-permute-start(bf16[8,64,128]{2,1,0:T(8,128)(2,1)S(1)} %get-tuple-element.78), channel_id=1, source_target_pairs={{0,16},{16,0},{1,17},{17,1},{2,18},{18,2},{3,19},{19,3},{4,20},{20... | collective-permute-start | bytes 393224 | tf_op jit(solution)/shard_map/ppermute | solution.py:543
  34.6 1.3 %collective-permute-start.8 = (bf16[8,64,128]{2,1,0:T(8,128)(2,1)S(1)}, bf16[8,64,128]{2,1,0:T(8,128)(2,1)S(1)}, u32[]{:S(2)}, u32[]{:S(2)}) collective-permute-start(bf16[8,64,128]{2,1,0:T(8,128)(2,1)S(1)} %get-tuple-element.81), channel_id=1, source_target_pairs={{0,16},{16,0},{1,17},{17,1},{2,18},{18,2},{3,19},{19,3},{4,20},{20... | collective-permute-start | bytes 393224 | tf_op jit(solution)/shard_map/ppermute | solution.py:543
  34.7 1.5 %collective-permute-start.9 = (bf16[8,64,128]{2,1,0:T(8,128)(2,1)S(1)}, bf16[8,64,128]{2,1,0:T(8,128)(2,1)S(1)}, u32[]{:S(2)}, u32[]{:S(2)}) collective-permute-start(bf16[8,64,128]{2,1,0:T(8,128)(2,1)S(1)} %get-tuple-element.80), channel_id=1, source_target_pairs={{0,16},{16,0},{1,17},{17,1},{2,18},{18,2},{3,19},{19,3},{4,20},{20... | collective-permute-start | bytes 393224 | tf_op jit(solution)/shard_map/ppermute | solution.py:543
  39.4 1.5 %collective-permute-start.12 = (bf16[16,64,128]{2,1,0:T(8,128)(2,1)S(1)}, bf16[16,64,128]{2,1,0:T(8,128)(2,1)S(1)}, u32[]{:S(2)}, u32[]{:S(2)}) collective-permute-start(bf16[16,64,128]{2,1,0:T(8,128)(2,1)S(1)} %gate.5.args_0_), channel_id=1, source_target_pairs={{0,16},{16,0},{1,17},{17,1},{2,18},{18,2},{3,19},{19,3},{4,20},{20... | collective-permute-start | bytes 786440 | tf_op jit(solution)/shard_map/ppermute | solution.py:543
  45.0 3.7 %collective-permute-start.13 = (f32[8,192]{1,0:T(8,128)S(1)}, f32[8,192]{1,0:T(8,128)S(1)}, u32[]{:S(2)}, u32[]{:S(2)}) collective-permute-start(f32[8,192]{1,0:T(8,128)S(1)} %get-tuple-element.59.mine), channel_id=1, source_target_pairs={{0,1},{1,0},{2,3},{3,2},{4,5},{5,4},{6,7},{7,6},{8,9},{9,8},{10,11... | collective-permute-start | bytes 18440 | tf_op jit(solution)/shard_map/ppermute | solution.py:552
  50.1 12.7 %collective-permute-start.14 = (bf16[4,500,128]{2,1,0:T(8,128)(2,1)S(1)}, bf16[4,500,128]{2,1,0:T(8,128)(2,1)S(1)}, u32[]{:S(2)}, u32[]{:S(2)}) collective-permute-start(bf16[4,500,128]{2,1,0:T(8,128)(2,1)S(1)} %get-tuple-element.63.after), channel_id=1, source_target_pairs={{0,2},{2,0},{4,6},{6,4},{8,10},{10,8},{12,14},{14,12},{1,3},{3,1},... | collective-permute-start | bytes 1536008 | tf_op jit(solution)/shard_map/ppermute | solution.py:556
  52.7 14.4 %collective-permute-start.18 = (bf16[2,300,128]{2,1,0:T(8,128)(2,1)S(1)}, bf16[2,300,128]{2,1,0:T(8,128)(2,1)S(1)}, u32[]{:S(2)}, u32[]{:S(2)}) collective-permute-start(bf16[2,300,128]{2,1,0:T(8,128)(2,1)S(1)} %get-tuple-element.71), channel_id=1, source_target_pairs={{0,8},{2,10},{4,12},{6,14},{8,0},{10,2},{12,4},{14,6},{1,9},{3,11}... | collective-permute-start | bytes 460808 | tf_op jit(solution)/shard_map/ppermute | solution.py:556
  55.4 12.0 %collective-permute-start.19 = (bf16[2,300,128]{2,1,0:T(8,128)(2,1)S(1)}, bf16[2,300,128]{2,1,0:T(8,128)(2,1)S(1)}, u32[]{:S(2)}, u32[]{:S(2)}) collective-permute-start(bf16[2,300,128]{2,1,0:T(8,128)(2,1)S(1)} %get-tuple-element.72), channel_id=1, source_target_pairs={{0,12},{2,14},{4,8},{6,10},{8,4},{10,6},{12,0},{14,2},{1,13},{3,15... | collective-permute-start | bytes 460808 | tf_op jit(solution)/shard_map/ppermute | solution.py:556
  56.7 10.7 %collective-permute-start.20 = (bf16[2,300,128]{2,1,0:T(8,128)(2,1)S(1)}, bf16[2,300,128]{2,1,0:T(8,128)(2,1)S(1)}, u32[]{:S(2)}, u32[]{:S(2)}) collective-permute-start(bf16[2,300,128]{2,1,0:T(8,128)(2,1)S(1)} %get-tuple-element.64.after), channel_id=1, source_target_pairs={{0,4},{2,6},{4,0},{6,2},{8,12},{10,14},{12,8},{14,10},{1,5},{3,7},... | collective-permute-start | bytes 460808 | tf_op jit(solution)/shard_map/ppermute | solution.py:556
  62.9 14.9 %collective-permute-start.15 = (bf16[1,500,128]{2,1,0:T(8,128)(2,1)S(1)}, bf16[1,500,128]{2,1,0:T(8,128)(2,1)S(1)}, u32[]{:S(2)}, u32[]{:S(2)}) collective-permute-start(bf16[1,500,128]{2,1,0:T(8,128)(2,1)S(1)} %get-tuple-element.67), channel_id=1, source_target_pairs={{0,8},{2,10},{4,12},{6,14},{8,0},{10,2},{12,4},{14,6},{1,9},{3,11}... | collective-permute-start | bytes 384008 | tf_op jit(solution)/shard_map/ppermute | solution.py:556
  65.8 12.0 %collective-permute-start.16 = (bf16[1,500,128]{2,1,0:T(8,128)(2,1)S(1)}, bf16[1,500,128]{2,1,0:T(8,128)(2,1)S(1)}, u32[]{:S(2)}, u32[]{:S(2)}) collective-permute-start(bf16[1,500,128]{2,1,0:T(8,128)(2,1)S(1)} %get-tuple-element.68), channel_id=1, source_target_pairs={{0,12},{2,14},{4,8},{6,10},{8,4},{10,6},{12,0},{14,2},{1,13},{3,15... | collective-permute-start | bytes 384008 | tf_op jit(solution)/shard_map/ppermute | solution.py:556
  67.2 10.6 %collective-permute-start.17 = (bf16[1,500,128]{2,1,0:T(8,128)(2,1)S(1)}, bf16[1,500,128]{2,1,0:T(8,128)(2,1)S(1)}, u32[]{:S(2)}, u32[]{:S(2)}) collective-permute-start(bf16[1,500,128]{2,1,0:T(8,128)(2,1)S(1)} %get-tuple-element.69), channel_id=1, source_target_pairs={{0,4},{2,6},{4,0},{6,2},{8,12},{10,14},{12,8},{14,10},{1,5},{3,7},... | collective-permute-start | bytes 384008 | tf_op jit(solution)/shard_map/ppermute | solution.py:556
  67.5 4.5 %collective-permute-start.21 = (bf16[1,300,128]{2,1,0:T(8,128)(2,1)S(1)}, bf16[1,300,128]{2,1,0:T(8,128)(2,1)S(1)}, u32[]{:S(2)}, u32[]{:S(2)}) collective-permute-start(bf16[1,300,128]{2,1,0:T(8,128)(2,1)S(1)} %get-tuple-element.74), channel_id=1, source_target_pairs={{0,2},{2,0},{4,6},{6,4},{8,10},{10,8},{12,14},{14,12},{1,3},{3,1},... | collective-permute-start | bytes 230408 | tf_op jit(solution)/shard_map/ppermute | solution.py:556

commit v13 on v12

--- a/solution.py
+++ b/solution.py
@@ -555,9 +555,9 @@
     def along(x, mask):
         return lax.ppermute(x, "dom", [(i, i ^ mask) for i in range(dom)])
 
-    def spread(sends, bit):
-        far_first = sorted(range(len(sends)), key=lambda m: m == 0)
-        return [along(sends[m], (m + 1) << bit) for m in far_first]
+    def spread(sends, bit, order):
+        order = [m for m in order if m < len(sends)]
+        return [along(sends[m], (m + 1) << bit) for m in order]
 
     inner, outer = row_pieces(half // dom, dom)
     images_in = (held(plain), held(turned))
@@ -589,7 +589,7 @@
             (jax.ShapeDtypeStruct(shape, BF16),) * (count - 1),
             outer,
         )
-        got_b = spread(sends_b, 1)
+        got_b = spread(sends_b, 1, (1, 2, 0))
         keep_shape += (pinned(shape, F32),)
         after = sends_b[0]
     keep, *keep_b = call_sums(
@@ -605,7 +605,7 @@
         got = along(send, 1 << bit)
         bit += 1
     keep, *sends = fold(keep, got, (), keep.shape[0], bit)
-    done = [[keep] + spread(sends, bit)]
+    done = [[keep] + spread(sends, bit, (2, 0, 1))]
     if outer:
         keep_b, send_b = gather(keep_b[0], got_b)
         done.append([keep_b, along(send_b, 1)])

time: 79.2 us -> 80.4 us (1.015)
  waiting for transfers between devices: 23.3 us -> 24.7 us
    ppermute x8, waiting for transfers between devices: 13.1 us -> 14.4 us  [along(): return lax.ppermute(x, 'dom', [(i, i ^ mask) for i in range(dom)])]
  transfers between devices with their start and end apart: 22 -> 22, of which waited for: 13 -> 14; matrix products, arithmetic and copies ran while one was open for 3% -> 3% of each run, Pallas kernels for 31% -> 30%
where the time goes in v13:
time: 80.4 us; the launch traced here: 80.3 us
  Pallas kernels  30.7 us (38%)
  waiting for transfers between devices  24.7 us (31%)
  starting transfers between devices  22.2 us (28%)
  local copies, waits for them, and re-layouts  2.4 us (3%)
    ppermute x8, waiting for transfers between devices, along(): return lax.ppermute(x, 'dom', [(i, i ^ mask) for i in range(dom)])  14.4 us
    pallas_call x4, Pallas kernels, filter_chunk(): pl.pallas_call(functools.partial(filter_kernel, picked=picked, parts=part...  12.3 us
    ppermute x8, starting transfers between devices, along(): return lax.ppermute(x, 'dom', [(i, i ^ mask) for i in range(dom)])  12.2 us
    pallas_call x1, Pallas kernels, lay_refs(): pl.pallas_call(functools.partial(refs_kernel, padded=padded), grid=(rots,...  8.81 us
    ppermute x3, starting transfers between devices, local(): remote = [over_cls(images[a:a + n]) for a, n in zip(starts, sizes)]  5.82 us
    ppermute x3, waiting for transfers between devices, local(): remote = [over_cls(images[a:a + n]) for a, n in zip(starts, sizes)]  5.61 us
    pallas_call x3, Pallas kernels, call_sums(): pl.pallas_call(kernel, in_specs=[vmem] * len(args) + [pl.BlockSpec(memory...  3.76 us
    pallas_call x1, Pallas kernels, score(): pl.pallas_call(score_kernel, out_shape=(pinned((height, count), F32), pin...  3.1 us
  transfers between devices with their start and end apart: 22, of which 14 were waited for; matrix products, arithmetic and copies ran while one was open for 3% of the time, Pallas kernels for 30%

profile of v13, /device:TPU:0, one launch (start us, length us, event | category | flops | bytes accessed | tf_op | source)
XLA Modules:
  0.0 80.3 jit_solution(16198630567930786909)
XLA Ops:
  0.0 0.5 collective-permute-start.4
  0.5 1.2 %slice.32 = bf16[48,64,128]{2,1,0:T(8,128)(2,1)S(1)} slice(bf16[96,64,128]{2,1,0:T(8,128)(2,1)} %args_1_.4), slice={[0:48], [0:64], [0:128]} | slice | bytes 1572864 | tf_op jit(solution)/shard_map/slice | solution.py:526
  1.7 0.0 copy-start
  1.7 0.0 copy-start.1
  1.8 2.6 %collective-permute-start.3 = (bf16[48,64,128]{2,1,0:T(8,128)(2,1)S(1)}, bf16[48,64,128]{2,1,0:T(8,128)(2,1)S(1)}, u32[]{:S(2)}, u32[]{:S(2)}) collective-permute-start(bf16[48,64,128]{2,1,0:T(8,128)(2,1)S(1)} %slice.32), channel_id=1, source_target_pairs={{0,1},{1,0},{2,3},{3,2},{4,5},{5,4},{6,7},{7,6},{8,9},{9,8},{10,11... | collective-permute-start | bytes 2359304 | tf_op jit(solution)/shard_map/ppermute | solution.py:526
  4.4 0.1 collective-permute-start.1
  4.4 1.1 %slice.31 = bf16[32,64,128]{2,1,0:T(8,128)(2,1)S(1)} slice(bf16[96,64,128]{2,1,0:T(8,128)(2,1)} %args_1_.4), slice={[48:80], [0:64], [0:128]} | slice | bytes 1048576 | tf_op jit(solution)/shard_map/slice | solution.py:526
  5.5 2.0 %collective-permute-start.2 = (bf16[32,64,128]{2,1,0:T(8,128)(2,1)S(1)}, bf16[32,64,128]{2,1,0:T(8,128)(2,1)S(1)}, u32[]{:S(2)}, u32[]{:S(2)}) collective-permute-start(bf16[32,64,128]{2,1,0:T(8,128)(2,1)S(1)} %slice.31), channel_id=1, source_target_pairs={{0,1},{1,0},{2,3},{3,2},{4,5},{5,4},{6,7},{7,6},{8,9},{9,8},{10,11... | collective-permute-start | bytes 1572872 | tf_op jit(solution)/shard_map/ppermute | solution.py:526
  7.5 8.8 %refs.2 = (bf16[128,336,128]{2,1,0:T(8,128)(2,1)S(1)}, f32[336,128]{1,0:T(8,128)S(1)}) custom-call(bf16[100,3,128,128]{3,2,1,0:T(8,128)(2,1)} %refs.3), custom_call_target="tpu_custom_call" | custom-call | flops 900000000 | bytes 2700000 | tf_op jit(solution)/shard_map/refs/pallas_call | solution.py:165
  16.4 0.8 %prepare.1 = (bf16[16,128,128]{2,1,0:T(8,128)(2,1)S(1)}, bf16[16,128,128]{2,1,0:T(8,128)(2,1)S(1)}, f32[112,192]{1,0:T(8,128)S(1)}, f32[1,192]{1,0:T(1,128)S(1)}, f32[3,112,128]{2,1,0:T(8,128)S(1)}) custom-call(f32[16,128]{1,0:T(8,128)S(1)} %copy-done.3, f32[1,128]{1,0:T(1,128)S(1)} %bitcast.6, s32[192,100]{1,0:T(8,128)S(1)} %copy-done.2, ...), custom_call_target="tpu_custom_call" | custom-call | flops 300000000 | bytes 900000 | tf_op jit(solution)/shard_map/prepare/pallas_call | solution.py:96
  17.2 0.0 collective-permute-done.4.args_4_
  17.2 6.4 %filter.4 = (bf16[128,192,128]{2,1,0:T(8,128)(2,1)S(1)}, bf16[128,192,128]{2,1,0:T(8,128)(2,1)S(1)}, f32[8,128]{1,0:T(8,128)S(1)}) custom-call(s32[96]{0:T(128)S(1)} %copy-done.1, bf16[96,64,128]{2,1,0:T(8,128)(2,1)S(1)} %copy-done, bf16[16,128,128]{2,1,0:T(8,128)(2,1)S(1)} %get-tuple-element.41.args_2_.left, ...), custom_call_target="tpu_custom_call" | custom-call | flops 960000000 | bytes 2880000 | tf_op jit(solution)/shard_map/filter/pallas_call | solution.py:233
  23.6 0.0 collective-permute-done.1.bins.args_0_
  23.6 0.6 pick.1
  24.2 0.0 collective-permute-done.3.refs_0_
  24.3 0.1 fusion
  24.3 0.1 collective-permute-start.5
  24.4 0.5 collective-permute-start.6
  24.9 0.1 collective-permute-start.7
  25.0 1.2 %collective-permute-start = (bf16[16,64,128]{2,1,0:T(8,128)(2,1)S(1)}, bf16[16,64,128]{2,1,0:T(8,128)(2,1)S(1)}, u32[]{:S(2)}, u32[]{:S(2)}) collective-permute-start(bf16[16,64,128]{2,1,0:T(8,128)(2,1)S(1)} %slice.30), channel_id=1, source_target_pairs={{0,1},{1,0},{2,3},{3,2},{4,5},{5,4},{6,7},{7,6},{8,9},{9,8},{10,11... | collective-permute-start | bytes 786440 | tf_op jit(solution)/shard_map/ppermute | solution.py:526
  26.2 0.0 collective-permute-done.5.args_4_
  26.2 0.1 collective-permute-done.6.args_5_
  26.3 0.4 collective-permute-done.7.args_6_
  26.7 2.8 %filter.5 = (bf16[128,192,128]{2,1,0:T(8,128)(2,1)S(1)}, bf16[128,192,128]{2,1,0:T(8,128)(2,1)S(1)}, f32[8,128]{1,0:T(8,128)S(1)}) custom-call(s32[96]{0:T(128)S(1)} %collective-permute-done.1.bins.args_0_, bf16[48,64,128]{2,1,0:T(8,128)(2,1)S(1)} %gate.3.args_1_, ...), custom_call_target="tpu_custom_call", output_to_operand_aliasing={{0}: (7, {}), {1}: (8, {})} | custom-call | flops 480000000 | bytes 1440000 | tf_op jit(solution)/shard_map/filter/pallas_call | solution.py:233
  29.5 4.5 %collective-permute-done.2.refs_0_ = bf16[32,64,128]{2,1,0:T(8,128)(2,1)S(1)} collective-permute-done((bf16[32,64,128]{2,1,0:T(8,128)(2,1)S(1)}, bf16[32,64,128]{2,1,0:T(8,128)(2,1)S(1)}, u32[]{:S(2)}, u32[]{:S(2)}) %collective-permute-start.2) | collective-permute-done | bytes 524320 | tf_op jit(solution)/shard_map/ppermute | solution.py:526
  34.0 0.1 collective-permute-start.10
  34.1 0.5 collective-permute-start.11
  34.6 0.1 collective-permute-start.8
  34.7 0.4 collective-permute-start.9
  35.1 0.3 collective-permute-done.10.args_6_
  35.5 0.2 collective-permute-done.11.args_7_
  35.6 0.3 collective-permute-done.8.args_4_
  36.0 0.2 collective-permute-done.9.args_5_
  36.1 2.1 %filter.6 = (bf16[128,192,128]{2,1,0:T(8,128)(2,1)S(1)}, bf16[128,192,128]{2,1,0:T(8,128)(2,1)S(1)}, f32[8,128]{1,0:T(8,128)S(1)}) custom-call(s32[96]{0:T(128)S(1)} %collective-permute-done.1.bins.args_0_, bf16[32,64,128]{2,1,0:T(8,128)(2,1)S(1)} %gate.4.args_1_, ...), custom_call_target="tpu_custom_call", output_to_operand_aliasing={{0}: (8, {}), {1}: (9, {})} | custom-call | flops 320000000 | bytes 960000 | tf_op jit(solution)/shard_map/filter/pallas_call | solution.py:233
  38.3 1.1 %collective-permute-done.refs_0_ = bf16[16,64,128]{2,1,0:T(8,128)(2,1)S(1)} collective-permute-done((bf16[16,64,128]{2,1,0:T(8,128)(2,1)S(1)}, bf16[16,64,128]{2,1,0:T(8,128)(2,1)S(1)}, u32[]{:S(2)}, u32[]{:S(2)}) %collective-permute-start) | collective-permute-done | bytes 262176 | tf_op jit(solution)/shard_map/ppermute | solution.py:526
  39.4 0.0 collective-permute-start.12
  39.4 1.5 %collective-permute-done.12.args_3_ = bf16[16,64,128]{2,1,0:T(8,128)(2,1)S(1)} collective-permute-done((bf16[16,64,128]{2,1,0:T(8,128)(2,1)S(1)}, bf16[16,64,128]{2,1,0:T(8,128)(2,1)S(1)}, u32[]{:S(2)}, u32[]{:S(2)}) %collective-permute-start.12) | collective-permute-done | bytes 262176 | tf_op jit(solution)/shard_map/ppermute | solution.py:543
  41.0 1.0 %filter.7 = (bf16[128,192,128]{2,1,0:T(8,128)(2,1)S(1)}, bf16[128,192,128]{2,1,0:T(8,128)(2,1)S(1)}) custom-call(bf16[16,64,128]{2,1,0:T(8,128)(2,1)S(1)} %gate.5.args_0_, bf16[16,128,128]{2,1,0:T(8,128)(2,1)S(1)} %get-tuple-element.44.refs_1_.args_1_, ...), custom_call_target="tpu_custom_call", output_to_operand_aliasing={{0}: (4, {}), {1}: (5, {})} | custom-call | flops 160000000 | bytes 480000 | tf_op jit(solution)/shard_map/filter/pallas_call | solution.py:233
  41.9 3.1 %score.1 = (f32[336,192]{1,0:T(8,128)S(1)}, f32[8,192]{1,0:T(8,128)S(1)}) custom-call(bf16[128,192,128]{2,1,0:T(8,128)(2,1)S(1)} %get-tuple-element.54.plain, bf16[128,336,128]{2,1,0:T(8,128)(2,1)S(1)} %get-tuple-element.55.refs, f32[336,128]{1,0:T(8,128)S(1)} %get-tuple-element.40.after.norm, f32[112,192]{1,0:T(8,128)S(1)} %get-tuple-element.56.mask, ...), custom_call_target="tpu_custom_call" | custom-call | flops 500000000 | bytes 1500000 | tf_op jit(solution)/shard_map/score/pallas_call | solution.py:293
  45.0 1.8 %collective-permute-start.13 = (f32[8,192]{1,0:T(8,128)S(1)}, f32[8,192]{1,0:T(8,128)S(1)}, u32[]{:S(2)}, u32[]{:S(2)}) collective-permute-start(f32[8,192]{1,0:T(8,128)S(1)} %get-tuple-element.59.mine), channel_id=1, source_target_pairs={{0,1},{1,0},{2,3},{3,2},{4,5},{5,4},{6,7},{7,6},{8,9},{9,8},{10,11... | collective-permute-start | bytes 18440 | tf_op jit(solution)/shard_map/ppermute | solution.py:552
  46.8 0.2 shares.1
  47.1 1.6 %collective-permute-done.13.other = f32[8,192]{1,0:T(8,128)S(1)} collective-permute-done((f32[8,192]{1,0:T(8,128)S(1)}, f32[8,192]{1,0:T(8,128)S(1)}, u32[]{:S(2)}, u32[]{:S(2)}) %collective-permute-start.13) | collective-permute-done | bytes 6176 | tf_op jit(solution)/shard_map/ppermute | solution.py:552
  48.7 1.3 %sums.3 = (bf16[4,500,128]{2,1,0:T(8,128)(2,1)S(1)}, bf16[2,112,384]{2,1,0:T(8,128)(2,1)S(1)}) custom-call(f32[4,112,192]{2,1,0:T(8,128)S(1)} %shares.1, f32[8,192]{1,0:T(8,128)S(1)} %get-tuple-element.59.mine, f32[8,192]{1,0:T(8,128)S(1)} %collective-permute-done.13.other, bf16[128,192,128]{2,1,0:T(8,128)(2,1)S(1)} %get-tuple-element.54.plain, ...), custom_call_target="tpu_custom_call" | custom-call | flops 400000000 | bytes 1200000 | tf_op jit(solution)/shard_map/sums/pallas_call | solution.py:413
  50.1 1.8 %collective-permute-start.14 = (bf16[4,500,128]{2,1,0:T(8,128)(2,1)S(1)}, bf16[4,500,128]{2,1,0:T(8,128)(2,1)S(1)}, u32[]{:S(2)}, u32[]{:S(2)}) collective-permute-start(bf16[4,500,128]{2,1,0:T(8,128)(2,1)S(1)} %get-tuple-element.63.after), channel_id=1, source_target_pairs={{0,2},{2,0},{4,6},{6,4},{8,10},{10,8},{12,14},{14,12},{1,3},{3,1},... | collective-permute-start | bytes 1536008 | tf_op jit(solution)/shard_map/ppermute | solution.py:556
  51.9 0.8 %sums.4 = (bf16[2,300,128]{2,1,0:T(8,128)(2,1)S(1)}, bf16[2,300,128]{2,1,0:T(8,128)(2,1)S(1)}, bf16[2,300,128]{2,1,0:T(8,128)(2,1)S(1)}) custom-call(bf16[2,112,384]{2,1,0:T(8,128)(2,1)S(1)} %get-tuple-element.62.weights, bf16[128,192,128]{2,1,0:T(8,128)(2,1)S(1)} %get-tuple-element.54.plain, bf16[128,192,128]{2,1,0:T(8,128)(2,1)S(1)} %get-tuple-element.61.turned, ...), custom_call_target="tpu_custom_call" | custom-call | flops 240000000 | bytes 720000 | tf_op jit(solution)/shard_map/sums/pallas_call | solution.py:413
  52.7 2.7 %collective-permute-start.18 = (bf16[2,300,128]{2,1,0:T(8,128)(2,1)S(1)}, bf16[2,300,128]{2,1,0:T(8,128)(2,1)S(1)}, u32[]{:S(2)}, u32[]{:S(2)}) collective-permute-start(bf16[2,300,128]{2,1,0:T(8,128)(2,1)S(1)} %get-tuple-element.71), channel_id=1, source_target_pairs={{0,8},{2,10},{4,12},{6,14},{8,0},{10,2},{12,4},{14,6},{1,9},{3,11}... | collective-permute-start | bytes 460808 | tf_op jit(solution)/shard_map/ppermute | solution.py:556
  55.4 1.4 %collective-permute-start.19 = (bf16[2,300,128]{2,1,0:T(8,128)(2,1)S(1)}, bf16[2,300,128]{2,1,0:T(8,128)(2,1)S(1)}, u32[]{:S(2)}, u32[]{:S(2)}) collective-permute-start(bf16[2,300,128]{2,1,0:T(8,128)(2,1)S(1)} %get-tuple-element.72), channel_id=1, source_target_pairs={{0,12},{2,14},{4,8},{6,10},{8,4},{10,6},{12,0},{14,2},{1,13},{3,15... | collective-permute-start | bytes 460808 | tf_op jit(solution)/shard_map/ppermute | solution.py:556
  56.7 0.2 collective-permute-start.20
  57.0 1.6 %sums.5 = (f32[4,500,128]{2,1,0:T(8,128)S(1)}, f32[2,300,128]{2,1,0:T(8,128)S(1)}) custom-call(bf16[2,112,384]{2,1,0:T(8,128)(2,1)S(1)} %get-tuple-element.62.weights, bf16[128,192,128]{2,1,0:T(8,128)(2,1)S(1)} %get-tuple-element.54.plain, bf16[128,192,128]{2,1,0:T(8,128)(2,1)S(1)} %get-tuple-element.61.turned, bf16[2,300,128]{2,1,0:T(8,128)(2,1)S(1)} %get-tuple-element.64.after), custom_call_target="tpu_custom_call" | custom-call | flops 400000000 | bytes 1200000 | tf_op jit(solution)/shard_map/sums/pallas_call | solution.py:413
  58.5 4.3 %collective-permute-done.14.got = bf16[4,500,128]{2,1,0:T(8,128)(2,1)S(1)} collective-permute-done((bf16[4,500,128]{2,1,0:T(8,128)(2,1)S(1)}, bf16[4,500,128]{2,1,0:T(8,128)(2,1)S(1)}, u32[]{:S(2)}, u32[]{:S(2)}) %collective-permute-start.14) | collective-permute-done | bytes 512032 | tf_op jit(solution)/shard_map/ppermute | solution.py:556
  62.8 0.1 fold.1
  62.9 3.9 %collective-permute-start.15 = (bf16[1,500,128]{2,1,0:T(8,128)(2,1)S(1)}, bf16[1,500,128]{2,1,0:T(8,128)(2,1)S(1)}, u32[]{:S(2)}, u32[]{:S(2)}) collective-permute-start(bf16[1,500,128]{2,1,0:T(8,128)(2,1)S(1)} %get-tuple-element.67), channel_id=1, source_target_pairs={{0,12},{2,14},{4,8},{6,10},{8,4},{10,6},{12,0},{14,2},{1,13},{3,15... | collective-permute-start | bytes 384008 | tf_op jit(solution)/shard_map/ppermute | solution.py:556
  66.8 0.0 collective-permute-start.16
  66.8 0.0 collective-permute-done.18.rest_0_
  66.8 0.6 collective-permute-start.17
  67.5 0.0 collective-permute-done.19.rest_1_
  67.5 0.0 collective-permute-done.20.rest_2_
  67.5 0.1 gather.1
  67.6 1.7 %collective-permute-start.21 = (bf16[1,300,128]{2,1,0:T(8,128)(2,1)S(1)}, bf16[1,300,128]{2,1,0:T(8,128)(2,1)S(1)}, u32[]{:S(2)}, u32[]{:S(2)}) collective-permute-start(bf16[1,300,128]{2,1,0:T(8,128)(2,1)S(1)} %get-tuple-element.74), channel_id=1, source_target_pairs={{0,2},{2,0},{4,6},{6,4},{8,10},{10,8},{12,14},{14,12},{1,3},{3,1},... | collective-permute-start | bytes 230408 | tf_op jit(solution)/shard_map/ppermute | solution.py:556
  69.3 2.8 %collective-permute-done.21.args_5_ = bf16[1,300,128]{2,1,0:T(8,128)(2,1)S(1)} collective-permute-done((bf16[1,300,128]{2,1,0:T(8,128)(2,1)S(1)}, bf16[1,300,128]{2,1,0:T(8,128)(2,1)S(1)}, u32[]{:S(2)}, u32[]{:S(2)}) %collective-permute-start.21) | collective-permute-done | bytes 76832 | tf_op jit(solution)/shard_map/ppermute | solution.py:556
  72.0 0.0 collective-permute-done.15.args_1_
  72.0 0.2 collective-permute-done.16.args_2_
  72.2 7.2 %collective-permute-done.17.args_3_ = bf16[1,500,128]{2,1,0:T(8,128)(2,1)S(1)} collective-permute-done((bf16[1,500,128]{2,1,0:T(8,128)(2,1)S(1)}, bf16[1,500,128]{2,1,0:T(8,128)(2,1)S(1)}, u32[]{:S(2)}, u32[]{:S(2)}) %collective-permute-start.17) | collective-permute-done | bytes 128032 | tf_op jit(solution)/shard_map/ppermute | solution.py:556
  79.4 0.9 %finish.1 = f32[800,128]{1,0:T(8,128)} custom-call(f32[1,500,128]{2,1,0:T(8,128)S(1)} %get-tuple-element.66.args_0_, bf16[1,500,128]{2,1,0:T(8,128)(2,1)S(1)} %collective-permute-done.15.args_1_, bf16[1,500,128]{2,1,0:T(8,128)(2,1)S(1)} %collective-permute-done.16.args_2_, bf16[1,500,128]{2,1,0:T(8,128)(2,1)S(1)} %collective-permute-done.17.args_3_, ...), custom_call_target="tpu_custom_call" | custom-call | flops 100000000 | bytes 300000 | tf_op jit(solution)/shard_map/finish/pallas_call | solution.py:490
  (17 shorter events, 0.1 us)
Async XLA Ops:
  0.0 16.3 %copy-start.6 = (f32[128]{0:T(128)S(1)}, f32[128]{0:T(128)}, u32[]{:S(2)}) copy-start(f32[128]{0:T(128)} %param.11) | copy-start | bytes 1540
  0.0 16.3 %copy-start.5 = (f32[192]{0:T(256)S(1)}, f32[192]{0:T(256)}, u32[]{:S(2)}) copy-start(f32[192]{0:T(256)} %param.15) | copy-start | bytes 2308
  0.0 16.3 %copy-start.4 = (s32[100,3]{0,1:T(4,128)S(1)}, s32[100,3]{0,1:T(4,128)}, u32[]{:S(2)}) copy-start(s32[100,3]{0,1:T(4,128)} %param.13) | copy-start | bytes 3604
  0.0 16.3 %copy-start.3 = (f32[16,128]{1,0:T(8,128)S(1)}, f32[16,128]{1,0:T(8,128)}, u32[]{:S(2)}) copy-start(f32[16,128]{1,0:T(8,128)} %ctf.1) | copy-start | bytes 24580
  0.0 16.4 %copy-start.2 = (s32[192,100]{1,0:T(8,128)S(1)}, s32[192,100]{1,0:T(8,128)}, u32[]{:S(2)}) copy-start(s32[192,100]{1,0:T(8,128)} %mask.1) | copy-start | bytes 230404
  0.0 17.2 %collective-permute-start.4 = (bf16[96,64,128]{2,1,0:T(8,128)(2,1)}, bf16[96,64,128]{2,1,0:T(8,128)(2,1)S(1)}, u32[]{:S(2)}, u32[]{:S(2)}) collective-permute-start(bf16[96,64,128]{2,1,0:T(8,128)(2,1)} %args_1_.4), channel_id=1, source_target_pairs={{0,16},{16,0},{1,17},{17,1},{2,18},{18,2},{3,19},{19,3},{4,20},{20... | collective-permute-start | bytes 4718600 | tf_op jit(solution)/shard_map/ppermute | solution.py:528
  1.7 15.5 %copy-start = (bf16[96,64,128]{2,1,0:T(8,128)(2,1)S(1)}, bf16[96,64,128]{2,1,0:T(8,128)(2,1)}, u32[]{:S(2)}) copy-start(bf16[96,64,128]{2,1,0:T(8,128)(2,1)} %args_1_.4) | copy-start | bytes 4718596
  1.7 15.5 %copy-start.1 = (s32[96]{0:T(128)S(1)}, s32[96]{0:T(128)}, u32[]{:S(2)}) copy-start(s32[96]{0:T(128)} %args_0_.4) | copy-start | bytes 1156
  1.8 22.5 %collective-permute-start.3 = (bf16[48,64,128]{2,1,0:T(8,128)(2,1)S(1)}, bf16[48,64,128]{2,1,0:T(8,128)(2,1)S(1)}, u32[]{:S(2)}, u32[]{:S(2)}) collective-permute-start(bf16[48,64,128]{2,1,0:T(8,128)(2,1)S(1)} %slice.32), channel_id=1, source_target_pairs={{0,1},{1,0},{2,3},{3,2},{4,5},{5,4},{6,7},{7,6},{8,9},{9,8},{10,11... | collective-permute-start | bytes 2359304 | tf_op jit(solution)/shard_map/ppermute | solution.py:526
  4.4 19.2 %collective-permute-start.1 = (s32[96]{0:T(128)}, s32[96]{0:T(128)S(1)}, u32[]{:S(2)}, u32[]{:S(2)}) collective-permute-start(s32[96]{0:T(128)} %args_0_.4), channel_id=1, source_target_pairs={{0,1},{1,0},{2,3},{3,2},{4,5},{5,4},{6,7},{7,6},{8,9},{9,8},{10,11... | collective-permute-start | bytes 1160 | tf_op jit(solution)/shard_map/ppermute | solution.py:527
  5.5 28.5 %collective-permute-start.2 = (bf16[32,64,128]{2,1,0:T(8,128)(2,1)S(1)}, bf16[32,64,128]{2,1,0:T(8,128)(2,1)S(1)}, u32[]{:S(2)}, u32[]{:S(2)}) collective-permute-start(bf16[32,64,128]{2,1,0:T(8,128)(2,1)S(1)} %slice.31), channel_id=1, source_target_pairs={{0,1},{1,0},{2,3},{3,2},{4,5},{5,4},{6,7},{7,6},{8,9},{9,8},{10,11... | collective-permute-start | bytes 1572872 | tf_op jit(solution)/shard_map/ppermute | solution.py:526
  24.3 1.9 %collective-permute-start.5 = (bf16[16,64,128]{2,1,0:T(8,128)(2,1)S(1)}, bf16[16,64,128]{2,1,0:T(8,128)(2,1)S(1)}, u32[]{:S(2)}, u32[]{:S(2)}) collective-permute-start(bf16[16,64,128]{2,1,0:T(8,128)(2,1)S(1)} %get-tuple-element.77), channel_id=1, source_target_pairs={{0,16},{16,0},{1,17},{17,1},{2,18},{18,2},{3,19},{19,3},{4,20},{20... | collective-permute-start | bytes 786440 | tf_op jit(solution)/shard_map/ppermute | solution.py:543
  24.4 1.9 %collective-permute-start.6 = (bf16[16,64,128]{2,1,0:T(8,128)(2,1)S(1)}, bf16[16,64,128]{2,1,0:T(8,128)(2,1)S(1)}, u32[]{:S(2)}, u32[]{:S(2)}) collective-permute-start(bf16[16,64,128]{2,1,0:T(8,128)(2,1)S(1)} %get-tuple-element.76), channel_id=1, source_target_pairs={{0,16},{16,0},{1,17},{17,1},{2,18},{18,2},{3,19},{19,3},{4,20},{20... | collective-permute-start | bytes 786440 | tf_op jit(solution)/shard_map/ppermute | solution.py:543
  24.9 1.8 %collective-permute-start.7 = (bf16[16,64,128]{2,1,0:T(8,128)(2,1)S(1)}, bf16[16,64,128]{2,1,0:T(8,128)(2,1)S(1)}, u32[]{:S(2)}, u32[]{:S(2)}) collective-permute-start(bf16[16,64,128]{2,1,0:T(8,128)(2,1)S(1)} %get-tuple-element.75), channel_id=1, source_target_pairs={{0,16},{16,0},{1,17},{17,1},{2,18},{18,2},{3,19},{19,3},{4,20},{20... | collective-permute-start | bytes 786440 | tf_op jit(solution)/shard_map/ppermute | solution.py:543
  25.0 14.4 %collective-permute-start = (bf16[16,64,128]{2,1,0:T(8,128)(2,1)S(1)}, bf16[16,64,128]{2,1,0:T(8,128)(2,1)S(1)}, u32[]{:S(2)}, u32[]{:S(2)}) collective-permute-start(bf16[16,64,128]{2,1,0:T(8,128)(2,1)S(1)} %slice.30), channel_id=1, source_target_pairs={{0,1},{1,0},{2,3},{3,2},{4,5},{5,4},{6,7},{7,6},{8,9},{9,8},{10,11... | collective-permute-start | bytes 786440 | tf_op jit(solution)/shard_map/ppermute | solution.py:526
  34.0 1.4 %collective-permute-start.10 = (bf16[8,64,128]{2,1,0:T(8,128)(2,1)S(1)}, bf16[8,64,128]{2,1,0:T(8,128)(2,1)S(1)}, u32[]{:S(2)}, u32[]{:S(2)}) collective-permute-start(bf16[8,64,128]{2,1,0:T(8,128)(2,1)S(1)} %get-tuple-element.79), channel_id=1, source_target_pairs={{0,16},{16,0},{1,17},{17,1},{2,18},{18,2},{3,19},{19,3},{4,20},{20... | collective-permute-start | bytes 393224 | tf_op jit(solution)/shard_map/ppermute | solution.py:543
  34.1 1.5 %collective-permute-start.11 = (bf16[8,64,128]{2,1,0:T(8,128)(2,1)S(1)}, bf16[8,64,128]{2,1,0:T(8,128)(2,1)S(1)}, u32[]{:S(2)}, u32[]{:S(2)}) collective-permute-start(bf16[8,64,128]{2,1,0:T(8,128)(2,1)S(1)} %get-tuple-element.78), channel_id=1, source_target_pairs={{0,16},{16,0},{1,17},{17,1},{2,18},{18,2},{3,19},{19,3},{4,20},{20... | collective-permute-start | bytes 393224 | tf_op jit(solution)/shard_map/ppermute | solution.py:543
  34.6 1.3 %collective-permute-start.8 = (bf16[8,64,128]{2,1,0:T(8,128)(2,1)S(1)}, bf16[8,64,128]{2,1,0:T(8,128)(2,1)S(1)}, u32[]{:S(2)}, u32[]{:S(2)}) collective-permute-start(bf16[8,64,128]{2,1,0:T(8,128)(2,1)S(1)} %get-tuple-element.81), channel_id=1, source_target_pairs={{0,16},{16,0},{1,17},{17,1},{2,18},{18,2},{3,19},{19,3},{4,20},{20... | collective-permute-start | bytes 393224 | tf_op jit(solution)/shard_map/ppermute | solution.py:543
  34.7 1.5 %collective-permute-start.9 = (bf16[8,64,128]{2,1,0:T(8,128)(2,1)S(1)}, bf16[8,64,128]{2,1,0:T(8,128)(2,1)S(1)}, u32[]{:S(2)}, u32[]{:S(2)}) collective-permute-start(bf16[8,64,128]{2,1,0:T(8,128)(2,1)S(1)} %get-tuple-element.80), channel_id=1, source_target_pairs={{0,16},{16,0},{1,17},{17,1},{2,18},{18,2},{3,19},{19,3},{4,20},{20... | collective-permute-start | bytes 393224 | tf_op jit(solution)/shard_map/ppermute | solution.py:543
  39.4 1.5 %collective-permute-start.12 = (bf16[16,64,128]{2,1,0:T(8,128)(2,1)S(1)}, bf16[16,64,128]{2,1,0:T(8,128)(2,1)S(1)}, u32[]{:S(2)}, u32[]{:S(2)}) collective-permute-start(bf16[16,64,128]{2,1,0:T(8,128)(2,1)S(1)} %gate.5.args_0_), channel_id=1, source_target_pairs={{0,16},{16,0},{1,17},{17,1},{2,18},{18,2},{3,19},{19,3},{4,20},{20... | collective-permute-start | bytes 786440 | tf_op jit(solution)/shard_map/ppermute | solution.py:543
  45.0 3.7 %collective-permute-start.13 = (f32[8,192]{1,0:T(8,128)S(1)}, f32[8,192]{1,0:T(8,128)S(1)}, u32[]{:S(2)}, u32[]{:S(2)}) collective-permute-start(f32[8,192]{1,0:T(8,128)S(1)} %get-tuple-element.59.mine), channel_id=1, source_target_pairs={{0,1},{1,0},{2,3},{3,2},{4,5},{5,4},{6,7},{7,6},{8,9},{9,8},{10,11... | collective-permute-start | bytes 18440 | tf_op jit(solution)/shard_map/ppermute | solution.py:552
  50.1 12.7 %collective-permute-start.14 = (bf16[4,500,128]{2,1,0:T(8,128)(2,1)S(1)}, bf16[4,500,128]{2,1,0:T(8,128)(2,1)S(1)}, u32[]{:S(2)}, u32[]{:S(2)}) collective-permute-start(bf16[4,500,128]{2,1,0:T(8,128)(2,1)S(1)} %get-tuple-element.63.after), channel_id=1, source_target_pairs={{0,2},{2,0},{4,6},{6,4},{8,10},{10,8},{12,14},{14,12},{1,3},{3,1},... | collective-permute-start | bytes 1536008 | tf_op jit(solution)/shard_map/ppermute | solution.py:556
  52.7 14.1 %collective-permute-start.18 = (bf16[2,300,128]{2,1,0:T(8,128)(2,1)S(1)}, bf16[2,300,128]{2,1,0:T(8,128)(2,1)S(1)}, u32[]{:S(2)}, u32[]{:S(2)}) collective-permute-start(bf16[2,300,128]{2,1,0:T(8,128)(2,1)S(1)} %get-tuple-element.71), channel_id=1, source_target_pairs={{0,8},{2,10},{4,12},{6,14},{8,0},{10,2},{12,4},{14,6},{1,9},{3,11}... | collective-permute-start | bytes 460808 | tf_op jit(solution)/shard_map/ppermute | solution.py:556
  55.4 12.1 %collective-permute-start.19 = (bf16[2,300,128]{2,1,0:T(8,128)(2,1)S(1)}, bf16[2,300,128]{2,1,0:T(8,128)(2,1)S(1)}, u32[]{:S(2)}, u32[]{:S(2)}) collective-permute-start(bf16[2,300,128]{2,1,0:T(8,128)(2,1)S(1)} %get-tuple-element.72), channel_id=1, source_target_pairs={{0,12},{2,14},{4,8},{6,10},{8,4},{10,6},{12,0},{14,2},{1,13},{3,15... | collective-permute-start | bytes 460808 | tf_op jit(solution)/shard_map/ppermute | solution.py:556
  56.7 10.7 %collective-permute-start.20 = (bf16[2,300,128]{2,1,0:T(8,128)(2,1)S(1)}, bf16[2,300,128]{2,1,0:T(8,128)(2,1)S(1)}, u32[]{:S(2)}, u32[]{:S(2)}) collective-permute-start(bf16[2,300,128]{2,1,0:T(8,128)(2,1)S(1)} %get-tuple-element.64.after), channel_id=1, source_target_pairs={{0,4},{2,6},{4,0},{6,2},{8,12},{10,14},{12,8},{14,10},{1,5},{3,7},... | collective-permute-start | bytes 460808 | tf_op jit(solution)/shard_map/ppermute | solution.py:556
  62.9 9.1 %collective-permute-start.15 = (bf16[1,500,128]{2,1,0:T(8,128)(2,1)S(1)}, bf16[1,500,128]{2,1,0:T(8,128)(2,1)S(1)}, u32[]{:S(2)}, u32[]{:S(2)}) collective-permute-start(bf16[1,500,128]{2,1,0:T(8,128)(2,1)S(1)} %get-tuple-element.67), channel_id=1, source_target_pairs={{0,12},{2,14},{4,8},{6,10},{8,4},{10,6},{12,0},{14,2},{1,13},{3,15... | collective-permute-start | bytes 384008 | tf_op jit(solution)/shard_map/ppermute | solution.py:556
  66.8 5.4 %collective-permute-start.16 = (bf16[1,500,128]{2,1,0:T(8,128)(2,1)S(1)}, bf16[1,500,128]{2,1,0:T(8,128)(2,1)S(1)}, u32[]{:S(2)}, u32[]{:S(2)}) collective-permute-start(bf16[1,500,128]{2,1,0:T(8,128)(2,1)S(1)} %get-tuple-element.68), channel_id=1, source_target_pairs={{0,4},{2,6},{4,0},{6,2},{8,12},{10,14},{12,8},{14,10},{1,5},{3,7},... | collective-permute-start | bytes 384008 | tf_op jit(solution)/shard_map/ppermute | solution.py:556
  66.8 12.6 %collective-permute-start.17 = (bf16[1,500,128]{2,1,0:T(8,128)(2,1)S(1)}, bf16[1,500,128]{2,1,0:T(8,128)(2,1)S(1)}, u32[]{:S(2)}, u32[]{:S(2)}) collective-permute-start(bf16[1,500,128]{2,1,0:T(8,128)(2,1)S(1)} %get-tuple-element.69), channel_id=1, source_target_pairs={{0,8},{2,10},{4,12},{6,14},{8,0},{10,2},{12,4},{14,6},{1,9},{3,11}... | collective-permute-start | bytes 384008 | tf_op jit(solution)/shard_map/ppermute | solution.py:556
  67.6 4.5 %collective-permute-start.21 = (bf16[1,300,128]{2,1,0:T(8,128)(2,1)S(1)}, bf16[1,300,128]{2,1,0:T(8,128)(2,1)S(1)}, u32[]{:S(2)}, u32[]{:S(2)}) collective-permute-start(bf16[1,300,128]{2,1,0:T(8,128)(2,1)S(1)} %get-tuple-element.74), channel_id=1, source_target_pairs={{0,2},{2,0},{4,6},{6,4},{8,10},{10,8},{12,14},{14,12},{1,3},{3,1},... | collective-permute-start | bytes 230408 | tf_op jit(solution)/shard_map/ppermute | solution.py:556

commit v14 on v12

--- a/solution.py
+++ b/solution.py
@@ -556,7 +556,7 @@
         return lax.ppermute(x, "dom", [(i, i ^ mask) for i in range(dom)])
 
     def spread(sends, bit):
-        far_first = sorted(range(len(sends)), key=lambda m: m == 0)
+        far_first = sorted(range(len(sends)), reverse=True)
         return [along(sends[m], (m + 1) << bit) for m in far_first]
 
     inner, outer = row_pieces(half // dom, dom)

time: 79.2 us -> 80.6 us (1.018)
  starting transfers between devices: 22 us -> 23.8 us
    ppermute x8, starting transfers between devices: 12 us -> 13.9 us  [along(): return lax.ppermute(x, 'dom', [(i, i ^ mask) for i in range(dom)])]
  transfers between devices with their start and end apart: 22 -> 22, of which waited for: 13 -> 13; matrix products, arithmetic and copies ran while one was open for 3% -> 3% of each run, Pallas kernels for 31% -> 30%
where the time goes in v14:
time: 80.6 us; the launch traced here: 80.4 us
  Pallas kernels  30.7 us (38%)
  starting transfers between devices  23.8 us (30%)
  waiting for transfers between devices  23.2 us (29%)
  local copies, waits for them, and re-layouts  2.4 us (3%)
    ppermute x8, starting transfers between devices, along(): return lax.ppermute(x, 'dom', [(i, i ^ mask) for i in range(dom)])  13.9 us
    ppermute x8, waiting for transfers between devices, along(): return lax.ppermute(x, 'dom', [(i, i ^ mask) for i in range(dom)])  12.9 us
    pallas_call x4, Pallas kernels, filter_chunk(): pl.pallas_call(functools.partial(filter_kernel, picked=picked, parts=part...  12.3 us
    pallas_call x1, Pallas kernels, lay_refs(): pl.pallas_call(functools.partial(refs_kernel, padded=padded), grid=(rots,...  8.81 us
    ppermute x3, starting transfers between devices, local(): remote = [over_cls(images[a:a + n]) for a, n in zip(starts, sizes)]  5.82 us
    ppermute x3, waiting for transfers between devices, local(): remote = [over_cls(images[a:a + n]) for a, n in zip(starts, sizes)]  5.61 us
    pallas_call x3, Pallas kernels, call_sums(): pl.pallas_call(kernel, in_specs=[vmem] * len(args) + [pl.BlockSpec(memory...  3.75 us
    pallas_call x1, Pallas kernels, score(): pl.pallas_call(score_kernel, out_shape=(pinned((height, count), F32), pin...  3.1 us
  transfers between devices with their start and end apart: 22, of which 13 were waited for; matrix products, arithmetic and copies ran while one was open for 3% of the time, Pallas kernels for 30%

profile of v14, /device:TPU:0, one launch (start us, length us, event | category | flops | bytes accessed | tf_op | source)
XLA Modules:
  0.0 80.4 jit_solution(6761845748424333437)
XLA Ops:
  0.0 0.5 collective-permute-start.4
  0.5 1.2 %slice.32 = bf16[48,64,128]{2,1,0:T(8,128)(2,1)S(1)} slice(bf16[96,64,128]{2,1,0:T(8,128)(2,1)} %args_1_.4), slice={[0:48], [0:64], [0:128]} | slice | bytes 1572864 | tf_op jit(solution)/shard_map/slice | solution.py:526
  1.7 0.0 copy-start
  1.7 0.0 copy-start.1
  1.8 2.6 %collective-permute-start.3 = (bf16[48,64,128]{2,1,0:T(8,128)(2,1)S(1)}, bf16[48,64,128]{2,1,0:T(8,128)(2,1)S(1)}, u32[]{:S(2)}, u32[]{:S(2)}) collective-permute-start(bf16[48,64,128]{2,1,0:T(8,128)(2,1)S(1)} %slice.32), channel_id=1, source_target_pairs={{0,1},{1,0},{2,3},{3,2},{4,5},{5,4},{6,7},{7,6},{8,9},{9,8},{10,11... | collective-permute-start | bytes 2359304 | tf_op jit(solution)/shard_map/ppermute | solution.py:526
  4.4 0.1 collective-permute-start.1
  4.4 1.1 %slice.31 = bf16[32,64,128]{2,1,0:T(8,128)(2,1)S(1)} slice(bf16[96,64,128]{2,1,0:T(8,128)(2,1)} %args_1_.4), slice={[48:80], [0:64], [0:128]} | slice | bytes 1048576 | tf_op jit(solution)/shard_map/slice | solution.py:526
  5.5 2.0 %collective-permute-start.2 = (bf16[32,64,128]{2,1,0:T(8,128)(2,1)S(1)}, bf16[32,64,128]{2,1,0:T(8,128)(2,1)S(1)}, u32[]{:S(2)}, u32[]{:S(2)}) collective-permute-start(bf16[32,64,128]{2,1,0:T(8,128)(2,1)S(1)} %slice.31), channel_id=1, source_target_pairs={{0,1},{1,0},{2,3},{3,2},{4,5},{5,4},{6,7},{7,6},{8,9},{9,8},{10,11... | collective-permute-start | bytes 1572872 | tf_op jit(solution)/shard_map/ppermute | solution.py:526
  7.5 8.8 %refs.2 = (bf16[128,336,128]{2,1,0:T(8,128)(2,1)S(1)}, f32[336,128]{1,0:T(8,128)S(1)}) custom-call(bf16[100,3,128,128]{3,2,1,0:T(8,128)(2,1)} %refs.3), custom_call_target="tpu_custom_call" | custom-call | flops 900000000 | bytes 2700000 | tf_op jit(solution)/shard_map/refs/pallas_call | solution.py:165
  16.4 0.8 %prepare.1 = (bf16[16,128,128]{2,1,0:T(8,128)(2,1)S(1)}, bf16[16,128,128]{2,1,0:T(8,128)(2,1)S(1)}, f32[112,192]{1,0:T(8,128)S(1)}, f32[1,192]{1,0:T(1,128)S(1)}, f32[3,112,128]{2,1,0:T(8,128)S(1)}) custom-call(f32[16,128]{1,0:T(8,128)S(1)} %copy-done.3, f32[1,128]{1,0:T(1,128)S(1)} %bitcast.6, s32[192,100]{1,0:T(8,128)S(1)} %copy-done.2, ...), custom_call_target="tpu_custom_call" | custom-call | flops 300000000 | bytes 900000 | tf_op jit(solution)/shard_map/prepare/pallas_call | solution.py:96
  17.2 0.0 collective-permute-done.4.args_4_
  17.2 6.4 %filter.4 = (bf16[128,192,128]{2,1,0:T(8,128)(2,1)S(1)}, bf16[128,192,128]{2,1,0:T(8,128)(2,1)S(1)}, f32[8,128]{1,0:T(8,128)S(1)}) custom-call(s32[96]{0:T(128)S(1)} %copy-done.1, bf16[96,64,128]{2,1,0:T(8,128)(2,1)S(1)} %copy-done, bf16[16,128,128]{2,1,0:T(8,128)(2,1)S(1)} %get-tuple-element.41.args_2_.left, ...), custom_call_target="tpu_custom_call" | custom-call | flops 960000000 | bytes 2880000 | tf_op jit(solution)/shard_map/filter/pallas_call | solution.py:233
  23.6 0.0 collective-permute-done.1.bins.args_0_
  23.6 0.6 pick.1
  24.2 0.0 collective-permute-done.3.refs_0_
  24.3 0.1 fusion
  24.3 0.1 collective-permute-start.5
  24.4 0.5 collective-permute-start.6
  24.9 0.1 collective-permute-start.7
  25.0 1.2 %collective-permute-start = (bf16[16,64,128]{2,1,0:T(8,128)(2,1)S(1)}, bf16[16,64,128]{2,1,0:T(8,128)(2,1)S(1)}, u32[]{:S(2)}, u32[]{:S(2)}) collective-permute-start(bf16[16,64,128]{2,1,0:T(8,128)(2,1)S(1)} %slice.30), channel_id=1, source_target_pairs={{0,1},{1,0},{2,3},{3,2},{4,5},{5,4},{6,7},{7,6},{8,9},{9,8},{10,11... | collective-permute-start | bytes 786440 | tf_op jit(solution)/shard_map/ppermute | solution.py:526
  26.2 0.0 collective-permute-done.5.args_4_
  26.2 0.1 collective-permute-done.6.args_5_
  26.3 0.4 collective-permute-done.7.args_6_
  26.7 2.8 %filter.5 = (bf16[128,192,128]{2,1,0:T(8,128)(2,1)S(1)}, bf16[128,192,128]{2,1,0:T(8,128)(2,1)S(1)}, f32[8,128]{1,0:T(8,128)S(1)}) custom-call(s32[96]{0:T(128)S(1)} %collective-permute-done.1.bins.args_0_, bf16[48,64,128]{2,1,0:T(8,128)(2,1)S(1)} %gate.3.args_1_, ...), custom_call_target="tpu_custom_call", output_to_operand_aliasing={{0}: (7, {}), {1}: (8, {})} | custom-call | flops 480000000 | bytes 1440000 | tf_op jit(solution)/shard_map/filter/pallas_call | solution.py:233
  29.5 4.5 %collective-permute-done.2.refs_0_ = bf16[32,64,128]{2,1,0:T(8,128)(2,1)S(1)} collective-permute-done((bf16[32,64,128]{2,1,0:T(8,128)(2,1)S(1)}, bf16[32,64,128]{2,1,0:T(8,128)(2,1)S(1)}, u32[]{:S(2)}, u32[]{:S(2)}) %collective-permute-start.2) | collective-permute-done | bytes 524320 | tf_op jit(solution)/shard_map/ppermute | solution.py:526
  34.0 0.1 collective-permute-start.10
  34.1 0.5 collective-permute-start.11
  34.6 0.1 collective-permute-start.8
  34.7 0.4 collective-permute-start.9
  35.1 0.3 collective-permute-done.10.args_6_
  35.5 0.2 collective-permute-done.11.args_7_
  35.6 0.3 collective-permute-done.8.args_4_
  36.0 0.2 collective-permute-done.9.args_5_
  36.1 2.1 %filter.6 = (bf16[128,192,128]{2,1,0:T(8,128)(2,1)S(1)}, bf16[128,192,128]{2,1,0:T(8,128)(2,1)S(1)}, f32[8,128]{1,0:T(8,128)S(1)}) custom-call(s32[96]{0:T(128)S(1)} %collective-permute-done.1.bins.args_0_, bf16[32,64,128]{2,1,0:T(8,128)(2,1)S(1)} %gate.4.args_1_, ...), custom_call_target="tpu_custom_call", output_to_operand_aliasing={{0}: (8, {}), {1}: (9, {})} | custom-call | flops 320000000 | bytes 960000 | tf_op jit(solution)/shard_map/filter/pallas_call | solution.py:233
  38.3 1.1 %collective-permute-done.refs_0_ = bf16[16,64,128]{2,1,0:T(8,128)(2,1)S(1)} collective-permute-done((bf16[16,64,128]{2,1,0:T(8,128)(2,1)S(1)}, bf16[16,64,128]{2,1,0:T(8,128)(2,1)S(1)}, u32[]{:S(2)}, u32[]{:S(2)}) %collective-permute-start) | collective-permute-done | bytes 262176 | tf_op jit(solution)/shard_map/ppermute | solution.py:526
  39.4 0.0 collective-permute-start.12
  39.4 1.5 %collective-permute-done.12.args_3_ = bf16[16,64,128]{2,1,0:T(8,128)(2,1)S(1)} collective-permute-done((bf16[16,64,128]{2,1,0:T(8,128)(2,1)S(1)}, bf16[16,64,128]{2,1,0:T(8,128)(2,1)S(1)}, u32[]{:S(2)}, u32[]{:S(2)}) %collective-permute-start.12) | collective-permute-done | bytes 262176 | tf_op jit(solution)/shard_map/ppermute | solution.py:543
  41.0 1.0 %filter.7 = (bf16[128,192,128]{2,1,0:T(8,128)(2,1)S(1)}, bf16[128,192,128]{2,1,0:T(8,128)(2,1)S(1)}) custom-call(bf16[16,64,128]{2,1,0:T(8,128)(2,1)S(1)} %gate.5.args_0_, bf16[16,128,128]{2,1,0:T(8,128)(2,1)S(1)} %get-tuple-element.44.refs_1_.args_1_, ...), custom_call_target="tpu_custom_call", output_to_operand_aliasing={{0}: (4, {}), {1}: (5, {})} | custom-call | flops 160000000 | bytes 480000 | tf_op jit(solution)/shard_map/filter/pallas_call | solution.py:233
  41.9 3.1 %score.1 = (f32[336,192]{1,0:T(8,128)S(1)}, f32[8,192]{1,0:T(8,128)S(1)}) custom-call(bf16[128,192,128]{2,1,0:T(8,128)(2,1)S(1)} %get-tuple-element.54.plain, bf16[128,336,128]{2,1,0:T(8,128)(2,1)S(1)} %get-tuple-element.55.refs, f32[336,128]{1,0:T(8,128)S(1)} %get-tuple-element.40.after.norm, f32[112,192]{1,0:T(8,128)S(1)} %get-tuple-element.56.mask, ...), custom_call_target="tpu_custom_call" | custom-call | flops 500000000 | bytes 1500000 | tf_op jit(solution)/shard_map/score/pallas_call | solution.py:293
  45.0 1.8 %collective-permute-start.13 = (f32[8,192]{1,0:T(8,128)S(1)}, f32[8,192]{1,0:T(8,128)S(1)}, u32[]{:S(2)}, u32[]{:S(2)}) collective-permute-start(f32[8,192]{1,0:T(8,128)S(1)} %get-tuple-element.59.mine), channel_id=1, source_target_pairs={{0,1},{1,0},{2,3},{3,2},{4,5},{5,4},{6,7},{7,6},{8,9},{9,8},{10,11... | collective-permute-start | bytes 18440 | tf_op jit(solution)/shard_map/ppermute | solution.py:552
  46.8 0.2 shares.1
  47.1 1.6 %collective-permute-done.13.other = f32[8,192]{1,0:T(8,128)S(1)} collective-permute-done((f32[8,192]{1,0:T(8,128)S(1)}, f32[8,192]{1,0:T(8,128)S(1)}, u32[]{:S(2)}, u32[]{:S(2)}) %collective-permute-start.13) | collective-permute-done | bytes 6176 | tf_op jit(solution)/shard_map/ppermute | solution.py:552
  48.7 1.3 %sums.3 = (bf16[4,500,128]{2,1,0:T(8,128)(2,1)S(1)}, bf16[2,112,384]{2,1,0:T(8,128)(2,1)S(1)}) custom-call(f32[4,112,192]{2,1,0:T(8,128)S(1)} %shares.1, f32[8,192]{1,0:T(8,128)S(1)} %get-tuple-element.59.mine, f32[8,192]{1,0:T(8,128)S(1)} %collective-permute-done.13.other, bf16[128,192,128]{2,1,0:T(8,128)(2,1)S(1)} %get-tuple-element.54.plain, ...), custom_call_target="tpu_custom_call" | custom-call | flops 400000000 | bytes 1200000 | tf_op jit(solution)/shard_map/sums/pallas_call | solution.py:413
  50.1 1.8 %collective-permute-start.14 = (bf16[4,500,128]{2,1,0:T(8,128)(2,1)S(1)}, bf16[4,500,128]{2,1,0:T(8,128)(2,1)S(1)}, u32[]{:S(2)}, u32[]{:S(2)}) collective-permute-start(bf16[4,500,128]{2,1,0:T(8,128)(2,1)S(1)} %get-tuple-element.63.after), channel_id=1, source_target_pairs={{0,2},{2,0},{4,6},{6,4},{8,10},{10,8},{12,14},{14,12},{1,3},{3,1},... | collective-permute-start | bytes 1536008 | tf_op jit(solution)/shard_map/ppermute | solution.py:556
  51.9 0.8 %sums.4 = (bf16[2,300,128]{2,1,0:T(8,128)(2,1)S(1)}, bf16[2,300,128]{2,1,0:T(8,128)(2,1)S(1)}, bf16[2,300,128]{2,1,0:T(8,128)(2,1)S(1)}) custom-call(bf16[2,112,384]{2,1,0:T(8,128)(2,1)S(1)} %get-tuple-element.62.weights, bf16[128,192,128]{2,1,0:T(8,128)(2,1)S(1)} %get-tuple-element.54.plain, bf16[128,192,128]{2,1,0:T(8,128)(2,1)S(1)} %get-tuple-element.61.turned, ...), custom_call_target="tpu_custom_call" | custom-call | flops 240000000 | bytes 720000 | tf_op jit(solution)/shard_map/sums/pallas_call | solution.py:413
  52.7 3.7 %collective-permute-start.18 = (bf16[2,300,128]{2,1,0:T(8,128)(2,1)S(1)}, bf16[2,300,128]{2,1,0:T(8,128)(2,1)S(1)}, u32[]{:S(2)}, u32[]{:S(2)}) collective-permute-start(bf16[2,300,128]{2,1,0:T(8,128)(2,1)S(1)} %get-tuple-element.71), channel_id=1, source_target_pairs={{0,12},{2,14},{4,8},{6,10},{8,4},{10,6},{12,0},{14,2},{1,13},{3,15... | collective-permute-start | bytes 460808 | tf_op jit(solution)/shard_map/ppermute | solution.py:556
  56.4 0.0 collective-permute-start.19
  56.4 0.8 collective-permute-start.20
  57.2 1.6 %sums.5 = (f32[4,500,128]{2,1,0:T(8,128)S(1)}, f32[2,300,128]{2,1,0:T(8,128)S(1)}) custom-call(bf16[2,112,384]{2,1,0:T(8,128)(2,1)S(1)} %get-tuple-element.62.weights, bf16[128,192,128]{2,1,0:T(8,128)(2,1)S(1)} %get-tuple-element.54.plain, bf16[128,192,128]{2,1,0:T(8,128)(2,1)S(1)} %get-tuple-element.61.turned, bf16[2,300,128]{2,1,0:T(8,128)(2,1)S(1)} %get-tuple-element.64.after), custom_call_target="tpu_custom_call" | custom-call | flops 400000000 | bytes 1200000 | tf_op jit(solution)/shard_map/sums/pallas_call | solution.py:413
  58.8 4.1 %collective-permute-done.14.got = bf16[4,500,128]{2,1,0:T(8,128)(2,1)S(1)} collective-permute-done((bf16[4,500,128]{2,1,0:T(8,128)(2,1)S(1)}, bf16[4,500,128]{2,1,0:T(8,128)(2,1)S(1)}, u32[]{:S(2)}, u32[]{:S(2)}) %collective-permute-start.14) | collective-permute-done | bytes 512032 | tf_op jit(solution)/shard_map/ppermute | solution.py:556
  62.8 0.1 fold.1
  62.9 3.9 %collective-permute-start.15 = (bf16[1,500,128]{2,1,0:T(8,128)(2,1)S(1)}, bf16[1,500,128]{2,1,0:T(8,128)(2,1)S(1)}, u32[]{:S(2)}, u32[]{:S(2)}) collective-permute-start(bf16[1,500,128]{2,1,0:T(8,128)(2,1)S(1)} %get-tuple-element.67), channel_id=1, source_target_pairs={{0,12},{2,14},{4,8},{6,10},{8,4},{10,6},{12,0},{14,2},{1,13},{3,15... | collective-permute-start | bytes 384008 | tf_op jit(solution)/shard_map/ppermute | solution.py:556
  66.8 0.0 collective-permute-start.16
  66.8 0.0 collective-permute-done.18.rest_0_
  66.8 3.1 %collective-permute-start.17 = (bf16[1,500,128]{2,1,0:T(8,128)(2,1)S(1)}, bf16[1,500,128]{2,1,0:T(8,128)(2,1)S(1)}, u32[]{:S(2)}, u32[]{:S(2)}) collective-permute-start(bf16[1,500,128]{2,1,0:T(8,128)(2,1)S(1)} %get-tuple-element.69), channel_id=1, source_target_pairs={{0,4},{2,6},{4,0},{6,2},{8,12},{10,14},{12,8},{14,10},{1,5},{3,7},... | collective-permute-start | bytes 384008 | tf_op jit(solution)/shard_map/ppermute | solution.py:556
  70.0 5.0 %collective-permute-done.19.rest_1_ = bf16[2,300,128]{2,1,0:T(8,128)(2,1)S(1)} collective-permute-done((bf16[2,300,128]{2,1,0:T(8,128)(2,1)S(1)}, bf16[2,300,128]{2,1,0:T(8,128)(2,1)S(1)}, u32[]{:S(2)}, u32[]{:S(2)}) %collective-permute-start.19) | collective-permute-done | bytes 153632 | tf_op jit(solution)/shard_map/ppermute | solution.py:556
  75.0 0.0 collective-permute-done.20.rest_2_
  75.0 0.1 gather.1
  75.1 0.6 collective-permute-start.21
  75.7 3.9 %collective-permute-done.21.args_5_ = bf16[1,300,128]{2,1,0:T(8,128)(2,1)S(1)} collective-permute-done((bf16[1,300,128]{2,1,0:T(8,128)(2,1)S(1)}, bf16[1,300,128]{2,1,0:T(8,128)(2,1)S(1)}, u32[]{:S(2)}, u32[]{:S(2)}) %collective-permute-start.21) | collective-permute-done | bytes 76832 | tf_op jit(solution)/shard_map/ppermute | solution.py:556
  79.5 0.0 collective-permute-done.15.args_1_
  79.5 0.0 collective-permute-done.16.args_2_
  79.5 0.0 collective-permute-done.17.args_3_
  79.5 0.9 %finish.1 = f32[800,128]{1,0:T(8,128)} custom-call(f32[1,500,128]{2,1,0:T(8,128)S(1)} %get-tuple-element.66.args_0_, bf16[1,500,128]{2,1,0:T(8,128)(2,1)S(1)} %collective-permute-done.15.args_1_, bf16[1,500,128]{2,1,0:T(8,128)(2,1)S(1)} %collective-permute-done.16.args_2_, bf16[1,500,128]{2,1,0:T(8,128)(2,1)S(1)} %collective-permute-done.17.args_3_, ...), custom_call_target="tpu_custom_call" | custom-call | flops 100000000 | bytes 300000 | tf_op jit(solution)/shard_map/finish/pallas_call | solution.py:490
  (17 shorter events, 0.1 us)
Async XLA Ops:
  0.0 16.3 %copy-start.6 = (f32[128]{0:T(128)S(1)}, f32[128]{0:T(128)}, u32[]{:S(2)}) copy-start(f32[128]{0:T(128)} %param.11) | copy-start | bytes 1540
  0.0 16.3 %copy-start.5 = (f32[192]{0:T(256)S(1)}, f32[192]{0:T(256)}, u32[]{:S(2)}) copy-start(f32[192]{0:T(256)} %param.15) | copy-start | bytes 2308
  0.0 16.3 %copy-start.4 = (s32[100,3]{0,1:T(4,128)S(1)}, s32[100,3]{0,1:T(4,128)}, u32[]{:S(2)}) copy-start(s32[100,3]{0,1:T(4,128)} %param.13) | copy-start | bytes 3604
  0.0 16.3 %copy-start.3 = (f32[16,128]{1,0:T(8,128)S(1)}, f32[16,128]{1,0:T(8,128)}, u32[]{:S(2)}) copy-start(f32[16,128]{1,0:T(8,128)} %ctf.1) | copy-start | bytes 24580
  0.0 16.4 %copy-start.2 = (s32[192,100]{1,0:T(8,128)S(1)}, s32[192,100]{1,0:T(8,128)}, u32[]{:S(2)}) copy-start(s32[192,100]{1,0:T(8,128)} %mask.1) | copy-start | bytes 230404
  0.0 17.2 %collective-permute-start.4 = (bf16[96,64,128]{2,1,0:T(8,128)(2,1)}, bf16[96,64,128]{2,1,0:T(8,128)(2,1)S(1)}, u32[]{:S(2)}, u32[]{:S(2)}) collective-permute-start(bf16[96,64,128]{2,1,0:T(8,128)(2,1)} %args_1_.4), channel_id=1, source_target_pairs={{0,16},{16,0},{1,17},{17,1},{2,18},{18,2},{3,19},{19,3},{4,20},{20... | collective-permute-start | bytes 4718600 | tf_op jit(solution)/shard_map/ppermute | solution.py:528
  1.7 15.5 %copy-start = (bf16[96,64,128]{2,1,0:T(8,128)(2,1)S(1)}, bf16[96,64,128]{2,1,0:T(8,128)(2,1)}, u32[]{:S(2)}) copy-start(bf16[96,64,128]{2,1,0:T(8,128)(2,1)} %args_1_.4) | copy-start | bytes 4718596
  1.7 15.5 %copy-start.1 = (s32[96]{0:T(128)S(1)}, s32[96]{0:T(128)}, u32[]{:S(2)}) copy-start(s32[96]{0:T(128)} %args_0_.4) | copy-start | bytes 1156
  1.8 22.5 %collective-permute-start.3 = (bf16[48,64,128]{2,1,0:T(8,128)(2,1)S(1)}, bf16[48,64,128]{2,1,0:T(8,128)(2,1)S(1)}, u32[]{:S(2)}, u32[]{:S(2)}) collective-permute-start(bf16[48,64,128]{2,1,0:T(8,128)(2,1)S(1)} %slice.32), channel_id=1, source_target_pairs={{0,1},{1,0},{2,3},{3,2},{4,5},{5,4},{6,7},{7,6},{8,9},{9,8},{10,11... | collective-permute-start | bytes 2359304 | tf_op jit(solution)/shard_map/ppermute | solution.py:526
  4.4 19.2 %collective-permute-start.1 = (s32[96]{0:T(128)}, s32[96]{0:T(128)S(1)}, u32[]{:S(2)}, u32[]{:S(2)}) collective-permute-start(s32[96]{0:T(128)} %args_0_.4), channel_id=1, source_target_pairs={{0,1},{1,0},{2,3},{3,2},{4,5},{5,4},{6,7},{7,6},{8,9},{9,8},{10,11... | collective-permute-start | bytes 1160 | tf_op jit(solution)/shard_map/ppermute | solution.py:527
  5.5 28.5 %collective-permute-start.2 = (bf16[32,64,128]{2,1,0:T(8,128)(2,1)S(1)}, bf16[32,64,128]{2,1,0:T(8,128)(2,1)S(1)}, u32[]{:S(2)}, u32[]{:S(2)}) collective-permute-start(bf16[32,64,128]{2,1,0:T(8,128)(2,1)S(1)} %slice.31), channel_id=1, source_target_pairs={{0,1},{1,0},{2,3},{3,2},{4,5},{5,4},{6,7},{7,6},{8,9},{9,8},{10,11... | collective-permute-start | bytes 1572872 | tf_op jit(solution)/shard_map/ppermute | solution.py:526
  24.3 1.9 %collective-permute-start.5 = (bf16[16,64,128]{2,1,0:T(8,128)(2,1)S(1)}, bf16[16,64,128]{2,1,0:T(8,128)(2,1)S(1)}, u32[]{:S(2)}, u32[]{:S(2)}) collective-permute-start(bf16[16,64,128]{2,1,0:T(8,128)(2,1)S(1)} %get-tuple-element.77), channel_id=1, source_target_pairs={{0,16},{16,0},{1,17},{17,1},{2,18},{18,2},{3,19},{19,3},{4,20},{20... | collective-permute-start | bytes 786440 | tf_op jit(solution)/shard_map/ppermute | solution.py:543
  24.4 1.9 %collective-permute-start.6 = (bf16[16,64,128]{2,1,0:T(8,128)(2,1)S(1)}, bf16[16,64,128]{2,1,0:T(8,128)(2,1)S(1)}, u32[]{:S(2)}, u32[]{:S(2)}) collective-permute-start(bf16[16,64,128]{2,1,0:T(8,128)(2,1)S(1)} %get-tuple-element.76), channel_id=1, source_target_pairs={{0,16},{16,0},{1,17},{17,1},{2,18},{18,2},{3,19},{19,3},{4,20},{20... | collective-permute-start | bytes 786440 | tf_op jit(solution)/shard_map/ppermute | solution.py:543
  24.9 1.8 %collective-permute-start.7 = (bf16[16,64,128]{2,1,0:T(8,128)(2,1)S(1)}, bf16[16,64,128]{2,1,0:T(8,128)(2,1)S(1)}, u32[]{:S(2)}, u32[]{:S(2)}) collective-permute-start(bf16[16,64,128]{2,1,0:T(8,128)(2,1)S(1)} %get-tuple-element.75), channel_id=1, source_target_pairs={{0,16},{16,0},{1,17},{17,1},{2,18},{18,2},{3,19},{19,3},{4,20},{20... | collective-permute-start | bytes 786440 | tf_op jit(solution)/shard_map/ppermute | solution.py:543
  25.0 14.4 %collective-permute-start = (bf16[16,64,128]{2,1,0:T(8,128)(2,1)S(1)}, bf16[16,64,128]{2,1,0:T(8,128)(2,1)S(1)}, u32[]{:S(2)}, u32[]{:S(2)}) collective-permute-start(bf16[16,64,128]{2,1,0:T(8,128)(2,1)S(1)} %slice.30), channel_id=1, source_target_pairs={{0,1},{1,0},{2,3},{3,2},{4,5},{5,4},{6,7},{7,6},{8,9},{9,8},{10,11... | collective-permute-start | bytes 786440 | tf_op jit(solution)/shard_map/ppermute | solution.py:526
  34.0 1.4 %collective-permute-start.10 = (bf16[8,64,128]{2,1,0:T(8,128)(2,1)S(1)}, bf16[8,64,128]{2,1,0:T(8,128)(2,1)S(1)}, u32[]{:S(2)}, u32[]{:S(2)}) collective-permute-start(bf16[8,64,128]{2,1,0:T(8,128)(2,1)S(1)} %get-tuple-element.79), channel_id=1, source_target_pairs={{0,16},{16,0},{1,17},{17,1},{2,18},{18,2},{3,19},{19,3},{4,20},{20... | collective-permute-start | bytes 393224 | tf_op jit(solution)/shard_map/ppermute | solution.py:543
  34.1 1.5 %collective-permute-start.11 = (bf16[8,64,128]{2,1,0:T(8,128)(2,1)S(1)}, bf16[8,64,128]{2,1,0:T(8,128)(2,1)S(1)}, u32[]{:S(2)}, u32[]{:S(2)}) collective-permute-start(bf16[8,64,128]{2,1,0:T(8,128)(2,1)S(1)} %get-tuple-element.78), channel_id=1, source_target_pairs={{0,16},{16,0},{1,17},{17,1},{2,18},{18,2},{3,19},{19,3},{4,20},{20... | collective-permute-start | bytes 393224 | tf_op jit(solution)/shard_map/ppermute | solution.py:543
  34.6 1.3 %collective-permute-start.8 = (bf16[8,64,128]{2,1,0:T(8,128)(2,1)S(1)}, bf16[8,64,128]{2,1,0:T(8,128)(2,1)S(1)}, u32[]{:S(2)}, u32[]{:S(2)}) collective-permute-start(bf16[8,64,128]{2,1,0:T(8,128)(2,1)S(1)} %get-tuple-element.81), channel_id=1, source_target_pairs={{0,16},{16,0},{1,17},{17,1},{2,18},{18,2},{3,19},{19,3},{4,20},{20... | collective-permute-start | bytes 393224 | tf_op jit(solution)/shard_map/ppermute | solution.py:543
  34.7 1.5 %collective-permute-start.9 = (bf16[8,64,128]{2,1,0:T(8,128)(2,1)S(1)}, bf16[8,64,128]{2,1,0:T(8,128)(2,1)S(1)}, u32[]{:S(2)}, u32[]{:S(2)}) collective-permute-start(bf16[8,64,128]{2,1,0:T(8,128)(2,1)S(1)} %get-tuple-element.80), channel_id=1, source_target_pairs={{0,16},{16,0},{1,17},{17,1},{2,18},{18,2},{3,19},{19,3},{4,20},{20... | collective-permute-start | bytes 393224 | tf_op jit(solution)/shard_map/ppermute | solution.py:543
  39.4 1.5 %collective-permute-start.12 = (bf16[16,64,128]{2,1,0:T(8,128)(2,1)S(1)}, bf16[16,64,128]{2,1,0:T(8,128)(2,1)S(1)}, u32[]{:S(2)}, u32[]{:S(2)}) collective-permute-start(bf16[16,64,128]{2,1,0:T(8,128)(2,1)S(1)} %gate.5.args_0_), channel_id=1, source_target_pairs={{0,16},{16,0},{1,17},{17,1},{2,18},{18,2},{3,19},{19,3},{4,20},{20... | collective-permute-start | bytes 786440 | tf_op jit(solution)/shard_map/ppermute | solution.py:543
  45.0 3.7 %collective-permute-start.13 = (f32[8,192]{1,0:T(8,128)S(1)}, f32[8,192]{1,0:T(8,128)S(1)}, u32[]{:S(2)}, u32[]{:S(2)}) collective-permute-start(f32[8,192]{1,0:T(8,128)S(1)} %get-tuple-element.59.mine), channel_id=1, source_target_pairs={{0,1},{1,0},{2,3},{3,2},{4,5},{5,4},{6,7},{7,6},{8,9},{9,8},{10,11... | collective-permute-start | bytes 18440 | tf_op jit(solution)/shard_map/ppermute | solution.py:552
  50.1 12.7 %collective-permute-start.14 = (bf16[4,500,128]{2,1,0:T(8,128)(2,1)S(1)}, bf16[4,500,128]{2,1,0:T(8,128)(2,1)S(1)}, u32[]{:S(2)}, u32[]{:S(2)}) collective-permute-start(bf16[4,500,128]{2,1,0:T(8,128)(2,1)S(1)} %get-tuple-element.63.after), channel_id=1, source_target_pairs={{0,2},{2,0},{4,6},{6,4},{8,10},{10,8},{12,14},{14,12},{1,3},{3,1},... | collective-permute-start | bytes 1536008 | tf_op jit(solution)/shard_map/ppermute | solution.py:556
  52.7 14.1 %collective-permute-start.18 = (bf16[2,300,128]{2,1,0:T(8,128)(2,1)S(1)}, bf16[2,300,128]{2,1,0:T(8,128)(2,1)S(1)}, u32[]{:S(2)}, u32[]{:S(2)}) collective-permute-start(bf16[2,300,128]{2,1,0:T(8,128)(2,1)S(1)} %get-tuple-element.71), channel_id=1, source_target_pairs={{0,12},{2,14},{4,8},{6,10},{8,4},{10,6},{12,0},{14,2},{1,13},{3,15... | collective-permute-start | bytes 460808 | tf_op jit(solution)/shard_map/ppermute | solution.py:556
  56.4 18.6 %collective-permute-start.19 = (bf16[2,300,128]{2,1,0:T(8,128)(2,1)S(1)}, bf16[2,300,128]{2,1,0:T(8,128)(2,1)S(1)}, u32[]{:S(2)}, u32[]{:S(2)}) collective-permute-start(bf16[2,300,128]{2,1,0:T(8,128)(2,1)S(1)} %get-tuple-element.72), channel_id=1, source_target_pairs={{0,8},{2,10},{4,12},{6,14},{8,0},{10,2},{12,4},{14,6},{1,9},{3,11}... | collective-permute-start | bytes 460808 | tf_op jit(solution)/shard_map/ppermute | solution.py:556
  56.4 18.6 %collective-permute-start.20 = (bf16[2,300,128]{2,1,0:T(8,128)(2,1)S(1)}, bf16[2,300,128]{2,1,0:T(8,128)(2,1)S(1)}, u32[]{:S(2)}, u32[]{:S(2)}) collective-permute-start(bf16[2,300,128]{2,1,0:T(8,128)(2,1)S(1)} %get-tuple-element.64.after), channel_id=1, source_target_pairs={{0,4},{2,6},{4,0},{6,2},{8,12},{10,14},{12,8},{14,10},{1,5},{3,7},... | collective-permute-start | bytes 460808 | tf_op jit(solution)/shard_map/ppermute | solution.py:556
  62.9 16.6 %collective-permute-start.15 = (bf16[1,500,128]{2,1,0:T(8,128)(2,1)S(1)}, bf16[1,500,128]{2,1,0:T(8,128)(2,1)S(1)}, u32[]{:S(2)}, u32[]{:S(2)}) collective-permute-start(bf16[1,500,128]{2,1,0:T(8,128)(2,1)S(1)} %get-tuple-element.67), channel_id=1, source_target_pairs={{0,12},{2,14},{4,8},{6,10},{8,4},{10,6},{12,0},{14,2},{1,13},{3,15... | collective-permute-start | bytes 384008 | tf_op jit(solution)/shard_map/ppermute | solution.py:556
  66.8 12.7 %collective-permute-start.16 = (bf16[1,500,128]{2,1,0:T(8,128)(2,1)S(1)}, bf16[1,500,128]{2,1,0:T(8,128)(2,1)S(1)}, u32[]{:S(2)}, u32[]{:S(2)}) collective-permute-start(bf16[1,500,128]{2,1,0:T(8,128)(2,1)S(1)} %get-tuple-element.68), channel_id=1, source_target_pairs={{0,8},{2,10},{4,12},{6,14},{8,0},{10,2},{12,4},{14,6},{1,9},{3,11}... | collective-permute-start | bytes 384008 | tf_op jit(solution)/shard_map/ppermute | solution.py:556
  66.8 12.7 %collective-permute-start.17 = (bf16[1,500,128]{2,1,0:T(8,128)(2,1)S(1)}, bf16[1,500,128]{2,1,0:T(8,128)(2,1)S(1)}, u32[]{:S(2)}, u32[]{:S(2)}) collective-permute-start(bf16[1,500,128]{2,1,0:T(8,128)(2,1)S(1)} %get-tuple-element.69), channel_id=1, source_target_pairs={{0,4},{2,6},{4,0},{6,2},{8,12},{10,14},{12,8},{14,10},{1,5},{3,7},... | collective-permute-start | bytes 384008 | tf_op jit(solution)/shard_map/ppermute | solution.py:556
  75.1 4.5 %collective-permute-start.21 = (bf16[1,300,128]{2,1,0:T(8,128)(2,1)S(1)}, bf16[1,300,128]{2,1,0:T(8,128)(2,1)S(1)}, u32[]{:S(2)}, u32[]{:S(2)}) collective-permute-start(bf16[1,300,128]{2,1,0:T(8,128)(2,1)S(1)} %get-tuple-element.74), channel_id=1, source_target_pairs={{0,2},{2,0},{4,6},{6,4},{8,10},{10,8},{12,14},{14,12},{1,3},{3,1},... | collective-permute-start | bytes 230408 | tf_op jit(solution)/shard_map/ppermute | solution.py:556
